TPU v7x, 32 devices: a whole 2x2x4 slice. The times are simulated.
32 devices in a mesh: row: 8 (over y, x, core), col: 4 (over z).
Axes of the slice: x: 2, y: 2, z: 4, core: 2. Of those that a mesh axis runs over, the one named last changes fastest.
Arguments:
- site_tensors: float32 [8, 4, 144, 144], P('row', 'col'), may hold values from -4 to 4
- start_basis: float32 [3, 12, 144], replicated, may hold values from -4 to 4
Outputs:
- coarse: float32 [8, 4, 144, 144], P('row', 'col')
- log_scale: float32 [8, 4], P('row', 'col')
All inputs are finite; a program needn't handle non-finite values.
Results may differ from a plain program's by a relative error of at most 0.03.
Values may be sent and summed in bfloat16 or wider, within the bound.
No kernel may reach another device: no remote copies, remote signals or barrier semaphores. Data moves between devices by JAX's collectives and lax.ppermute only.
A program may use at most 64 MiB of HBM per device.

v0:
```python
import functools

import jax
import jax.numpy as jnp
from jax import lax
from jax.experimental import pallas as pl
from jax.experimental.pallas import tpu as pltpu
from jax.sharding import PartitionSpec as P

CHI = 12
LEVELS = 3
SWEEPS = 2
PAD = 16
SHIFT = 4
ROWS = CHI * PAD
LANES = PAD * PAD
F32 = jnp.float32
BF16 = jnp.bfloat16

NN = (((1,), (0,)), ((), ()))
NT = (((1,), (1,)), ((), ()))
TN = (((0,), (0,)), ((), ()))


def mm(a, b, dims=NN):
    return lax.dot_general(a, b, dims, preferred_element_type=F32)


def iota(shape, dim):
    return lax.broadcasted_iota(jnp.int32, shape, dim)


def group(index):
    return lax.shift_right_logical(index, SHIFT)


def minor(index):
    return lax.bitwise_and(index, PAD - 1)


def one_hot(mask):
    return jnp.where(mask, 1.0, 0.0).astype(BF16)


def swap_matrix(rows=LANES):
    i, j = iota((rows, LANES), 0), iota((rows, LANES), 1)
    return one_hot((group(i) == minor(j)) & (minor(i) == group(j)))


def spread_matrix(mirror):
    i, j = iota((CHI * CHI, LANES), 0), iota((CHI * CHI, LANES), 1)
    s, t = group(j), minor(j)
    source = jnp.where(mirror, t * CHI + s, s * CHI + t)
    return one_hot((i == source) & (s < CHI) & (t < CHI))


def row_spread():
    i, j = iota((ROWS, CHI * CHI), 0), iota((ROWS, CHI * CHI), 1)
    return one_hot((j == minor(i) * CHI + group(i)) & (minor(i) < CHI))


def block_swap(x):
    lane_group = group(iota((PAD, 128), 1))
    zero = jnp.zeros((PAD, 128), x.dtype)
    tiles = {}
    for p in range(PAD):
        for t in range(2):
            src, src_tile = (p & 7) | (t << 3), p >> 3
            if src < CHI:
                tiles[p, t] = x[src * PAD : (src + 1) * PAD, src_tile * 128 : (src_tile + 1) * 128]
            else:
                tiles[p, t] = None
    for bit in range(3):
        step = 1 << bit
        low = lax.bitwise_and(lane_group, step) == 0
        new = {}
        for p in range(PAD):
            if p & step:
                continue
            for t in range(2):
                a, b = tiles[p, t], tiles[p | step, t]
                if a is None and b is None:
                    new[p, t] = new[p | step, t] = None
                    continue
                a_moved = zero if a is None else pltpu.roll(a, 128 - step * PAD, 1)
                b_moved = zero if b is None else pltpu.roll(b, step * PAD, 1)
                a = zero if a is None else a
                b = zero if b is None else b
                new[p, t] = jnp.where(low, a, b_moved)
                new[p | step, t] = jnp.where(low, a_moved, b)
        tiles = new
    rows = []
    for p in range(CHI):
        pair = [zero if tiles[p, t] is None else tiles[p, t] for t in range(2)]
        rows.append(jnp.concatenate(pair, axis=1))
    return jnp.concatenate(rows, axis=0)


def widen(x):
    return jnp.concatenate([x, jnp.zeros((x.shape[0], LANES - x.shape[1]), x.dtype)], axis=1)


def parts3(x):
    a = x.astype(BF16)
    rest = x - a.astype(F32)
    b = rest.astype(BF16)
    c = (rest - b.astype(F32)).astype(BF16)
    return jnp.concatenate([a, b, c], axis=0)


def fold3(y):
    n = y.shape[0] // 3
    return (y[2 * n :] + y[n : 2 * n]) + y[:n]


def gram_body(upper, lower, swap):
    turned = block_swap(mm(upper, swap).astype(BF16))
    row_swap = swap[:ROWS, :ROWS]
    lower_m = mm(swap[:, :ROWS], lower).astype(BF16)
    prod_b = mm(lower_m[:ROWS], lower, NT).astype(BF16)
    prod_b = block_swap(widen(prod_b))
    prod_b = mm(row_swap, prod_b).astype(BF16)
    turned_m = mm(turned, swap).astype(BF16)
    prod_a = mm(turned_m, turned, TN).astype(BF16)
    prod_a = block_swap(prod_a[:ROWS])
    outer = mm(prod_a, prod_b, NT).astype(BF16)
    return block_swap(widen(outer)), turned


def start_body(start, swap):
    start = jnp.concatenate([start, jnp.zeros((PAD - CHI, CHI * CHI), F32)], axis=0)
    pieces = parts3(start)
    spread = spread_matrix(False)
    plain = mm(pieces, spread)
    turned = mm(plain.astype(BF16), swap)
    return fold3(plain), fold3(turned)


def orthonormal(y):
    gram = lax.dot_general(
        y, y, NT, preferred_element_type=F32, precision=lax.Precision.HIGHEST
    )
    width = y.shape[1]
    row = iota((PAD, 128), 0)
    cols = [jnp.broadcast_to(gram[:, k : k + 1], (PAD, 128)) for k in range(CHI)]
    scale = jnp.zeros((PAD, 128), F32)
    for k in range(CHI):
        pivot = jnp.broadcast_to(cols[k][k : k + 1, :], (PAD, 128))
        scale = jnp.where(row == k, lax.rsqrt(pivot), scale)
        factor = jnp.where(row > k, cols[k] / pivot, 0.0)
        for j in range(k + 1, CHI):
            cols[j] = cols[j] - factor * jnp.broadcast_to(cols[j][k : k + 1, :], (PAD, 128))
        wide = jnp.concatenate([factor] * (width // 128), axis=1)
        y = y - wide * jnp.broadcast_to(y[k : k + 1, :], (PAD, width))
    return y * jnp.concatenate([scale] * (width // 128), axis=1)


def iso_body(own, other, start, start_turned, swap):
    total = own.astype(F32) + other.astype(F32)
    i, j = iota((ROWS, LANES), 0), iota((ROWS, LANES), 1)
    diagonal = (group(i) == minor(j)) & (minor(i) == group(j))
    shift = jnp.sum(jnp.where(diagonal, total, 0.0)) / (CHI * CHI)
    pieces = parts3(start)
    image = fold3(mm(pieces, own, NT) + mm(pieces, other, NT))
    image = widen(image) + shift * start_turned
    basis = orthonormal(image)
    pieces = parts3(basis)
    image = fold3(mm(pieces[:, :ROWS], own) + mm(pieces[:, :ROWS], other))
    image = image + shift * fold3(mm(pieces, swap))
    return orthonormal(image).astype(BF16)


def first_second(turned, lower, left, second_ref):
    lane = iota((PAD, LANES), 1)
    masked = [jnp.where(group(lane) == k, left.astype(F32), 0.0) for k in range(CHI)]
    masked = jnp.concatenate(masked, axis=0).astype(BF16)
    i, j = iota((LANES, LANES), 0), iota((LANES, LANES), 1)
    values = mm(masked, one_hot(minor(i) == group(j)))
    eye = minor(lane) == iota((PAD, LANES), 0)
    for a in range(CHI):
        blocks = []
        for k in range(CHI):
            line = jnp.broadcast_to(values[k * PAD + a : k * PAD + a + 1, :], (PAD, LANES))
            blocks.append(jnp.where(eye, line, 0.0).astype(BF16))
        kron = jnp.concatenate(blocks, axis=0)
        first = mm(turned[:, :ROWS], kron).astype(BF16)
        second = mm(first[:, :ROWS], lower).astype(BF16)
        for k in range(CHI):
            second_ref[a * PAD : (a + 1) * PAD, k * LANES : (k + 1) * LANES] = second[
                k * PAD : (k + 1) * PAD, :
            ]


def third(second_ref, right, kron_ref):
    tile = one_hot(minor(iota((PAD, LANES), 1)) == iota((PAD, LANES), 0))
    values = mm(right, tile, TN)
    lane_group = group(iota((PAD, LANES), 1))
    for k in range(CHI):
        block = values[k * PAD : (k + 1) * PAD, :]
        for d in range(PAD):
            kept = jnp.where(lane_group == d, block, 0.0) if d < CHI else jnp.zeros_like(block)
            start = k * LANES + d * PAD
            kron_ref[start : start + PAD, :] = kept.astype(BF16)
    return mm(second_ref[...], kron_ref[...])


def pick(is_upper, own, other):
    return jnp.where(is_upper, own, other), jnp.where(is_upper, other, own)


def first_gram_kernel(role, own, other, start, lower_o, turned_o, gram_o, starts_o):
    mirror, is_upper = role[0] != 0, role[1] != 0
    swap = swap_matrix()
    rows, spread = row_spread(), spread_matrix(mirror)

    def placed(site):
        spaced = mm(rows, site[...].astype(BF16)).astype(BF16)
        return block_swap(mm(spaced, spread).astype(BF16))

    upper, lower = pick(is_upper, placed(own), placed(other))
    gram, turned = gram_body(upper, lower, swap)
    lower_o[...], turned_o[...], gram_o[...] = lower, turned, gram
    for level in range(LEVELS):
        plain, turn = start_body(start[level], swap)
        starts_o[level, :PAD], starts_o[level, PAD:] = plain, turn


def gram_kernel(role, own, other, lower_o, turned_o, gram_o):
    upper, lower = pick(role[0] != 0, own[...], other[...])
    gram, turned = gram_body(upper, lower, swap_matrix())
    lower_o[...], turned_o[...], gram_o[...] = lower, turned, gram


def iso_kernel(own, other, starts, iso_o):
    iso_o[...] = iso_body(own[...], other[...], starts[:PAD], starts[PAD:], swap_matrix())


def second_kernel(turned, lower, left, second_o):
    first_second(turned[...], lower[...], left[...], second_o)


def scaled(merged):
    mean = jnp.sum(merged * merged) / (CHI**4)
    return jnp.sqrt(jnp.full((1, LANES), mean) + 1e-06)


def third_kernel(second, right, log_in, next_o, log_o, kron):
    merged = third(second, right[...], kron)
    norm = scaled(merged)
    next_o[...] = (merged / norm).astype(BF16)
    log_o[...] = log_in[...] + jnp.log(norm)


def last_kernel(role, second, right, log_in, coarse_o, log_o, kron):
    merged = third(second, right[...], kron)
    norm = scaled(merged)
    log_o[...] = log_in[...] + jnp.log(norm)
    wide = block_swap(merged / norm)
    spread, rows = spread_matrix(role[0] != 0), row_spread()
    total = jnp.zeros((CHI * CHI, CHI * CHI), F32)
    high = wide.astype(BF16)
    low = (wide - high.astype(F32)).astype(BF16)
    for part in (high, low):
        narrow = mm(part, spread, NT).astype(BF16)
        total = total + mm(rows, narrow, TN)
    coarse_o[...] = total


def call(kernel, outs, smem, n_in, scratch=()):
    specs = [pl.BlockSpec(memory_space=pltpu.VMEM)] * n_in
    if smem:
        specs[0] = pl.BlockSpec(memory_space=pltpu.SMEM)
    return pl.pallas_call(
        kernel,
        out_shape=[jax.ShapeDtypeStruct(s, d) for s, d in outs],
        in_specs=specs,
        out_specs=[pl.BlockSpec(memory_space=pltpu.VMEM)] * len(outs),
        scratch_shapes=list(scratch),
    )


def from_partner(array, stride):
    count = lax.axis_size("row")
    return lax.ppermute(array, "row", [(i, i ^ 1 << stride) for i in range(count)])


def from_bond(array):
    rows, cols = lax.axis_size("row"), lax.axis_size("col")
    pairs = []
    for i in range(rows):
        for c in range(cols):
            target = (c - 1) % cols if i % 2 == 0 else (c + 1) % cols
            pairs.append((i * cols + c, (i ^ 1) * cols + target))
    return lax.ppermute(array, ("row", "col"), pairs)


def per_device(site_tensors, start_basis):
    square = CHI * CHI
    row = lax.axis_index("row")
    mirror = row % 2
    mat = ((ROWS, LANES), BF16)
    kron = [pltpu.VMEM((CHI * LANES, LANES), BF16)]
    log_total = jnp.zeros((1, LANES), F32)
    own = site_tensors[0, 0]
    for level in range(LEVELS):
        other = from_partner(own, level)
        is_upper = 1 - row // 2**level % 2
        if level == 0:
            role = jnp.stack([mirror, is_upper]).astype(jnp.int32)
            lower, turned, gram, starts = call(
                first_gram_kernel,
                [mat, mat, mat, ((LEVELS, 2 * PAD, LANES), F32)],
                True,
                4,
            )(role, own, other, start_basis)
        else:
            role = is_upper.reshape(1).astype(jnp.int32)
            lower, turned, gram = call(gram_kernel, [mat, mat, mat], True, 3)(role, own, other)
        gram_other = from_bond(gram)
        (left,) = call(iso_kernel, [((PAD, LANES), BF16)], False, 3)(gram, gram_other, starts[level])
        right = from_partner(left, 0)
        (second,) = call(second_kernel, [((ROWS, CHI * LANES), BF16)], False, 3)(turned, lower, left)
        if level < LEVELS - 1:
            own, log_total = call(third_kernel, [mat, ((1, LANES), F32)], False, 3, kron)(
                second, right, log_total
            )
        else:
            role = mirror.reshape(1).astype(jnp.int32)
            coarse, log_total = call(
                last_kernel, [((square, square), F32), ((1, LANES), F32)], True, 4, kron
            )(role, second, right, log_total)
    return (coarse[None, None], log_total[:, :1])


def solution(mesh):
    return jax.shard_map(
        per_device,
        mesh=mesh,
        in_specs=(P("row", "col", None, None), P()),
        out_specs=(P("row", "col", None, None), P("row", "col")),
        check_vma=False,
    )
```

profile of v0, /device:TPU:0, one launch (start us, length us, event | category | flops | bytes accessed | tf_op | source)
XLA Modules:
  0.0 76.5 jit_solution(6859868795191413764)
XLA Ops:
  0.6 0.6 collective-permute-start
  1.2 0.6 pad_add_fusion.role
  1.8 0.6 collective-permute-done.other
  2.4 0.0 copy-start
  2.4 0.7 copy-done
  3.1 3.6 %shard_map.41 = (bf16[192,256]{1,0:T(8,128)(2,1)}, bf16[192,256]{1,0:T(8,128)(2,1)}, bf16[192,256]{1,0:T(8,128)(2,1)}, f32[3,32,256]{2,1,0:T(8,128)}) custom-call(s32[2]{0:T(128)} %pad_add_fusion.role, f32[144,144]{1,0:T(8,128)} %bitcast.13, f32[144,144]{1,0:T(8,128)} %copy-done, f32[3,12,144]{2,1,0:T(8,128)} %start.1), custom_call_target="tpu_custom_call" | custom-call | tf_op jit(solution)/shard_map/pallas_call | solution.py:310
  6.7 4.7 %collective-permute-start.1 = (bf16[192,256]{1,0:T(8,128)(2,1)}, bf16[192,256]{1,0:T(8,128)(2,1)S(1)}, u32[]{:S(2)}, u32[]{:S(2)}) collective-permute-start(bf16[192,256]{1,0:T(8,128)(2,1)} %get-tuple-element.20.own), channel_id=1, source_target_pairs={{0,7},{1,4},{2,5},{3,6},{4,1},{5,2},{6,3},{7,0},{8,15},{9,12},{10,... | collective-permute-start | bytes 294920 | tf_op jit(solution)/shard_map/ppermute | solution.py:294
  11.4 1.4 %slice_bitcast_fusion = (f32[32,256]{1,0:T(8,128)}, f32[32,256]{1,0:T(8,128)}, f32[32,256]{1,0:T(8,128)}) fusion(f32[3,32,256]{2,1,0:T(8,128)} %get-tuple-element.21), kind=kLoop, calls=%fused_computation | loop fusion | bytes 196608 | tf_op jit(solution)/shard_map/squeeze | solution.py:320
  12.8 1.4 %collective-permute-done.1.other = bf16[192,256]{1,0:T(8,128)(2,1)S(1)} collective-permute-done((bf16[192,256]{1,0:T(8,128)(2,1)}, bf16[192,256]{1,0:T(8,128)(2,1)S(1)}, u32[]{:S(2)}, u32[]{:S(2)}) %collective-permute-start.1) | collective-permute-done | bytes 98336 | tf_op jit(solution)/shard_map/ppermute | solution.py:294
  14.2 0.0 copy-start.3
  14.2 0.6 copy-done.3
  14.8 2.7 %shard_map.42.left = bf16[16,256]{1,0:T(8,128)(2,1)} custom-call(bf16[192,256]{1,0:T(8,128)(2,1)} %get-tuple-element.20.own, bf16[192,256]{1,0:T(8,128)(2,1)} %copy-done.3, f32[32,256]{1,0:T(8,128)} %get-tuple-element.36.starts), custom_call_target="tpu_custom_call" | custom-call | tf_op jit(solution)/shard_map/pallas_call | solution.py:320
  17.6 0.0 collective-permute-start.2
  17.6 3.0 %shard_map.43.second = bf16[192,3072]{1,0:T(8,128)(2,1)} custom-call(bf16[192,256]{1,0:T(8,128)(2,1)} %get-tuple-element.18.turned, bf16[192,256]{1,0:T(8,128)(2,1)} %get-tuple-element.19.lower, bf16[16,256]{1,0:T(8,128)(2,1)} %shard_map.42.left), custom_call_target="tpu_custom_call" | custom-call | tf_op jit(solution)/shard_map/pallas_call | solution.py:322
  20.6 0.0 collective-permute-done.2.right
  20.6 0.0 copy-start.7
  20.6 0.6 broadcast_in_dim.6.log_in
  21.2 0.0 copy-done.7
  21.2 2.8 %shard_map.44 = (bf16[192,256]{1,0:T(8,128)(2,1)}, f32[1,256]{1,0:T(1,128)}) custom-call(bf16[192,3072]{1,0:T(8,128)(2,1)} %shard_map.43.second, bf16[16,256]{1,0:T(8,128)(2,1)} %copy-done.7, f32[1,256]{1,0:T(1,128)} %broadcast_in_dim.6.log_in), custom_call_target="tpu_custom_call" | custom-call | tf_op jit(solution)/shard_map/pallas_call | solution.py:324
  24.0 1.9 %collective-permute-start.3 = (bf16[192,256]{1,0:T(8,128)(2,1)}, bf16[192,256]{1,0:T(8,128)(2,1)S(1)}, u32[]{:S(2)}, u32[]{:S(2)}) collective-permute-start(bf16[192,256]{1,0:T(8,128)(2,1)} %get-tuple-element.22.own), channel_id=1, source_target_pairs={{0,8},{4,12},{8,0},{12,4},{16,24},{20,28},{24,16},{28,20},{1,9},{5... | collective-permute-start | bytes 294920 | tf_op jit(solution)/shard_map/ppermute | solution.py:284
  25.8 3.7 %collective-permute-done.3.other = bf16[192,256]{1,0:T(8,128)(2,1)S(1)} collective-permute-done((bf16[192,256]{1,0:T(8,128)(2,1)}, bf16[192,256]{1,0:T(8,128)(2,1)S(1)}, u32[]{:S(2)}, u32[]{:S(2)}) %collective-permute-start.3) | collective-permute-done | bytes 98336 | tf_op jit(solution)/shard_map/ppermute | solution.py:284
  29.5 0.0 copy-start.2
  29.5 0.6 copy-done.2
  30.2 3.0 %shard_map.45 = (bf16[192,256]{1,0:T(8,128)(2,1)}, bf16[192,256]{1,0:T(8,128)(2,1)}, bf16[192,256]{1,0:T(8,128)(2,1)}) custom-call(s32[1]{0:T(128)} %bitcast.2.role, bf16[192,256]{1,0:T(8,128)(2,1)} %get-tuple-element.22.own, bf16[192,256]{1,0:T(8,128)(2,1)} %copy-done.2), custom_call_target="tpu_custom_call" | custom-call | tf_op jit(solution)/shard_map/pallas_call | solution.py:318
  33.2 1.7 %collective-permute-start.4 = (bf16[192,256]{1,0:T(8,128)(2,1)}, bf16[192,256]{1,0:T(8,128)(2,1)S(1)}, u32[]{:S(2)}, u32[]{:S(2)}) collective-permute-start(bf16[192,256]{1,0:T(8,128)(2,1)} %get-tuple-element.25.own), channel_id=1, source_target_pairs={{0,7},{1,4},{2,5},{3,6},{4,1},{5,2},{6,3},{7,0},{8,15},{9,12},{10,... | collective-permute-start | bytes 294920 | tf_op jit(solution)/shard_map/ppermute | solution.py:294
  34.9 5.1 %collective-permute-done.4.other = bf16[192,256]{1,0:T(8,128)(2,1)S(1)} collective-permute-done((bf16[192,256]{1,0:T(8,128)(2,1)}, bf16[192,256]{1,0:T(8,128)(2,1)S(1)}, u32[]{:S(2)}, u32[]{:S(2)}) %collective-permute-start.4) | collective-permute-done | bytes 98336 | tf_op jit(solution)/shard_map/ppermute | solution.py:294
  40.0 0.0 copy-start.5
  40.0 0.6 copy-done.5
  40.7 2.7 %shard_map.46.left = bf16[16,256]{1,0:T(8,128)(2,1)} custom-call(bf16[192,256]{1,0:T(8,128)(2,1)} %get-tuple-element.25.own, bf16[192,256]{1,0:T(8,128)(2,1)} %copy-done.5, f32[32,256]{1,0:T(8,128)} %get-tuple-element.35.starts), custom_call_target="tpu_custom_call" | custom-call | tf_op jit(solution)/shard_map/pallas_call | solution.py:320
  43.4 0.0 collective-permute-start.5
  43.4 3.0 %shard_map.47.second = bf16[192,3072]{1,0:T(8,128)(2,1)} custom-call(bf16[192,256]{1,0:T(8,128)(2,1)} %get-tuple-element.23.turned, bf16[192,256]{1,0:T(8,128)(2,1)} %get-tuple-element.24.lower, bf16[16,256]{1,0:T(8,128)(2,1)} %shard_map.46.left), custom_call_target="tpu_custom_call" | custom-call | tf_op jit(solution)/shard_map/pallas_call | solution.py:322
  46.4 0.0 collective-permute-done.5.right
  46.4 0.0 copy-start.8
  46.4 0.6 copy-done.8
  47.0 2.8 %shard_map.48 = (bf16[192,256]{1,0:T(8,128)(2,1)}, f32[1,256]{1,0:T(1,128)}) custom-call(bf16[192,3072]{1,0:T(8,128)(2,1)} %shard_map.47.second, bf16[16,256]{1,0:T(8,128)(2,1)} %copy-done.8, f32[1,256]{1,0:T(1,128)} %get-tuple-element.26.log_in), custom_call_target="tpu_custom_call" | custom-call | tf_op jit(solution)/shard_map/pallas_call | solution.py:324
  49.8 1.5 %collective-permute-start.6 = (bf16[192,256]{1,0:T(8,128)(2,1)}, bf16[192,256]{1,0:T(8,128)(2,1)S(1)}, u32[]{:S(2)}, u32[]{:S(2)}) collective-permute-start(bf16[192,256]{1,0:T(8,128)(2,1)} %get-tuple-element.27.own), channel_id=1, source_target_pairs={{0,16},{4,20},{8,24},{12,28},{16,0},{20,4},{24,8},{28,12},{1,17},{... | collective-permute-start | bytes 294920 | tf_op jit(solution)/shard_map/ppermute | solution.py:284
  51.3 3.9 %collective-permute-done.6.other = bf16[192,256]{1,0:T(8,128)(2,1)S(1)} collective-permute-done((bf16[192,256]{1,0:T(8,128)(2,1)}, bf16[192,256]{1,0:T(8,128)(2,1)S(1)}, u32[]{:S(2)}, u32[]{:S(2)}) %collective-permute-start.6) | collective-permute-done | bytes 98336 | tf_op jit(solution)/shard_map/ppermute | solution.py:284
  55.2 0.0 copy-start.1
  55.2 0.6 copy-done.1
  55.8 3.0 %shard_map.49 = (bf16[192,256]{1,0:T(8,128)(2,1)}, bf16[192,256]{1,0:T(8,128)(2,1)}, bf16[192,256]{1,0:T(8,128)(2,1)}) custom-call(s32[1]{0:T(128)} %bitcast.1.role, bf16[192,256]{1,0:T(8,128)(2,1)} %get-tuple-element.27.own, bf16[192,256]{1,0:T(8,128)(2,1)} %copy-done.1), custom_call_target="tpu_custom_call" | custom-call | tf_op jit(solution)/shard_map/pallas_call | solution.py:318
  58.9 0.0 collective-permute-start.7
  58.9 6.0 %collective-permute-done.7.other = bf16[192,256]{1,0:T(8,128)(2,1)S(1)} collective-permute-done((bf16[192,256]{1,0:T(8,128)(2,1)}, bf16[192,256]{1,0:T(8,128)(2,1)S(1)}, u32[]{:S(2)}, u32[]{:S(2)}) %collective-permute-start.7) | collective-permute-done | bytes 98336 | tf_op jit(solution)/shard_map/ppermute | solution.py:294
  64.9 0.0 copy-start.4
  64.9 0.6 copy-done.4
  65.5 2.7 %shard_map.50.left = bf16[16,256]{1,0:T(8,128)(2,1)} custom-call(bf16[192,256]{1,0:T(8,128)(2,1)} %get-tuple-element.30.own, bf16[192,256]{1,0:T(8,128)(2,1)} %copy-done.4, f32[32,256]{1,0:T(8,128)} %get-tuple-element.34.starts), custom_call_target="tpu_custom_call" | custom-call | tf_op jit(solution)/shard_map/pallas_call | solution.py:320
  68.3 0.0 collective-permute-start.8
  68.3 3.0 %shard_map.51.second = bf16[192,3072]{1,0:T(8,128)(2,1)} custom-call(bf16[192,256]{1,0:T(8,128)(2,1)} %get-tuple-element.28.turned, bf16[192,256]{1,0:T(8,128)(2,1)} %get-tuple-element.29.lower, bf16[16,256]{1,0:T(8,128)(2,1)} %shard_map.50.left), custom_call_target="tpu_custom_call" | custom-call | tf_op jit(solution)/shard_map/pallas_call | solution.py:322
  71.3 0.0 collective-permute-done.8.right
  71.3 0.0 copy-start.6
  71.3 0.6 copy-done.6
  71.9 3.5 %shard_map.52 = (f32[144,144]{1,0:T(8,128)}, f32[1,256]{1,0:T(1,128)}) custom-call(s32[1]{0:T(128)} %bitcast.role, bf16[192,3072]{1,0:T(8,128)(2,1)} %shard_map.51.second, bf16[16,256]{1,0:T(8,128)(2,1)} %copy-done.6, f32[1,256]{1,0:T(1,128)} %get-tuple-element.31.log_in), custom_call_target="tpu_custom_call" | custom-call | tf_op jit(solution)/shard_map/pallas_call | solution.py:329
  75.4 1.1 %slice.15 = f32[1,1]{1,0:T(1,128)} slice(f32[1,256]{1,0:T(1,128)} %get-tuple-element.33), slice={[0:1], [0:1]} | slice | bytes 8 | tf_op jit(solution)/shard_map/slice | solution.py:332
Async XLA Ops:
  0.6 1.8 %collective-permute-start = (f32[144,144]{1,0:T(8,128)}, f32[144,144]{1,0:T(8,128)S(1)}, u32[]{:S(2)}, u32[]{:S(2)}) collective-permute-start(f32[144,144]{1,0:T(8,128)} %bitcast.12), channel_id=1, source_target_pairs={{0,4},{4,0},{8,12},{12,8},{16,20},{20,16},{24,28},{28,24},{1,5},{5... | collective-permute-start | bytes 248840 | tf_op jit(solution)/shard_map/ppermute | solution.py:284
  2.4 0.7 copy-start
  6.7 7.5 %collective-permute-start.1 = (bf16[192,256]{1,0:T(8,128)(2,1)}, bf16[192,256]{1,0:T(8,128)(2,1)S(1)}, u32[]{:S(2)}, u32[]{:S(2)}) collective-permute-start(bf16[192,256]{1,0:T(8,128)(2,1)} %get-tuple-element.20.own), channel_id=1, source_target_pairs={{0,7},{1,4},{2,5},{3,6},{4,1},{5,2},{6,3},{7,0},{8,15},{9,12},{10,... | collective-permute-start | bytes 294920 | tf_op jit(solution)/shard_map/ppermute | solution.py:294
  14.2 0.6 copy-start.3
  17.6 3.0 %collective-permute-start.2 = (bf16[16,256]{1,0:T(8,128)(2,1)}, bf16[16,256]{1,0:T(8,128)(2,1)S(1)}, u32[]{:S(2)}, u32[]{:S(2)}) collective-permute-start(bf16[16,256]{1,0:T(8,128)(2,1)} %shard_map.42.left), channel_id=1, source_target_pairs={{0,4},{4,0},{8,12},{12,8},{16,20},{20,16},{24,28},{28,24},{1,5},{5... | collective-permute-start | bytes 24584 | tf_op jit(solution)/shard_map/ppermute | solution.py:284
  20.6 0.6 copy-start.7
  24.0 5.6 %collective-permute-start.3 = (bf16[192,256]{1,0:T(8,128)(2,1)}, bf16[192,256]{1,0:T(8,128)(2,1)S(1)}, u32[]{:S(2)}, u32[]{:S(2)}) collective-permute-start(bf16[192,256]{1,0:T(8,128)(2,1)} %get-tuple-element.22.own), channel_id=1, source_target_pairs={{0,8},{4,12},{8,0},{12,4},{16,24},{20,28},{24,16},{28,20},{1,9},{5... | collective-permute-start | bytes 294920 | tf_op jit(solution)/shard_map/ppermute | solution.py:284
  29.5 0.6 copy-start.2
  33.2 6.8 %collective-permute-start.4 = (bf16[192,256]{1,0:T(8,128)(2,1)}, bf16[192,256]{1,0:T(8,128)(2,1)S(1)}, u32[]{:S(2)}, u32[]{:S(2)}) collective-permute-start(bf16[192,256]{1,0:T(8,128)(2,1)} %get-tuple-element.25.own), channel_id=1, source_target_pairs={{0,7},{1,4},{2,5},{3,6},{4,1},{5,2},{6,3},{7,0},{8,15},{9,12},{10,... | collective-permute-start | bytes 294920 | tf_op jit(solution)/shard_map/ppermute | solution.py:294
  40.0 0.6 copy-start.5
  43.4 3.0 %collective-permute-start.5 = (bf16[16,256]{1,0:T(8,128)(2,1)}, bf16[16,256]{1,0:T(8,128)(2,1)S(1)}, u32[]{:S(2)}, u32[]{:S(2)}) collective-permute-start(bf16[16,256]{1,0:T(8,128)(2,1)} %shard_map.46.left), channel_id=1, source_target_pairs={{0,4},{4,0},{8,12},{12,8},{16,20},{20,16},{24,28},{28,24},{1,5},{5... | collective-permute-start | bytes 24584 | tf_op jit(solution)/shard_map/ppermute | solution.py:284
  46.4 0.6 copy-start.8
  49.8 5.4 %collective-permute-start.6 = (bf16[192,256]{1,0:T(8,128)(2,1)}, bf16[192,256]{1,0:T(8,128)(2,1)S(1)}, u32[]{:S(2)}, u32[]{:S(2)}) collective-permute-start(bf16[192,256]{1,0:T(8,128)(2,1)} %get-tuple-element.27.own), channel_id=1, source_target_pairs={{0,16},{4,20},{8,24},{12,28},{16,0},{20,4},{24,8},{28,12},{1,17},{... | collective-permute-start | bytes 294920 | tf_op jit(solution)/shard_map/ppermute | solution.py:284
  55.2 0.6 copy-start.1
  58.9 6.1 %collective-permute-start.7 = (bf16[192,256]{1,0:T(8,128)(2,1)}, bf16[192,256]{1,0:T(8,128)(2,1)S(1)}, u32[]{:S(2)}, u32[]{:S(2)}) collective-permute-start(bf16[192,256]{1,0:T(8,128)(2,1)} %get-tuple-element.30.own), channel_id=1, source_target_pairs={{0,7},{1,4},{2,5},{3,6},{4,1},{5,2},{6,3},{7,0},{8,15},{9,12},{10,... | collective-permute-start | bytes 294920 | tf_op jit(solution)/shard_map/ppermute | solution.py:294
  64.9 0.6 copy-start.4
  68.3 3.0 %collective-permute-start.8 = (bf16[16,256]{1,0:T(8,128)(2,1)}, bf16[16,256]{1,0:T(8,128)(2,1)S(1)}, u32[]{:S(2)}, u32[]{:S(2)}) collective-permute-start(bf16[16,256]{1,0:T(8,128)(2,1)} %shard_map.50.left), channel_id=1, source_target_pairs={{0,4},{4,0},{8,12},{12,8},{16,20},{20,16},{24,28},{28,24},{1,5},{5... | collective-permute-start | bytes 24584 | tf_op jit(solution)/shard_map/ppermute | solution.py:284
  71.3 0.6 copy-start.6
where the time goes:
time: 77.1 us; the launch traced here: 76.5 us
  Pallas kernels  35.9 us (47%)
  waiting for transfers between devices  20.7 us (27%)
  starting transfers between devices  10.4 us (13%)
  local copies, waits for them, and re-layouts  8.24 us (11%)
    ppermute x3, waiting for transfers between devices, from_bond(): return lax.ppermute(array, ('row', 'col'), pairs)  12.5 us
    pallas_call x3, Pallas kernels, per_device(): call(second_kernel, [((ROWS, CHI * LANES), BF16)], False, 3)  9.07 us
    ppermute x6, waiting for transfers between devices, from_partner(): lax.ppermute(array, 'row', [(i, i ^ 1 << stride) for i in range(count)])  8.16 us
    pallas_call x3, Pallas kernels, per_device(): call(iso_kernel, [((PAD, LANES), BF16)], False, 3)  8.16 us
    ppermute x3, starting transfers between devices, from_bond(): return lax.ppermute(array, ('row', 'col'), pairs)  6.43 us
    pallas_call x2, Pallas kernels, per_device(): call(gram_kernel, [mat, mat, mat], True, 3)(role, own, other)  6.04 us
    pallas_call x2, Pallas kernels, per_device(): call(third_kernel, [mat, ((1, LANES), F32)], False, 3, kron)  5.51 us
    unnamed x18, local copies, waits for them, and re-layouts  5.07 us
  transfers between devices with their start and end apart: 9, of which 6 were waited for; matrix products, arithmetic and copies ran while one was open for 3% of the time, Pallas kernels for 12%

commit v1 on v0

--- a/solution.py
+++ b/solution.py
@@ -14,6 +14,7 @@
 SHIFT = 4
 ROWS = CHI * PAD
 LANES = PAD * PAD
+VMEM_BYTES = 8 << 20
 F32 = jnp.float32
 BF16 = jnp.bfloat16
 
@@ -276,6 +277,7 @@
         in_specs=specs,
         out_specs=[pl.BlockSpec(memory_space=pltpu.VMEM)] * len(outs),
         scratch_shapes=list(scratch),
+        compiler_params=pltpu.CompilerParams(vmem_limit_bytes=VMEM_BYTES),
     )
 
 

time: 77.1 us -> 51.9 us (0.67)
  Pallas kernels: 35.9 us -> 15.9 us
  local copies, waits for them, and re-layouts: 8.24 us -> 2.23 us
  waiting for transfers between devices: 20.7 us -> 21.6 us
    pallas_call x3, Pallas kernels: 9.07 us -> 3.16 us  [per_device(): call(second_kernel, [((ROWS, CHI * LANES), BF16)], False, 3)]
    pallas_call x3, Pallas kernels: 8.16 us -> 3.53 us  [per_device(): call(iso_kernel, [((PAD, LANES), BF16)], False, 3)]
    pallas_call x2, Pallas kernels: 5.51 us -> 1.65 us  [per_device(): call(third_kernel, [mat, ((1, LANES), F32)], False, 3, kron)]
    unnamed x18 -> x4, local copies, waits for them, and re-layouts: 5.07 us -> 1.71 us
    pallas_call x2, Pallas kernels: 6.04 us -> 2.86 us  [per_device(): call(gram_kernel, [mat, mat, mat], True, 3)(role, own, other)]
    squeeze x1, local copies, waits for them, and re-layouts: 1.44 us -> 0.01 us  [per_device(): starts[level]]
    pallas_call x1, Pallas kernels: 3.46 us -> 2.18 us  [per_device(): call(last_kernel, [((square, square), F32), ((1, LANES), F32)], True, 4,...]
    pallas_call x1, Pallas kernels: 3.62 us -> 2.52 us  [per_device(): call(first_gram_kernel, [mat, mat, mat, ((LEVELS, 2 * PAD, LANES), F32)],...]
  transfers between devices with their start and end apart: 9 -> 9, of which waited for: 6 -> 9; matrix products, arithmetic and copies ran while one was open for 3% -> 0% of each run, Pallas kernels for 12% -> 6%
where the time goes in v1:
time: 51.9 us; the launch traced here: 51.7 us
  waiting for transfers between devices  21.6 us (42%)
  Pallas kernels  15.9 us (31%)
  starting transfers between devices  11.1 us (21%)
  local copies, waits for them, and re-layouts  2.23 us (4%)
  between operations  0.76 us (1%)
    ppermute x3, waiting for transfers between devices, from_bond(): return lax.ppermute(array, ('row', 'col'), pairs)  13.2 us
    ppermute x6, waiting for transfers between devices, from_partner(): lax.ppermute(array, 'row', [(i, i ^ 1 << stride) for i in range(count)])  8.4 us
    ppermute x3, starting transfers between devices, from_bond(): return lax.ppermute(array, ('row', 'col'), pairs)  6.81 us
    ppermute x6, starting transfers between devices, from_partner(): lax.ppermute(array, 'row', [(i, i ^ 1 << stride) for i in range(count)])  4.29 us
    pallas_call x3, Pallas kernels, per_device(): call(iso_kernel, [((PAD, LANES), BF16)], False, 3)  3.53 us
    pallas_call x3, Pallas kernels, per_device(): call(second_kernel, [((ROWS, CHI * LANES), BF16)], False, 3)  3.16 us
    pallas_call x2, Pallas kernels, per_device(): call(gram_kernel, [mat, mat, mat], True, 3)(role, own, other)  2.86 us
    pallas_call x1, Pallas kernels, per_device(): call(first_gram_kernel, [mat, mat, mat, ((LEVELS, 2 * PAD, LANES), F32)],...  2.52 us
  transfers between devices with their start and end apart: 9, of which 9 were waited for; matrix products, arithmetic and copies ran while one was open for 0% of the time, Pallas kernels for 6%

profile of v1, /device:TPU:0, one launch (start us, length us, event | category | flops | bytes accessed | tf_op | source)
XLA Modules:
  0.0 51.7 jit_solution(5055877230071882599)
XLA Ops:
  0.6 0.6 %collective-permute-start = (f32[144,144]{1,0:T(8,128)}, f32[144,144]{1,0:T(8,128)S(1)}, u32[]{:S(2)}, u32[]{:S(2)}) collective-permute-start(f32[144,144]{1,0:T(8,128)} %bitcast.12), channel_id=1, source_target_pairs={{0,4},{4,0},{8,12},{12,8},{16,20},{20,16},{24,28},{28,24},{1,5},{5... | collective-permute-start | bytes 248840 | tf_op jit(solution)/shard_map/ppermute | solution.py:286
  1.2 0.1 pad_add_fusion.role
  1.3 1.1 %collective-permute-done.other = f32[144,144]{1,0:T(8,128)S(1)} collective-permute-done((f32[144,144]{1,0:T(8,128)}, f32[144,144]{1,0:T(8,128)S(1)}, u32[]{:S(2)}, u32[]{:S(2)}) %collective-permute-start) | collective-permute-done | bytes 82976 | tf_op jit(solution)/shard_map/ppermute | solution.py:286
  2.4 0.0 copy-start
  2.4 0.9 %copy-done = f32[1,1,144,144]{3,2,1,0:T(8,128)S(1)} copy-done((f32[1,1,144,144]{3,2,1,0:T(8,128)S(1)}, f32[1,1,144,144]{3,2,1,0:T(8,128)}, u32[]{:S(2)}) %copy-start) | copy-done | bytes 82968
  3.3 0.0 copy-start.1
  3.3 0.8 %copy-done.1 = f32[3,12,144]{2,1,0:T(8,128)S(1)} copy-done((f32[3,12,144]{2,1,0:T(8,128)S(1)}, f32[3,12,144]{2,1,0:T(8,128)}, u32[]{:S(2)}) %copy-start.1) | copy-done | bytes 20760
  4.1 2.5 %shard_map.41 = (bf16[192,256]{1,0:T(8,128)(2,1)S(1)}, bf16[192,256]{1,0:T(8,128)(2,1)S(1)}, bf16[192,256]{1,0:T(8,128)(2,1)S(1)}, f32[3,32,256]{2,1,0:T(8,128)S(1)}) custom-call(s32[2]{0:T(128)S(1)} %pad_add_fusion.role, f32[144,144]{1,0:T(8,128)S(1)} %bitcast.13, f32[144,144]{1,0:T(8,128)S(1)} %collective-permute-done.other, f32[3,12,144]{2,1,0:T(8,128)S(1)} %copy-done.1), custom_call_target="tpu_custom_call" | custom-call | tf_op jit(solution)/shard_map/pallas_call | solution.py:312
  6.6 4.8 %collective-permute-start.1 = (bf16[192,256]{1,0:T(8,128)(2,1)S(1)}, bf16[192,256]{1,0:T(8,128)(2,1)S(1)}, u32[]{:S(2)}, u32[]{:S(2)}) collective-permute-start(bf16[192,256]{1,0:T(8,128)(2,1)S(1)} %get-tuple-element.20.own), channel_id=1, source_target_pairs={{0,7},{1,4},{2,5},{3,6},{4,1},{5,2},{6,3},{7,0},{8,15},{9,12},{10,... | collective-permute-start | bytes 294920 | tf_op jit(solution)/shard_map/ppermute | solution.py:296
  11.4 2.6 %collective-permute-done.1.other = bf16[192,256]{1,0:T(8,128)(2,1)S(1)} collective-permute-done((bf16[192,256]{1,0:T(8,128)(2,1)S(1)}, bf16[192,256]{1,0:T(8,128)(2,1)S(1)}, u32[]{:S(2)}, u32[]{:S(2)}) %collective-permute-start.1) | collective-permute-done | bytes 98336 | tf_op jit(solution)/shard_map/ppermute | solution.py:296
  14.0 1.2 %shard_map.42.left = bf16[16,256]{1,0:T(8,128)(2,1)S(1)} custom-call(bf16[192,256]{1,0:T(8,128)(2,1)S(1)} %get-tuple-element.20.own, bf16[192,256]{1,0:T(8,128)(2,1)S(1)} %collective-permute-done.1.other, f32[32,256]{1,0:T(8,128)S(1)} %get-tuple-element.36.starts), custom_call_target="tpu_custom_call" | custom-call | tf_op jit(solution)/shard_map/pallas_call | solution.py:322
  15.2 0.1 collective-permute-start.2
  15.3 1.1 %shard_map.43.second = bf16[192,3072]{1,0:T(8,128)(2,1)S(1)} custom-call(bf16[192,256]{1,0:T(8,128)(2,1)S(1)} %get-tuple-element.18.turned, bf16[192,256]{1,0:T(8,128)(2,1)S(1)} %get-tuple-element.19.lower, bf16[16,256]{1,0:T(8,128)(2,1)S(1)} %shard_map.42.left), custom_call_target="tpu_custom_call" | custom-call | tf_op jit(solution)/shard_map/pallas_call | solution.py:324
  16.3 0.1 collective-permute-done.2.right
  16.4 0.8 %shard_map.44 = (bf16[192,256]{1,0:T(8,128)(2,1)S(1)}, f32[1,256]{1,0:T(1,128)S(1)}) custom-call(bf16[192,3072]{1,0:T(8,128)(2,1)S(1)} %shard_map.43.second, bf16[16,256]{1,0:T(8,128)(2,1)S(1)} %collective-permute-done.2.right, f32[1,256]{1,0:T(1,128)S(1)} %broadcast_in_dim.6.log_in), custom_call_target="tpu_custom_call" | custom-call | tf_op jit(solution)/shard_map/pallas_call | solution.py:326
  17.3 1.9 %collective-permute-start.3 = (bf16[192,256]{1,0:T(8,128)(2,1)S(1)}, bf16[192,256]{1,0:T(8,128)(2,1)S(1)}, u32[]{:S(2)}, u32[]{:S(2)}) collective-permute-start(bf16[192,256]{1,0:T(8,128)(2,1)S(1)} %get-tuple-element.22.own), channel_id=1, source_target_pairs={{0,8},{4,12},{8,0},{12,4},{16,24},{20,28},{24,16},{28,20},{1,9},{5... | collective-permute-start | bytes 294920 | tf_op jit(solution)/shard_map/ppermute | solution.py:286
  19.2 3.4 %collective-permute-done.3.other = bf16[192,256]{1,0:T(8,128)(2,1)S(1)} collective-permute-done((bf16[192,256]{1,0:T(8,128)(2,1)S(1)}, bf16[192,256]{1,0:T(8,128)(2,1)S(1)}, u32[]{:S(2)}, u32[]{:S(2)}) %collective-permute-start.3) | collective-permute-done | bytes 98336 | tf_op jit(solution)/shard_map/ppermute | solution.py:286
  22.6 1.4 %shard_map.45 = (bf16[192,256]{1,0:T(8,128)(2,1)S(1)}, bf16[192,256]{1,0:T(8,128)(2,1)S(1)}, bf16[192,256]{1,0:T(8,128)(2,1)S(1)}) custom-call(s32[1]{0:T(128)} %bitcast.2.role, bf16[192,256]{1,0:T(8,128)(2,1)S(1)} %get-tuple-element.22.own, bf16[192,256]{1,0:T(8,128)(2,1)S(1)} %collective-permute-done.3.other), custom_call_target="tpu_custom_call" | custom-call | tf_op jit(solution)/shard_map/pallas_call | solution.py:320
  24.0 2.0 %collective-permute-start.4 = (bf16[192,256]{1,0:T(8,128)(2,1)S(1)}, bf16[192,256]{1,0:T(8,128)(2,1)S(1)}, u32[]{:S(2)}, u32[]{:S(2)}) collective-permute-start(bf16[192,256]{1,0:T(8,128)(2,1)S(1)} %get-tuple-element.25.own), channel_id=1, source_target_pairs={{0,7},{1,4},{2,5},{3,6},{4,1},{5,2},{6,3},{7,0},{8,15},{9,12},{10,... | collective-permute-start | bytes 294920 | tf_op jit(solution)/shard_map/ppermute | solution.py:296
  26.0 4.8 %collective-permute-done.4.other = bf16[192,256]{1,0:T(8,128)(2,1)S(1)} collective-permute-done((bf16[192,256]{1,0:T(8,128)(2,1)S(1)}, bf16[192,256]{1,0:T(8,128)(2,1)S(1)}, u32[]{:S(2)}, u32[]{:S(2)}) %collective-permute-start.4) | collective-permute-done | bytes 98336 | tf_op jit(solution)/shard_map/ppermute | solution.py:296
  30.8 1.2 %shard_map.46.left = bf16[16,256]{1,0:T(8,128)(2,1)S(1)} custom-call(bf16[192,256]{1,0:T(8,128)(2,1)S(1)} %get-tuple-element.25.own, bf16[192,256]{1,0:T(8,128)(2,1)S(1)} %collective-permute-done.4.other, f32[32,256]{1,0:T(8,128)S(1)} %get-tuple-element.35.starts), custom_call_target="tpu_custom_call" | custom-call | tf_op jit(solution)/shard_map/pallas_call | solution.py:322
  32.0 0.1 collective-permute-start.5
  32.1 1.1 %shard_map.47.second = bf16[192,3072]{1,0:T(8,128)(2,1)S(1)} custom-call(bf16[192,256]{1,0:T(8,128)(2,1)S(1)} %get-tuple-element.23.turned, bf16[192,256]{1,0:T(8,128)(2,1)S(1)} %get-tuple-element.24.lower, bf16[16,256]{1,0:T(8,128)(2,1)S(1)} %shard_map.46.left), custom_call_target="tpu_custom_call" | custom-call | tf_op jit(solution)/shard_map/pallas_call | solution.py:324
  33.1 0.1 collective-permute-done.5.right
  33.2 0.8 %shard_map.48 = (bf16[192,256]{1,0:T(8,128)(2,1)S(1)}, f32[1,256]{1,0:T(1,128)S(1)}) custom-call(bf16[192,3072]{1,0:T(8,128)(2,1)S(1)} %shard_map.47.second, bf16[16,256]{1,0:T(8,128)(2,1)S(1)} %collective-permute-done.5.right, f32[1,256]{1,0:T(1,128)S(1)} %get-tuple-element.26.log_in), custom_call_target="tpu_custom_call" | custom-call | tf_op jit(solution)/shard_map/pallas_call | solution.py:326
  34.1 1.6 %collective-permute-start.6 = (bf16[192,256]{1,0:T(8,128)(2,1)S(1)}, bf16[192,256]{1,0:T(8,128)(2,1)S(1)}, u32[]{:S(2)}, u32[]{:S(2)}) collective-permute-start(bf16[192,256]{1,0:T(8,128)(2,1)S(1)} %get-tuple-element.27.own), channel_id=1, source_target_pairs={{0,16},{4,20},{8,24},{12,28},{16,0},{20,4},{24,8},{28,12},{1,17},{... | collective-permute-start | bytes 294920 | tf_op jit(solution)/shard_map/ppermute | solution.py:286
  35.7 3.6 %collective-permute-done.6.other = bf16[192,256]{1,0:T(8,128)(2,1)S(1)} collective-permute-done((bf16[192,256]{1,0:T(8,128)(2,1)S(1)}, bf16[192,256]{1,0:T(8,128)(2,1)S(1)}, u32[]{:S(2)}, u32[]{:S(2)}) %collective-permute-start.6) | collective-permute-done | bytes 98336 | tf_op jit(solution)/shard_map/ppermute | solution.py:286
  39.2 1.4 %shard_map.49 = (bf16[192,256]{1,0:T(8,128)(2,1)S(1)}, bf16[192,256]{1,0:T(8,128)(2,1)S(1)}, bf16[192,256]{1,0:T(8,128)(2,1)S(1)}) custom-call(s32[1]{0:T(128)} %bitcast.1.role, bf16[192,256]{1,0:T(8,128)(2,1)S(1)} %get-tuple-element.27.own, bf16[192,256]{1,0:T(8,128)(2,1)S(1)} %collective-permute-done.6.other), custom_call_target="tpu_custom_call" | custom-call | tf_op jit(solution)/shard_map/pallas_call | solution.py:320
  40.7 0.1 collective-permute-start.7
  40.8 5.8 %collective-permute-done.7.other = bf16[192,256]{1,0:T(8,128)(2,1)S(1)} collective-permute-done((bf16[192,256]{1,0:T(8,128)(2,1)S(1)}, bf16[192,256]{1,0:T(8,128)(2,1)S(1)}, u32[]{:S(2)}, u32[]{:S(2)}) %collective-permute-start.7) | collective-permute-done | bytes 98336 | tf_op jit(solution)/shard_map/ppermute | solution.py:296
  46.6 1.2 %shard_map.50.left = bf16[16,256]{1,0:T(8,128)(2,1)S(1)} custom-call(bf16[192,256]{1,0:T(8,128)(2,1)S(1)} %get-tuple-element.30.own, bf16[192,256]{1,0:T(8,128)(2,1)S(1)} %collective-permute-done.7.other, f32[32,256]{1,0:T(8,128)S(1)} %get-tuple-element.34.starts), custom_call_target="tpu_custom_call" | custom-call | tf_op jit(solution)/shard_map/pallas_call | solution.py:322
  47.8 0.1 collective-permute-start.8
  47.8 1.1 %shard_map.51.second = bf16[192,3072]{1,0:T(8,128)(2,1)S(1)} custom-call(bf16[192,256]{1,0:T(8,128)(2,1)S(1)} %get-tuple-element.28.turned, bf16[192,256]{1,0:T(8,128)(2,1)S(1)} %get-tuple-element.29.lower, bf16[16,256]{1,0:T(8,128)(2,1)S(1)} %shard_map.50.left), custom_call_target="tpu_custom_call" | custom-call | tf_op jit(solution)/shard_map/pallas_call | solution.py:324
  48.9 0.1 collective-permute-done.8.right
  49.0 2.2 %shard_map.52 = (f32[144,144]{1,0:T(8,128)}, f32[1,256]{1,0:T(1,128)S(1)}) custom-call(s32[1]{0:T(128)} %bitcast.role, bf16[192,3072]{1,0:T(8,128)(2,1)S(1)} %shard_map.51.second, bf16[16,256]{1,0:T(8,128)(2,1)S(1)} %collective-permute-done.8.right, f32[1,256]{1,0:T(1,128)S(1)} %get-tuple-element.31.log_in), custom_call_target="tpu_custom_call" | custom-call | tf_op jit(solution)/shard_map/pallas_call | solution.py:331
  51.2 0.5 slice.15
  (2 shorter events, 0.0 us)
Async XLA Ops:
  0.6 1.8 %collective-permute-start = (f32[144,144]{1,0:T(8,128)}, f32[144,144]{1,0:T(8,128)S(1)}, u32[]{:S(2)}, u32[]{:S(2)}) collective-permute-start(f32[144,144]{1,0:T(8,128)} %bitcast.12), channel_id=1, source_target_pairs={{0,4},{4,0},{8,12},{12,8},{16,20},{20,16},{24,28},{28,24},{1,5},{5... | collective-permute-start | bytes 248840 | tf_op jit(solution)/shard_map/ppermute | solution.py:286
  2.4 0.9 %copy-start = (f32[1,1,144,144]{3,2,1,0:T(8,128)S(1)}, f32[1,1,144,144]{3,2,1,0:T(8,128)}, u32[]{:S(2)}) copy-start(f32[1,1,144,144]{3,2,1,0:T(8,128)} %param.2) | copy-start | bytes 248836
  3.3 0.8 %copy-start.1 = (f32[3,12,144]{2,1,0:T(8,128)S(1)}, f32[3,12,144]{2,1,0:T(8,128)}, u32[]{:S(2)}) copy-start(f32[3,12,144]{2,1,0:T(8,128)} %start.1) | copy-start | bytes 62212
  6.6 7.4 %collective-permute-start.1 = (bf16[192,256]{1,0:T(8,128)(2,1)S(1)}, bf16[192,256]{1,0:T(8,128)(2,1)S(1)}, u32[]{:S(2)}, u32[]{:S(2)}) collective-permute-start(bf16[192,256]{1,0:T(8,128)(2,1)S(1)} %get-tuple-element.20.own), channel_id=1, source_target_pairs={{0,7},{1,4},{2,5},{3,6},{4,1},{5,2},{6,3},{7,0},{8,15},{9,12},{10,... | collective-permute-start | bytes 294920 | tf_op jit(solution)/shard_map/ppermute | solution.py:296
  15.2 1.2 %collective-permute-start.2 = (bf16[16,256]{1,0:T(8,128)(2,1)S(1)}, bf16[16,256]{1,0:T(8,128)(2,1)S(1)}, u32[]{:S(2)}, u32[]{:S(2)}) collective-permute-start(bf16[16,256]{1,0:T(8,128)(2,1)S(1)} %shard_map.42.left), channel_id=1, source_target_pairs={{0,4},{4,0},{8,12},{12,8},{16,20},{20,16},{24,28},{28,24},{1,5},{5... | collective-permute-start | bytes 24584 | tf_op jit(solution)/shard_map/ppermute | solution.py:286
  17.3 5.3 %collective-permute-start.3 = (bf16[192,256]{1,0:T(8,128)(2,1)S(1)}, bf16[192,256]{1,0:T(8,128)(2,1)S(1)}, u32[]{:S(2)}, u32[]{:S(2)}) collective-permute-start(bf16[192,256]{1,0:T(8,128)(2,1)S(1)} %get-tuple-element.22.own), channel_id=1, source_target_pairs={{0,8},{4,12},{8,0},{12,4},{16,24},{20,28},{24,16},{28,20},{1,9},{5... | collective-permute-start | bytes 294920 | tf_op jit(solution)/shard_map/ppermute | solution.py:286
  24.0 6.8 %collective-permute-start.4 = (bf16[192,256]{1,0:T(8,128)(2,1)S(1)}, bf16[192,256]{1,0:T(8,128)(2,1)S(1)}, u32[]{:S(2)}, u32[]{:S(2)}) collective-permute-start(bf16[192,256]{1,0:T(8,128)(2,1)S(1)} %get-tuple-element.25.own), channel_id=1, source_target_pairs={{0,7},{1,4},{2,5},{3,6},{4,1},{5,2},{6,3},{7,0},{8,15},{9,12},{10,... | collective-permute-start | bytes 294920 | tf_op jit(solution)/shard_map/ppermute | solution.py:296
  32.0 1.2 %collective-permute-start.5 = (bf16[16,256]{1,0:T(8,128)(2,1)S(1)}, bf16[16,256]{1,0:T(8,128)(2,1)S(1)}, u32[]{:S(2)}, u32[]{:S(2)}) collective-permute-start(bf16[16,256]{1,0:T(8,128)(2,1)S(1)} %shard_map.46.left), channel_id=1, source_target_pairs={{0,4},{4,0},{8,12},{12,8},{16,20},{20,16},{24,28},{28,24},{1,5},{5... | collective-permute-start | bytes 24584 | tf_op jit(solution)/shard_map/ppermute | solution.py:286
  34.1 5.2 %collective-permute-start.6 = (bf16[192,256]{1,0:T(8,128)(2,1)S(1)}, bf16[192,256]{1,0:T(8,128)(2,1)S(1)}, u32[]{:S(2)}, u32[]{:S(2)}) collective-permute-start(bf16[192,256]{1,0:T(8,128)(2,1)S(1)} %get-tuple-element.27.own), channel_id=1, source_target_pairs={{0,16},{4,20},{8,24},{12,28},{16,0},{20,4},{24,8},{28,12},{1,17},{... | collective-permute-start | bytes 294920 | tf_op jit(solution)/shard_map/ppermute | solution.py:286
  40.7 5.9 %collective-permute-start.7 = (bf16[192,256]{1,0:T(8,128)(2,1)S(1)}, bf16[192,256]{1,0:T(8,128)(2,1)S(1)}, u32[]{:S(2)}, u32[]{:S(2)}) collective-permute-start(bf16[192,256]{1,0:T(8,128)(2,1)S(1)} %get-tuple-element.30.own), channel_id=1, source_target_pairs={{0,7},{1,4},{2,5},{3,6},{4,1},{5,2},{6,3},{7,0},{8,15},{9,12},{10,... | collective-permute-start | bytes 294920 | tf_op jit(solution)/shard_map/ppermute | solution.py:296
  47.8 1.2 %collective-permute-start.8 = (bf16[16,256]{1,0:T(8,128)(2,1)S(1)}, bf16[16,256]{1,0:T(8,128)(2,1)S(1)}, u32[]{:S(2)}, u32[]{:S(2)}) collective-permute-start(bf16[16,256]{1,0:T(8,128)(2,1)S(1)} %shard_map.50.left), channel_id=1, source_target_pairs={{0,4},{4,0},{8,12},{12,8},{16,20},{20,16},{24,28},{28,24},{1,5},{5... | collective-permute-start | bytes 24584 | tf_op jit(solution)/shard_map/ppermute | solution.py:286

commit v2 on v1

--- a/solution.py
+++ b/solution.py
@@ -114,18 +114,41 @@
     return (y[2 * n :] + y[n : 2 * n]) + y[:n]
 
 
-def gram_body(upper, lower, swap):
+def pack(x):
+    half = ROWS // 2
+    side, used = x[:, 128:], ROWS - 128
+    lane = iota((half, 128), 1)
+    folded = jnp.where(lane < used, side[:half], pltpu.roll(side[half:], used, 1))
+    return jnp.concatenate([x[:, :128], folded], axis=0)
+
+
+def unpack(x):
+    half, used = ROWS // 2, ROWS - 128
+    folded = x[ROWS:]
+    lane = iota((half, 128), 1)
+    zero = jnp.zeros((half, 128), x.dtype)
+    first = jnp.where(lane < used, folded, zero)
+    last = jnp.where(lane < used, pltpu.roll(folded, 128 - used, 1), zero)
+    return jnp.concatenate([x[:ROWS], jnp.concatenate([first, last], axis=0)], axis=1)
+
+
+def upper_part(upper, swap):
     turned = block_swap(mm(upper, swap).astype(BF16))
-    row_swap = swap[:ROWS, :ROWS]
+    turned_m = mm(turned, swap).astype(BF16)
+    product = mm(turned_m, turned, TN).astype(BF16)
+    return turned, block_swap(product[:ROWS])
+
+
+def lower_part(lower, swap):
     lower_m = mm(swap[:, :ROWS], lower).astype(BF16)
-    prod_b = mm(lower_m[:ROWS], lower, NT).astype(BF16)
-    prod_b = block_swap(widen(prod_b))
-    prod_b = mm(row_swap, prod_b).astype(BF16)
-    turned_m = mm(turned, swap).astype(BF16)
-    prod_a = mm(turned_m, turned, TN).astype(BF16)
-    prod_a = block_swap(prod_a[:ROWS])
-    outer = mm(prod_a, prod_b, NT).astype(BF16)
-    return block_swap(widen(outer)), turned
+    product = mm(lower_m[:ROWS], lower, NT).astype(BF16)
+    product = block_swap(widen(product))
+    return mm(swap[:ROWS, :ROWS], product).astype(BF16)
+
+
+def outer_part(upper_product, lower_product):
+    outer = mm(upper_product, lower_product, NT).astype(BF16)
+    return block_swap(widen(outer))
 
 
 def start_body(start, swap):
@@ -205,35 +228,72 @@
     return mm(second_ref[...], kron_ref[...])
 
 
-def pick(is_upper, own, other):
-    return jnp.where(is_upper, own, other), jnp.where(is_upper, other, own)
-
-
-def first_gram_kernel(role, own, other, start, lower_o, turned_o, gram_o, starts_o):
-    mirror, is_upper = role[0] != 0, role[1] != 0
+def placed(site, mirror):
+    spaced = mm(row_spread(), site.astype(BF16)).astype(BF16)
+    return block_swap(mm(spaced, spread_matrix(mirror)).astype(BF16))
+
+
+def first_own_kernel(role, own, start, own_o, starts_o, site, basis, sems):
+    copies = [
+        pltpu.make_async_copy(own, site, sems.at[0]),
+        pltpu.make_async_copy(start, basis, sems.at[1]),
+    ]
+    for copy in copies:
+        copy.start()
+    copies[0].wait()
+    own_o[...] = placed(site[...], role[0] != 0)
+    copies[1].wait()
     swap = swap_matrix()
-    rows, spread = row_spread(), spread_matrix(mirror)
-
-    def placed(site):
-        spaced = mm(rows, site[...].astype(BF16)).astype(BF16)
-        return block_swap(mm(spaced, spread).astype(BF16))
-
-    upper, lower = pick(is_upper, placed(own), placed(other))
-    gram, turned = gram_body(upper, lower, swap)
-    lower_o[...], turned_o[...], gram_o[...] = lower, turned, gram
     for level in range(LEVELS):
-        plain, turn = start_body(start[level], swap)
+        plain, turn = start_body(basis[level], swap)
         starts_o[level, :PAD], starts_o[level, PAD:] = plain, turn
 
 
-def gram_kernel(role, own, other, lower_o, turned_o, gram_o):
-    upper, lower = pick(role[0] != 0, own[...], other[...])
-    gram, turned = gram_body(upper, lower, swap_matrix())
-    lower_o[...], turned_o[...], gram_o[...] = lower, turned, gram
+def first_gram_kernel(role, own, other, lower_o, turned_o, gram_o):
+    swap = swap_matrix()
+    mine, theirs = own[...], placed(other[...], role[0] != 0)
+    is_upper = role[1] != 0
+    upper, lower = jnp.where(is_upper, mine, theirs), jnp.where(is_upper, theirs, mine)
+    turned, upper_product = upper_part(upper, swap)
+    gram_o[...] = pack(outer_part(upper_product, lower_part(lower, swap)))
+    lower_o[...], turned_o[...] = lower, turned
+
+
+def own_kernel(role, own, wide_o, turned_o, product_o):
+    swap = swap_matrix()
+    wide = unpack(own[...])
+    wide_o[...] = wide
+
+    @pl.when(role[0] != 0)
+    def _():
+        turned_o[...], product_o[...] = upper_part(wide, swap)
+
+    @pl.when(role[0] == 0)
+    def _():
+        turned_o[...] = jnp.zeros_like(turned_o)
+        product_o[...] = lower_part(wide, swap)
+
+
+def gram_kernel(role, wide, own_turned, product, other, lower_o, turned_o, gram_o, up, low):
+    swap = swap_matrix()
+    theirs = unpack(other[...])
+
+    @pl.when(role[0] != 0)
+    def _():
+        lower_o[...], turned_o[...] = theirs, own_turned[...]
+        up[...], low[...] = product[...], lower_part(theirs, swap)
+
+    @pl.when(role[0] == 0)
+    def _():
+        lower_o[...] = wide[...]
+        turned_o[...], up[...] = upper_part(theirs, swap)
+        low[...] = product[...]
+
+    gram_o[...] = pack(outer_part(up[...], low[...]))
 
 
 def iso_kernel(own, other, starts, iso_o):
-    iso_o[...] = iso_body(own[...], other[...], starts[:PAD], starts[PAD:], swap_matrix())
+    iso_o[...] = iso_body(unpack(own[...]), unpack(other[...]), starts[:PAD], starts[PAD:], swap_matrix())
 
 
 def second_kernel(turned, lower, left, second_o):
@@ -248,14 +308,14 @@
 def third_kernel(second, right, log_in, next_o, log_o, kron):
     merged = third(second, right[...], kron)
     norm = scaled(merged)
-    next_o[...] = (merged / norm).astype(BF16)
+    next_o[...] = pack((merged / norm).astype(BF16))
     log_o[...] = log_in[...] + jnp.log(norm)
 
 
 def last_kernel(role, second, right, log_in, coarse_o, log_o, kron):
     merged = third(second, right[...], kron)
     norm = scaled(merged)
-    log_o[...] = log_in[...] + jnp.log(norm)
+    log_o[...] = (log_in[...] + jnp.log(norm))[:, :1]
     wide = block_swap(merged / norm)
     spread, rows = spread_matrix(role[0] != 0), row_spread()
     total = jnp.zeros((CHI * CHI, CHI * CHI), F32)
@@ -267,23 +327,28 @@
     coarse_o[...] = total
 
 
-def call(kernel, outs, smem, n_in, scratch=()):
-    specs = [pl.BlockSpec(memory_space=pltpu.VMEM)] * n_in
-    if smem:
-        specs[0] = pl.BlockSpec(memory_space=pltpu.SMEM)
+def call(kernel, outs, places, scratch=()):
     return pl.pallas_call(
         kernel,
         out_shape=[jax.ShapeDtypeStruct(s, d) for s, d in outs],
-        in_specs=specs,
+        in_specs=[pl.BlockSpec(memory_space=place) for place in places],
         out_specs=[pl.BlockSpec(memory_space=pltpu.VMEM)] * len(outs),
         scratch_shapes=list(scratch),
         compiler_params=pltpu.CompilerParams(vmem_limit_bytes=VMEM_BYTES),
+        cost_estimate=pl.CostEstimate(flops=10**8, bytes_accessed=10**6, transcendentals=0),
     )
 
 
-def from_partner(array, stride):
+def from_partner(array, flip):
     count = lax.axis_size("row")
-    return lax.ppermute(array, "row", [(i, i ^ 1 << stride) for i in range(count)])
+    return lax.ppermute(array, "row", [(i, i ^ flip) for i in range(count)])
+
+
+def mirrored(row):
+    parity = row * 0
+    for bit in range(LEVELS):
+        parity = parity ^ (row >> bit & 1)
+    return parity
 
 
 def from_bond(array):
@@ -291,7 +356,7 @@
     pairs = []
     for i in range(rows):
         for c in range(cols):
-            target = (c - 1) % cols if i % 2 == 0 else (c + 1) % cols
+            target = (c + 1) % cols if mirrored(i) else (c - 1) % cols
             pairs.append((i * cols + c, (i ^ 1) * cols + target))
     return lax.ppermute(array, ("row", "col"), pairs)
 
@@ -299,39 +364,58 @@
 def per_device(site_tensors, start_basis):
     square = CHI * CHI
     row = lax.axis_index("row")
-    mirror = row % 2
-    mat = ((ROWS, LANES), BF16)
-    kron = [pltpu.VMEM((CHI * LANES, LANES), BF16)]
+    mirror = mirrored(row)
+    vmem, smem, hbm = pltpu.VMEM, pltpu.SMEM, pltpu.HBM
+    mat, packed = ((ROWS, LANES), BF16), ((ROWS * 3 // 2, 128), BF16)
+    kron = [vmem((CHI * LANES, LANES), BF16)]
     log_total = jnp.zeros((1, LANES), F32)
     own = site_tensors[0, 0]
     for level in range(LEVELS):
-        other = from_partner(own, level)
-        is_upper = 1 - row // 2**level % 2
+        is_upper = 1 - (row >> level & 1)
         if level == 0:
+            other = from_partner(own, 1)
             role = jnp.stack([mirror, is_upper]).astype(jnp.int32)
-            lower, turned, gram, starts = call(
-                first_gram_kernel,
-                [mat, mat, mat, ((LEVELS, 2 * PAD, LANES), F32)],
-                True,
-                4,
-            )(role, own, other, start_basis)
+            wide, starts = call(
+                first_own_kernel,
+                [mat, ((LEVELS, 2 * PAD, LANES), F32)],
+                [smem, hbm, hbm],
+                [
+                    vmem((square, square), F32),
+                    vmem((LEVELS, CHI, square), F32),
+                    pltpu.SemaphoreType.DMA((2,)),
+                ],
+            )(role, own, start_basis)
+            lower, turned, gram = call(first_gram_kernel, [mat, mat, packed], [smem, vmem, vmem])(
+                role, wide, other
+            )
         else:
+            other = from_partner(own, 1 << level | 1)
             role = is_upper.reshape(1).astype(jnp.int32)
-            lower, turned, gram = call(gram_kernel, [mat, mat, mat], True, 3)(role, own, other)
+            wide, own_turned, product = call(own_kernel, [mat, mat, mat], [smem, vmem])(role, own)
+            lower, turned, gram = call(
+                gram_kernel,
+                [mat, mat, packed],
+                [smem, vmem, vmem, vmem, vmem],
+                [vmem(*mat), vmem(*mat)],
+            )(role, wide, own_turned, product, other)
         gram_other = from_bond(gram)
-        (left,) = call(iso_kernel, [((PAD, LANES), BF16)], False, 3)(gram, gram_other, starts[level])
-        right = from_partner(left, 0)
-        (second,) = call(second_kernel, [((ROWS, CHI * LANES), BF16)], False, 3)(turned, lower, left)
+        (left,) = call(iso_kernel, [((PAD, LANES), BF16)], [vmem] * 3)(
+            gram, gram_other, starts[level]
+        )
+        right = from_partner(left, 1)
+        (second,) = call(second_kernel, [((ROWS, CHI * LANES), BF16)], [vmem] * 3)(
+            turned, lower, left
+        )
         if level < LEVELS - 1:
-            own, log_total = call(third_kernel, [mat, ((1, LANES), F32)], False, 3, kron)(
+            own, log_total = call(third_kernel, [packed, ((1, LANES), F32)], [vmem] * 3, kron)(
                 second, right, log_total
             )
         else:
             role = mirror.reshape(1).astype(jnp.int32)
             coarse, log_total = call(
-                last_kernel, [((square, square), F32), ((1, LANES), F32)], True, 4, kron
+                last_kernel, [((square, square), F32), ((1, 1), F32)], [smem] + [vmem] * 3, kron
             )(role, second, right, log_total)
-    return (coarse[None, None], log_total[:, :1])
+    return (coarse[None, None], log_total)
 
 
 def solution(mesh):

time: 51.9 us -> 48.4 us (0.933)
  waiting for transfers between devices: 21.6 us -> 9.52 us
  starting transfers between devices: 11.1 us -> 16.2 us
  Pallas kernels: 15.9 us -> 19.9 us
    ppermute x3, waiting for transfers between devices: 13.2 us -> 6.63 us  [from_bond(): return lax.ppermute(array, ('row', 'col'), pairs)]
    ppermute x6, waiting for transfers between devices: 8.4 us -> 2.89 us  [from_partner(): return lax.ppermute(array, 'row', [(i, i ^ flip) for i in range(count)])]
    ppermute x3, starting transfers between devices: 6.81 us -> 12.2 us  [from_bond(): return lax.ppermute(array, ('row', 'col'), pairs)]
    pallas_call x12 -> x15, Pallas kernels: 15.9 us -> 19.9 us  [the longest x3 3.68 us: per_device(): call(iso_kernel, [((PAD, LANES), BF16)], [vmem] * 3)]
  transfers between devices with their start and end apart: 9 -> 9, of which waited for: 9 -> 8; matrix products, arithmetic and copies ran while one was open for 0% -> 0% of each run, Pallas kernels for 6% -> 15%
where the time goes in v2:
time: 48.4 us; the launch traced here: 48.2 us
  Pallas kernels  19.9 us (41%)
  starting transfers between devices  16.2 us (33%)
  waiting for transfers between devices  9.52 us (20%)
  local copies, waits for them, and re-layouts  1.72 us (4%)
  between operations  0.74 us (2%)
    ppermute x3, starting transfers between devices, from_bond(): return lax.ppermute(array, ('row', 'col'), pairs)  12.2 us
    ppermute x3, waiting for transfers between devices, from_bond(): return lax.ppermute(array, ('row', 'col'), pairs)  6.63 us
    ppermute x6, starting transfers between devices, from_partner(): return lax.ppermute(array, 'row', [(i, i ^ flip) for i in range(count)])  4.09 us
    pallas_call x3, Pallas kernels, per_device(): call(iso_kernel, [((PAD, LANES), BF16)], [vmem] * 3)  3.68 us
    pallas_call x3, Pallas kernels, per_device(): call(second_kernel, [((ROWS, CHI * LANES), BF16)], [vmem] * 3)  3.16 us
    ppermute x6, waiting for transfers between devices, from_partner(): return lax.ppermute(array, 'row', [(i, i ^ flip) for i in range(count)])  2.89 us
    pallas_call x1, Pallas kernels, per_device(): call(first_gram_kernel, [mat, mat, packed], [smem, vmem, vmem])  2.66 us
    pallas_call x2, Pallas kernels, per_device(): call(gram_kernel, [mat, mat, packed], [smem, vmem, vmem, vmem, vmem], [vm...  2.53 us
  transfers between devices with their start and end apart: 9, of which 8 were waited for; matrix products, arithmetic and copies ran while one was open for 0% of the time, Pallas kernels for 15%

profile of v2, /device:TPU:0, one launch (start us, length us, event | category | flops | bytes accessed | tf_op | source)
XLA Modules:
  0.0 48.2 jit_solution(4469633077887664836)
XLA Ops:
  0.6 0.6 %collective-permute-start = (f32[144,144]{1,0:T(8,128)}, f32[144,144]{1,0:T(8,128)S(1)}, u32[]{:S(2)}, u32[]{:S(2)}) collective-permute-start(f32[144,144]{1,0:T(8,128)} %bitcast.12), channel_id=1, source_target_pairs={{0,4},{4,0},{8,12},{12,8},{16,20},{20,16},{24,28},{28,24},{1,5},{5... | collective-permute-start | bytes 248840 | tf_op jit(solution)/shard_map/ppermute | solution.py:344
  1.2 0.1 pad_add_fusion.role
  1.3 0.0 copy-start
  1.3 0.9 %copy-done = f32[1,1,144,144]{3,2,1,0:T(8,128)S(1)} copy-done((f32[1,1,144,144]{3,2,1,0:T(8,128)S(1)}, f32[1,1,144,144]{3,2,1,0:T(8,128)}, u32[]{:S(2)}) %copy-start) | copy-done | bytes 82968
  2.2 0.0 copy-start.1
  2.2 0.8 %copy-done.1 = f32[3,12,144]{2,1,0:T(8,128)S(1)} copy-done((f32[3,12,144]{2,1,0:T(8,128)S(1)}, f32[3,12,144]{2,1,0:T(8,128)}, u32[]{:S(2)}) %copy-start.1) | copy-done | bytes 20760
  3.0 1.7 %shard_map.41 = (bf16[192,256]{1,0:T(8,128)(2,1)S(1)}, f32[3,32,256]{2,1,0:T(8,128)S(1)}) custom-call(s32[2]{0:T(128)S(1)} %pad_add_fusion.role, f32[144,144]{1,0:T(8,128)S(1)} %bitcast.13, f32[3,12,144]{2,1,0:T(8,128)S(1)} %copy-done.1), custom_call_target="tpu_custom_call" | custom-call | flops 100000000 | bytes 1000000 | tf_op jit(solution)/shard_map/pallas_call | solution.py:378
  4.7 0.0 collective-permute-done.other
  4.7 2.7 %shard_map.42 = (bf16[192,256]{1,0:T(8,128)(2,1)S(1)}, bf16[192,256]{1,0:T(8,128)(2,1)S(1)}, bf16[288,128]{1,0:T(8,128)(2,1)S(1)}) custom-call(s32[2]{0:T(128)S(1)} %pad_add_fusion.role, bf16[192,256]{1,0:T(8,128)(2,1)S(1)} %get-tuple-element.25.own, f32[144,144]{1,0:T(8,128)S(1)} %collective-permute-done.other), custom_call_target="tpu_custom_call" | custom-call | flops 100000000 | bytes 1000000 | tf_op jit(solution)/shard_map/pallas_call | solution.py:388
  7.3 4.8 %collective-permute-start.1 = (bf16[288,128]{1,0:T(8,128)(2,1)S(1)}, bf16[288,128]{1,0:T(8,128)(2,1)S(1)}, u32[]{:S(2)}, u32[]{:S(2)}) collective-permute-start(bf16[288,128]{1,0:T(8,128)(2,1)S(1)} %get-tuple-element.28.own), channel_id=1, source_target_pairs={{0,7},{1,4},{2,5},{3,6},{4,1},{5,2},{6,3},{7,0},{8,13},{9,14},{10,... | collective-permute-start | bytes 221192 | tf_op jit(solution)/shard_map/ppermute | solution.py:361
  12.1 2.1 %collective-permute-done.1.other = bf16[288,128]{1,0:T(8,128)(2,1)S(1)} collective-permute-done((bf16[288,128]{1,0:T(8,128)(2,1)S(1)}, bf16[288,128]{1,0:T(8,128)(2,1)S(1)}, u32[]{:S(2)}, u32[]{:S(2)}) %collective-permute-start.1) | collective-permute-done | bytes 73760 | tf_op jit(solution)/shard_map/ppermute | solution.py:361
  14.2 1.2 %shard_map.43.left = bf16[16,256]{1,0:T(8,128)(2,1)S(1)} custom-call(bf16[288,128]{1,0:T(8,128)(2,1)S(1)} %get-tuple-element.28.own, bf16[288,128]{1,0:T(8,128)(2,1)S(1)} %collective-permute-done.1.other, f32[32,256]{1,0:T(8,128)S(1)} %get-tuple-element.50.starts), custom_call_target="tpu_custom_call" | custom-call | flops 100000000 | bytes 1000000 | tf_op jit(solution)/shard_map/pallas_call | solution.py:402
  15.5 0.1 collective-permute-start.2
  15.5 1.1 %shard_map.44.second = bf16[192,3072]{1,0:T(8,128)(2,1)S(1)} custom-call(bf16[192,256]{1,0:T(8,128)(2,1)S(1)} %get-tuple-element.26.turned, bf16[192,256]{1,0:T(8,128)(2,1)S(1)} %get-tuple-element.27.lower, bf16[16,256]{1,0:T(8,128)(2,1)S(1)} %shard_map.43.left), custom_call_target="tpu_custom_call" | custom-call | flops 100000000 | bytes 1000000 | tf_op jit(solution)/shard_map/pallas_call | solution.py:406
  16.6 0.1 collective-permute-done.2.right
  16.7 0.9 %shard_map.45 = (bf16[288,128]{1,0:T(8,128)(2,1)S(1)}, f32[1,256]{1,0:T(1,128)S(1)}) custom-call(bf16[192,3072]{1,0:T(8,128)(2,1)S(1)} %shard_map.44.second, bf16[16,256]{1,0:T(8,128)(2,1)S(1)} %collective-permute-done.2.right, f32[1,256]{1,0:T(1,128)S(1)} %broadcast_in_dim.6.log_in), custom_call_target="tpu_custom_call" | custom-call | flops 100000000 | bytes 1000000 | tf_op jit(solution)/shard_map/pallas_call | solution.py:410
  17.6 1.7 %collective-permute-start.3 = (bf16[288,128]{1,0:T(8,128)(2,1)S(1)}, bf16[288,128]{1,0:T(8,128)(2,1)S(1)}, u32[]{:S(2)}, u32[]{:S(2)}) collective-permute-start(bf16[288,128]{1,0:T(8,128)(2,1)S(1)} %get-tuple-element.30.own), channel_id=1, source_target_pairs={{0,12},{4,8},{8,4},{12,0},{16,28},{20,24},{24,20},{28,16},{1,13},{... | collective-permute-start | bytes 221192 | tf_op jit(solution)/shard_map/ppermute | solution.py:344
  19.3 1.1 %shard_map.46 = (bf16[192,256]{1,0:T(8,128)(2,1)S(1)}, bf16[192,256]{1,0:T(8,128)(2,1)S(1)}, bf16[192,256]{1,0:T(8,128)(2,1)S(1)}) custom-call(s32[1]{0:T(128)} %bitcast.2.role, bf16[288,128]{1,0:T(8,128)(2,1)S(1)} %get-tuple-element.30.own), custom_call_target="tpu_custom_call" | custom-call | flops 100000000 | bytes 1000000 | tf_op jit(solution)/shard_map/pallas_call | solution.py:394
  20.4 1.3 %collective-permute-done.3.other = bf16[288,128]{1,0:T(8,128)(2,1)S(1)} collective-permute-done((bf16[288,128]{1,0:T(8,128)(2,1)S(1)}, bf16[288,128]{1,0:T(8,128)(2,1)S(1)}, u32[]{:S(2)}, u32[]{:S(2)}) %collective-permute-start.3) | collective-permute-done | bytes 73760 | tf_op jit(solution)/shard_map/ppermute | solution.py:344
  21.7 1.3 %shard_map.47 = (bf16[192,256]{1,0:T(8,128)(2,1)S(1)}, bf16[192,256]{1,0:T(8,128)(2,1)S(1)}, bf16[288,128]{1,0:T(8,128)(2,1)S(1)}) custom-call(s32[1]{0:T(128)} %bitcast.2.role, bf16[192,256]{1,0:T(8,128)(2,1)S(1)} %get-tuple-element.31.wide, bf16[192,256]{1,0:T(8,128)(2,1)S(1)} %get-tuple-element.32.own_turned, ...), custom_call_target="tpu_custom_call" | custom-call | flops 100000000 | bytes 1000000 | tf_op jit(solution)/shard_map/pallas_call | solution.py:395
  23.0 3.7 %collective-permute-start.4 = (bf16[288,128]{1,0:T(8,128)(2,1)S(1)}, bf16[288,128]{1,0:T(8,128)(2,1)S(1)}, u32[]{:S(2)}, u32[]{:S(2)}) collective-permute-start(bf16[288,128]{1,0:T(8,128)(2,1)S(1)} %get-tuple-element.36.own), channel_id=1, source_target_pairs={{0,7},{1,4},{2,5},{3,6},{4,1},{5,2},{6,3},{7,0},{8,13},{9,14},{10,... | collective-permute-start | bytes 221192 | tf_op jit(solution)/shard_map/ppermute | solution.py:361
  26.7 2.3 %collective-permute-done.4.other = bf16[288,128]{1,0:T(8,128)(2,1)S(1)} collective-permute-done((bf16[288,128]{1,0:T(8,128)(2,1)S(1)}, bf16[288,128]{1,0:T(8,128)(2,1)S(1)}, u32[]{:S(2)}, u32[]{:S(2)}) %collective-permute-start.4) | collective-permute-done | bytes 73760 | tf_op jit(solution)/shard_map/ppermute | solution.py:361
  28.9 1.2 %shard_map.48.left = bf16[16,256]{1,0:T(8,128)(2,1)S(1)} custom-call(bf16[288,128]{1,0:T(8,128)(2,1)S(1)} %get-tuple-element.36.own, bf16[288,128]{1,0:T(8,128)(2,1)S(1)} %collective-permute-done.4.other, f32[32,256]{1,0:T(8,128)S(1)} %get-tuple-element.49.starts), custom_call_target="tpu_custom_call" | custom-call | flops 100000000 | bytes 1000000 | tf_op jit(solution)/shard_map/pallas_call | solution.py:402
  30.2 0.1 collective-permute-start.5
  30.3 1.1 %shard_map.49.second = bf16[192,3072]{1,0:T(8,128)(2,1)S(1)} custom-call(bf16[192,256]{1,0:T(8,128)(2,1)S(1)} %get-tuple-element.34.turned, bf16[192,256]{1,0:T(8,128)(2,1)S(1)} %get-tuple-element.35.lower, bf16[16,256]{1,0:T(8,128)(2,1)S(1)} %shard_map.48.left), custom_call_target="tpu_custom_call" | custom-call | flops 100000000 | bytes 1000000 | tf_op jit(solution)/shard_map/pallas_call | solution.py:406
  31.3 0.1 collective-permute-done.5.right
  31.4 0.9 %shard_map.50 = (bf16[288,128]{1,0:T(8,128)(2,1)S(1)}, f32[1,256]{1,0:T(1,128)S(1)}) custom-call(bf16[192,3072]{1,0:T(8,128)(2,1)S(1)} %shard_map.49.second, bf16[16,256]{1,0:T(8,128)(2,1)S(1)} %collective-permute-done.5.right, f32[1,256]{1,0:T(1,128)S(1)} %get-tuple-element.37.log_in), custom_call_target="tpu_custom_call" | custom-call | flops 100000000 | bytes 1000000 | tf_op jit(solution)/shard_map/pallas_call | solution.py:410
  32.3 1.6 %collective-permute-start.6 = (bf16[288,128]{1,0:T(8,128)(2,1)S(1)}, bf16[288,128]{1,0:T(8,128)(2,1)S(1)}, u32[]{:S(2)}, u32[]{:S(2)}) collective-permute-start(bf16[288,128]{1,0:T(8,128)(2,1)S(1)} %get-tuple-element.38.own), channel_id=1, source_target_pairs={{0,20},{4,16},{8,28},{12,24},{16,4},{20,0},{24,12},{28,8},{1,21},{... | collective-permute-start | bytes 221192 | tf_op jit(solution)/shard_map/ppermute | solution.py:344
  33.9 1.1 %shard_map.51 = (bf16[192,256]{1,0:T(8,128)(2,1)S(1)}, bf16[192,256]{1,0:T(8,128)(2,1)S(1)}, bf16[192,256]{1,0:T(8,128)(2,1)S(1)}) custom-call(s32[1]{0:T(128)} %bitcast.1.role, bf16[288,128]{1,0:T(8,128)(2,1)S(1)} %get-tuple-element.38.own), custom_call_target="tpu_custom_call" | custom-call | flops 100000000 | bytes 1000000 | tf_op jit(solution)/shard_map/pallas_call | solution.py:394
  35.0 1.3 %collective-permute-done.6.other = bf16[288,128]{1,0:T(8,128)(2,1)S(1)} collective-permute-done((bf16[288,128]{1,0:T(8,128)(2,1)S(1)}, bf16[288,128]{1,0:T(8,128)(2,1)S(1)}, u32[]{:S(2)}, u32[]{:S(2)}) %collective-permute-start.6) | collective-permute-done | bytes 73760 | tf_op jit(solution)/shard_map/ppermute | solution.py:344
  36.3 1.3 %shard_map.52 = (bf16[192,256]{1,0:T(8,128)(2,1)S(1)}, bf16[192,256]{1,0:T(8,128)(2,1)S(1)}, bf16[288,128]{1,0:T(8,128)(2,1)S(1)}) custom-call(s32[1]{0:T(128)} %bitcast.1.role, bf16[192,256]{1,0:T(8,128)(2,1)S(1)} %get-tuple-element.39.wide, bf16[192,256]{1,0:T(8,128)(2,1)S(1)} %get-tuple-element.40.own_turned, ...), custom_call_target="tpu_custom_call" | custom-call | flops 100000000 | bytes 1000000 | tf_op jit(solution)/shard_map/pallas_call | solution.py:395
  37.6 3.7 %collective-permute-start.7 = (bf16[288,128]{1,0:T(8,128)(2,1)S(1)}, bf16[288,128]{1,0:T(8,128)(2,1)S(1)}, u32[]{:S(2)}, u32[]{:S(2)}) collective-permute-start(bf16[288,128]{1,0:T(8,128)(2,1)S(1)} %get-tuple-element.44.own), channel_id=1, source_target_pairs={{0,7},{1,4},{2,5},{3,6},{4,1},{5,2},{6,3},{7,0},{8,13},{9,14},{10,... | collective-permute-start | bytes 221192 | tf_op jit(solution)/shard_map/ppermute | solution.py:361
  41.3 2.3 %collective-permute-done.7.other = bf16[288,128]{1,0:T(8,128)(2,1)S(1)} collective-permute-done((bf16[288,128]{1,0:T(8,128)(2,1)S(1)}, bf16[288,128]{1,0:T(8,128)(2,1)S(1)}, u32[]{:S(2)}, u32[]{:S(2)}) %collective-permute-start.7) | collective-permute-done | bytes 73760 | tf_op jit(solution)/shard_map/ppermute | solution.py:361
  43.5 1.2 %shard_map.53.left = bf16[16,256]{1,0:T(8,128)(2,1)S(1)} custom-call(bf16[288,128]{1,0:T(8,128)(2,1)S(1)} %get-tuple-element.44.own, bf16[288,128]{1,0:T(8,128)(2,1)S(1)} %collective-permute-done.7.other, f32[32,256]{1,0:T(8,128)S(1)} %get-tuple-element.48.starts), custom_call_target="tpu_custom_call" | custom-call | flops 100000000 | bytes 1000000 | tf_op jit(solution)/shard_map/pallas_call | solution.py:402
  44.8 0.1 collective-permute-start.8
  44.8 1.1 %shard_map.54.second = bf16[192,3072]{1,0:T(8,128)(2,1)S(1)} custom-call(bf16[192,256]{1,0:T(8,128)(2,1)S(1)} %get-tuple-element.42.turned, bf16[192,256]{1,0:T(8,128)(2,1)S(1)} %get-tuple-element.43.lower, bf16[16,256]{1,0:T(8,128)(2,1)S(1)} %shard_map.53.left), custom_call_target="tpu_custom_call" | custom-call | flops 100000000 | bytes 1000000 | tf_op jit(solution)/shard_map/pallas_call | solution.py:406
  45.9 0.1 collective-permute-done.8.right
  46.0 2.2 %shard_map.55 = (f32[144,144]{1,0:T(8,128)}, f32[1,1]{1,0:T(1,128)}) custom-call(s32[1]{0:T(128)} %bitcast.role, bf16[192,3072]{1,0:T(8,128)(2,1)S(1)} %shard_map.54.second, bf16[16,256]{1,0:T(8,128)(2,1)S(1)} %collective-permute-done.8.right, f32[1,256]{1,0:T(1,128)S(1)} %get-tuple-element.45.log_in), custom_call_target="tpu_custom_call" | custom-call | flops 100000000 | bytes 1000000 | tf_op jit(solution)/shard_map/pallas_call | solution.py:415
  (2 shorter events, 0.0 us)
Async XLA Ops:
  0.6 4.0 %collective-permute-start = (f32[144,144]{1,0:T(8,128)}, f32[144,144]{1,0:T(8,128)S(1)}, u32[]{:S(2)}, u32[]{:S(2)}) collective-permute-start(f32[144,144]{1,0:T(8,128)} %bitcast.12), channel_id=1, source_target_pairs={{0,4},{4,0},{8,12},{12,8},{16,20},{20,16},{24,28},{28,24},{1,5},{5... | collective-permute-start | bytes 248840 | tf_op jit(solution)/shard_map/ppermute | solution.py:344
  1.3 0.9 %copy-start = (f32[1,1,144,144]{3,2,1,0:T(8,128)S(1)}, f32[1,1,144,144]{3,2,1,0:T(8,128)}, u32[]{:S(2)}) copy-start(f32[1,1,144,144]{3,2,1,0:T(8,128)} %param.2) | copy-start | bytes 248836
  2.2 0.8 %copy-start.1 = (f32[3,12,144]{2,1,0:T(8,128)S(1)}, f32[3,12,144]{2,1,0:T(8,128)}, u32[]{:S(2)}) copy-start(f32[3,12,144]{2,1,0:T(8,128)} %start.1) | copy-start | bytes 62212
  7.3 6.9 %collective-permute-start.1 = (bf16[288,128]{1,0:T(8,128)(2,1)S(1)}, bf16[288,128]{1,0:T(8,128)(2,1)S(1)}, u32[]{:S(2)}, u32[]{:S(2)}) collective-permute-start(bf16[288,128]{1,0:T(8,128)(2,1)S(1)} %get-tuple-element.28.own), channel_id=1, source_target_pairs={{0,7},{1,4},{2,5},{3,6},{4,1},{5,2},{6,3},{7,0},{8,13},{9,14},{10,... | collective-permute-start | bytes 221192 | tf_op jit(solution)/shard_map/ppermute | solution.py:361
  15.5 1.2 %collective-permute-start.2 = (bf16[16,256]{1,0:T(8,128)(2,1)S(1)}, bf16[16,256]{1,0:T(8,128)(2,1)S(1)}, u32[]{:S(2)}, u32[]{:S(2)}) collective-permute-start(bf16[16,256]{1,0:T(8,128)(2,1)S(1)} %shard_map.43.left), channel_id=1, source_target_pairs={{0,4},{4,0},{8,12},{12,8},{16,20},{20,16},{24,28},{28,24},{1,5},{5... | collective-permute-start | bytes 24584 | tf_op jit(solution)/shard_map/ppermute | solution.py:344
  17.6 4.1 %collective-permute-start.3 = (bf16[288,128]{1,0:T(8,128)(2,1)S(1)}, bf16[288,128]{1,0:T(8,128)(2,1)S(1)}, u32[]{:S(2)}, u32[]{:S(2)}) collective-permute-start(bf16[288,128]{1,0:T(8,128)(2,1)S(1)} %get-tuple-element.30.own), channel_id=1, source_target_pairs={{0,12},{4,8},{8,4},{12,0},{16,28},{20,24},{24,20},{28,16},{1,13},{... | collective-permute-start | bytes 221192 | tf_op jit(solution)/shard_map/ppermute | solution.py:344
  23.0 6.0 %collective-permute-start.4 = (bf16[288,128]{1,0:T(8,128)(2,1)S(1)}, bf16[288,128]{1,0:T(8,128)(2,1)S(1)}, u32[]{:S(2)}, u32[]{:S(2)}) collective-permute-start(bf16[288,128]{1,0:T(8,128)(2,1)S(1)} %get-tuple-element.36.own), channel_id=1, source_target_pairs={{0,7},{1,4},{2,5},{3,6},{4,1},{5,2},{6,3},{7,0},{8,13},{9,14},{10,... | collective-permute-start | bytes 221192 | tf_op jit(solution)/shard_map/ppermute | solution.py:361
  30.2 1.2 %collective-permute-start.5 = (bf16[16,256]{1,0:T(8,128)(2,1)S(1)}, bf16[16,256]{1,0:T(8,128)(2,1)S(1)}, u32[]{:S(2)}, u32[]{:S(2)}) collective-permute-start(bf16[16,256]{1,0:T(8,128)(2,1)S(1)} %shard_map.48.left), channel_id=1, source_target_pairs={{0,4},{4,0},{8,12},{12,8},{16,20},{20,16},{24,28},{28,24},{1,5},{5... | collective-permute-start | bytes 24584 | tf_op jit(solution)/shard_map/ppermute | solution.py:344
  32.3 4.0 %collective-permute-start.6 = (bf16[288,128]{1,0:T(8,128)(2,1)S(1)}, bf16[288,128]{1,0:T(8,128)(2,1)S(1)}, u32[]{:S(2)}, u32[]{:S(2)}) collective-permute-start(bf16[288,128]{1,0:T(8,128)(2,1)S(1)} %get-tuple-element.38.own), channel_id=1, source_target_pairs={{0,20},{4,16},{8,28},{12,24},{16,4},{20,0},{24,12},{28,8},{1,21},{... | collective-permute-start | bytes 221192 | tf_op jit(solution)/shard_map/ppermute | solution.py:344
  37.6 5.9 %collective-permute-start.7 = (bf16[288,128]{1,0:T(8,128)(2,1)S(1)}, bf16[288,128]{1,0:T(8,128)(2,1)S(1)}, u32[]{:S(2)}, u32[]{:S(2)}) collective-permute-start(bf16[288,128]{1,0:T(8,128)(2,1)S(1)} %get-tuple-element.44.own), channel_id=1, source_target_pairs={{0,7},{1,4},{2,5},{3,6},{4,1},{5,2},{6,3},{7,0},{8,13},{9,14},{10,... | collective-permute-start | bytes 221192 | tf_op jit(solution)/shard_map/ppermute | solution.py:361
  44.8 1.2 %collective-permute-start.8 = (bf16[16,256]{1,0:T(8,128)(2,1)S(1)}, bf16[16,256]{1,0:T(8,128)(2,1)S(1)}, u32[]{:S(2)}, u32[]{:S(2)}) collective-permute-start(bf16[16,256]{1,0:T(8,128)(2,1)S(1)} %shard_map.53.left), channel_id=1, source_target_pairs={{0,4},{4,0},{8,12},{12,8},{16,20},{20,16},{24,28},{28,24},{1,5},{5... | collective-permute-start | bytes 24584 | tf_op jit(solution)/shard_map/ppermute | solution.py:344

commit v3 on v2

--- a/solution.py
+++ b/solution.py
@@ -15,6 +15,7 @@
 ROWS = CHI * PAD
 LANES = PAD * PAD
 VMEM_BYTES = 8 << 20
+PIVOT = 1.0 / 64
 F32 = jnp.float32
 BF16 = jnp.bfloat16
 
@@ -55,9 +56,11 @@
     return one_hot((i == source) & (s < CHI) & (t < CHI))
 
 
-def row_spread():
+def row_spread(turn):
     i, j = iota((ROWS, CHI * CHI), 0), iota((ROWS, CHI * CHI), 1)
-    return one_hot((j == minor(i) * CHI + group(i)) & (minor(i) < CHI))
+    s, t = group(i), minor(i)
+    source = t * CHI + s if turn else s * CHI + t
+    return one_hot((j == source) & (t < CHI))
 
 
 def block_swap(x):
@@ -109,6 +112,16 @@
     return jnp.concatenate([a, b, c], axis=0)
 
 
+def parts2(x):
+    a = x.astype(BF16)
+    return jnp.concatenate([a, (x - a.astype(F32)).astype(BF16)], axis=0)
+
+
+def fold2(y):
+    n = y.shape[0] // 2
+    return y[n:] + y[:n]
+
+
 def fold3(y):
     n = y.shape[0] // 3
     return (y[2 * n :] + y[n : 2 * n]) + y[:n]
@@ -132,22 +145,31 @@
     return jnp.concatenate([x[:ROWS], jnp.concatenate([first, last], axis=0)], axis=1)
 
 
+def turn(upper, swap):
+    return block_swap(mm(upper, swap).astype(BF16))
+
+
+def upper_product(crossed, crossed_m):
+    product = mm(crossed_m, crossed, NT).astype(BF16)
+    return block_swap(widen(product))
+
+
 def upper_part(upper, swap):
-    turned = block_swap(mm(upper, swap).astype(BF16))
-    turned_m = mm(turned, swap).astype(BF16)
-    product = mm(turned_m, turned, TN).astype(BF16)
-    return turned, block_swap(product[:ROWS])
+    row_swap = swap[:ROWS, :ROWS]
+    crossed_m = block_swap(mm(row_swap, upper).astype(BF16))
+    return upper_product(mm(row_swap, crossed_m).astype(BF16), crossed_m)
 
 
 def lower_part(lower, swap):
-    lower_m = mm(swap[:, :ROWS], lower).astype(BF16)
-    product = mm(lower_m[:ROWS], lower, NT).astype(BF16)
+    row_swap = swap[:ROWS, :ROWS]
+    lower_m = mm(row_swap, lower).astype(BF16)
+    product = mm(lower_m, lower, NT).astype(BF16)
     product = block_swap(widen(product))
-    return mm(swap[:ROWS, :ROWS], product).astype(BF16)
-
-
-def outer_part(upper_product, lower_product):
-    outer = mm(upper_product, lower_product, NT).astype(BF16)
+    return mm(row_swap, product).astype(BF16)
+
+
+def outer_part(high, low):
+    outer = mm(high, low, NT).astype(BF16)
     return block_swap(widen(outer))
 
 
@@ -161,37 +183,59 @@
 
 
 def orthonormal(y):
-    gram = lax.dot_general(
-        y, y, NT, preferred_element_type=F32, precision=lax.Precision.HIGHEST
-    )
+    pieces = parts2(y)
+    high, low = pieces[:PAD], pieces[PAD:]
+    gram = fold2(mm(pieces, high, NT)) + mm(high, low, NT)
     width = y.shape[1]
     row = iota((PAD, 128), 0)
     cols = [jnp.broadcast_to(gram[:, k : k + 1], (PAD, 128)) for k in range(CHI)]
+    floors = [jnp.broadcast_to(cols[k][k : k + 1, :], (PAD, 128)) * PIVOT for k in range(CHI)]
     scale = jnp.zeros((PAD, 128), F32)
+    good = jnp.ones((PAD, 128), F32)
     for k in range(CHI):
         pivot = jnp.broadcast_to(cols[k][k : k + 1, :], (PAD, 128))
-        scale = jnp.where(row == k, lax.rsqrt(pivot), scale)
-        factor = jnp.where(row > k, cols[k] / pivot, 0.0)
+        good = jnp.where(pivot >= floors[k], good, 0.0)
+        inverse = lax.rsqrt(pivot)
+        scale = jnp.where(row == k, inverse, scale)
+        factor = jnp.where(row > k, cols[k] * (inverse * inverse), 0.0)
         for j in range(k + 1, CHI):
             cols[j] = cols[j] - factor * jnp.broadcast_to(cols[j][k : k + 1, :], (PAD, 128))
         wide = jnp.concatenate([factor] * (width // 128), axis=1)
         y = y - wide * jnp.broadcast_to(y[k : k + 1, :], (PAD, width))
-    return y * jnp.concatenate([scale] * (width // 128), axis=1)
-
-
-def iso_body(own, other, start, start_turned, swap):
+    return y * jnp.concatenate([scale] * (width // 128), axis=1), good
+
+
+def exact_iso(own, other, start, start_turned, shift, swap):
+    pieces = parts3(start)
+    image = fold3(mm(pieces, own, NT) + mm(pieces, other, NT))
+    basis, _ = orthonormal(widen(image) + shift * start_turned)
+    pieces = parts3(basis)
+    image = fold3(mm(pieces[:, :ROWS], own) + mm(pieces[:, :ROWS], other))
+    basis, _ = orthonormal(image + shift * fold3(mm(pieces, swap)))
+    return basis
+
+
+def iso_kernel(own, other, starts, iso_o):
+    own, other = unpack(own[...]), unpack(other[...])
+    start, start_turned = starts[:PAD], starts[PAD:]
+    swap = swap_matrix()
     total = own.astype(F32) + other.astype(F32)
     i, j = iota((ROWS, LANES), 0), iota((ROWS, LANES), 1)
     diagonal = (group(i) == minor(j)) & (minor(i) == group(j))
-    shift = jnp.sum(jnp.where(diagonal, total, 0.0)) / (CHI * CHI)
-    pieces = parts3(start)
-    image = fold3(mm(pieces, own, NT) + mm(pieces, other, NT))
-    image = widen(image) + shift * start_turned
-    basis = orthonormal(image)
-    pieces = parts3(basis)
-    image = fold3(mm(pieces[:, :ROWS], own) + mm(pieces[:, :ROWS], other))
-    image = image + shift * fold3(mm(pieces, swap))
-    return orthonormal(image).astype(BF16)
+    trace = jnp.sum(jnp.where(diagonal, total, 0.0), axis=0, keepdims=True)
+    shift = jnp.sum(trace, axis=1, keepdims=True) / (CHI * CHI)
+    unit = 1.0 / shift
+    pieces = parts2(start)
+    image = fold2(mm(pieces, own, NT) + mm(pieces, other, NT))
+    image = widen(image) * unit + start_turned
+    pieces = parts2(image)
+    image = fold2(mm(pieces[:, :ROWS], own) + mm(pieces[:, :ROWS], other)) * unit
+    basis, good = orthonormal(image + fold2(mm(pieces, swap)))
+    iso_o[...] = basis.astype(BF16)
+
+    @pl.when(jnp.logical_not(jnp.min(good[:1]) > 0.5))
+    def _():
+        iso_o[...] = exact_iso(own, other, start, start_turned, shift, swap).astype(BF16)
 
 
 def first_second(turned, lower, left, second_ref):
@@ -228,103 +272,98 @@
     return mm(second_ref[...], kron_ref[...])
 
 
-def placed(site, mirror):
-    spaced = mm(row_spread(), site.astype(BF16)).astype(BF16)
+def placed(site, mirror, turned):
+    spaced = mm(row_spread(turned), site).astype(BF16)
     return block_swap(mm(spaced, spread_matrix(mirror)).astype(BF16))
 
 
-def first_own_kernel(role, own, start, own_o, starts_o, site, basis, sems):
-    copies = [
-        pltpu.make_async_copy(own, site, sems.at[0]),
-        pltpu.make_async_copy(start, basis, sems.at[1]),
-    ]
-    for copy in copies:
-        copy.start()
-    copies[0].wait()
-    own_o[...] = placed(site[...], role[0] != 0)
-    copies[1].wait()
+def pick(is_upper, own, other):
+    return jnp.where(is_upper, own, other), jnp.where(is_upper, other, own)
+
+
+def cast_kernel(own, cast_o):
+    cast_o[...] = own[...].astype(BF16)
+
+
+def first_gram_kernel(role, own, other, lower_o, gram_o):
     swap = swap_matrix()
+    mirror = role[0] != 0
+    upper, lower = pick(role[1] != 0, own[...], other[...].astype(BF16))
+    crossed = placed(upper, mirror, False)
+    crossed_m = mm(swap[:ROWS, :ROWS], crossed).astype(BF16)
+    lower = placed(lower, mirror, True)
+    lower_o[...] = lower
+    high = upper_product(crossed, crossed_m)
+    gram_o[...] = pack(outer_part(high, lower_part(lower, swap)))
+
+
+def first_turn_kernel(role, own, other, start, turned_o, starts_o):
+    swap = swap_matrix()
+    upper, _ = pick(role[1] != 0, own[...], other[...].astype(BF16))
+    turned_o[...] = turn(placed(upper, role[0] != 0, True), swap)
     for level in range(LEVELS):
-        plain, turn = start_body(basis[level], swap)
-        starts_o[level, :PAD], starts_o[level, PAD:] = plain, turn
-
-
-def first_gram_kernel(role, own, other, lower_o, turned_o, gram_o):
-    swap = swap_matrix()
-    mine, theirs = own[...], placed(other[...], role[0] != 0)
-    is_upper = role[1] != 0
-    upper, lower = jnp.where(is_upper, mine, theirs), jnp.where(is_upper, theirs, mine)
-    turned, upper_product = upper_part(upper, swap)
-    gram_o[...] = pack(outer_part(upper_product, lower_part(lower, swap)))
-    lower_o[...], turned_o[...] = lower, turned
-
-
-def own_kernel(role, own, wide_o, turned_o, product_o):
+        plain, turned = start_body(start[level], swap)
+        starts_o[level, :PAD], starts_o[level, PAD:] = plain, turned
+
+
+def own_kernel(role, own, wide_o, product_o):
     swap = swap_matrix()
     wide = unpack(own[...])
     wide_o[...] = wide
 
     @pl.when(role[0] != 0)
     def _():
-        turned_o[...], product_o[...] = upper_part(wide, swap)
+        product_o[...] = upper_part(wide, swap)
 
     @pl.when(role[0] == 0)
     def _():
-        turned_o[...] = jnp.zeros_like(turned_o)
         product_o[...] = lower_part(wide, swap)
 
 
-def gram_kernel(role, wide, own_turned, product, other, lower_o, turned_o, gram_o, up, low):
+def gram_kernel(role, wide, product, other, upper_o, lower_o, gram_o, high, low):
     swap = swap_matrix()
     theirs = unpack(other[...])
 
     @pl.when(role[0] != 0)
     def _():
-        lower_o[...], turned_o[...] = theirs, own_turned[...]
-        up[...], low[...] = product[...], lower_part(theirs, swap)
+        upper_o[...], lower_o[...] = wide[...], theirs
+        high[...], low[...] = product[...], lower_part(theirs, swap)
 
     @pl.when(role[0] == 0)
     def _():
-        lower_o[...] = wide[...]
-        turned_o[...], up[...] = upper_part(theirs, swap)
-        low[...] = product[...]
-
-    gram_o[...] = pack(outer_part(up[...], low[...]))
-
-
-def iso_kernel(own, other, starts, iso_o):
-    iso_o[...] = iso_body(unpack(own[...]), unpack(other[...]), starts[:PAD], starts[PAD:], swap_matrix())
+        upper_o[...], lower_o[...] = theirs, wide[...]
+        high[...], low[...] = upper_part(theirs, swap), product[...]
+
+    gram_o[...] = pack(outer_part(high[...], low[...]))
+
+
+def turn_kernel(upper, turned_o):
+    turned_o[...] = turn(upper[...], swap_matrix())
 
 
 def second_kernel(turned, lower, left, second_o):
     first_second(turned[...], lower[...], left[...], second_o)
 
 
-def scaled(merged):
-    mean = jnp.sum(merged * merged) / (CHI**4)
-    return jnp.sqrt(jnp.full((1, LANES), mean) + 1e-06)
+def mean_square(merged):
+    total = jnp.sum(jnp.sum(merged * merged, axis=0, keepdims=True), axis=1, keepdims=True)
+    return total / (CHI**4) + 1e-06
 
 
 def third_kernel(second, right, log_in, next_o, log_o, kron):
     merged = third(second, right[...], kron)
-    norm = scaled(merged)
-    next_o[...] = pack((merged / norm).astype(BF16))
-    log_o[...] = log_in[...] + jnp.log(norm)
+    mean = mean_square(merged)
+    next_o[...] = pack((merged * lax.rsqrt(mean)).astype(BF16))
+    log_o[...] = log_in[...] + 0.5 * jnp.log(mean)
 
 
 def last_kernel(role, second, right, log_in, coarse_o, log_o, kron):
     merged = third(second, right[...], kron)
-    norm = scaled(merged)
-    log_o[...] = (log_in[...] + jnp.log(norm))[:, :1]
-    wide = block_swap(merged / norm)
-    spread, rows = spread_matrix(role[0] != 0), row_spread()
-    total = jnp.zeros((CHI * CHI, CHI * CHI), F32)
-    high = wide.astype(BF16)
-    low = (wide - high.astype(F32)).astype(BF16)
-    for part in (high, low):
-        narrow = mm(part, spread, NT).astype(BF16)
-        total = total + mm(rows, narrow, TN)
-    coarse_o[...] = total
+    mean = mean_square(merged)
+    log_o[...] = log_in[...] + 0.5 * jnp.log(mean)
+    wide = block_swap(merged.astype(BF16))
+    narrow = mm(wide, spread_matrix(role[0] != 0), NT).astype(BF16)
+    coarse_o[...] = mm(row_spread(True), narrow, TN) * lax.rsqrt(mean)
 
 
 def call(kernel, outs, places, scratch=()):
@@ -365,40 +404,38 @@
     square = CHI * CHI
     row = lax.axis_index("row")
     mirror = mirrored(row)
-    vmem, smem, hbm = pltpu.VMEM, pltpu.SMEM, pltpu.HBM
+    vmem, smem = pltpu.VMEM, pltpu.SMEM
     mat, packed = ((ROWS, LANES), BF16), ((ROWS * 3 // 2, 128), BF16)
     kron = [vmem((CHI * LANES, LANES), BF16)]
-    log_total = jnp.zeros((1, LANES), F32)
+    log_total = jnp.zeros((1, 1), F32)
     own = site_tensors[0, 0]
     for level in range(LEVELS):
         is_upper = 1 - (row >> level & 1)
         if level == 0:
             other = from_partner(own, 1)
             role = jnp.stack([mirror, is_upper]).astype(jnp.int32)
-            wide, starts = call(
-                first_own_kernel,
+            (own,) = call(cast_kernel, [((square, square), BF16)], [vmem])(own)
+            lower, gram = call(first_gram_kernel, [mat, packed], [smem, vmem, vmem])(
+                role, own, other
+            )
+            gram_other = from_bond(gram)
+            turned, starts = call(
+                first_turn_kernel,
                 [mat, ((LEVELS, 2 * PAD, LANES), F32)],
-                [smem, hbm, hbm],
-                [
-                    vmem((square, square), F32),
-                    vmem((LEVELS, CHI, square), F32),
-                    pltpu.SemaphoreType.DMA((2,)),
-                ],
-            )(role, own, start_basis)
-            lower, turned, gram = call(first_gram_kernel, [mat, mat, packed], [smem, vmem, vmem])(
-                role, wide, other
-            )
+                [smem, vmem, vmem, vmem],
+            )(role, own, other, start_basis)
         else:
             other = from_partner(own, 1 << level | 1)
             role = is_upper.reshape(1).astype(jnp.int32)
-            wide, own_turned, product = call(own_kernel, [mat, mat, mat], [smem, vmem])(role, own)
-            lower, turned, gram = call(
+            wide, product = call(own_kernel, [mat, mat], [smem, vmem])(role, own)
+            upper, lower, gram = call(
                 gram_kernel,
                 [mat, mat, packed],
-                [smem, vmem, vmem, vmem, vmem],
+                [smem, vmem, vmem, vmem],
                 [vmem(*mat), vmem(*mat)],
-            )(role, wide, own_turned, product, other)
-        gram_other = from_bond(gram)
+            )(role, wide, product, other)
+            gram_other = from_bond(gram)
+            (turned,) = call(turn_kernel, [mat], [vmem])(upper)
         (left,) = call(iso_kernel, [((PAD, LANES), BF16)], [vmem] * 3)(
             gram, gram_other, starts[level]
         )
@@ -407,7 +444,7 @@
             turned, lower, left
         )
         if level < LEVELS - 1:
-            own, log_total = call(third_kernel, [packed, ((1, LANES), F32)], [vmem] * 3, kron)(
+            own, log_total = call(third_kernel, [packed, ((1, 1), F32)], [vmem] * 3, kron)(
                 second, right, log_total
             )
         else:

time: 48.4 us -> 47.4 us (0.979)
  waiting for transfers between devices: 9.52 us -> 7.85 us
  Pallas kernels: 19.9 us -> 21.2 us
  starting transfers between devices: 16.2 us -> 15.6 us
    ppermute x3, waiting for transfers between devices: 6.63 us -> 4.67 us  [from_bond(): return lax.ppermute(array, ('row', 'col'), pairs)]
    pallas_call x8 -> x11, Pallas kernels: 10.9 us -> 12.8 us  [the longest x2 3.25 us: per_device(): call(third_kernel, [packed, ((1, 1), F32)], [vmem] * 3, kron)]
    pallas_call x3, Pallas kernels: 3.68 us -> 2.65 us  [per_device(): call(iso_kernel, [((PAD, LANES), BF16)], [vmem] * 3)]
    ppermute x3, starting transfers between devices: 12.2 us -> 11.4 us  [from_bond(): return lax.ppermute(array, ('row', 'col'), pairs)]
  transfers between devices with their start and end apart: 9 -> 9, of which waited for: 8 -> 8; matrix products, arithmetic and copies ran while one was open for 0% -> 0% of each run, Pallas kernels for 15% -> 16%
where the time goes in v3:
time: 47.4 us; the launch traced here: 47.2 us
  Pallas kernels  21.2 us (45%)
  starting transfers between devices  15.6 us (33%)
  waiting for transfers between devices  7.85 us (17%)
  local copies, waits for them, and re-layouts  1.72 us (4%)
  between operations  0.78 us (2%)
    ppermute x3, starting transfers between devices, from_bond(): return lax.ppermute(array, ('row', 'col'), pairs)  11.4 us
    ppermute x3, waiting for transfers between devices, from_bond(): return lax.ppermute(array, ('row', 'col'), pairs)  4.67 us
    ppermute x6, starting transfers between devices, from_partner(): return lax.ppermute(array, 'row', [(i, i ^ flip) for i in range(count)])  4.18 us
    pallas_call x2, Pallas kernels, per_device(): call(third_kernel, [packed, ((1, 1), F32)], [vmem] * 3, kron)  3.25 us
    ppermute x6, waiting for transfers between devices, from_partner(): return lax.ppermute(array, 'row', [(i, i ^ flip) for i in range(count)])  3.18 us
    pallas_call x3, Pallas kernels, per_device(): call(second_kernel, [((ROWS, CHI * LANES), BF16)], [vmem] * 3)  3.16 us
    pallas_call x3, Pallas kernels, per_device(): call(iso_kernel, [((PAD, LANES), BF16)], [vmem] * 3)  2.65 us
    pallas_call x1, Pallas kernels, per_device(): call(first_gram_kernel, [mat, packed], [smem, vmem, vmem])(role, own, other)  2.63 us
  transfers between devices with their start and end apart: 9, of which 8 were waited for; matrix products, arithmetic and copies ran while one was open for 0% of the time, Pallas kernels for 16%

profile of v3, /device:TPU:0, one launch (start us, length us, event | category | flops | bytes accessed | tf_op | source)
XLA Modules:
  0.0 47.2 jit_solution(16671390198119190566)
XLA Ops:
  0.6 0.6 %collective-permute-start = (f32[144,144]{1,0:T(8,128)}, f32[144,144]{1,0:T(8,128)S(1)}, u32[]{:S(2)}, u32[]{:S(2)}) collective-permute-start(f32[144,144]{1,0:T(8,128)} %bitcast.12), channel_id=1, source_target_pairs={{0,4},{4,0},{8,12},{12,8},{16,20},{20,16},{24,28},{28,24},{1,5},{5... | collective-permute-start | bytes 248840 | tf_op jit(solution)/shard_map/ppermute | solution.py:383
  1.2 0.0 copy-start
  1.2 0.9 %copy-done = f32[1,1,144,144]{3,2,1,0:T(8,128)S(1)} copy-done((f32[1,1,144,144]{3,2,1,0:T(8,128)S(1)}, f32[1,1,144,144]{3,2,1,0:T(8,128)}, u32[]{:S(2)}) %copy-start) | copy-done | bytes 82968
  2.1 0.1 pad_add_fusion.role
  2.2 0.2 collective-permute-done.other
  2.4 2.6 %shard_map.43 = (bf16[192,256]{1,0:T(8,128)(2,1)S(1)}, bf16[288,128]{1,0:T(8,128)(2,1)S(1)}) custom-call(s32[2]{0:T(128)S(1)} %pad_add_fusion.role, bf16[144,144]{1,0:T(8,128)(2,1)S(1)} %shard_map.41.own, f32[144,144]{1,0:T(8,128)S(1)} %collective-permute-done.other), custom_call_target="tpu_custom_call" | custom-call | flops 100000000 | bytes 1000000 | tf_op jit(solution)/shard_map/pallas_call | solution.py:418
  5.0 4.7 %collective-permute-start.1 = (bf16[288,128]{1,0:T(8,128)(2,1)S(1)}, bf16[288,128]{1,0:T(8,128)(2,1)S(1)}, u32[]{:S(2)}, u32[]{:S(2)}) collective-permute-start(bf16[288,128]{1,0:T(8,128)(2,1)S(1)} %get-tuple-element.24.own), channel_id=1, source_target_pairs={{0,7},{1,4},{2,5},{3,6},{4,1},{5,2},{6,3},{7,0},{8,13},{9,14},{10,... | collective-permute-start | bytes 221192 | tf_op jit(solution)/shard_map/ppermute | solution.py:400
  9.8 0.0 copy-start.1
  9.8 0.8 %copy-done.1 = f32[3,12,144]{2,1,0:T(8,128)S(1)} copy-done((f32[3,12,144]{2,1,0:T(8,128)S(1)}, f32[3,12,144]{2,1,0:T(8,128)}, u32[]{:S(2)}) %copy-start.1) | copy-done | bytes 20760
  10.6 1.5 %shard_map.42 = (bf16[192,256]{1,0:T(8,128)(2,1)S(1)}, f32[3,32,256]{2,1,0:T(8,128)S(1)}) custom-call(s32[2]{0:T(128)S(1)} %pad_add_fusion.role, bf16[144,144]{1,0:T(8,128)(2,1)S(1)} %shard_map.41.own, f32[144,144]{1,0:T(8,128)S(1)} %collective-permute-done.other, f32[3,12,144]{2,1,0:T(8,128)S(1)} %copy-done.1), custom_call_target="tpu_custom_call" | custom-call | flops 100000000 | bytes 1000000 | tf_op jit(solution)/shard_map/pallas_call | solution.py:422
  12.0 0.0 collective-permute-done.1.other
  12.1 0.9 %shard_map.44.left = bf16[16,256]{1,0:T(8,128)(2,1)S(1)} custom-call(bf16[288,128]{1,0:T(8,128)(2,1)S(1)} %get-tuple-element.24.own, bf16[288,128]{1,0:T(8,128)(2,1)S(1)} %collective-permute-done.1.other, f32[32,256]{1,0:T(8,128)S(1)} %get-tuple-element.44.starts), custom_call_target="tpu_custom_call" | custom-call | flops 100000000 | bytes 1000000 | tf_op jit(solution)/shard_map/pallas_call | solution.py:439
  13.0 0.1 collective-permute-start.2
  13.0 1.1 %shard_map.45.second = bf16[192,3072]{1,0:T(8,128)(2,1)S(1)} custom-call(bf16[192,256]{1,0:T(8,128)(2,1)S(1)} %get-tuple-element.22.turned, bf16[192,256]{1,0:T(8,128)(2,1)S(1)} %get-tuple-element.23.lower, bf16[16,256]{1,0:T(8,128)(2,1)S(1)} %shard_map.44.left), custom_call_target="tpu_custom_call" | custom-call | flops 100000000 | bytes 1000000 | tf_op jit(solution)/shard_map/pallas_call | solution.py:443
  14.1 0.1 collective-permute-done.2.right
  14.2 1.3 %shard_map.46 = (bf16[288,128]{1,0:T(8,128)(2,1)S(1)}, f32[1,1]{1,0:T(1,128)}) custom-call(bf16[192,3072]{1,0:T(8,128)(2,1)S(1)} %shard_map.45.second, bf16[16,256]{1,0:T(8,128)(2,1)S(1)} %collective-permute-done.2.right, f32[1,1]{1,0:T(1,128)} %constant.13.clone.1.log_in), custom_call_target="tpu_custom_call" | custom-call | flops 100000000 | bytes 1000000 | tf_op jit(solution)/shard_map/pallas_call | solution.py:447
  15.5 1.9 %collective-permute-start.3 = (bf16[288,128]{1,0:T(8,128)(2,1)S(1)}, bf16[288,128]{1,0:T(8,128)(2,1)S(1)}, u32[]{:S(2)}, u32[]{:S(2)}) collective-permute-start(bf16[288,128]{1,0:T(8,128)(2,1)S(1)} %get-tuple-element.26.own), channel_id=1, source_target_pairs={{0,12},{4,8},{8,4},{12,0},{16,28},{20,24},{24,20},{28,16},{1,13},{... | collective-permute-start | bytes 221192 | tf_op jit(solution)/shard_map/ppermute | solution.py:383
  17.4 1.1 %shard_map.47 = (bf16[192,256]{1,0:T(8,128)(2,1)S(1)}, bf16[192,256]{1,0:T(8,128)(2,1)S(1)}) custom-call(s32[1]{0:T(128)} %bitcast.2.role, bf16[288,128]{1,0:T(8,128)(2,1)S(1)} %get-tuple-element.26.own), custom_call_target="tpu_custom_call" | custom-call | flops 100000000 | bytes 1000000 | tf_op jit(solution)/shard_map/pallas_call | solution.py:430
  18.4 1.3 %collective-permute-done.3.other = bf16[288,128]{1,0:T(8,128)(2,1)S(1)} collective-permute-done((bf16[288,128]{1,0:T(8,128)(2,1)S(1)}, bf16[288,128]{1,0:T(8,128)(2,1)S(1)}, u32[]{:S(2)}, u32[]{:S(2)}) %collective-permute-start.3) | collective-permute-done | bytes 73760 | tf_op jit(solution)/shard_map/ppermute | solution.py:383
  19.7 1.3 %shard_map.48 = (bf16[192,256]{1,0:T(8,128)(2,1)S(1)}, bf16[192,256]{1,0:T(8,128)(2,1)S(1)}, bf16[288,128]{1,0:T(8,128)(2,1)S(1)}) custom-call(s32[1]{0:T(128)} %bitcast.2.role, bf16[192,256]{1,0:T(8,128)(2,1)S(1)} %get-tuple-element.27.wide, bf16[192,256]{1,0:T(8,128)(2,1)S(1)} %get-tuple-element.28.product, bf16[288,128]{1,0:T(8,128)(2,1)S(1)} %collective-permute-done.3.other), custom_call_target="tpu_custom_call" | custom-call | flops 100000000 | bytes 1000000 | tf_op jit(solution)/shard_map/pallas_call | solution.py:431
  21.0 3.4 %collective-permute-start.4 = (bf16[288,128]{1,0:T(8,128)(2,1)S(1)}, bf16[288,128]{1,0:T(8,128)(2,1)S(1)}, u32[]{:S(2)}, u32[]{:S(2)}) collective-permute-start(bf16[288,128]{1,0:T(8,128)(2,1)S(1)} %get-tuple-element.31.own), channel_id=1, source_target_pairs={{0,7},{1,4},{2,5},{3,6},{4,1},{5,2},{6,3},{7,0},{8,13},{9,14},{10,... | collective-permute-start | bytes 221192 | tf_op jit(solution)/shard_map/ppermute | solution.py:400
  24.4 0.4 shard_map.49.turned
  24.8 2.2 %collective-permute-done.4.other = bf16[288,128]{1,0:T(8,128)(2,1)S(1)} collective-permute-done((bf16[288,128]{1,0:T(8,128)(2,1)S(1)}, bf16[288,128]{1,0:T(8,128)(2,1)S(1)}, u32[]{:S(2)}, u32[]{:S(2)}) %collective-permute-start.4) | collective-permute-done | bytes 73760 | tf_op jit(solution)/shard_map/ppermute | solution.py:400
  27.0 0.9 %shard_map.50.left = bf16[16,256]{1,0:T(8,128)(2,1)S(1)} custom-call(bf16[288,128]{1,0:T(8,128)(2,1)S(1)} %get-tuple-element.31.own, bf16[288,128]{1,0:T(8,128)(2,1)S(1)} %collective-permute-done.4.other, f32[32,256]{1,0:T(8,128)S(1)} %get-tuple-element.43.starts), custom_call_target="tpu_custom_call" | custom-call | flops 100000000 | bytes 1000000 | tf_op jit(solution)/shard_map/pallas_call | solution.py:439
  27.9 0.1 collective-permute-start.5
  28.0 1.1 %shard_map.51.second = bf16[192,3072]{1,0:T(8,128)(2,1)S(1)} custom-call(bf16[192,256]{1,0:T(8,128)(2,1)S(1)} %shard_map.49.turned, bf16[192,256]{1,0:T(8,128)(2,1)S(1)} %get-tuple-element.30.lower, bf16[16,256]{1,0:T(8,128)(2,1)S(1)} %shard_map.50.left), custom_call_target="tpu_custom_call" | custom-call | flops 100000000 | bytes 1000000 | tf_op jit(solution)/shard_map/pallas_call | solution.py:443
  29.1 0.1 collective-permute-done.5.right
  29.2 2.0 %shard_map.52 = (bf16[288,128]{1,0:T(8,128)(2,1)S(1)}, f32[1,1]{1,0:T(1,128)}) custom-call(bf16[192,3072]{1,0:T(8,128)(2,1)S(1)} %shard_map.51.second, bf16[16,256]{1,0:T(8,128)(2,1)S(1)} %collective-permute-done.5.right, f32[1,1]{1,0:T(1,128)} %get-tuple-element.32.log_in), custom_call_target="tpu_custom_call" | custom-call | flops 100000000 | bytes 1000000 | tf_op jit(solution)/shard_map/pallas_call | solution.py:447
  31.1 1.5 %collective-permute-start.6 = (bf16[288,128]{1,0:T(8,128)(2,1)S(1)}, bf16[288,128]{1,0:T(8,128)(2,1)S(1)}, u32[]{:S(2)}, u32[]{:S(2)}) collective-permute-start(bf16[288,128]{1,0:T(8,128)(2,1)S(1)} %get-tuple-element.33.own), channel_id=1, source_target_pairs={{0,20},{4,16},{8,28},{12,24},{16,4},{20,0},{24,12},{28,8},{1,21},{... | collective-permute-start | bytes 221192 | tf_op jit(solution)/shard_map/ppermute | solution.py:383
  32.6 1.1 %shard_map.53 = (bf16[192,256]{1,0:T(8,128)(2,1)S(1)}, bf16[192,256]{1,0:T(8,128)(2,1)S(1)}) custom-call(s32[1]{0:T(128)} %bitcast.1.role, bf16[288,128]{1,0:T(8,128)(2,1)S(1)} %get-tuple-element.33.own), custom_call_target="tpu_custom_call" | custom-call | flops 100000000 | bytes 1000000 | tf_op jit(solution)/shard_map/pallas_call | solution.py:430
  33.7 1.4 %collective-permute-done.6.other = bf16[288,128]{1,0:T(8,128)(2,1)S(1)} collective-permute-done((bf16[288,128]{1,0:T(8,128)(2,1)S(1)}, bf16[288,128]{1,0:T(8,128)(2,1)S(1)}, u32[]{:S(2)}, u32[]{:S(2)}) %collective-permute-start.6) | collective-permute-done | bytes 73760 | tf_op jit(solution)/shard_map/ppermute | solution.py:383
  35.1 1.3 %shard_map.54 = (bf16[192,256]{1,0:T(8,128)(2,1)S(1)}, bf16[192,256]{1,0:T(8,128)(2,1)S(1)}, bf16[288,128]{1,0:T(8,128)(2,1)S(1)}) custom-call(s32[1]{0:T(128)} %bitcast.1.role, bf16[192,256]{1,0:T(8,128)(2,1)S(1)} %get-tuple-element.34.wide, bf16[192,256]{1,0:T(8,128)(2,1)S(1)} %get-tuple-element.35.product, bf16[288,128]{1,0:T(8,128)(2,1)S(1)} %collective-permute-done.6.other), custom_call_target="tpu_custom_call" | custom-call | flops 100000000 | bytes 1000000 | tf_op jit(solution)/shard_map/pallas_call | solution.py:431
  36.4 3.3 %collective-permute-start.7 = (bf16[288,128]{1,0:T(8,128)(2,1)S(1)}, bf16[288,128]{1,0:T(8,128)(2,1)S(1)}, u32[]{:S(2)}, u32[]{:S(2)}) collective-permute-start(bf16[288,128]{1,0:T(8,128)(2,1)S(1)} %get-tuple-element.38.own), channel_id=1, source_target_pairs={{0,7},{1,4},{2,5},{3,6},{4,1},{5,2},{6,3},{7,0},{8,13},{9,14},{10,... | collective-permute-start | bytes 221192 | tf_op jit(solution)/shard_map/ppermute | solution.py:400
  39.6 0.4 shard_map.55.turned
  40.1 2.4 %collective-permute-done.7.other = bf16[288,128]{1,0:T(8,128)(2,1)S(1)} collective-permute-done((bf16[288,128]{1,0:T(8,128)(2,1)S(1)}, bf16[288,128]{1,0:T(8,128)(2,1)S(1)}, u32[]{:S(2)}, u32[]{:S(2)}) %collective-permute-start.7) | collective-permute-done | bytes 73760 | tf_op jit(solution)/shard_map/ppermute | solution.py:400
  42.5 0.9 %shard_map.56.left = bf16[16,256]{1,0:T(8,128)(2,1)S(1)} custom-call(bf16[288,128]{1,0:T(8,128)(2,1)S(1)} %get-tuple-element.38.own, bf16[288,128]{1,0:T(8,128)(2,1)S(1)} %collective-permute-done.7.other, f32[32,256]{1,0:T(8,128)S(1)} %get-tuple-element.42.starts), custom_call_target="tpu_custom_call" | custom-call | flops 100000000 | bytes 1000000 | tf_op jit(solution)/shard_map/pallas_call | solution.py:439
  43.4 0.1 collective-permute-start.8
  43.5 1.1 %shard_map.57.second = bf16[192,3072]{1,0:T(8,128)(2,1)S(1)} custom-call(bf16[192,256]{1,0:T(8,128)(2,1)S(1)} %shard_map.55.turned, bf16[192,256]{1,0:T(8,128)(2,1)S(1)} %get-tuple-element.37.lower, bf16[16,256]{1,0:T(8,128)(2,1)S(1)} %shard_map.56.left), custom_call_target="tpu_custom_call" | custom-call | flops 100000000 | bytes 1000000 | tf_op jit(solution)/shard_map/pallas_call | solution.py:443
  44.5 0.1 collective-permute-done.8.right
  44.6 2.5 %shard_map.58 = (f32[144,144]{1,0:T(8,128)}, f32[1,1]{1,0:T(1,128)}) custom-call(s32[1]{0:T(128)} %bitcast.role, bf16[192,3072]{1,0:T(8,128)(2,1)S(1)} %shard_map.57.second, bf16[16,256]{1,0:T(8,128)(2,1)S(1)} %collective-permute-done.8.right, f32[1,1]{1,0:T(1,128)} %get-tuple-element.39.log_in), custom_call_target="tpu_custom_call" | custom-call | flops 100000000 | bytes 1000000 | tf_op jit(solution)/shard_map/pallas_call | solution.py:452
  (2 shorter events, 0.0 us)
Async XLA Ops:
  0.6 1.8 %collective-permute-start = (f32[144,144]{1,0:T(8,128)}, f32[144,144]{1,0:T(8,128)S(1)}, u32[]{:S(2)}, u32[]{:S(2)}) collective-permute-start(f32[144,144]{1,0:T(8,128)} %bitcast.12), channel_id=1, source_target_pairs={{0,4},{4,0},{8,12},{12,8},{16,20},{20,16},{24,28},{28,24},{1,5},{5... | collective-permute-start | bytes 248840 | tf_op jit(solution)/shard_map/ppermute | solution.py:383
  1.2 0.9 %copy-start = (f32[1,1,144,144]{3,2,1,0:T(8,128)S(1)}, f32[1,1,144,144]{3,2,1,0:T(8,128)}, u32[]{:S(2)}) copy-start(f32[1,1,144,144]{3,2,1,0:T(8,128)} %param.2) | copy-start | bytes 248836
  5.0 7.0 %collective-permute-start.1 = (bf16[288,128]{1,0:T(8,128)(2,1)S(1)}, bf16[288,128]{1,0:T(8,128)(2,1)S(1)}, u32[]{:S(2)}, u32[]{:S(2)}) collective-permute-start(bf16[288,128]{1,0:T(8,128)(2,1)S(1)} %get-tuple-element.24.own), channel_id=1, source_target_pairs={{0,7},{1,4},{2,5},{3,6},{4,1},{5,2},{6,3},{7,0},{8,13},{9,14},{10,... | collective-permute-start | bytes 221192 | tf_op jit(solution)/shard_map/ppermute | solution.py:400
  9.8 0.8 %copy-start.1 = (f32[3,12,144]{2,1,0:T(8,128)S(1)}, f32[3,12,144]{2,1,0:T(8,128)}, u32[]{:S(2)}) copy-start(f32[3,12,144]{2,1,0:T(8,128)} %start.1) | copy-start | bytes 62212
  13.0 1.2 %collective-permute-start.2 = (bf16[16,256]{1,0:T(8,128)(2,1)S(1)}, bf16[16,256]{1,0:T(8,128)(2,1)S(1)}, u32[]{:S(2)}, u32[]{:S(2)}) collective-permute-start(bf16[16,256]{1,0:T(8,128)(2,1)S(1)} %shard_map.44.left), channel_id=1, source_target_pairs={{0,4},{4,0},{8,12},{12,8},{16,20},{20,16},{24,28},{28,24},{1,5},{5... | collective-permute-start | bytes 24584 | tf_op jit(solution)/shard_map/ppermute | solution.py:383
  15.5 4.3 %collective-permute-start.3 = (bf16[288,128]{1,0:T(8,128)(2,1)S(1)}, bf16[288,128]{1,0:T(8,128)(2,1)S(1)}, u32[]{:S(2)}, u32[]{:S(2)}) collective-permute-start(bf16[288,128]{1,0:T(8,128)(2,1)S(1)} %get-tuple-element.26.own), channel_id=1, source_target_pairs={{0,12},{4,8},{8,4},{12,0},{16,28},{20,24},{24,20},{28,16},{1,13},{... | collective-permute-start | bytes 221192 | tf_op jit(solution)/shard_map/ppermute | solution.py:383
  21.0 6.0 %collective-permute-start.4 = (bf16[288,128]{1,0:T(8,128)(2,1)S(1)}, bf16[288,128]{1,0:T(8,128)(2,1)S(1)}, u32[]{:S(2)}, u32[]{:S(2)}) collective-permute-start(bf16[288,128]{1,0:T(8,128)(2,1)S(1)} %get-tuple-element.31.own), channel_id=1, source_target_pairs={{0,7},{1,4},{2,5},{3,6},{4,1},{5,2},{6,3},{7,0},{8,13},{9,14},{10,... | collective-permute-start | bytes 221192 | tf_op jit(solution)/shard_map/ppermute | solution.py:400
  27.9 1.2 %collective-permute-start.5 = (bf16[16,256]{1,0:T(8,128)(2,1)S(1)}, bf16[16,256]{1,0:T(8,128)(2,1)S(1)}, u32[]{:S(2)}, u32[]{:S(2)}) collective-permute-start(bf16[16,256]{1,0:T(8,128)(2,1)S(1)} %shard_map.50.left), channel_id=1, source_target_pairs={{0,4},{4,0},{8,12},{12,8},{16,20},{20,16},{24,28},{28,24},{1,5},{5... | collective-permute-start | bytes 24584 | tf_op jit(solution)/shard_map/ppermute | solution.py:383
  31.1 4.0 %collective-permute-start.6 = (bf16[288,128]{1,0:T(8,128)(2,1)S(1)}, bf16[288,128]{1,0:T(8,128)(2,1)S(1)}, u32[]{:S(2)}, u32[]{:S(2)}) collective-permute-start(bf16[288,128]{1,0:T(8,128)(2,1)S(1)} %get-tuple-element.33.own), channel_id=1, source_target_pairs={{0,20},{4,16},{8,28},{12,24},{16,4},{20,0},{24,12},{28,8},{1,21},{... | collective-permute-start | bytes 221192 | tf_op jit(solution)/shard_map/ppermute | solution.py:383
  36.4 6.1 %collective-permute-start.7 = (bf16[288,128]{1,0:T(8,128)(2,1)S(1)}, bf16[288,128]{1,0:T(8,128)(2,1)S(1)}, u32[]{:S(2)}, u32[]{:S(2)}) collective-permute-start(bf16[288,128]{1,0:T(8,128)(2,1)S(1)} %get-tuple-element.38.own), channel_id=1, source_target_pairs={{0,7},{1,4},{2,5},{3,6},{4,1},{5,2},{6,3},{7,0},{8,13},{9,14},{10,... | collective-permute-start | bytes 221192 | tf_op jit(solution)/shard_map/ppermute | solution.py:400
  43.4 1.2 %collective-permute-start.8 = (bf16[16,256]{1,0:T(8,128)(2,1)S(1)}, bf16[16,256]{1,0:T(8,128)(2,1)S(1)}, u32[]{:S(2)}, u32[]{:S(2)}) collective-permute-start(bf16[16,256]{1,0:T(8,128)(2,1)S(1)} %shard_map.56.left), channel_id=1, source_target_pairs={{0,4},{4,0},{8,12},{12,8},{16,20},{20,16},{24,28},{28,24},{1,5},{5... | collective-permute-start | bytes 24584 | tf_op jit(solution)/shard_map/ppermute | solution.py:383

commit v4 on v3

--- a/solution.py
+++ b/solution.py
@@ -1,3 +1,5 @@
+import functools
+
 import functools
 
 import jax
@@ -59,7 +61,7 @@
 def row_spread(turn):
     i, j = iota((ROWS, CHI * CHI), 0), iota((ROWS, CHI * CHI), 1)
     s, t = group(i), minor(i)
-    source = t * CHI + s if turn else s * CHI + t
+    source = jnp.where(turn, t * CHI + s, s * CHI + t)
     return one_hot((j == source) & (t < CHI))
 
 
@@ -145,32 +147,25 @@
     return jnp.concatenate([x[:ROWS], jnp.concatenate([first, last], axis=0)], axis=1)
 
 
-def turn(upper, swap):
-    return block_swap(mm(upper, swap).astype(BF16))
-
-
-def upper_product(crossed, crossed_m):
-    product = mm(crossed_m, crossed, NT).astype(BF16)
+def row_swap(x):
+    legs = x.astype(F32).reshape(CHI, PAD, x.shape[1])[:, :CHI]
+    turned = jnp.transpose(legs, (1, 0, 2))
+    rest = jnp.zeros((CHI, PAD - CHI, x.shape[1]), F32)
+    return jnp.concatenate([turned, rest], axis=1).reshape(x.shape).astype(BF16)
+
+
+def product_part(x):
+    product = mm(row_swap(x), x, NT).astype(BF16)
     return block_swap(widen(product))
 
 
-def upper_part(upper, swap):
-    row_swap = swap[:ROWS, :ROWS]
-    crossed_m = block_swap(mm(row_swap, upper).astype(BF16))
-    return upper_product(mm(row_swap, crossed_m).astype(BF16), crossed_m)
-
-
-def lower_part(lower, swap):
-    row_swap = swap[:ROWS, :ROWS]
-    lower_m = mm(row_swap, lower).astype(BF16)
-    product = mm(lower_m, lower, NT).astype(BF16)
-    product = block_swap(widen(product))
-    return mm(row_swap, product).astype(BF16)
-
-
-def outer_part(high, low):
-    outer = mm(high, low, NT).astype(BF16)
+def outer_part(first, second):
+    outer = mm(first, row_swap(second), NT).astype(BF16)
     return block_swap(widen(outer))
+
+
+def turn(first):
+    return widen(row_swap(first.T[:ROWS]))
 
 
 def start_body(start, swap):
@@ -272,73 +267,48 @@
     return mm(second_ref[...], kron_ref[...])
 
 
-def placed(site, mirror, turned):
-    spaced = mm(row_spread(turned), site).astype(BF16)
+def placed(site, mirror, lower):
+    spaced = mm(row_spread(lower), site).astype(BF16)
     return block_swap(mm(spaced, spread_matrix(mirror)).astype(BF16))
 
 
-def pick(is_upper, own, other):
-    return jnp.where(is_upper, own, other), jnp.where(is_upper, other, own)
+def pick(own_first, own, other):
+    return jnp.where(own_first, own, other), jnp.where(own_first, other, own)
 
 
 def cast_kernel(own, cast_o):
     cast_o[...] = own[...].astype(BF16)
 
 
-def first_gram_kernel(role, own, other, lower_o, gram_o):
-    swap = swap_matrix()
-    mirror = role[0] != 0
-    upper, lower = pick(role[1] != 0, own[...], other[...].astype(BF16))
-    crossed = placed(upper, mirror, False)
-    crossed_m = mm(swap[:ROWS, :ROWS], crossed).astype(BF16)
-    lower = placed(lower, mirror, True)
-    lower_o[...] = lower
-    high = upper_product(crossed, crossed_m)
-    gram_o[...] = pack(outer_part(high, lower_part(lower, swap)))
-
-
-def first_turn_kernel(role, own, other, start, turned_o, starts_o):
-    swap = swap_matrix()
-    upper, _ = pick(role[1] != 0, own[...], other[...].astype(BF16))
-    turned_o[...] = turn(placed(upper, role[0] != 0, True), swap)
-    for level in range(LEVELS):
-        plain, turned = start_body(start[level], swap)
-        starts_o[level, :PAD], starts_o[level, PAD:] = plain, turned
-
-
-def own_kernel(role, own, wide_o, product_o):
-    swap = swap_matrix()
+def first_gram_kernel(role, own, other, first_o, second_o, gram_o):
+    own_first, own_lower, mirror = role[0] != 0, role[2] != 0, role[3] != 0
+    mine = placed(own[...], mirror, own_lower)
+    theirs = placed(other[...].astype(BF16), mirror, jnp.logical_not(own_lower))
+    first_o[...], second_o[...] = pick(own_first, mine, theirs)
+    products = pick(own_first, product_part(mine), product_part(theirs))
+    gram_o[...] = pack(outer_part(*products))
+
+
+def own_kernel(own, wide_o, product_o):
     wide = unpack(own[...])
     wide_o[...] = wide
-
-    @pl.when(role[0] != 0)
-    def _():
-        product_o[...] = upper_part(wide, swap)
-
-    @pl.when(role[0] == 0)
-    def _():
-        product_o[...] = lower_part(wide, swap)
-
-
-def gram_kernel(role, wide, product, other, upper_o, lower_o, gram_o, high, low):
-    swap = swap_matrix()
+    product_o[...] = product_part(wide)
+
+
+def gram_kernel(role, wide, product, other, first_o, second_o, gram_o):
+    own_first = role[0] != 0
     theirs = unpack(other[...])
-
-    @pl.when(role[0] != 0)
-    def _():
-        upper_o[...], lower_o[...] = wide[...], theirs
-        high[...], low[...] = product[...], lower_part(theirs, swap)
-
-    @pl.when(role[0] == 0)
-    def _():
-        upper_o[...], lower_o[...] = theirs, wide[...]
-        high[...], low[...] = upper_part(theirs, swap), product[...]
-
-    gram_o[...] = pack(outer_part(high[...], low[...]))
-
-
-def turn_kernel(upper, turned_o):
-    turned_o[...] = turn(upper[...], swap_matrix())
+    products = pick(own_first, product[...], product_part(theirs))
+    gram_o[...] = pack(outer_part(*products))
+    first_o[...], second_o[...] = pick(own_first, wide[...], theirs)
+
+
+def turn_kernel(level, role, first, start, turned_o, starts_o):
+    turned_o[...] = turn(first[...])
+    plain, turned = start_body(start[level], swap_matrix())
+    first_upper = role[1] != 0
+    starts_o[:PAD] = jnp.where(first_upper, plain, turned)
+    starts_o[PAD:] = jnp.where(first_upper, turned, plain)
 
 
 def second_kernel(turned, lower, left, second_o):
@@ -360,9 +330,9 @@
 def last_kernel(role, second, right, log_in, coarse_o, log_o, kron):
     merged = third(second, right[...], kron)
     mean = mean_square(merged)
-    log_o[...] = log_in[...] + 0.5 * jnp.log(mean)
+    log_o[...] = (log_in[...] + 0.5 * jnp.log(mean))[:1, :1]
     wide = block_swap(merged.astype(BF16))
-    narrow = mm(wide, spread_matrix(role[0] != 0), NT).astype(BF16)
+    narrow = mm(wide, spread_matrix(role[3] != 0), NT).astype(BF16)
     coarse_o[...] = mm(row_spread(True), narrow, TN) * lax.rsqrt(mean)
 
 
@@ -405,50 +375,42 @@
     row = lax.axis_index("row")
     mirror = mirrored(row)
     vmem, smem = pltpu.VMEM, pltpu.SMEM
-    mat, packed = ((ROWS, LANES), BF16), ((ROWS * 3 // 2, 128), BF16)
+    mat, packed, logs = ((ROWS, LANES), BF16), ((ROWS * 3 // 2, 128), BF16), ((8, 128), F32)
     kron = [vmem((CHI * LANES, LANES), BF16)]
-    log_total = jnp.zeros((1, 1), F32)
+    log_total = jnp.zeros(*logs)
     own = site_tensors[0, 0]
     for level in range(LEVELS):
-        is_upper = 1 - (row >> level & 1)
+        own_lower = row >> level & 1
+        first_upper = row >> level + 1 & 1 if level < LEVELS - 1 else row * 0 + 1
+        role = jnp.stack([own_lower ^ first_upper, first_upper, own_lower, mirror]).astype(jnp.int32)
         if level == 0:
             other = from_partner(own, 1)
-            role = jnp.stack([mirror, is_upper]).astype(jnp.int32)
             (own,) = call(cast_kernel, [((square, square), BF16)], [vmem])(own)
-            lower, gram = call(first_gram_kernel, [mat, packed], [smem, vmem, vmem])(
+            first, lower, gram = call(first_gram_kernel, [mat, mat, packed], [smem, vmem, vmem])(
                 role, own, other
             )
-            gram_other = from_bond(gram)
-            turned, starts = call(
-                first_turn_kernel,
-                [mat, ((LEVELS, 2 * PAD, LANES), F32)],
-                [smem, vmem, vmem, vmem],
-            )(role, own, other, start_basis)
         else:
             other = from_partner(own, 1 << level | 1)
-            role = is_upper.reshape(1).astype(jnp.int32)
-            wide, product = call(own_kernel, [mat, mat], [smem, vmem])(role, own)
-            upper, lower, gram = call(
-                gram_kernel,
-                [mat, mat, packed],
-                [smem, vmem, vmem, vmem],
-                [vmem(*mat), vmem(*mat)],
-            )(role, wide, product, other)
-            gram_other = from_bond(gram)
-            (turned,) = call(turn_kernel, [mat], [vmem])(upper)
-        (left,) = call(iso_kernel, [((PAD, LANES), BF16)], [vmem] * 3)(
-            gram, gram_other, starts[level]
-        )
+            wide, product = call(own_kernel, [mat, mat], [vmem])(own)
+            first, lower, gram = call(gram_kernel, [mat, mat, packed], [smem, vmem, vmem, vmem])(
+                role, wide, product, other
+            )
+        gram_other = from_bond(gram)
+        turned, starts = call(
+            functools.partial(turn_kernel, level),
+            [mat, ((2 * PAD, LANES), F32)],
+            [smem, vmem, vmem],
+        )(role, first, start_basis)
+        (left,) = call(iso_kernel, [((PAD, LANES), BF16)], [vmem] * 3)(gram, gram_other, starts)
         right = from_partner(left, 1)
         (second,) = call(second_kernel, [((ROWS, CHI * LANES), BF16)], [vmem] * 3)(
             turned, lower, left
         )
         if level < LEVELS - 1:
-            own, log_total = call(third_kernel, [packed, ((1, 1), F32)], [vmem] * 3, kron)(
+            own, log_total = call(third_kernel, [packed, logs], [vmem] * 3, kron)(
                 second, right, log_total
             )
         else:
-            role = mirror.reshape(1).astype(jnp.int32)
             coarse, log_total = call(
                 last_kernel, [((square, square), F32), ((1, 1), F32)], [smem] + [vmem] * 3, kron
             )(role, second, right, log_total)

time: 47.4 us -> 45.8 us (0.966)
  Pallas kernels: 21.2 us -> 18.5 us
  waiting for transfers between devices: 7.85 us -> 8.62 us
    pallas_call x10, Pallas kernels: 12.8 us -> 10.2 us  [the longest x2 3.02 us: per_device(): call(gram_kernel, [mat, mat, packed], [smem, vmem, vmem, vmem])]
    ppermute x6, waiting for transfers between devices: 3.18 us -> 4.21 us  [from_partner(): return lax.ppermute(array, 'row', [(i, i ^ flip) for i in range(count)])]
    unnamed x4 -> x6, local copies, waits for them, and re-layouts: 1.71 us -> 1.71 us
  transfers between devices with their start and end apart: 9 -> 9, of which waited for: 8 -> 9; matrix products, arithmetic and copies ran while one was open for 0% -> 1% of each run, Pallas kernels for 16% -> 14%
where the time goes in v4:
time: 45.8 us; the launch traced here: 45.6 us
  Pallas kernels  18.5 us (40%)
  starting transfers between devices  15.8 us (34%)
  waiting for transfers between devices  8.62 us (19%)
  local copies, waits for them, and re-layouts  1.72 us (4%)
  between operations  0.76 us (2%)
    ppermute x3, starting transfers between devices, from_bond(): return lax.ppermute(array, ('row', 'col'), pairs)  11.4 us
    ppermute x6, starting transfers between devices, from_partner(): return lax.ppermute(array, 'row', [(i, i ^ flip) for i in range(count)])  4.42 us
    ppermute x3, waiting for transfers between devices, from_bond(): return lax.ppermute(array, ('row', 'col'), pairs)  4.41 us
    ppermute x6, waiting for transfers between devices, from_partner(): return lax.ppermute(array, 'row', [(i, i ^ flip) for i in range(count)])  4.21 us
    pallas_call x3, Pallas kernels, per_device(): call(second_kernel, [((ROWS, CHI * LANES), BF16)], [vmem] * 3)  3.15 us
    pallas_call x2, Pallas kernels, per_device(): call(gram_kernel, [mat, mat, packed], [smem, vmem, vmem, vmem])  3.02 us
    pallas_call x3, Pallas kernels, per_device(): call(iso_kernel, [((PAD, LANES), BF16)], [vmem] * 3)  2.65 us
    pallas_call x1, Pallas kernels, per_device(): call(last_kernel, [((square, square), F32), ((1, 1), F32)], [smem] + [vme...  2.45 us
  transfers between devices with their start and end apart: 9, of which 9 were waited for; matrix products, arithmetic and copies ran while one was open for 1% of the time, Pallas kernels for 14%

profile of v4, /device:TPU:0, one launch (start us, length us, event | category | flops | bytes accessed | tf_op | source)
XLA Modules:
  0.0 45.6 jit_solution(9496619766763932794)
XLA Ops:
  0.6 0.6 %collective-permute-start = (f32[144,144]{1,0:T(8,128)}, f32[144,144]{1,0:T(8,128)S(1)}, u32[]{:S(2)}, u32[]{:S(2)}) collective-permute-start(f32[144,144]{1,0:T(8,128)} %bitcast.9), channel_id=1, source_target_pairs={{0,4},{4,0},{8,12},{12,8},{16,20},{20,16},{24,28},{28,24},{1,5},{5... | collective-permute-start | bytes 248840 | tf_op jit(solution)/shard_map/ppermute | solution.py:353
  1.2 0.0 copy-start
  1.2 0.9 %copy-done = f32[1,1,144,144]{3,2,1,0:T(8,128)S(1)} copy-done((f32[1,1,144,144]{3,2,1,0:T(8,128)S(1)}, f32[1,1,144,144]{3,2,1,0:T(8,128)}, u32[]{:S(2)}) %copy-start) | copy-done | bytes 82968
  2.1 0.1 add_add_fusion.2.role
  2.2 0.2 collective-permute-done.other
  2.4 2.1 %shard_map.42 = (bf16[192,256]{1,0:T(8,128)(2,1)S(1)}, bf16[192,256]{1,0:T(8,128)(2,1)S(1)}, bf16[288,128]{1,0:T(8,128)(2,1)S(1)}) custom-call(s32[4]{0:T(128)S(1)} %add_add_fusion.2.role, bf16[144,144]{1,0:T(8,128)(2,1)S(1)} %shard_map.41.own, f32[144,144]{1,0:T(8,128)S(1)} %collective-permute-done.other), custom_call_target="tpu_custom_call" | custom-call | flops 100000000 | bytes 1000000 | tf_op jit(solution)/shard_map/pallas_call | solution.py:389
  4.5 4.7 %collective-permute-start.1 = (bf16[288,128]{1,0:T(8,128)(2,1)S(1)}, bf16[288,128]{1,0:T(8,128)(2,1)S(1)}, u32[]{:S(2)}, u32[]{:S(2)}) collective-permute-start(bf16[288,128]{1,0:T(8,128)(2,1)S(1)} %get-tuple-element.30.own), channel_id=1, source_target_pairs={{0,7},{1,4},{2,5},{3,6},{4,1},{5,2},{6,3},{7,0},{8,13},{9,14},{10,... | collective-permute-start | bytes 221192 | tf_op jit(solution)/shard_map/ppermute | solution.py:370
  9.2 0.0 copy-start.1
  9.2 0.8 %copy-done.1 = f32[3,12,144]{2,1,0:T(8,128)S(1)} copy-done((f32[3,12,144]{2,1,0:T(8,128)S(1)}, f32[3,12,144]{2,1,0:T(8,128)}, u32[]{:S(2)}) %copy-start.1) | copy-done | bytes 20760
  10.0 0.8 %shard_map.43 = (bf16[192,256]{1,0:T(8,128)(2,1)S(1)}, f32[32,256]{1,0:T(8,128)S(1)}) custom-call(s32[4]{0:T(128)S(1)} %add_add_fusion.2.role, bf16[192,256]{1,0:T(8,128)(2,1)S(1)} %get-tuple-element.27.first, f32[3,12,144]{2,1,0:T(8,128)S(1)} %copy-done.1), custom_call_target="tpu_custom_call" | custom-call | flops 100000000 | bytes 1000000 | tf_op jit(solution)/shard_map/pallas_call | solution.py:399
  10.9 0.5 %collective-permute-done.1.other = bf16[288,128]{1,0:T(8,128)(2,1)S(1)} collective-permute-done((bf16[288,128]{1,0:T(8,128)(2,1)S(1)}, bf16[288,128]{1,0:T(8,128)(2,1)S(1)}, u32[]{:S(2)}, u32[]{:S(2)}) %collective-permute-start.1) | collective-permute-done | bytes 73760 | tf_op jit(solution)/shard_map/ppermute | solution.py:370
  11.4 0.9 %shard_map.44.left = bf16[16,256]{1,0:T(8,128)(2,1)S(1)} custom-call(bf16[288,128]{1,0:T(8,128)(2,1)S(1)} %get-tuple-element.30.own, bf16[288,128]{1,0:T(8,128)(2,1)S(1)} %collective-permute-done.1.other, f32[32,256]{1,0:T(8,128)S(1)} %get-tuple-element.31.starts), custom_call_target="tpu_custom_call" | custom-call | flops 100000000 | bytes 1000000 | tf_op jit(solution)/shard_map/pallas_call | solution.py:404
  12.3 0.1 collective-permute-start.2
  12.4 1.1 %shard_map.45.second = bf16[192,3072]{1,0:T(8,128)(2,1)S(1)} custom-call(bf16[192,256]{1,0:T(8,128)(2,1)S(1)} %get-tuple-element.28.turned, bf16[192,256]{1,0:T(8,128)(2,1)S(1)} %get-tuple-element.29.lower, bf16[16,256]{1,0:T(8,128)(2,1)S(1)} %shard_map.44.left), custom_call_target="tpu_custom_call" | custom-call | flops 100000000 | bytes 1000000 | tf_op jit(solution)/shard_map/pallas_call | solution.py:406
  13.4 0.0 copy-start.2
  13.4 0.1 collective-permute-done.2.right
  13.5 0.9 %shard_map.46 = (bf16[288,128]{1,0:T(8,128)(2,1)S(1)}, f32[8,128]{1,0:T(8,128)S(1)}) custom-call(bf16[192,3072]{1,0:T(8,128)(2,1)S(1)} %shard_map.45.second, bf16[16,256]{1,0:T(8,128)(2,1)S(1)} %collective-permute-done.2.right, f32[8,128]{1,0:T(8,128)S(1)} %broadcast_in_dim.6.log_in), custom_call_target="tpu_custom_call" | custom-call | flops 100000000 | bytes 1000000 | tf_op jit(solution)/shard_map/pallas_call | solution.py:410
  14.4 2.0 %collective-permute-start.3 = (bf16[288,128]{1,0:T(8,128)(2,1)S(1)}, bf16[288,128]{1,0:T(8,128)(2,1)S(1)}, u32[]{:S(2)}, u32[]{:S(2)}) collective-permute-start(bf16[288,128]{1,0:T(8,128)(2,1)S(1)} %get-tuple-element.32.own), channel_id=1, source_target_pairs={{0,12},{4,8},{8,4},{12,0},{16,28},{20,24},{24,20},{28,16},{1,13},{... | collective-permute-start | bytes 221192 | tf_op jit(solution)/shard_map/ppermute | solution.py:353
  16.4 0.1 add_add_fusion.1.role
  16.5 0.5 %shard_map.47 = (bf16[192,256]{1,0:T(8,128)(2,1)S(1)}, bf16[192,256]{1,0:T(8,128)(2,1)S(1)}) custom-call(bf16[288,128]{1,0:T(8,128)(2,1)S(1)} %get-tuple-element.32.own), custom_call_target="tpu_custom_call" | custom-call | flops 100000000 | bytes 1000000 | tf_op jit(solution)/shard_map/pallas_call | solution.py:394
  17.0 1.8 %collective-permute-done.3.other = bf16[288,128]{1,0:T(8,128)(2,1)S(1)} collective-permute-done((bf16[288,128]{1,0:T(8,128)(2,1)S(1)}, bf16[288,128]{1,0:T(8,128)(2,1)S(1)}, u32[]{:S(2)}, u32[]{:S(2)}) %collective-permute-start.3) | collective-permute-done | bytes 73760 | tf_op jit(solution)/shard_map/ppermute | solution.py:353
  18.8 1.5 %shard_map.48 = (bf16[192,256]{1,0:T(8,128)(2,1)S(1)}, bf16[192,256]{1,0:T(8,128)(2,1)S(1)}, bf16[288,128]{1,0:T(8,128)(2,1)S(1)}) custom-call(s32[4]{0:T(128)S(1)} %add_add_fusion.1.role, bf16[192,256]{1,0:T(8,128)(2,1)S(1)} %get-tuple-element.33.wide, bf16[192,256]{1,0:T(8,128)(2,1)S(1)} %get-tuple-element.34.product, ...), custom_call_target="tpu_custom_call" | custom-call | flops 100000000 | bytes 1000000 | tf_op jit(solution)/shard_map/pallas_call | solution.py:395
  20.3 3.4 %collective-permute-start.4 = (bf16[288,128]{1,0:T(8,128)(2,1)S(1)}, bf16[288,128]{1,0:T(8,128)(2,1)S(1)}, u32[]{:S(2)}, u32[]{:S(2)}) collective-permute-start(bf16[288,128]{1,0:T(8,128)(2,1)S(1)} %get-tuple-element.38.own), channel_id=1, source_target_pairs={{0,7},{1,4},{2,5},{3,6},{4,1},{5,2},{6,3},{7,0},{8,13},{9,14},{10,... | collective-permute-start | bytes 221192 | tf_op jit(solution)/shard_map/ppermute | solution.py:370
  23.7 0.0 copy-done.2
  23.7 0.8 %shard_map.49 = (bf16[192,256]{1,0:T(8,128)(2,1)S(1)}, f32[32,256]{1,0:T(8,128)S(1)}) custom-call(s32[4]{0:T(128)S(1)} %add_add_fusion.1.role, bf16[192,256]{1,0:T(8,128)(2,1)S(1)} %get-tuple-element.35.first, f32[3,12,144]{2,1,0:T(8,128)S(1)} %copy-done.2), custom_call_target="tpu_custom_call" | custom-call | flops 100000000 | bytes 1000000 | tf_op jit(solution)/shard_map/pallas_call | solution.py:399
  24.5 1.8 %collective-permute-done.4.other = bf16[288,128]{1,0:T(8,128)(2,1)S(1)} collective-permute-done((bf16[288,128]{1,0:T(8,128)(2,1)S(1)}, bf16[288,128]{1,0:T(8,128)(2,1)S(1)}, u32[]{:S(2)}, u32[]{:S(2)}) %collective-permute-start.4) | collective-permute-done | bytes 73760 | tf_op jit(solution)/shard_map/ppermute | solution.py:370
  26.4 0.9 %shard_map.50.left = bf16[16,256]{1,0:T(8,128)(2,1)S(1)} custom-call(bf16[288,128]{1,0:T(8,128)(2,1)S(1)} %get-tuple-element.38.own, bf16[288,128]{1,0:T(8,128)(2,1)S(1)} %collective-permute-done.4.other, f32[32,256]{1,0:T(8,128)S(1)} %get-tuple-element.39.starts), custom_call_target="tpu_custom_call" | custom-call | flops 100000000 | bytes 1000000 | tf_op jit(solution)/shard_map/pallas_call | solution.py:404
  27.3 0.1 collective-permute-start.5
  27.3 1.1 %shard_map.51.second = bf16[192,3072]{1,0:T(8,128)(2,1)S(1)} custom-call(bf16[192,256]{1,0:T(8,128)(2,1)S(1)} %get-tuple-element.36.turned, bf16[192,256]{1,0:T(8,128)(2,1)S(1)} %get-tuple-element.37.lower, bf16[16,256]{1,0:T(8,128)(2,1)S(1)} %shard_map.50.left), custom_call_target="tpu_custom_call" | custom-call | flops 100000000 | bytes 1000000 | tf_op jit(solution)/shard_map/pallas_call | solution.py:406
  28.4 0.1 collective-permute-done.5.right
  28.5 0.9 %shard_map.52 = (bf16[288,128]{1,0:T(8,128)(2,1)S(1)}, f32[8,128]{1,0:T(8,128)S(1)}) custom-call(bf16[192,3072]{1,0:T(8,128)(2,1)S(1)} %shard_map.51.second, bf16[16,256]{1,0:T(8,128)(2,1)S(1)} %collective-permute-done.5.right, f32[8,128]{1,0:T(8,128)S(1)} %get-tuple-element.40.log_in), custom_call_target="tpu_custom_call" | custom-call | flops 100000000 | bytes 1000000 | tf_op jit(solution)/shard_map/pallas_call | solution.py:410
  29.3 1.6 %collective-permute-start.6 = (bf16[288,128]{1,0:T(8,128)(2,1)S(1)}, bf16[288,128]{1,0:T(8,128)(2,1)S(1)}, u32[]{:S(2)}, u32[]{:S(2)}) collective-permute-start(bf16[288,128]{1,0:T(8,128)(2,1)S(1)} %get-tuple-element.41.own), channel_id=1, source_target_pairs={{0,20},{4,16},{8,28},{12,24},{16,4},{20,0},{24,12},{28,8},{1,21},{... | collective-permute-start | bytes 221192 | tf_op jit(solution)/shard_map/ppermute | solution.py:353
  30.9 0.1 add_add_fusion.role
  31.0 0.5 %shard_map.53 = (bf16[192,256]{1,0:T(8,128)(2,1)S(1)}, bf16[192,256]{1,0:T(8,128)(2,1)S(1)}) custom-call(bf16[288,128]{1,0:T(8,128)(2,1)S(1)} %get-tuple-element.41.own), custom_call_target="tpu_custom_call" | custom-call | flops 100000000 | bytes 1000000 | tf_op jit(solution)/shard_map/pallas_call | solution.py:394
  31.5 1.9 %collective-permute-done.6.other = bf16[288,128]{1,0:T(8,128)(2,1)S(1)} collective-permute-done((bf16[288,128]{1,0:T(8,128)(2,1)S(1)}, bf16[288,128]{1,0:T(8,128)(2,1)S(1)}, u32[]{:S(2)}, u32[]{:S(2)}) %collective-permute-start.6) | collective-permute-done | bytes 73760 | tf_op jit(solution)/shard_map/ppermute | solution.py:353
  33.4 1.5 %shard_map.54 = (bf16[192,256]{1,0:T(8,128)(2,1)S(1)}, bf16[192,256]{1,0:T(8,128)(2,1)S(1)}, bf16[288,128]{1,0:T(8,128)(2,1)S(1)}) custom-call(s32[4]{0:T(128)S(1)} %add_add_fusion.role, bf16[192,256]{1,0:T(8,128)(2,1)S(1)} %get-tuple-element.42.wide, bf16[192,256]{1,0:T(8,128)(2,1)S(1)} %get-tuple-element.43.product, ...), custom_call_target="tpu_custom_call" | custom-call | flops 100000000 | bytes 1000000 | tf_op jit(solution)/shard_map/pallas_call | solution.py:395
  34.9 3.3 %collective-permute-start.7 = (bf16[288,128]{1,0:T(8,128)(2,1)S(1)}, bf16[288,128]{1,0:T(8,128)(2,1)S(1)}, u32[]{:S(2)}, u32[]{:S(2)}) collective-permute-start(bf16[288,128]{1,0:T(8,128)(2,1)S(1)} %get-tuple-element.47.own), channel_id=1, source_target_pairs={{0,7},{1,4},{2,5},{3,6},{4,1},{5,2},{6,3},{7,0},{8,13},{9,14},{10,... | collective-permute-start | bytes 221192 | tf_op jit(solution)/shard_map/ppermute | solution.py:370
  38.1 0.8 %shard_map.55 = (bf16[192,256]{1,0:T(8,128)(2,1)S(1)}, f32[32,256]{1,0:T(8,128)S(1)}) custom-call(s32[4]{0:T(128)S(1)} %add_add_fusion.role, bf16[192,256]{1,0:T(8,128)(2,1)S(1)} %get-tuple-element.44.first, f32[3,12,144]{2,1,0:T(8,128)S(1)} %copy-done.2), custom_call_target="tpu_custom_call" | custom-call | flops 100000000 | bytes 1000000 | tf_op jit(solution)/shard_map/pallas_call | solution.py:399
  39.0 2.1 %collective-permute-done.7.other = bf16[288,128]{1,0:T(8,128)(2,1)S(1)} collective-permute-done((bf16[288,128]{1,0:T(8,128)(2,1)S(1)}, bf16[288,128]{1,0:T(8,128)(2,1)S(1)}, u32[]{:S(2)}, u32[]{:S(2)}) %collective-permute-start.7) | collective-permute-done | bytes 73760 | tf_op jit(solution)/shard_map/ppermute | solution.py:370
  41.0 0.9 %shard_map.56.left = bf16[16,256]{1,0:T(8,128)(2,1)S(1)} custom-call(bf16[288,128]{1,0:T(8,128)(2,1)S(1)} %get-tuple-element.47.own, bf16[288,128]{1,0:T(8,128)(2,1)S(1)} %collective-permute-done.7.other, f32[32,256]{1,0:T(8,128)S(1)} %get-tuple-element.48.starts), custom_call_target="tpu_custom_call" | custom-call | flops 100000000 | bytes 1000000 | tf_op jit(solution)/shard_map/pallas_call | solution.py:404
  41.9 0.1 collective-permute-start.8
  42.0 1.0 %shard_map.57.second = bf16[192,3072]{1,0:T(8,128)(2,1)S(1)} custom-call(bf16[192,256]{1,0:T(8,128)(2,1)S(1)} %get-tuple-element.45.turned, bf16[192,256]{1,0:T(8,128)(2,1)S(1)} %get-tuple-element.46.lower, bf16[16,256]{1,0:T(8,128)(2,1)S(1)} %shard_map.56.left), custom_call_target="tpu_custom_call" | custom-call | flops 100000000 | bytes 1000000 | tf_op jit(solution)/shard_map/pallas_call | solution.py:406
  43.0 0.1 collective-permute-done.8.right
  43.1 2.4 %shard_map.58 = (f32[144,144]{1,0:T(8,128)}, f32[1,1]{1,0:T(1,128)}) custom-call(s32[4]{0:T(128)S(1)} %add_add_fusion.role, bf16[192,3072]{1,0:T(8,128)(2,1)S(1)} %shard_map.57.second, bf16[16,256]{1,0:T(8,128)(2,1)S(1)} %collective-permute-done.8.right, f32[8,128]{1,0:T(8,128)S(1)} %get-tuple-element.49.log_in), custom_call_target="tpu_custom_call" | custom-call | flops 100000000 | bytes 1000000 | tf_op jit(solution)/shard_map/pallas_call | solution.py:414
  (2 shorter events, 0.0 us)
Async XLA Ops:
  0.6 1.8 %collective-permute-start = (f32[144,144]{1,0:T(8,128)}, f32[144,144]{1,0:T(8,128)S(1)}, u32[]{:S(2)}, u32[]{:S(2)}) collective-permute-start(f32[144,144]{1,0:T(8,128)} %bitcast.9), channel_id=1, source_target_pairs={{0,4},{4,0},{8,12},{12,8},{16,20},{20,16},{24,28},{28,24},{1,5},{5... | collective-permute-start | bytes 248840 | tf_op jit(solution)/shard_map/ppermute | solution.py:353
  1.2 0.9 %copy-start = (f32[1,1,144,144]{3,2,1,0:T(8,128)S(1)}, f32[1,1,144,144]{3,2,1,0:T(8,128)}, u32[]{:S(2)}) copy-start(f32[1,1,144,144]{3,2,1,0:T(8,128)} %param.2) | copy-start | bytes 248836
  4.5 6.9 %collective-permute-start.1 = (bf16[288,128]{1,0:T(8,128)(2,1)S(1)}, bf16[288,128]{1,0:T(8,128)(2,1)S(1)}, u32[]{:S(2)}, u32[]{:S(2)}) collective-permute-start(bf16[288,128]{1,0:T(8,128)(2,1)S(1)} %get-tuple-element.30.own), channel_id=1, source_target_pairs={{0,7},{1,4},{2,5},{3,6},{4,1},{5,2},{6,3},{7,0},{8,13},{9,14},{10,... | collective-permute-start | bytes 221192 | tf_op jit(solution)/shard_map/ppermute | solution.py:370
  9.2 0.8 %copy-start.1 = (f32[3,12,144]{2,1,0:T(8,128)S(1)}, f32[3,12,144]{2,1,0:T(8,128)}, u32[]{:S(2)}) copy-start(f32[3,12,144]{2,1,0:T(8,128)} %start.5) | copy-start | bytes 62212
  12.3 1.2 %collective-permute-start.2 = (bf16[16,256]{1,0:T(8,128)(2,1)S(1)}, bf16[16,256]{1,0:T(8,128)(2,1)S(1)}, u32[]{:S(2)}, u32[]{:S(2)}) collective-permute-start(bf16[16,256]{1,0:T(8,128)(2,1)S(1)} %shard_map.44.left), channel_id=1, source_target_pairs={{0,4},{4,0},{8,12},{12,8},{16,20},{20,16},{24,28},{28,24},{1,5},{5... | collective-permute-start | bytes 24584 | tf_op jit(solution)/shard_map/ppermute | solution.py:353
  13.4 10.3 %copy-start.2 = (f32[3,12,144]{2,1,0:T(8,128)S(1)}, f32[3,12,144]{2,1,0:T(8,128)}, u32[]{:S(2)}) copy-start(f32[3,12,144]{2,1,0:T(8,128)} %start.5) | copy-start | bytes 62212
  14.4 4.5 %collective-permute-start.3 = (bf16[288,128]{1,0:T(8,128)(2,1)S(1)}, bf16[288,128]{1,0:T(8,128)(2,1)S(1)}, u32[]{:S(2)}, u32[]{:S(2)}) collective-permute-start(bf16[288,128]{1,0:T(8,128)(2,1)S(1)} %get-tuple-element.32.own), channel_id=1, source_target_pairs={{0,12},{4,8},{8,4},{12,0},{16,28},{20,24},{24,20},{28,16},{1,13},{... | collective-permute-start | bytes 221192 | tf_op jit(solution)/shard_map/ppermute | solution.py:353
  20.3 6.0 %collective-permute-start.4 = (bf16[288,128]{1,0:T(8,128)(2,1)S(1)}, bf16[288,128]{1,0:T(8,128)(2,1)S(1)}, u32[]{:S(2)}, u32[]{:S(2)}) collective-permute-start(bf16[288,128]{1,0:T(8,128)(2,1)S(1)} %get-tuple-element.38.own), channel_id=1, source_target_pairs={{0,7},{1,4},{2,5},{3,6},{4,1},{5,2},{6,3},{7,0},{8,13},{9,14},{10,... | collective-permute-start | bytes 221192 | tf_op jit(solution)/shard_map/ppermute | solution.py:370
  27.3 1.2 %collective-permute-start.5 = (bf16[16,256]{1,0:T(8,128)(2,1)S(1)}, bf16[16,256]{1,0:T(8,128)(2,1)S(1)}, u32[]{:S(2)}, u32[]{:S(2)}) collective-permute-start(bf16[16,256]{1,0:T(8,128)(2,1)S(1)} %shard_map.50.left), channel_id=1, source_target_pairs={{0,4},{4,0},{8,12},{12,8},{16,20},{20,16},{24,28},{28,24},{1,5},{5... | collective-permute-start | bytes 24584 | tf_op jit(solution)/shard_map/ppermute | solution.py:353
  29.3 4.0 %collective-permute-start.6 = (bf16[288,128]{1,0:T(8,128)(2,1)S(1)}, bf16[288,128]{1,0:T(8,128)(2,1)S(1)}, u32[]{:S(2)}, u32[]{:S(2)}) collective-permute-start(bf16[288,128]{1,0:T(8,128)(2,1)S(1)} %get-tuple-element.41.own), channel_id=1, source_target_pairs={{0,20},{4,16},{8,28},{12,24},{16,4},{20,0},{24,12},{28,8},{1,21},{... | collective-permute-start | bytes 221192 | tf_op jit(solution)/shard_map/ppermute | solution.py:353
  34.9 6.1 %collective-permute-start.7 = (bf16[288,128]{1,0:T(8,128)(2,1)S(1)}, bf16[288,128]{1,0:T(8,128)(2,1)S(1)}, u32[]{:S(2)}, u32[]{:S(2)}) collective-permute-start(bf16[288,128]{1,0:T(8,128)(2,1)S(1)} %get-tuple-element.47.own), channel_id=1, source_target_pairs={{0,7},{1,4},{2,5},{3,6},{4,1},{5,2},{6,3},{7,0},{8,13},{9,14},{10,... | collective-permute-start | bytes 221192 | tf_op jit(solution)/shard_map/ppermute | solution.py:370
  41.9 1.2 %collective-permute-start.8 = (bf16[16,256]{1,0:T(8,128)(2,1)S(1)}, bf16[16,256]{1,0:T(8,128)(2,1)S(1)}, u32[]{:S(2)}, u32[]{:S(2)}) collective-permute-start(bf16[16,256]{1,0:T(8,128)(2,1)S(1)} %shard_map.56.left), channel_id=1, source_target_pairs={{0,4},{4,0},{8,12},{12,8},{16,20},{20,16},{24,28},{28,24},{1,5},{5... | collective-permute-start | bytes 24584 | tf_op jit(solution)/shard_map/ppermute | solution.py:353

commit v5 on v4

--- a/solution.py
+++ b/solution.py
@@ -276,12 +276,20 @@
     return jnp.where(own_first, own, other), jnp.where(own_first, other, own)
 
 
+def roles(level):
+    row = lax.axis_index("row")
+    own_lower = row >> level & 1
+    first_upper = row >> level + 1 & 1 if level < LEVELS - 1 else row * 0 + 1
+    flags = own_lower ^ first_upper, first_upper, own_lower, mirrored(row)
+    return [flag != 0 for flag in flags]
+
+
 def cast_kernel(own, cast_o):
     cast_o[...] = own[...].astype(BF16)
 
 
-def first_gram_kernel(role, own, other, first_o, second_o, gram_o):
-    own_first, own_lower, mirror = role[0] != 0, role[2] != 0, role[3] != 0
+def first_gram_kernel(own, other, first_o, second_o, gram_o):
+    own_first, _, own_lower, mirror = roles(0)
     mine = placed(own[...], mirror, own_lower)
     theirs = placed(other[...].astype(BF16), mirror, jnp.logical_not(own_lower))
     first_o[...], second_o[...] = pick(own_first, mine, theirs)
@@ -295,18 +303,18 @@
     product_o[...] = product_part(wide)
 
 
-def gram_kernel(role, wide, product, other, first_o, second_o, gram_o):
-    own_first = role[0] != 0
+def gram_kernel(level, wide, product, other, first_o, second_o, gram_o):
+    own_first = roles(level)[0]
     theirs = unpack(other[...])
     products = pick(own_first, product[...], product_part(theirs))
     gram_o[...] = pack(outer_part(*products))
     first_o[...], second_o[...] = pick(own_first, wide[...], theirs)
 
 
-def turn_kernel(level, role, first, start, turned_o, starts_o):
+def turn_kernel(level, first, start, turned_o, starts_o):
     turned_o[...] = turn(first[...])
     plain, turned = start_body(start[level], swap_matrix())
-    first_upper = role[1] != 0
+    first_upper = roles(level)[1]
     starts_o[:PAD] = jnp.where(first_upper, plain, turned)
     starts_o[PAD:] = jnp.where(first_upper, turned, plain)
 
@@ -327,25 +335,30 @@
     log_o[...] = log_in[...] + 0.5 * jnp.log(mean)
 
 
-def last_kernel(role, second, right, log_in, coarse_o, log_o, kron):
+def last_kernel(second, right, log_in, coarse_o, log_o, kron):
     merged = third(second, right[...], kron)
     mean = mean_square(merged)
     log_o[...] = (log_in[...] + 0.5 * jnp.log(mean))[:1, :1]
     wide = block_swap(merged.astype(BF16))
-    narrow = mm(wide, spread_matrix(role[3] != 0), NT).astype(BF16)
+    narrow = mm(wide, spread_matrix(roles(LEVELS - 1)[3]), NT).astype(BF16)
     coarse_o[...] = mm(row_spread(True), narrow, TN) * lax.rsqrt(mean)
 
 
-def call(kernel, outs, places, scratch=()):
-    return pl.pallas_call(
-        kernel,
-        out_shape=[jax.ShapeDtypeStruct(s, d) for s, d in outs],
-        in_specs=[pl.BlockSpec(memory_space=place) for place in places],
-        out_specs=[pl.BlockSpec(memory_space=pltpu.VMEM)] * len(outs),
-        scratch_shapes=list(scratch),
-        compiler_params=pltpu.CompilerParams(vmem_limit_bytes=VMEM_BYTES),
-        cost_estimate=pl.CostEstimate(flops=10**8, bytes_accessed=10**6, transcendentals=0),
-    )
+def call(kernel, outs, scratch=()):
+    vmem = pl.BlockSpec(memory_space=pltpu.VMEM)
+
+    def run(*args):
+        return pl.pallas_call(
+            kernel,
+            out_shape=[jax.ShapeDtypeStruct(s, d) for s, d in outs],
+            in_specs=[vmem] * len(args),
+            out_specs=[vmem] * len(outs),
+            scratch_shapes=list(scratch),
+            compiler_params=pltpu.CompilerParams(vmem_limit_bytes=VMEM_BYTES),
+            cost_estimate=pl.CostEstimate(flops=10**8, bytes_accessed=10**6, transcendentals=0),
+        )(*args)
+
+    return run
 
 
 def from_partner(array, flip):
@@ -372,48 +385,34 @@
 
 def per_device(site_tensors, start_basis):
     square = CHI * CHI
-    row = lax.axis_index("row")
-    mirror = mirrored(row)
-    vmem, smem = pltpu.VMEM, pltpu.SMEM
     mat, packed, logs = ((ROWS, LANES), BF16), ((ROWS * 3 // 2, 128), BF16), ((8, 128), F32)
-    kron = [vmem((CHI * LANES, LANES), BF16)]
+    kron = [pltpu.VMEM((CHI * LANES, LANES), BF16)]
     log_total = jnp.zeros(*logs)
     own = site_tensors[0, 0]
     for level in range(LEVELS):
-        own_lower = row >> level & 1
-        first_upper = row >> level + 1 & 1 if level < LEVELS - 1 else row * 0 + 1
-        role = jnp.stack([own_lower ^ first_upper, first_upper, own_lower, mirror]).astype(jnp.int32)
         if level == 0:
             other = from_partner(own, 1)
-            (own,) = call(cast_kernel, [((square, square), BF16)], [vmem])(own)
-            first, lower, gram = call(first_gram_kernel, [mat, mat, packed], [smem, vmem, vmem])(
-                role, own, other
-            )
+            (own,) = call(cast_kernel, [((square, square), BF16)])(own)
+            first, lower, gram = call(first_gram_kernel, [mat, mat, packed])(own, other)
         else:
             other = from_partner(own, 1 << level | 1)
-            wide, product = call(own_kernel, [mat, mat], [vmem])(own)
-            first, lower, gram = call(gram_kernel, [mat, mat, packed], [smem, vmem, vmem, vmem])(
-                role, wide, product, other
-            )
+            wide, product = call(own_kernel, [mat, mat])(own)
+            first, lower, gram = call(
+                functools.partial(gram_kernel, level), [mat, mat, packed]
+            )(wide, product, other)
         gram_other = from_bond(gram)
         turned, starts = call(
-            functools.partial(turn_kernel, level),
-            [mat, ((2 * PAD, LANES), F32)],
-            [smem, vmem, vmem],
-        )(role, first, start_basis)
-        (left,) = call(iso_kernel, [((PAD, LANES), BF16)], [vmem] * 3)(gram, gram_other, starts)
+            functools.partial(turn_kernel, level), [mat, ((2 * PAD, LANES), F32)]
+        )(first, start_basis)
+        (left,) = call(iso_kernel, [((PAD, LANES), BF16)])(gram, gram_other, starts)
         right = from_partner(left, 1)
-        (second,) = call(second_kernel, [((ROWS, CHI * LANES), BF16)], [vmem] * 3)(
-            turned, lower, left
-        )
+        (second,) = call(second_kernel, [((ROWS, CHI * LANES), BF16)])(turned, lower, left)
         if level < LEVELS - 1:
-            own, log_total = call(third_kernel, [packed, logs], [vmem] * 3, kron)(
+            own, log_total = call(third_kernel, [packed, logs], kron)(second, right, log_total)
+        else:
+            coarse, log_total = call(last_kernel, [((square, square), F32), ((1, 1), F32)], kron)(
                 second, right, log_total
             )
-        else:
-            coarse, log_total = call(
-                last_kernel, [((square, square), F32), ((1, 1), F32)], [smem] + [vmem] * 3, kron
-            )(role, second, right, log_total)
     return (coarse[None, None], log_total)
 
 

time: 45.8 us -> 43.5 us (0.950)
  Pallas kernels: 18.5 us -> 14.7 us
  waiting for transfers between devices: 8.62 us -> 10.3 us
    pallas_call x18, Pallas kernels: 18.5 us -> 14.7 us  [run(): pl.pallas_call(kernel, out_shape=[jax.ShapeDtypeStruct(s, d) for s, d in...]
    ppermute x3, waiting for transfers between devices: 4.41 us -> 5.85 us  [from_bond(): return lax.ppermute(array, ('row', 'col'), pairs)]
  transfers between devices with their start and end apart: 9 -> 9, of which waited for: 9 -> 9; matrix products, arithmetic and copies ran while one was open for 1% -> 0% of each run, Pallas kernels for 14% -> 11%
where the time goes in v5:
time: 43.5 us; the launch traced here: 43.3 us
  starting transfers between devices  15.9 us (37%)
  Pallas kernels  14.7 us (34%)
  waiting for transfers between devices  10.3 us (24%)
  local copies, waits for them, and re-layouts  1.72 us (4%)
  between operations  0.74 us (2%)
    pallas_call x18, Pallas kernels, run(): pl.pallas_call(kernel, out_shape=[jax.ShapeDtypeStruct(s, d) for s, d in...  14.7 us
    ppermute x3, starting transfers between devices, from_bond(): return lax.ppermute(array, ('row', 'col'), pairs)  11.5 us
    ppermute x3, waiting for transfers between devices, from_bond(): return lax.ppermute(array, ('row', 'col'), pairs)  5.85 us
    ppermute x6, starting transfers between devices, from_partner(): return lax.ppermute(array, 'row', [(i, i ^ flip) for i in range(count)])  4.43 us
    ppermute x6, waiting for transfers between devices, from_partner(): return lax.ppermute(array, 'row', [(i, i ^ flip) for i in range(count)])  4.42 us
    unnamed x6, local copies, waits for them, and re-layouts  1.71 us
  transfers between devices with their start and end apart: 9, of which 9 were waited for; matrix products, arithmetic and copies ran while one was open for 0% of the time, Pallas kernels for 11%

profile of v5, /device:TPU:0, one launch (start us, length us, event | category | flops | bytes accessed | tf_op | source)
XLA Modules:
  0.0 43.3 jit_solution(14862736065359186779)
XLA Ops:
  0.6 0.6 %collective-permute-start = (f32[144,144]{1,0:T(8,128)}, f32[144,144]{1,0:T(8,128)S(1)}, u32[]{:S(2)}, u32[]{:S(2)}) collective-permute-start(f32[144,144]{1,0:T(8,128)} %bitcast.2), channel_id=1, source_target_pairs={{0,4},{4,0},{8,12},{12,8},{16,20},{20,16},{24,28},{28,24},{1,5},{5... | collective-permute-start | bytes 248840 | tf_op jit(solution)/shard_map/ppermute | solution.py:366
  1.2 0.0 copy-start
  1.2 0.9 %copy-done = f32[1,1,144,144]{3,2,1,0:T(8,128)S(1)} copy-done((f32[1,1,144,144]{3,2,1,0:T(8,128)S(1)}, f32[1,1,144,144]{3,2,1,0:T(8,128)}, u32[]{:S(2)}) %copy-start) | copy-done | bytes 82968
  2.1 0.3 collective-permute-done.other
  2.4 1.6 %shard_map.42 = (bf16[192,256]{1,0:T(8,128)(2,1)S(1)}, bf16[192,256]{1,0:T(8,128)(2,1)S(1)}, bf16[288,128]{1,0:T(8,128)(2,1)S(1)}) custom-call(bf16[144,144]{1,0:T(8,128)(2,1)S(1)} %shard_map.41.own, f32[144,144]{1,0:T(8,128)S(1)} %collective-permute-done.other), custom_call_target="tpu_custom_call" | custom-call | flops 100000000 | bytes 1000000 | tf_op jit(solution)/shard_map/pallas_call | solution.py:351
  4.0 4.7 %collective-permute-start.1 = (bf16[288,128]{1,0:T(8,128)(2,1)S(1)}, bf16[288,128]{1,0:T(8,128)(2,1)S(1)}, u32[]{:S(2)}, u32[]{:S(2)}) collective-permute-start(bf16[288,128]{1,0:T(8,128)(2,1)S(1)} %get-tuple-element.30.own), channel_id=1, source_target_pairs={{0,7},{1,4},{2,5},{3,6},{4,1},{5,2},{6,3},{7,0},{8,13},{9,14},{10,... | collective-permute-start | bytes 221192 | tf_op jit(solution)/shard_map/ppermute | solution.py:383
  8.7 0.0 copy-start.1
  8.7 0.8 %copy-done.1 = f32[3,12,144]{2,1,0:T(8,128)S(1)} copy-done((f32[3,12,144]{2,1,0:T(8,128)S(1)}, f32[3,12,144]{2,1,0:T(8,128)}, u32[]{:S(2)}) %copy-start.1) | copy-done | bytes 20760
  9.5 0.3 shard_map.43
  9.8 1.1 %collective-permute-done.1.other = bf16[288,128]{1,0:T(8,128)(2,1)S(1)} collective-permute-done((bf16[288,128]{1,0:T(8,128)(2,1)S(1)}, bf16[288,128]{1,0:T(8,128)(2,1)S(1)}, u32[]{:S(2)}, u32[]{:S(2)}) %collective-permute-start.1) | collective-permute-done | bytes 73760 | tf_op jit(solution)/shard_map/ppermute | solution.py:383
  10.9 0.9 %shard_map.44.left = bf16[16,256]{1,0:T(8,128)(2,1)S(1)} custom-call(bf16[288,128]{1,0:T(8,128)(2,1)S(1)} %get-tuple-element.30.own, bf16[288,128]{1,0:T(8,128)(2,1)S(1)} %collective-permute-done.1.other, f32[32,256]{1,0:T(8,128)S(1)} %get-tuple-element.31.starts), custom_call_target="tpu_custom_call" | custom-call | flops 100000000 | bytes 1000000 | tf_op jit(solution)/shard_map/pallas_call | solution.py:351
  11.7 0.1 collective-permute-start.2
  11.8 1.1 %shard_map.45.second = bf16[192,3072]{1,0:T(8,128)(2,1)S(1)} custom-call(bf16[192,256]{1,0:T(8,128)(2,1)S(1)} %get-tuple-element.28.turned, bf16[192,256]{1,0:T(8,128)(2,1)S(1)} %get-tuple-element.29.lower, bf16[16,256]{1,0:T(8,128)(2,1)S(1)} %shard_map.44.left), custom_call_target="tpu_custom_call" | custom-call | flops 100000000 | bytes 1000000 | tf_op jit(solution)/shard_map/pallas_call | solution.py:351
  12.9 0.0 copy-start.2
  12.9 0.1 collective-permute-done.2.right
  13.0 0.9 %shard_map.46 = (bf16[288,128]{1,0:T(8,128)(2,1)S(1)}, f32[8,128]{1,0:T(8,128)S(1)}) custom-call(bf16[192,3072]{1,0:T(8,128)(2,1)S(1)} %shard_map.45.second, bf16[16,256]{1,0:T(8,128)(2,1)S(1)} %collective-permute-done.2.right, f32[8,128]{1,0:T(8,128)S(1)} %broadcast_in_dim.6.log_in), custom_call_target="tpu_custom_call" | custom-call | flops 100000000 | bytes 1000000 | tf_op jit(solution)/shard_map/pallas_call | solution.py:351
  13.8 2.0 %collective-permute-start.3 = (bf16[288,128]{1,0:T(8,128)(2,1)S(1)}, bf16[288,128]{1,0:T(8,128)(2,1)S(1)}, u32[]{:S(2)}, u32[]{:S(2)}) collective-permute-start(bf16[288,128]{1,0:T(8,128)(2,1)S(1)} %get-tuple-element.32.own), channel_id=1, source_target_pairs={{0,12},{4,8},{8,4},{12,0},{16,28},{20,24},{24,20},{28,16},{1,13},{... | collective-permute-start | bytes 221192 | tf_op jit(solution)/shard_map/ppermute | solution.py:366
  15.9 0.5 %shard_map.47 = (bf16[192,256]{1,0:T(8,128)(2,1)S(1)}, bf16[192,256]{1,0:T(8,128)(2,1)S(1)}) custom-call(bf16[288,128]{1,0:T(8,128)(2,1)S(1)} %get-tuple-element.32.own), custom_call_target="tpu_custom_call" | custom-call | flops 100000000 | bytes 1000000 | tf_op jit(solution)/shard_map/pallas_call | solution.py:351
  16.4 1.9 %collective-permute-done.3.other = bf16[288,128]{1,0:T(8,128)(2,1)S(1)} collective-permute-done((bf16[288,128]{1,0:T(8,128)(2,1)S(1)}, bf16[288,128]{1,0:T(8,128)(2,1)S(1)}, u32[]{:S(2)}, u32[]{:S(2)}) %collective-permute-start.3) | collective-permute-done | bytes 73760 | tf_op jit(solution)/shard_map/ppermute | solution.py:366
  18.3 1.0 %shard_map.48 = (bf16[192,256]{1,0:T(8,128)(2,1)S(1)}, bf16[192,256]{1,0:T(8,128)(2,1)S(1)}, bf16[288,128]{1,0:T(8,128)(2,1)S(1)}) custom-call(bf16[192,256]{1,0:T(8,128)(2,1)S(1)} %get-tuple-element.33.wide, bf16[192,256]{1,0:T(8,128)(2,1)S(1)} %get-tuple-element.34.product, bf16[288,128]{1,0:T(8,128)(2,1)S(1)} %collective-permute-done.3.other), custom_call_target="tpu_custom_call" | custom-call | flops 100000000 | bytes 1000000 | tf_op jit(solution)/shard_map/pallas_call | solution.py:351
  19.3 3.4 %collective-permute-start.4 = (bf16[288,128]{1,0:T(8,128)(2,1)S(1)}, bf16[288,128]{1,0:T(8,128)(2,1)S(1)}, u32[]{:S(2)}, u32[]{:S(2)}) collective-permute-start(bf16[288,128]{1,0:T(8,128)(2,1)S(1)} %get-tuple-element.38.own), channel_id=1, source_target_pairs={{0,7},{1,4},{2,5},{3,6},{4,1},{5,2},{6,3},{7,0},{8,13},{9,14},{10,... | collective-permute-start | bytes 221192 | tf_op jit(solution)/shard_map/ppermute | solution.py:383
  22.7 0.0 copy-done.2
  22.7 0.3 shard_map.49
  22.9 2.3 %collective-permute-done.4.other = bf16[288,128]{1,0:T(8,128)(2,1)S(1)} collective-permute-done((bf16[288,128]{1,0:T(8,128)(2,1)S(1)}, bf16[288,128]{1,0:T(8,128)(2,1)S(1)}, u32[]{:S(2)}, u32[]{:S(2)}) %collective-permute-start.4) | collective-permute-done | bytes 73760 | tf_op jit(solution)/shard_map/ppermute | solution.py:383
  25.2 0.9 %shard_map.50.left = bf16[16,256]{1,0:T(8,128)(2,1)S(1)} custom-call(bf16[288,128]{1,0:T(8,128)(2,1)S(1)} %get-tuple-element.38.own, bf16[288,128]{1,0:T(8,128)(2,1)S(1)} %collective-permute-done.4.other, f32[32,256]{1,0:T(8,128)S(1)} %get-tuple-element.39.starts), custom_call_target="tpu_custom_call" | custom-call | flops 100000000 | bytes 1000000 | tf_op jit(solution)/shard_map/pallas_call | solution.py:351
  26.1 0.1 collective-permute-start.5
  26.2 1.1 %shard_map.51.second = bf16[192,3072]{1,0:T(8,128)(2,1)S(1)} custom-call(bf16[192,256]{1,0:T(8,128)(2,1)S(1)} %get-tuple-element.36.turned, bf16[192,256]{1,0:T(8,128)(2,1)S(1)} %get-tuple-element.37.lower, bf16[16,256]{1,0:T(8,128)(2,1)S(1)} %shard_map.50.left), custom_call_target="tpu_custom_call" | custom-call | flops 100000000 | bytes 1000000 | tf_op jit(solution)/shard_map/pallas_call | solution.py:351
  27.3 0.1 collective-permute-done.5.right
  27.4 0.9 %shard_map.52 = (bf16[288,128]{1,0:T(8,128)(2,1)S(1)}, f32[8,128]{1,0:T(8,128)S(1)}) custom-call(bf16[192,3072]{1,0:T(8,128)(2,1)S(1)} %shard_map.51.second, bf16[16,256]{1,0:T(8,128)(2,1)S(1)} %collective-permute-done.5.right, f32[8,128]{1,0:T(8,128)S(1)} %get-tuple-element.40.log_in), custom_call_target="tpu_custom_call" | custom-call | flops 100000000 | bytes 1000000 | tf_op jit(solution)/shard_map/pallas_call | solution.py:351
  28.2 1.6 %collective-permute-start.6 = (bf16[288,128]{1,0:T(8,128)(2,1)S(1)}, bf16[288,128]{1,0:T(8,128)(2,1)S(1)}, u32[]{:S(2)}, u32[]{:S(2)}) collective-permute-start(bf16[288,128]{1,0:T(8,128)(2,1)S(1)} %get-tuple-element.41.own), channel_id=1, source_target_pairs={{0,20},{4,16},{8,28},{12,24},{16,4},{20,0},{24,12},{28,8},{1,21},{... | collective-permute-start | bytes 221192 | tf_op jit(solution)/shard_map/ppermute | solution.py:366
  29.9 0.5 %shard_map.53 = (bf16[192,256]{1,0:T(8,128)(2,1)S(1)}, bf16[192,256]{1,0:T(8,128)(2,1)S(1)}) custom-call(bf16[288,128]{1,0:T(8,128)(2,1)S(1)} %get-tuple-element.41.own), custom_call_target="tpu_custom_call" | custom-call | flops 100000000 | bytes 1000000 | tf_op jit(solution)/shard_map/pallas_call | solution.py:351
  30.3 1.9 %collective-permute-done.6.other = bf16[288,128]{1,0:T(8,128)(2,1)S(1)} collective-permute-done((bf16[288,128]{1,0:T(8,128)(2,1)S(1)}, bf16[288,128]{1,0:T(8,128)(2,1)S(1)}, u32[]{:S(2)}, u32[]{:S(2)}) %collective-permute-start.6) | collective-permute-done | bytes 73760 | tf_op jit(solution)/shard_map/ppermute | solution.py:366
  32.3 1.0 %shard_map.54 = (bf16[192,256]{1,0:T(8,128)(2,1)S(1)}, bf16[192,256]{1,0:T(8,128)(2,1)S(1)}, bf16[288,128]{1,0:T(8,128)(2,1)S(1)}) custom-call(bf16[192,256]{1,0:T(8,128)(2,1)S(1)} %get-tuple-element.42.wide, bf16[192,256]{1,0:T(8,128)(2,1)S(1)} %get-tuple-element.43.product, bf16[288,128]{1,0:T(8,128)(2,1)S(1)} %collective-permute-done.6.other), custom_call_target="tpu_custom_call" | custom-call | flops 100000000 | bytes 1000000 | tf_op jit(solution)/shard_map/pallas_call | solution.py:351
  33.2 3.3 %collective-permute-start.7 = (bf16[288,128]{1,0:T(8,128)(2,1)S(1)}, bf16[288,128]{1,0:T(8,128)(2,1)S(1)}, u32[]{:S(2)}, u32[]{:S(2)}) collective-permute-start(bf16[288,128]{1,0:T(8,128)(2,1)S(1)} %get-tuple-element.47.own), channel_id=1, source_target_pairs={{0,7},{1,4},{2,5},{3,6},{4,1},{5,2},{6,3},{7,0},{8,13},{9,14},{10,... | collective-permute-start | bytes 221192 | tf_op jit(solution)/shard_map/ppermute | solution.py:383
  36.5 0.3 shard_map.55
  36.8 2.5 %collective-permute-done.7.other = bf16[288,128]{1,0:T(8,128)(2,1)S(1)} collective-permute-done((bf16[288,128]{1,0:T(8,128)(2,1)S(1)}, bf16[288,128]{1,0:T(8,128)(2,1)S(1)}, u32[]{:S(2)}, u32[]{:S(2)}) %collective-permute-start.7) | collective-permute-done | bytes 73760 | tf_op jit(solution)/shard_map/ppermute | solution.py:383
  39.3 0.9 %shard_map.56.left = bf16[16,256]{1,0:T(8,128)(2,1)S(1)} custom-call(bf16[288,128]{1,0:T(8,128)(2,1)S(1)} %get-tuple-element.47.own, bf16[288,128]{1,0:T(8,128)(2,1)S(1)} %collective-permute-done.7.other, f32[32,256]{1,0:T(8,128)S(1)} %get-tuple-element.48.starts), custom_call_target="tpu_custom_call" | custom-call | flops 100000000 | bytes 1000000 | tf_op jit(solution)/shard_map/pallas_call | solution.py:351
  40.2 0.1 collective-permute-start.8
  40.3 1.1 %shard_map.57.second = bf16[192,3072]{1,0:T(8,128)(2,1)S(1)} custom-call(bf16[192,256]{1,0:T(8,128)(2,1)S(1)} %get-tuple-element.45.turned, bf16[192,256]{1,0:T(8,128)(2,1)S(1)} %get-tuple-element.46.lower, bf16[16,256]{1,0:T(8,128)(2,1)S(1)} %shard_map.56.left), custom_call_target="tpu_custom_call" | custom-call | flops 100000000 | bytes 1000000 | tf_op jit(solution)/shard_map/pallas_call | solution.py:351
  41.3 0.1 collective-permute-done.8.right
  41.4 1.9 %shard_map.58 = (f32[144,144]{1,0:T(8,128)}, f32[1,1]{1,0:T(1,128)}) custom-call(bf16[192,3072]{1,0:T(8,128)(2,1)S(1)} %shard_map.57.second, bf16[16,256]{1,0:T(8,128)(2,1)S(1)} %collective-permute-done.8.right, f32[8,128]{1,0:T(8,128)S(1)} %get-tuple-element.49.log_in), custom_call_target="tpu_custom_call" | custom-call | flops 100000000 | bytes 1000000 | tf_op jit(solution)/shard_map/pallas_call | solution.py:351
  (2 shorter events, 0.0 us)
Async XLA Ops:
  0.6 1.8 %collective-permute-start = (f32[144,144]{1,0:T(8,128)}, f32[144,144]{1,0:T(8,128)S(1)}, u32[]{:S(2)}, u32[]{:S(2)}) collective-permute-start(f32[144,144]{1,0:T(8,128)} %bitcast.2), channel_id=1, source_target_pairs={{0,4},{4,0},{8,12},{12,8},{16,20},{20,16},{24,28},{28,24},{1,5},{5... | collective-permute-start | bytes 248840 | tf_op jit(solution)/shard_map/ppermute | solution.py:366
  1.2 0.9 %copy-start = (f32[1,1,144,144]{3,2,1,0:T(8,128)S(1)}, f32[1,1,144,144]{3,2,1,0:T(8,128)}, u32[]{:S(2)}) copy-start(f32[1,1,144,144]{3,2,1,0:T(8,128)} %param.2) | copy-start | bytes 248836
  4.0 6.9 %collective-permute-start.1 = (bf16[288,128]{1,0:T(8,128)(2,1)S(1)}, bf16[288,128]{1,0:T(8,128)(2,1)S(1)}, u32[]{:S(2)}, u32[]{:S(2)}) collective-permute-start(bf16[288,128]{1,0:T(8,128)(2,1)S(1)} %get-tuple-element.30.own), channel_id=1, source_target_pairs={{0,7},{1,4},{2,5},{3,6},{4,1},{5,2},{6,3},{7,0},{8,13},{9,14},{10,... | collective-permute-start | bytes 221192 | tf_op jit(solution)/shard_map/ppermute | solution.py:383
  8.7 0.8 %copy-start.1 = (f32[3,12,144]{2,1,0:T(8,128)S(1)}, f32[3,12,144]{2,1,0:T(8,128)}, u32[]{:S(2)}) copy-start(f32[3,12,144]{2,1,0:T(8,128)} %start.5) | copy-start | bytes 62212
  11.7 1.2 %collective-permute-start.2 = (bf16[16,256]{1,0:T(8,128)(2,1)S(1)}, bf16[16,256]{1,0:T(8,128)(2,1)S(1)}, u32[]{:S(2)}, u32[]{:S(2)}) collective-permute-start(bf16[16,256]{1,0:T(8,128)(2,1)S(1)} %shard_map.44.left), channel_id=1, source_target_pairs={{0,4},{4,0},{8,12},{12,8},{16,20},{20,16},{24,28},{28,24},{1,5},{5... | collective-permute-start | bytes 24584 | tf_op jit(solution)/shard_map/ppermute | solution.py:366
  12.9 9.8 %copy-start.2 = (f32[3,12,144]{2,1,0:T(8,128)S(1)}, f32[3,12,144]{2,1,0:T(8,128)}, u32[]{:S(2)}) copy-start(f32[3,12,144]{2,1,0:T(8,128)} %start.5) | copy-start | bytes 62212
  13.8 4.4 %collective-permute-start.3 = (bf16[288,128]{1,0:T(8,128)(2,1)S(1)}, bf16[288,128]{1,0:T(8,128)(2,1)S(1)}, u32[]{:S(2)}, u32[]{:S(2)}) collective-permute-start(bf16[288,128]{1,0:T(8,128)(2,1)S(1)} %get-tuple-element.32.own), channel_id=1, source_target_pairs={{0,12},{4,8},{8,4},{12,0},{16,28},{20,24},{24,20},{28,16},{1,13},{... | collective-permute-start | bytes 221192 | tf_op jit(solution)/shard_map/ppermute | solution.py:366
  19.3 6.0 %collective-permute-start.4 = (bf16[288,128]{1,0:T(8,128)(2,1)S(1)}, bf16[288,128]{1,0:T(8,128)(2,1)S(1)}, u32[]{:S(2)}, u32[]{:S(2)}) collective-permute-start(bf16[288,128]{1,0:T(8,128)(2,1)S(1)} %get-tuple-element.38.own), channel_id=1, source_target_pairs={{0,7},{1,4},{2,5},{3,6},{4,1},{5,2},{6,3},{7,0},{8,13},{9,14},{10,... | collective-permute-start | bytes 221192 | tf_op jit(solution)/shard_map/ppermute | solution.py:383
  26.1 1.2 %collective-permute-start.5 = (bf16[16,256]{1,0:T(8,128)(2,1)S(1)}, bf16[16,256]{1,0:T(8,128)(2,1)S(1)}, u32[]{:S(2)}, u32[]{:S(2)}) collective-permute-start(bf16[16,256]{1,0:T(8,128)(2,1)S(1)} %shard_map.50.left), channel_id=1, source_target_pairs={{0,4},{4,0},{8,12},{12,8},{16,20},{20,16},{24,28},{28,24},{1,5},{5... | collective-permute-start | bytes 24584 | tf_op jit(solution)/shard_map/ppermute | solution.py:366
  28.2 4.0 %collective-permute-start.6 = (bf16[288,128]{1,0:T(8,128)(2,1)S(1)}, bf16[288,128]{1,0:T(8,128)(2,1)S(1)}, u32[]{:S(2)}, u32[]{:S(2)}) collective-permute-start(bf16[288,128]{1,0:T(8,128)(2,1)S(1)} %get-tuple-element.41.own), channel_id=1, source_target_pairs={{0,20},{4,16},{8,28},{12,24},{16,4},{20,0},{24,12},{28,8},{1,21},{... | collective-permute-start | bytes 221192 | tf_op jit(solution)/shard_map/ppermute | solution.py:366
  33.2 6.1 %collective-permute-start.7 = (bf16[288,128]{1,0:T(8,128)(2,1)S(1)}, bf16[288,128]{1,0:T(8,128)(2,1)S(1)}, u32[]{:S(2)}, u32[]{:S(2)}) collective-permute-start(bf16[288,128]{1,0:T(8,128)(2,1)S(1)} %get-tuple-element.47.own), channel_id=1, source_target_pairs={{0,7},{1,4},{2,5},{3,6},{4,1},{5,2},{6,3},{7,0},{8,13},{9,14},{10,... | collective-permute-start | bytes 221192 | tf_op jit(solution)/shard_map/ppermute | solution.py:383
  40.2 1.2 %collective-permute-start.8 = (bf16[16,256]{1,0:T(8,128)(2,1)S(1)}, bf16[16,256]{1,0:T(8,128)(2,1)S(1)}, u32[]{:S(2)}, u32[]{:S(2)}) collective-permute-start(bf16[16,256]{1,0:T(8,128)(2,1)S(1)} %shard_map.56.left), channel_id=1, source_target_pairs={{0,4},{4,0},{8,12},{12,8},{16,20},{20,16},{24,28},{28,24},{1,5},{5... | collective-permute-start | bytes 24584 | tf_op jit(solution)/shard_map/ppermute | solution.py:366

commit v6 on v5

--- a/solution.py
+++ b/solution.py
@@ -17,6 +17,7 @@
 ROWS = CHI * PAD
 LANES = PAD * PAD
 VMEM_BYTES = 8 << 20
+SECOND = (CHI + 2) * 128
 PIVOT = 1.0 / 64
 F32 = jnp.float32
 BF16 = jnp.bfloat16
@@ -233,37 +234,84 @@
         iso_o[...] = exact_iso(own, other, start, start_turned, shift, swap).astype(BF16)
 
 
+def packed_pair(index):
+    entry = jnp.where(index < 128, index, 128 + minor(index))
+    s = lax.shift_right_logical(entry * 171, 11)
+    return s, entry - s * CHI
+
+
+def packing():
+    s, t = packed_pair(iota((LANES, ROWS), 0))
+    j = iota((LANES, ROWS), 1)
+    return one_hot((group(j) == s) & (minor(j) == t))
+
+
 def first_second(turned, lower, left, second_ref):
     lane = iota((PAD, LANES), 1)
     masked = [jnp.where(group(lane) == k, left.astype(F32), 0.0) for k in range(CHI)]
     masked = jnp.concatenate(masked, axis=0).astype(BF16)
     i, j = iota((LANES, LANES), 0), iota((LANES, LANES), 1)
-    values = mm(masked, one_hot(minor(i) == group(j)))
-    eye = minor(lane) == iota((PAD, LANES), 0)
-    for a in range(CHI):
+    values = mm(masked, one_hot(minor(i) == packed_pair(j)[0]))
+    eye = packed_pair(lane)[1] == iota((PAD, LANES), 0)
+    lane_group = group(iota((PAD, 128), 1))
+    turned = turned[:, :ROWS]
+
+    def line(k, a, side):
+        at = k * PAD + a
+        return jnp.broadcast_to(values[at : at + 1, side * 128 : side * 128 + 128], (PAD, 128))
+
+    rests = []
+    for k in range(CHI):
+        pair = []
+        for side in range(2):
+            rest = jnp.zeros((PAD, 128), F32)
+            for a in range(side * 8, min(side * 8 + 8, CHI)):
+                rest = jnp.where(lane_group == a - side * 8, line(k, a, 1), rest)
+            pair.append(jnp.where(eye[:, 128:], rest, 0.0).astype(BF16))
+        rests.append(jnp.concatenate(pair, axis=1))
+    rest = mm(turned, jnp.concatenate(rests, axis=0)).astype(BF16)
+    row_group = group(iota((ROWS, 128), 1))
+    zero = jnp.zeros((PAD, 128), BF16)
+    for half in range(CHI // 2):
         blocks = []
         for k in range(CHI):
-            line = jnp.broadcast_to(values[k * PAD + a : k * PAD + a + 1, :], (PAD, LANES))
-            blocks.append(jnp.where(eye, line, 0.0).astype(BF16))
-        kron = jnp.concatenate(blocks, axis=0)
-        first = mm(turned[:, :ROWS], kron).astype(BF16)
-        second = mm(first[:, :ROWS], lower).astype(BF16)
-        for k in range(CHI):
-            second_ref[a * PAD : (a + 1) * PAD, k * LANES : (k + 1) * LANES] = second[
-                k * PAD : (k + 1) * PAD, :
+            pair = [
+                jnp.where(eye[:, :128], line(k, a, 0), 0.0).astype(BF16)
+                for a in (2 * half, 2 * half + 1)
             ]
+            blocks.append(jnp.concatenate(pair, axis=1))
+        both = mm(turned, jnp.concatenate(blocks, axis=0)).astype(BF16)
+        for a in (2 * half, 2 * half + 1):
+            tail = rest[:, (a >> 3) * 128 : (a >> 3) * 128 + 128]
+            tail = jnp.where(row_group == (a & 7), tail, jnp.zeros_like(tail))
+            head = both[:, (a & 1) * 128 : (a & 1) * 128 + 128]
+            second = mm(jnp.concatenate([head, tail], axis=1), lower).astype(BF16)
+            rows = slice(a * PAD, (a + 1) * PAD)
+            tails = [zero, zero]
+            for k in range(CHI):
+                block = second[k * PAD : (k + 1) * PAD]
+                second_ref[rows, k * 128 : (k + 1) * 128] = block[:, :128]
+                tails[k >> 3] = jnp.where(lane_group == (k & 7), block[:, 128:], tails[k >> 3])
+            for side in range(2):
+                at = (CHI + side) * 128
+                second_ref[rows, at : at + 128] = tails[side]
 
 
 def third(second_ref, right, kron_ref):
     tile = one_hot(minor(iota((PAD, LANES), 1)) == iota((PAD, LANES), 0))
     values = mm(right, tile, TN)
-    lane_group = group(iota((PAD, LANES), 1))
+    lane_group = group(iota((CHI * CHI, LANES), 1))
+    entry = iota((CHI * CHI, LANES), 0)
+    kept = lax.shift_right_logical(entry * 171, 11) == lane_group
     for k in range(CHI):
-        block = values[k * PAD : (k + 1) * PAD, :]
-        for d in range(PAD):
-            kept = jnp.where(lane_group == d, block, 0.0) if d < CHI else jnp.zeros_like(block)
-            start = k * LANES + d * PAD
-            kron_ref[start : start + PAD, :] = kept.astype(BF16)
+        block = values[k * PAD : k * PAD + CHI, :]
+        tall = jnp.concatenate([block] * CHI, axis=0)
+        tall = jnp.where(kept, tall, 0.0).astype(BF16)
+        kron_ref[k * 128 : (k + 1) * 128, :] = tall[:128]
+        at = CHI * 128 + k * PAD
+        kron_ref[at : at + PAD, :] = tall[128:]
+    used = CHI * 128 + CHI * PAD
+    kron_ref[used:, :] = jnp.zeros((SECOND - used, LANES), BF16)
     return mm(second_ref[...], kron_ref[...])
 
 
@@ -311,8 +359,11 @@
     first_o[...], second_o[...] = pick(own_first, wide[...], theirs)
 
 
-def turn_kernel(level, first, start, turned_o, starts_o):
+def turn_kernel(level, first, second, start, turned_o, lower_o, starts_o):
     turned_o[...] = turn(first[...])
+    packer = packing()
+    lower = mm(packer, second[...]).astype(BF16)
+    lower_o[...] = mm(lower[:, :ROWS], packer, NT).astype(BF16)
     plain, turned = start_body(start[level], swap_matrix())
     first_upper = roles(level)[1]
     starts_o[:PAD] = jnp.where(first_upper, plain, turned)
@@ -386,7 +437,8 @@
 def per_device(site_tensors, start_basis):
     square = CHI * CHI
     mat, packed, logs = ((ROWS, LANES), BF16), ((ROWS * 3 // 2, 128), BF16), ((8, 128), F32)
-    kron = [pltpu.VMEM((CHI * LANES, LANES), BF16)]
+    square_mat = ((LANES, LANES), BF16)
+    kron = [pltpu.VMEM((SECOND, LANES), BF16)]
     log_total = jnp.zeros(*logs)
     own = site_tensors[0, 0]
     for level in range(LEVELS):
@@ -401,12 +453,12 @@
                 functools.partial(gram_kernel, level), [mat, mat, packed]
             )(wide, product, other)
         gram_other = from_bond(gram)
-        turned, starts = call(
-            functools.partial(turn_kernel, level), [mat, ((2 * PAD, LANES), F32)]
-        )(first, start_basis)
+        turned, lower, starts = call(
+            functools.partial(turn_kernel, level), [mat, square_mat, ((2 * PAD, LANES), F32)]
+        )(first, lower, start_basis)
         (left,) = call(iso_kernel, [((PAD, LANES), BF16)])(gram, gram_other, starts)
         right = from_partner(left, 1)
-        (second,) = call(second_kernel, [((ROWS, CHI * LANES), BF16)])(turned, lower, left)
+        (second,) = call(second_kernel, [((ROWS, SECOND), BF16)])(turned, lower, left)
         if level < LEVELS - 1:
             own, log_total = call(third_kernel, [packed, logs], kron)(second, right, log_total)
         else:

time: 43.5 us -> 44.3 us (1.018)
  Pallas kernels: 14.7 us -> 15.9 us
  local copies, waits for them, and re-layouts: 1.72 us -> 0.92 us
    pallas_call x18, Pallas kernels: 14.7 us -> 15.9 us  [run(): pl.pallas_call(kernel, out_shape=[jax.ShapeDtypeStruct(s, d) for s, d in...]
    unnamed x6 -> x4, local copies, waits for them, and re-layouts: 1.71 us -> 0.92 us
  transfers between devices with their start and end apart: 9 -> 9, of which waited for: 9 -> 6; matrix products, arithmetic and copies ran while one was open for 0% -> 0% of each run, Pallas kernels for 11% -> 15%
where the time goes in v6:
time: 44.3 us; the launch traced here: 44.2 us
  starting transfers between devices  16.2 us (37%)
  Pallas kernels  15.9 us (36%)
  waiting for transfers between devices  10.4 us (23%)
  local copies, waits for them, and re-layouts  0.92 us (2%)
  between operations  0.77 us (2%)
    pallas_call x18, Pallas kernels, run(): pl.pallas_call(kernel, out_shape=[jax.ShapeDtypeStruct(s, d) for s, d in...  15.9 us
    ppermute x3, starting transfers between devices, from_bond(): return lax.ppermute(array, ('row', 'col'), pairs)  11.6 us
    ppermute x3, waiting for transfers between devices, from_bond(): return lax.ppermute(array, ('row', 'col'), pairs)  6.14 us
    ppermute x6, starting transfers between devices, from_partner(): return lax.ppermute(array, 'row', [(i, i ^ flip) for i in range(count)])  4.55 us
    ppermute x6, waiting for transfers between devices, from_partner(): return lax.ppermute(array, 'row', [(i, i ^ flip) for i in range(count)])  4.28 us
    unnamed x4, local copies, waits for them, and re-layouts  0.92 us
  transfers between devices with their start and end apart: 9, of which 6 were waited for; matrix products, arithmetic and copies ran while one was open for 0% of the time, Pallas kernels for 15%

profile of v6, /device:TPU:0, one launch (start us, length us, event | category | flops | bytes accessed | tf_op | source)
XLA Modules:
  0.0 44.2 jit_solution(1493918900413957098)
XLA Ops:
  0.6 0.6 %collective-permute-start = (f32[144,144]{1,0:T(8,128)}, f32[144,144]{1,0:T(8,128)S(1)}, u32[]{:S(2)}, u32[]{:S(2)}) collective-permute-start(f32[144,144]{1,0:T(8,128)} %bitcast.2), channel_id=1, source_target_pairs={{0,4},{4,0},{8,12},{12,8},{16,20},{20,16},{24,28},{28,24},{1,5},{5... | collective-permute-start | bytes 248840 | tf_op jit(solution)/shard_map/ppermute | solution.py:417
  1.2 0.0 copy-start
  1.2 0.9 %copy-done = f32[1,1,144,144]{3,2,1,0:T(8,128)S(1)} copy-done((f32[1,1,144,144]{3,2,1,0:T(8,128)S(1)}, f32[1,1,144,144]{3,2,1,0:T(8,128)}, u32[]{:S(2)}) %copy-start) | copy-done | bytes 82968
  2.1 0.0 copy-start.1
  2.1 0.3 collective-permute-done.other
  2.4 1.6 %shard_map.42 = (bf16[192,256]{1,0:T(8,128)(2,1)S(1)}, bf16[192,256]{1,0:T(8,128)(2,1)S(1)}, bf16[288,128]{1,0:T(8,128)(2,1)S(1)}) custom-call(bf16[144,144]{1,0:T(8,128)(2,1)S(1)} %shard_map.41.own, f32[144,144]{1,0:T(8,128)S(1)} %collective-permute-done.other), custom_call_target="tpu_custom_call" | custom-call | flops 100000000 | bytes 1000000 | tf_op jit(solution)/shard_map/pallas_call | solution.py:402
  4.0 4.7 %collective-permute-start.1 = (bf16[288,128]{1,0:T(8,128)(2,1)S(1)}, bf16[288,128]{1,0:T(8,128)(2,1)S(1)}, u32[]{:S(2)}, u32[]{:S(2)}) collective-permute-start(bf16[288,128]{1,0:T(8,128)(2,1)S(1)} %get-tuple-element.34.own), channel_id=1, source_target_pairs={{0,7},{1,4},{2,5},{3,6},{4,1},{5,2},{6,3},{7,0},{8,13},{9,14},{10,... | collective-permute-start | bytes 221192 | tf_op jit(solution)/shard_map/ppermute | solution.py:434
  8.7 0.0 copy-done.1
  8.7 0.3 shard_map.43
  9.1 1.8 %collective-permute-done.1.other = bf16[288,128]{1,0:T(8,128)(2,1)S(1)} collective-permute-done((bf16[288,128]{1,0:T(8,128)(2,1)S(1)}, bf16[288,128]{1,0:T(8,128)(2,1)S(1)}, u32[]{:S(2)}, u32[]{:S(2)}) %collective-permute-start.1) | collective-permute-done | bytes 73760 | tf_op jit(solution)/shard_map/ppermute | solution.py:434
  10.9 0.9 %shard_map.44.left = bf16[16,256]{1,0:T(8,128)(2,1)S(1)} custom-call(bf16[288,128]{1,0:T(8,128)(2,1)S(1)} %get-tuple-element.34.own, bf16[288,128]{1,0:T(8,128)(2,1)S(1)} %collective-permute-done.1.other, f32[32,256]{1,0:T(8,128)S(1)} %get-tuple-element.35.starts), custom_call_target="tpu_custom_call" | custom-call | flops 100000000 | bytes 1000000 | tf_op jit(solution)/shard_map/pallas_call | solution.py:402
  11.7 0.1 collective-permute-start.2
  11.8 1.5 %shard_map.45.second = bf16[192,1792]{1,0:T(8,128)(2,1)S(1)} custom-call(bf16[192,256]{1,0:T(8,128)(2,1)S(1)} %get-tuple-element.32.turned, bf16[256,256]{1,0:T(8,128)(2,1)S(1)} %get-tuple-element.33.lower, bf16[16,256]{1,0:T(8,128)(2,1)S(1)} %shard_map.44.left), custom_call_target="tpu_custom_call" | custom-call | flops 100000000 | bytes 1000000 | tf_op jit(solution)/shard_map/pallas_call | solution.py:402
  13.3 0.0 collective-permute-done.2.right
  13.4 0.7 %shard_map.46 = (bf16[288,128]{1,0:T(8,128)(2,1)S(1)}, f32[8,128]{1,0:T(8,128)S(1)}) custom-call(bf16[192,1792]{1,0:T(8,128)(2,1)S(1)} %shard_map.45.second, bf16[16,256]{1,0:T(8,128)(2,1)S(1)} %collective-permute-done.2.right, f32[8,128]{1,0:T(8,128)S(1)} %broadcast_in_dim.6.log_in), custom_call_target="tpu_custom_call" | custom-call | flops 100000000 | bytes 1000000 | tf_op jit(solution)/shard_map/pallas_call | solution.py:402
  14.1 2.1 %collective-permute-start.3 = (bf16[288,128]{1,0:T(8,128)(2,1)S(1)}, bf16[288,128]{1,0:T(8,128)(2,1)S(1)}, u32[]{:S(2)}, u32[]{:S(2)}) collective-permute-start(bf16[288,128]{1,0:T(8,128)(2,1)S(1)} %get-tuple-element.36.own), channel_id=1, source_target_pairs={{0,12},{4,8},{8,4},{12,0},{16,28},{20,24},{24,20},{28,16},{1,13},{... | collective-permute-start | bytes 221192 | tf_op jit(solution)/shard_map/ppermute | solution.py:417
  16.1 0.5 %shard_map.47 = (bf16[192,256]{1,0:T(8,128)(2,1)S(1)}, bf16[192,256]{1,0:T(8,128)(2,1)S(1)}) custom-call(bf16[288,128]{1,0:T(8,128)(2,1)S(1)} %get-tuple-element.36.own), custom_call_target="tpu_custom_call" | custom-call | flops 100000000 | bytes 1000000 | tf_op jit(solution)/shard_map/pallas_call | solution.py:402
  16.6 2.0 %collective-permute-done.3.other = bf16[288,128]{1,0:T(8,128)(2,1)S(1)} collective-permute-done((bf16[288,128]{1,0:T(8,128)(2,1)S(1)}, bf16[288,128]{1,0:T(8,128)(2,1)S(1)}, u32[]{:S(2)}, u32[]{:S(2)}) %collective-permute-start.3) | collective-permute-done | bytes 73760 | tf_op jit(solution)/shard_map/ppermute | solution.py:417
  18.6 1.0 %shard_map.48 = (bf16[192,256]{1,0:T(8,128)(2,1)S(1)}, bf16[192,256]{1,0:T(8,128)(2,1)S(1)}, bf16[288,128]{1,0:T(8,128)(2,1)S(1)}) custom-call(bf16[192,256]{1,0:T(8,128)(2,1)S(1)} %get-tuple-element.37.wide, bf16[192,256]{1,0:T(8,128)(2,1)S(1)} %get-tuple-element.38.product, bf16[288,128]{1,0:T(8,128)(2,1)S(1)} %collective-permute-done.3.other), custom_call_target="tpu_custom_call" | custom-call | flops 100000000 | bytes 1000000 | tf_op jit(solution)/shard_map/pallas_call | solution.py:402
  19.6 3.5 %collective-permute-start.4 = (bf16[288,128]{1,0:T(8,128)(2,1)S(1)}, bf16[288,128]{1,0:T(8,128)(2,1)S(1)}, u32[]{:S(2)}, u32[]{:S(2)}) collective-permute-start(bf16[288,128]{1,0:T(8,128)(2,1)S(1)} %get-tuple-element.43.own), channel_id=1, source_target_pairs={{0,7},{1,4},{2,5},{3,6},{4,1},{5,2},{6,3},{7,0},{8,13},{9,14},{10,... | collective-permute-start | bytes 221192 | tf_op jit(solution)/shard_map/ppermute | solution.py:434
  23.0 0.3 shard_map.49
  23.4 2.1 %collective-permute-done.4.other = bf16[288,128]{1,0:T(8,128)(2,1)S(1)} collective-permute-done((bf16[288,128]{1,0:T(8,128)(2,1)S(1)}, bf16[288,128]{1,0:T(8,128)(2,1)S(1)}, u32[]{:S(2)}, u32[]{:S(2)}) %collective-permute-start.4) | collective-permute-done | bytes 73760 | tf_op jit(solution)/shard_map/ppermute | solution.py:434
  25.5 0.9 %shard_map.50.left = bf16[16,256]{1,0:T(8,128)(2,1)S(1)} custom-call(bf16[288,128]{1,0:T(8,128)(2,1)S(1)} %get-tuple-element.43.own, bf16[288,128]{1,0:T(8,128)(2,1)S(1)} %collective-permute-done.4.other, f32[32,256]{1,0:T(8,128)S(1)} %get-tuple-element.44.starts), custom_call_target="tpu_custom_call" | custom-call | flops 100000000 | bytes 1000000 | tf_op jit(solution)/shard_map/pallas_call | solution.py:402
  26.4 0.1 collective-permute-start.5
  26.5 1.5 %shard_map.51.second = bf16[192,1792]{1,0:T(8,128)(2,1)S(1)} custom-call(bf16[192,256]{1,0:T(8,128)(2,1)S(1)} %get-tuple-element.41.turned, bf16[256,256]{1,0:T(8,128)(2,1)S(1)} %get-tuple-element.42.lower, bf16[16,256]{1,0:T(8,128)(2,1)S(1)} %shard_map.50.left), custom_call_target="tpu_custom_call" | custom-call | flops 100000000 | bytes 1000000 | tf_op jit(solution)/shard_map/pallas_call | solution.py:402
  28.0 0.0 collective-permute-done.5.right
  28.0 0.7 %shard_map.52 = (bf16[288,128]{1,0:T(8,128)(2,1)S(1)}, f32[8,128]{1,0:T(8,128)S(1)}) custom-call(bf16[192,1792]{1,0:T(8,128)(2,1)S(1)} %shard_map.51.second, bf16[16,256]{1,0:T(8,128)(2,1)S(1)} %collective-permute-done.5.right, f32[8,128]{1,0:T(8,128)S(1)} %get-tuple-element.45.log_in), custom_call_target="tpu_custom_call" | custom-call | flops 100000000 | bytes 1000000 | tf_op jit(solution)/shard_map/pallas_call | solution.py:402
  28.7 1.7 %collective-permute-start.6 = (bf16[288,128]{1,0:T(8,128)(2,1)S(1)}, bf16[288,128]{1,0:T(8,128)(2,1)S(1)}, u32[]{:S(2)}, u32[]{:S(2)}) collective-permute-start(bf16[288,128]{1,0:T(8,128)(2,1)S(1)} %get-tuple-element.46.own), channel_id=1, source_target_pairs={{0,20},{4,16},{8,28},{12,24},{16,4},{20,0},{24,12},{28,8},{1,21},{... | collective-permute-start | bytes 221192 | tf_op jit(solution)/shard_map/ppermute | solution.py:417
  30.5 0.5 %shard_map.53 = (bf16[192,256]{1,0:T(8,128)(2,1)S(1)}, bf16[192,256]{1,0:T(8,128)(2,1)S(1)}) custom-call(bf16[288,128]{1,0:T(8,128)(2,1)S(1)} %get-tuple-element.46.own), custom_call_target="tpu_custom_call" | custom-call | flops 100000000 | bytes 1000000 | tf_op jit(solution)/shard_map/pallas_call | solution.py:402
  31.0 2.0 %collective-permute-done.6.other = bf16[288,128]{1,0:T(8,128)(2,1)S(1)} collective-permute-done((bf16[288,128]{1,0:T(8,128)(2,1)S(1)}, bf16[288,128]{1,0:T(8,128)(2,1)S(1)}, u32[]{:S(2)}, u32[]{:S(2)}) %collective-permute-start.6) | collective-permute-done | bytes 73760 | tf_op jit(solution)/shard_map/ppermute | solution.py:417
  32.9 1.0 %shard_map.54 = (bf16[192,256]{1,0:T(8,128)(2,1)S(1)}, bf16[192,256]{1,0:T(8,128)(2,1)S(1)}, bf16[288,128]{1,0:T(8,128)(2,1)S(1)}) custom-call(bf16[192,256]{1,0:T(8,128)(2,1)S(1)} %get-tuple-element.47.wide, bf16[192,256]{1,0:T(8,128)(2,1)S(1)} %get-tuple-element.48.product, bf16[288,128]{1,0:T(8,128)(2,1)S(1)} %collective-permute-done.6.other), custom_call_target="tpu_custom_call" | custom-call | flops 100000000 | bytes 1000000 | tf_op jit(solution)/shard_map/pallas_call | solution.py:402
  33.9 3.4 %collective-permute-start.7 = (bf16[288,128]{1,0:T(8,128)(2,1)S(1)}, bf16[288,128]{1,0:T(8,128)(2,1)S(1)}, u32[]{:S(2)}, u32[]{:S(2)}) collective-permute-start(bf16[288,128]{1,0:T(8,128)(2,1)S(1)} %get-tuple-element.53.own), channel_id=1, source_target_pairs={{0,7},{1,4},{2,5},{3,6},{4,1},{5,2},{6,3},{7,0},{8,13},{9,14},{10,... | collective-permute-start | bytes 221192 | tf_op jit(solution)/shard_map/ppermute | solution.py:434
  37.3 0.3 shard_map.55
  37.7 2.2 %collective-permute-done.7.other = bf16[288,128]{1,0:T(8,128)(2,1)S(1)} collective-permute-done((bf16[288,128]{1,0:T(8,128)(2,1)S(1)}, bf16[288,128]{1,0:T(8,128)(2,1)S(1)}, u32[]{:S(2)}, u32[]{:S(2)}) %collective-permute-start.7) | collective-permute-done | bytes 73760 | tf_op jit(solution)/shard_map/ppermute | solution.py:434
  39.9 0.9 %shard_map.56.left = bf16[16,256]{1,0:T(8,128)(2,1)S(1)} custom-call(bf16[288,128]{1,0:T(8,128)(2,1)S(1)} %get-tuple-element.53.own, bf16[288,128]{1,0:T(8,128)(2,1)S(1)} %collective-permute-done.7.other, f32[32,256]{1,0:T(8,128)S(1)} %get-tuple-element.54.starts), custom_call_target="tpu_custom_call" | custom-call | flops 100000000 | bytes 1000000 | tf_op jit(solution)/shard_map/pallas_call | solution.py:402
  40.8 0.1 collective-permute-start.8
  40.9 1.5 %shard_map.57.second = bf16[192,1792]{1,0:T(8,128)(2,1)S(1)} custom-call(bf16[192,256]{1,0:T(8,128)(2,1)S(1)} %get-tuple-element.51.turned, bf16[256,256]{1,0:T(8,128)(2,1)S(1)} %get-tuple-element.52.lower, bf16[16,256]{1,0:T(8,128)(2,1)S(1)} %shard_map.56.left), custom_call_target="tpu_custom_call" | custom-call | flops 100000000 | bytes 1000000 | tf_op jit(solution)/shard_map/pallas_call | solution.py:402
  42.4 0.0 collective-permute-done.8.right
  42.4 1.8 %shard_map.58 = (f32[144,144]{1,0:T(8,128)}, f32[1,1]{1,0:T(1,128)}) custom-call(bf16[192,1792]{1,0:T(8,128)(2,1)S(1)} %shard_map.57.second, bf16[16,256]{1,0:T(8,128)(2,1)S(1)} %collective-permute-done.8.right, f32[8,128]{1,0:T(8,128)S(1)} %get-tuple-element.55.log_in), custom_call_target="tpu_custom_call" | custom-call | flops 100000000 | bytes 1000000 | tf_op jit(solution)/shard_map/pallas_call | solution.py:402
  (2 shorter events, 0.0 us)
Async XLA Ops:
  0.6 1.8 %collective-permute-start = (f32[144,144]{1,0:T(8,128)}, f32[144,144]{1,0:T(8,128)S(1)}, u32[]{:S(2)}, u32[]{:S(2)}) collective-permute-start(f32[144,144]{1,0:T(8,128)} %bitcast.2), channel_id=1, source_target_pairs={{0,4},{4,0},{8,12},{12,8},{16,20},{20,16},{24,28},{28,24},{1,5},{5... | collective-permute-start | bytes 248840 | tf_op jit(solution)/shard_map/ppermute | solution.py:417
  1.2 0.9 %copy-start = (f32[1,1,144,144]{3,2,1,0:T(8,128)S(1)}, f32[1,1,144,144]{3,2,1,0:T(8,128)}, u32[]{:S(2)}) copy-start(f32[1,1,144,144]{3,2,1,0:T(8,128)} %param.2) | copy-start | bytes 248836
  2.1 6.6 %copy-start.1 = (f32[3,12,144]{2,1,0:T(8,128)S(1)}, f32[3,12,144]{2,1,0:T(8,128)}, u32[]{:S(2)}) copy-start(f32[3,12,144]{2,1,0:T(8,128)} %start.5) | copy-start | bytes 62212
  4.0 6.9 %collective-permute-start.1 = (bf16[288,128]{1,0:T(8,128)(2,1)S(1)}, bf16[288,128]{1,0:T(8,128)(2,1)S(1)}, u32[]{:S(2)}, u32[]{:S(2)}) collective-permute-start(bf16[288,128]{1,0:T(8,128)(2,1)S(1)} %get-tuple-element.34.own), channel_id=1, source_target_pairs={{0,7},{1,4},{2,5},{3,6},{4,1},{5,2},{6,3},{7,0},{8,13},{9,14},{10,... | collective-permute-start | bytes 221192 | tf_op jit(solution)/shard_map/ppermute | solution.py:434
  11.7 1.6 %collective-permute-start.2 = (bf16[16,256]{1,0:T(8,128)(2,1)S(1)}, bf16[16,256]{1,0:T(8,128)(2,1)S(1)}, u32[]{:S(2)}, u32[]{:S(2)}) collective-permute-start(bf16[16,256]{1,0:T(8,128)(2,1)S(1)} %shard_map.44.left), channel_id=1, source_target_pairs={{0,4},{4,0},{8,12},{12,8},{16,20},{20,16},{24,28},{28,24},{1,5},{5... | collective-permute-start | bytes 24584 | tf_op jit(solution)/shard_map/ppermute | solution.py:417
  14.1 4.5 %collective-permute-start.3 = (bf16[288,128]{1,0:T(8,128)(2,1)S(1)}, bf16[288,128]{1,0:T(8,128)(2,1)S(1)}, u32[]{:S(2)}, u32[]{:S(2)}) collective-permute-start(bf16[288,128]{1,0:T(8,128)(2,1)S(1)} %get-tuple-element.36.own), channel_id=1, source_target_pairs={{0,12},{4,8},{8,4},{12,0},{16,28},{20,24},{24,20},{28,16},{1,13},{... | collective-permute-start | bytes 221192 | tf_op jit(solution)/shard_map/ppermute | solution.py:417
  19.6 5.9 %collective-permute-start.4 = (bf16[288,128]{1,0:T(8,128)(2,1)S(1)}, bf16[288,128]{1,0:T(8,128)(2,1)S(1)}, u32[]{:S(2)}, u32[]{:S(2)}) collective-permute-start(bf16[288,128]{1,0:T(8,128)(2,1)S(1)} %get-tuple-element.43.own), channel_id=1, source_target_pairs={{0,7},{1,4},{2,5},{3,6},{4,1},{5,2},{6,3},{7,0},{8,13},{9,14},{10,... | collective-permute-start | bytes 221192 | tf_op jit(solution)/shard_map/ppermute | solution.py:434
  26.4 1.6 %collective-permute-start.5 = (bf16[16,256]{1,0:T(8,128)(2,1)S(1)}, bf16[16,256]{1,0:T(8,128)(2,1)S(1)}, u32[]{:S(2)}, u32[]{:S(2)}) collective-permute-start(bf16[16,256]{1,0:T(8,128)(2,1)S(1)} %shard_map.50.left), channel_id=1, source_target_pairs={{0,4},{4,0},{8,12},{12,8},{16,20},{20,16},{24,28},{28,24},{1,5},{5... | collective-permute-start | bytes 24584 | tf_op jit(solution)/shard_map/ppermute | solution.py:417
  28.7 4.2 %collective-permute-start.6 = (bf16[288,128]{1,0:T(8,128)(2,1)S(1)}, bf16[288,128]{1,0:T(8,128)(2,1)S(1)}, u32[]{:S(2)}, u32[]{:S(2)}) collective-permute-start(bf16[288,128]{1,0:T(8,128)(2,1)S(1)} %get-tuple-element.46.own), channel_id=1, source_target_pairs={{0,20},{4,16},{8,28},{12,24},{16,4},{20,0},{24,12},{28,8},{1,21},{... | collective-permute-start | bytes 221192 | tf_op jit(solution)/shard_map/ppermute | solution.py:417
  33.9 6.0 %collective-permute-start.7 = (bf16[288,128]{1,0:T(8,128)(2,1)S(1)}, bf16[288,128]{1,0:T(8,128)(2,1)S(1)}, u32[]{:S(2)}, u32[]{:S(2)}) collective-permute-start(bf16[288,128]{1,0:T(8,128)(2,1)S(1)} %get-tuple-element.53.own), channel_id=1, source_target_pairs={{0,7},{1,4},{2,5},{3,6},{4,1},{5,2},{6,3},{7,0},{8,13},{9,14},{10,... | collective-permute-start | bytes 221192 | tf_op jit(solution)/shard_map/ppermute | solution.py:434
  40.8 1.6 %collective-permute-start.8 = (bf16[16,256]{1,0:T(8,128)(2,1)S(1)}, bf16[16,256]{1,0:T(8,128)(2,1)S(1)}, u32[]{:S(2)}, u32[]{:S(2)}) collective-permute-start(bf16[16,256]{1,0:T(8,128)(2,1)S(1)} %shard_map.56.left), channel_id=1, source_target_pairs={{0,4},{4,0},{8,12},{12,8},{16,20},{20,16},{24,28},{28,24},{1,5},{5... | collective-permute-start | bytes 24584 | tf_op jit(solution)/shard_map/ppermute | solution.py:417

commit v7 on v5

--- a/solution.py
+++ b/solution.py
@@ -17,6 +17,8 @@
 ROWS = CHI * PAD
 LANES = PAD * PAD
 VMEM_BYTES = 8 << 20
+SECOND = (CHI + 2) * 128
+FOLD = 64
 PIVOT = 1.0 / 64
 F32 = jnp.float32
 BF16 = jnp.bfloat16
@@ -65,41 +67,28 @@
     return one_hot((j == source) & (t < CHI))
 
 
-def block_swap(x):
+def swapped_tiles(x, fold):
     lane_group = group(iota((PAD, 128), 1))
     zero = jnp.zeros((PAD, 128), x.dtype)
-    tiles = {}
-    for p in range(PAD):
-        for t in range(2):
-            src, src_tile = (p & 7) | (t << 3), p >> 3
-            if src < CHI:
-                tiles[p, t] = x[src * PAD : (src + 1) * PAD, src_tile * 128 : (src_tile + 1) * 128]
-            else:
-                tiles[p, t] = None
-    for bit in range(3):
-        step = 1 << bit
-        low = lax.bitwise_and(lane_group, step) == 0
-        new = {}
-        for p in range(PAD):
-            if p & step:
-                continue
-            for t in range(2):
-                a, b = tiles[p, t], tiles[p | step, t]
-                if a is None and b is None:
-                    new[p, t] = new[p | step, t] = None
-                    continue
-                a_moved = zero if a is None else pltpu.roll(a, 128 - step * PAD, 1)
-                b_moved = zero if b is None else pltpu.roll(b, step * PAD, 1)
-                a = zero if a is None else a
-                b = zero if b is None else b
-                new[p, t] = jnp.where(low, a, b_moved)
-                new[p | step, t] = jnp.where(low, a_moved, b)
-        tiles = new
-    rows = []
-    for p in range(CHI):
-        pair = [zero if tiles[p, t] is None else tiles[p, t] for t in range(2)]
-        rows.append(jnp.concatenate(pair, axis=1))
-    return jnp.concatenate(rows, axis=0)
+    tiles = []
+    for s in range(CHI):
+        pair = []
+        for side in range(2):
+            lift = FOLD // PAD if fold and side and s >= CHI // 2 else 0
+            tile = zero
+            for p in range(side * 8, min(side * 8 + 8, CHI)):
+                at = (s >> 3) * 128
+                piece = x[p * PAD : (p + 1) * PAD, at : at + 128]
+                shift = (p + lift - s) % 8 * PAD
+                piece = pltpu.roll(piece, shift, 1) if shift else piece
+                tile = jnp.where(lane_group == (p & 7) + lift, piece, tile)
+            pair.append(tile)
+        tiles.append(pair)
+    return tiles
+
+
+def block_swap(x):
+    return jnp.concatenate([jnp.concatenate(pair, axis=1) for pair in swapped_tiles(x, False)], axis=0)
 
 
 def widen(x):
@@ -129,21 +118,29 @@
     return (y[2 * n :] + y[n : 2 * n]) + y[:n]
 
 
-def pack(x):
-    half = ROWS // 2
-    side, used = x[:, 128:], ROWS - 128
-    lane = iota((half, 128), 1)
-    folded = jnp.where(lane < used, side[:half], pltpu.roll(side[half:], used, 1))
-    return jnp.concatenate([x[:, :128], folded], axis=0)
-
-
-def unpack(x):
-    half, used = ROWS // 2, ROWS - 128
-    folded = x[ROWS:]
-    lane = iota((half, 128), 1)
-    zero = jnp.zeros((half, 128), x.dtype)
-    first = jnp.where(lane < used, folded, zero)
-    last = jnp.where(lane < used, pltpu.roll(folded, 128 - used, 1), zero)
+def folded(first, last):
+    return jnp.where(iota(first.shape, 1) < FOLD, first, last)
+
+
+def compact(x):
+    blocks = x.shape[0] // PAD
+    legs = x.astype(F32).reshape(blocks, PAD, 128)[:, :CHI]
+    return legs.reshape(blocks * CHI, 128).astype(BF16)
+
+
+def spaced(x):
+    blocks = x.shape[0] // CHI
+    legs = x.astype(F32).reshape(blocks, CHI, 128)
+    rest = jnp.zeros((blocks, PAD - CHI, 128), F32)
+    return jnp.concatenate([legs, rest], axis=1).reshape(blocks * PAD, 128).astype(BF16)
+
+
+def unfold(x):
+    side = x[ROWS:]
+    low = iota(side.shape, 1) < FOLD
+    zero = jnp.zeros_like(side)
+    first = jnp.where(low, side, zero)
+    last = jnp.where(low, pltpu.roll(side, 128 - FOLD, 1), zero)
     return jnp.concatenate([x[:ROWS], jnp.concatenate([first, last], axis=0)], axis=1)
 
 
@@ -161,7 +158,10 @@
 
 def outer_part(first, second):
     outer = mm(first, row_swap(second), NT).astype(BF16)
-    return block_swap(widen(outer))
+    tiles = swapped_tiles(widen(outer), True)
+    half = CHI // 2
+    side = folded(*(jnp.concatenate([t[1] for t in part], axis=0) for part in (tiles[:half], tiles[half:])))
+    return compact(jnp.concatenate([t[0] for t in tiles] + [side], axis=0))
 
 
 def turn(first):
@@ -210,30 +210,49 @@
     return basis
 
 
-def iso_kernel(own, other, starts, iso_o):
-    own, other = unpack(own[...]), unpack(other[...])
-    start, start_turned = starts[:PAD], starts[PAD:]
+def iso_kernel(own, other, starts, pieces, iso_o):
     swap = swap_matrix()
-    total = own.astype(F32) + other.astype(F32)
+    grams = [spaced(own[...]), spaced(other[...])]
+    doubled = [
+        jnp.concatenate([g[:ROWS], jnp.concatenate([g[ROWS:]] * 2, axis=0)], axis=1) for g in grams
+    ]
+    total = doubled[0].astype(F32) + doubled[1].astype(F32)
     i, j = iota((ROWS, LANES), 0), iota((ROWS, LANES), 1)
-    diagonal = (group(i) == minor(j)) & (minor(i) == group(j))
+    place = jnp.where(j < 128, j, 128 + lax.bitwise_and(j, FOLD - 1))
+    valid = (j < 128) | ((lax.bitwise_and(j, 127) < FOLD) == (i < ROWS // 2))
+    diagonal = valid & (group(i) == minor(place)) & (minor(i) == group(place))
     trace = jnp.sum(jnp.where(diagonal, total, 0.0), axis=0, keepdims=True)
     shift = jnp.sum(trace, axis=1, keepdims=True) / (CHI * CHI)
     unit = 1.0 / shift
-    pieces = parts2(start)
-    image = fold2(mm(pieces, own, NT) + mm(pieces, other, NT))
-    image = widen(image) * unit + start_turned
-    pieces = parts2(image)
-    image = fold2(mm(pieces[:, :ROWS], own) + mm(pieces[:, :ROWS], other)) * unit
-    basis, good = orthonormal(image + fold2(mm(pieces, swap)))
+    image = mm(pieces[...], doubled[0], NT) + mm(pieces[...], doubled[1], NT)
+    lane = iota((2 * PAD, ROWS), 1)
+    image = jnp.where(lane < ROWS // 2, image[: 2 * PAD], image[2 * PAD :])
+    image = widen(fold2(image)) * unit + starts[PAD:]
+    parts = parts2(image)
+    own, other = unfold(grams[0]), unfold(grams[1])
+    image = fold2(mm(parts[:, :ROWS], own) + mm(parts[:, :ROWS], other)) * unit
+    basis, good = orthonormal(image + fold2(mm(parts, swap)))
     iso_o[...] = basis.astype(BF16)
 
     @pl.when(jnp.logical_not(jnp.min(good[:1]) > 0.5))
     def _():
-        iso_o[...] = exact_iso(own, other, start, start_turned, shift, swap).astype(BF16)
-
-
-def first_second(turned, lower, left, second_ref):
+        basis = exact_iso(own, other, starts[:PAD], starts[PAD:], shift, swap)
+        iso_o[...] = basis.astype(BF16)
+
+
+def packed_pair(index):
+    entry = jnp.where(index < 128, index, 128 + minor(index))
+    s = lax.shift_right_logical(entry * 171, 11)
+    return s, entry - s * CHI
+
+
+def packing():
+    s, t = packed_pair(iota((LANES, ROWS), 0))
+    j = iota((LANES, ROWS), 1)
+    return one_hot((group(j) == s) & (minor(j) == t))
+
+
+def first_second(turned, lower, left, second_ref, first_ref):
     lane = iota((PAD, LANES), 1)
     masked = [jnp.where(group(lane) == k, left.astype(F32), 0.0) for k in range(CHI)]
     masked = jnp.concatenate(masked, axis=0).astype(BF16)
@@ -246,24 +265,38 @@
             line = jnp.broadcast_to(values[k * PAD + a : k * PAD + a + 1, :], (PAD, LANES))
             blocks.append(jnp.where(eye, line, 0.0).astype(BF16))
         kron = jnp.concatenate(blocks, axis=0)
-        first = mm(turned[:, :ROWS], kron).astype(BF16)
-        second = mm(first[:, :ROWS], lower).astype(BF16)
+        first = mm(turned[:, :ROWS], kron)
+        first_ref[a * ROWS : (a + 1) * ROWS, :] = first.astype(BF16)
+    second = mm(first_ref[:, :ROWS], lower).astype(BF16)
+    lane_group = group(iota((PAD, 128), 1))
+    for a in range(CHI):
+        rows = slice(a * PAD, (a + 1) * PAD)
+        tails = [jnp.zeros((PAD, 128), BF16)] * 2
         for k in range(CHI):
-            second_ref[a * PAD : (a + 1) * PAD, k * LANES : (k + 1) * LANES] = second[
-                k * PAD : (k + 1) * PAD, :
-            ]
+            block = second[a * ROWS + k * PAD : a * ROWS + (k + 1) * PAD]
+            second_ref[rows, k * 128 : (k + 1) * 128] = block[:, :128]
+            tails[k >> 3] = jnp.where(lane_group == (k & 7), block[:, 128:], tails[k >> 3])
+        for side in range(2):
+            at = (CHI + side) * 128
+            second_ref[rows, at : at + 128] = tails[side]
 
 
 def third(second_ref, right, kron_ref):
     tile = one_hot(minor(iota((PAD, LANES), 1)) == iota((PAD, LANES), 0))
     values = mm(right, tile, TN)
-    lane_group = group(iota((PAD, LANES), 1))
+    lane_group = group(iota((CHI * CHI, LANES), 1))
+    lane_group = jnp.where(lane_group < CHI, lane_group, lane_group - FOLD // PAD)
+    entry = iota((CHI * CHI, LANES), 0)
+    kept = lax.shift_right_logical(entry * 171, 11) == lane_group
     for k in range(CHI):
-        block = values[k * PAD : (k + 1) * PAD, :]
-        for d in range(PAD):
-            kept = jnp.where(lane_group == d, block, 0.0) if d < CHI else jnp.zeros_like(block)
-            start = k * LANES + d * PAD
-            kron_ref[start : start + PAD, :] = kept.astype(BF16)
+        block = values[k * PAD : k * PAD + CHI, :]
+        tall = jnp.concatenate([block] * CHI, axis=0)
+        tall = jnp.where(kept, tall, 0.0).astype(BF16)
+        kron_ref[k * 128 : (k + 1) * 128, :] = tall[:128]
+        at = CHI * 128 + k * PAD
+        kron_ref[at : at + PAD, :] = tall[128:]
+    used = CHI * 128 + CHI * PAD
+    kron_ref[used:, :] = jnp.zeros((SECOND - used, LANES), BF16)
     return mm(second_ref[...], kron_ref[...])
 
 
@@ -294,44 +327,53 @@
     theirs = placed(other[...].astype(BF16), mirror, jnp.logical_not(own_lower))
     first_o[...], second_o[...] = pick(own_first, mine, theirs)
     products = pick(own_first, product_part(mine), product_part(theirs))
-    gram_o[...] = pack(outer_part(*products))
+    gram_o[...] = outer_part(*products)
 
 
 def own_kernel(own, wide_o, product_o):
-    wide = unpack(own[...])
+    wide = unfold(spaced(own[...]))
     wide_o[...] = wide
     product_o[...] = product_part(wide)
 
 
 def gram_kernel(level, wide, product, other, first_o, second_o, gram_o):
     own_first = roles(level)[0]
-    theirs = unpack(other[...])
+    theirs = unfold(spaced(other[...]))
     products = pick(own_first, product[...], product_part(theirs))
-    gram_o[...] = pack(outer_part(*products))
+    gram_o[...] = outer_part(*products)
     first_o[...], second_o[...] = pick(own_first, wide[...], theirs)
 
 
-def turn_kernel(level, first, start, turned_o, starts_o):
+def turn_kernel(level, first, second, start, turned_o, lower_o, starts_o, pieces_o):
     turned_o[...] = turn(first[...])
+    lower_o[...] = mm(second[:, :ROWS], packing(), NT).astype(BF16)
     plain, turned = start_body(start[level], swap_matrix())
     first_upper = roles(level)[1]
-    starts_o[:PAD] = jnp.where(first_upper, plain, turned)
+    here = jnp.where(first_upper, plain, turned)
+    starts_o[:PAD] = here
     starts_o[PAD:] = jnp.where(first_upper, turned, plain)
-
-
-def second_kernel(turned, lower, left, second_o):
-    first_second(turned[...], lower[...], left[...], second_o)
+    pieces = parts2(here)
+    pieces_o[: 2 * PAD] = pieces
+    lifted = pltpu.roll(pieces[:, 128:], FOLD, 1)
+    pieces_o[2 * PAD :] = jnp.concatenate([pieces[:, :128], lifted], axis=1)
+
+
+def second_kernel(turned, lower, left, second_o, first):
+    first_second(turned[...], lower[...], left[...], second_o, first)
 
 
 def mean_square(merged):
-    total = jnp.sum(jnp.sum(merged * merged, axis=0, keepdims=True), axis=1, keepdims=True)
+    lines = jnp.sum(merged * merged, axis=0, keepdims=True)
+    total = jnp.sum(lines[:, :128] + 0.5 * lines[:, 128:], axis=1, keepdims=True)
     return total / (CHI**4) + 1e-06
 
 
 def third_kernel(second, right, log_in, next_o, log_o, kron):
     merged = third(second, right[...], kron)
     mean = mean_square(merged)
-    next_o[...] = pack((merged * lax.rsqrt(mean)).astype(BF16))
+    half = ROWS // 2
+    side = folded(merged[:half, 128:], merged[half:, 128:])
+    next_o[...] = compact(jnp.concatenate([merged[:, :128], side], axis=0) * lax.rsqrt(mean))
     log_o[...] = log_in[...] + 0.5 * jnp.log(mean)
 
 
@@ -385,8 +427,8 @@
 
 def per_device(site_tensors, start_basis):
     square = CHI * CHI
-    mat, packed, logs = ((ROWS, LANES), BF16), ((ROWS * 3 // 2, 128), BF16), ((8, 128), F32)
-    kron = [pltpu.VMEM((CHI * LANES, LANES), BF16)]
+    mat, packed, logs = ((ROWS, LANES), BF16), ((CHI * CHI * 3 // 2, 128), BF16), ((8, 128), F32)
+    kron, firsts = [pltpu.VMEM((SECOND, LANES), BF16)], [pltpu.VMEM((CHI * ROWS, LANES), BF16)]
     log_total = jnp.zeros(*logs)
     own = site_tensors[0, 0]
     for level in range(LEVELS):
@@ -401,12 +443,13 @@
                 functools.partial(gram_kernel, level), [mat, mat, packed]
             )(wide, product, other)
         gram_other = from_bond(gram)
-        turned, starts = call(
-            functools.partial(turn_kernel, level), [mat, ((2 * PAD, LANES), F32)]
-        )(first, start_basis)
-        (left,) = call(iso_kernel, [((PAD, LANES), BF16)])(gram, gram_other, starts)
+        turned, lower, starts, pieces = call(
+            functools.partial(turn_kernel, level),
+            [mat, mat, ((2 * PAD, LANES), F32), ((4 * PAD, LANES), BF16)],
+        )(first, lower, start_basis)
+        (left,) = call(iso_kernel, [((PAD, LANES), BF16)])(gram, gram_other, starts, pieces)
         right = from_partner(left, 1)
-        (second,) = call(second_kernel, [((ROWS, CHI * LANES), BF16)])(turned, lower, left)
+        (second,) = call(second_kernel, [((ROWS, SECOND), BF16)], firsts)(turned, lower, left)
         if level < LEVELS - 1:
             own, log_total = call(third_kernel, [packed, logs], kron)(second, right, log_total)
         else:

time: 43.5 us -> 40.2 us (0.924)
  waiting for transfers between devices: 10.3 us -> 8.57 us
  Pallas kernels: 14.7 us -> 13.3 us
  local copies, waits for them, and re-layouts: 1.72 us -> 0.92 us
  starting transfers between devices: 15.9 us -> 16.5 us
    pallas_call x18, Pallas kernels: 14.7 us -> 13.3 us  [run(): pl.pallas_call(kernel, out_shape=[jax.ShapeDtypeStruct(s, d) for s, d in...]
    ppermute x3, waiting for transfers between devices: 5.85 us -> 4.79 us  [from_bond(): return lax.ppermute(array, ('row', 'col'), pairs)]
    unnamed x6 -> x4, local copies, waits for them, and re-layouts: 1.71 us -> 0.92 us
    ppermute x6, waiting for transfers between devices: 4.42 us -> 3.79 us  [from_partner(): return lax.ppermute(array, 'row', [(i, i ^ flip) for i in range(count)])]
    ppermute x3, starting transfers between devices: 11.5 us -> 11.9 us  [from_bond(): return lax.ppermute(array, ('row', 'col'), pairs)]
  transfers between devices with their start and end apart: 9 -> 9, of which waited for: 9 -> 9; matrix products, arithmetic and copies ran while one was open for 0% -> 0% of each run, Pallas kernels for 11% -> 12%
where the time goes in v7:
time: 40.2 us; the launch traced here: 40.1 us
  starting transfers between devices  16.5 us (41%)
  Pallas kernels  13.3 us (33%)
  waiting for transfers between devices  8.57 us (21%)
  local copies, waits for them, and re-layouts  0.92 us (2%)
  between operations  0.79 us (2%)
    pallas_call x18, Pallas kernels, run(): pl.pallas_call(kernel, out_shape=[jax.ShapeDtypeStruct(s, d) for s, d in...  13.3 us
    ppermute x3, starting transfers between devices, from_bond(): return lax.ppermute(array, ('row', 'col'), pairs)  11.9 us
    ppermute x3, waiting for transfers between devices, from_bond(): return lax.ppermute(array, ('row', 'col'), pairs)  4.79 us
    ppermute x6, starting transfers between devices, from_partner(): return lax.ppermute(array, 'row', [(i, i ^ flip) for i in range(count)])  4.59 us
    ppermute x6, waiting for transfers between devices, from_partner(): return lax.ppermute(array, 'row', [(i, i ^ flip) for i in range(count)])  3.79 us
    unnamed x4, local copies, waits for them, and re-layouts  0.92 us
  transfers between devices with their start and end apart: 9, of which 9 were waited for; matrix products, arithmetic and copies ran while one was open for 0% of the time, Pallas kernels for 12%

profile of v7, /device:TPU:0, one launch (start us, length us, event | category | flops | bytes accessed | tf_op | source)
XLA Modules:
  0.0 40.1 jit_solution(2257727313450194268)
XLA Ops:
  0.6 0.6 %collective-permute-start = (f32[144,144]{1,0:T(8,128)}, f32[144,144]{1,0:T(8,128)S(1)}, u32[]{:S(2)}, u32[]{:S(2)}) collective-permute-start(f32[144,144]{1,0:T(8,128)} %bitcast.2), channel_id=1, source_target_pairs={{0,4},{4,0},{8,12},{12,8},{16,20},{20,16},{24,28},{28,24},{1,5},{5... | collective-permute-start | bytes 248840 | tf_op jit(solution)/shard_map/ppermute | solution.py:408
  1.2 0.0 copy-start
  1.2 0.9 %copy-done = f32[1,1,144,144]{3,2,1,0:T(8,128)S(1)} copy-done((f32[1,1,144,144]{3,2,1,0:T(8,128)S(1)}, f32[1,1,144,144]{3,2,1,0:T(8,128)}, u32[]{:S(2)}) %copy-start) | copy-done | bytes 82968
  2.1 0.0 copy-start.1
  2.1 0.3 collective-permute-done.other
  2.4 1.3 %shard_map.42 = (bf16[192,256]{1,0:T(8,128)(2,1)S(1)}, bf16[192,256]{1,0:T(8,128)(2,1)S(1)}, bf16[216,128]{1,0:T(8,128)(2,1)S(1)}) custom-call(bf16[144,144]{1,0:T(8,128)(2,1)S(1)} %shard_map.41.own, f32[144,144]{1,0:T(8,128)S(1)} %collective-permute-done.other), custom_call_target="tpu_custom_call" | custom-call | flops 100000000 | bytes 1000000 | tf_op jit(solution)/shard_map/pallas_call | solution.py:393
  3.7 4.8 %collective-permute-start.1 = (bf16[216,128]{1,0:T(8,128)(2,1)S(1)}, bf16[216,128]{1,0:T(8,128)(2,1)S(1)}, u32[]{:S(2)}, u32[]{:S(2)}) collective-permute-start(bf16[216,128]{1,0:T(8,128)(2,1)S(1)} %get-tuple-element.37.own), channel_id=1, source_target_pairs={{0,7},{1,4},{2,5},{3,6},{4,1},{5,2},{6,3},{7,0},{8,13},{9,14},{10,... | collective-permute-start | bytes 165896 | tf_op jit(solution)/shard_map/ppermute | solution.py:425
  8.5 0.0 copy-done.1
  8.5 0.4 shard_map.43
  8.9 1.6 %collective-permute-done.1.other = bf16[216,128]{1,0:T(8,128)(2,1)S(1)} collective-permute-done((bf16[216,128]{1,0:T(8,128)(2,1)S(1)}, bf16[216,128]{1,0:T(8,128)(2,1)S(1)}, u32[]{:S(2)}, u32[]{:S(2)}) %collective-permute-start.1) | collective-permute-done | bytes 55328 | tf_op jit(solution)/shard_map/ppermute | solution.py:425
  10.4 0.8 %shard_map.44.left = bf16[16,256]{1,0:T(8,128)(2,1)S(1)} custom-call(bf16[216,128]{1,0:T(8,128)(2,1)S(1)} %get-tuple-element.37.own, bf16[216,128]{1,0:T(8,128)(2,1)S(1)} %collective-permute-done.1.other, f32[32,256]{1,0:T(8,128)S(1)} %get-tuple-element.38.starts, bf16[64,256]{1,0:T(8,128)(2,1)S(1)} %get-tuple-element.39.pieces), custom_call_target="tpu_custom_call" | custom-call | flops 100000000 | bytes 1000000 | tf_op jit(solution)/shard_map/pallas_call | solution.py:393
  11.3 0.1 collective-permute-start.2
  11.4 1.0 %shard_map.45.second = bf16[192,1792]{1,0:T(8,128)(2,1)S(1)} custom-call(bf16[192,256]{1,0:T(8,128)(2,1)S(1)} %get-tuple-element.35.turned, bf16[192,256]{1,0:T(8,128)(2,1)S(1)} %get-tuple-element.36.lower, bf16[16,256]{1,0:T(8,128)(2,1)S(1)} %shard_map.44.left), custom_call_target="tpu_custom_call" | custom-call | flops 100000000 | bytes 1000000 | tf_op jit(solution)/shard_map/pallas_call | solution.py:393
  12.4 0.2 collective-permute-done.2.right
  12.5 0.7 %shard_map.46 = (bf16[216,128]{1,0:T(8,128)(2,1)S(1)}, f32[8,128]{1,0:T(8,128)S(1)}) custom-call(bf16[192,1792]{1,0:T(8,128)(2,1)S(1)} %shard_map.45.second, bf16[16,256]{1,0:T(8,128)(2,1)S(1)} %collective-permute-done.2.right, f32[8,128]{1,0:T(8,128)S(1)} %broadcast_in_dim.6.log_in), custom_call_target="tpu_custom_call" | custom-call | flops 100000000 | bytes 1000000 | tf_op jit(solution)/shard_map/pallas_call | solution.py:393
  13.2 1.9 %collective-permute-start.3 = (bf16[216,128]{1,0:T(8,128)(2,1)S(1)}, bf16[216,128]{1,0:T(8,128)(2,1)S(1)}, u32[]{:S(2)}, u32[]{:S(2)}) collective-permute-start(bf16[216,128]{1,0:T(8,128)(2,1)S(1)} %get-tuple-element.40.own), channel_id=1, source_target_pairs={{0,12},{4,8},{8,4},{12,0},{16,28},{20,24},{24,20},{28,16},{1,13},{... | collective-permute-start | bytes 165896 | tf_op jit(solution)/shard_map/ppermute | solution.py:408
  15.1 0.4 %shard_map.47 = (bf16[192,256]{1,0:T(8,128)(2,1)S(1)}, bf16[192,256]{1,0:T(8,128)(2,1)S(1)}) custom-call(bf16[216,128]{1,0:T(8,128)(2,1)S(1)} %get-tuple-element.40.own), custom_call_target="tpu_custom_call" | custom-call | flops 100000000 | bytes 1000000 | tf_op jit(solution)/shard_map/pallas_call | solution.py:393
  15.5 1.5 %collective-permute-done.3.other = bf16[216,128]{1,0:T(8,128)(2,1)S(1)} collective-permute-done((bf16[216,128]{1,0:T(8,128)(2,1)S(1)}, bf16[216,128]{1,0:T(8,128)(2,1)S(1)}, u32[]{:S(2)}, u32[]{:S(2)}) %collective-permute-start.3) | collective-permute-done | bytes 55328 | tf_op jit(solution)/shard_map/ppermute | solution.py:408
  17.0 0.8 %shard_map.48 = (bf16[192,256]{1,0:T(8,128)(2,1)S(1)}, bf16[192,256]{1,0:T(8,128)(2,1)S(1)}, bf16[216,128]{1,0:T(8,128)(2,1)S(1)}) custom-call(bf16[192,256]{1,0:T(8,128)(2,1)S(1)} %get-tuple-element.41.wide, bf16[192,256]{1,0:T(8,128)(2,1)S(1)} %get-tuple-element.42.product, bf16[216,128]{1,0:T(8,128)(2,1)S(1)} %collective-permute-done.3.other), custom_call_target="tpu_custom_call" | custom-call | flops 100000000 | bytes 1000000 | tf_op jit(solution)/shard_map/pallas_call | solution.py:393
  17.8 3.6 %collective-permute-start.4 = (bf16[216,128]{1,0:T(8,128)(2,1)S(1)}, bf16[216,128]{1,0:T(8,128)(2,1)S(1)}, u32[]{:S(2)}, u32[]{:S(2)}) collective-permute-start(bf16[216,128]{1,0:T(8,128)(2,1)S(1)} %get-tuple-element.47.own), channel_id=1, source_target_pairs={{0,7},{1,4},{2,5},{3,6},{4,1},{5,2},{6,3},{7,0},{8,13},{9,14},{10,... | collective-permute-start | bytes 165896 | tf_op jit(solution)/shard_map/ppermute | solution.py:425
  21.4 0.4 shard_map.49
  21.8 1.5 %collective-permute-done.4.other = bf16[216,128]{1,0:T(8,128)(2,1)S(1)} collective-permute-done((bf16[216,128]{1,0:T(8,128)(2,1)S(1)}, bf16[216,128]{1,0:T(8,128)(2,1)S(1)}, u32[]{:S(2)}, u32[]{:S(2)}) %collective-permute-start.4) | collective-permute-done | bytes 55328 | tf_op jit(solution)/shard_map/ppermute | solution.py:425
  23.3 0.8 %shard_map.50.left = bf16[16,256]{1,0:T(8,128)(2,1)S(1)} custom-call(bf16[216,128]{1,0:T(8,128)(2,1)S(1)} %get-tuple-element.47.own, bf16[216,128]{1,0:T(8,128)(2,1)S(1)} %collective-permute-done.4.other, f32[32,256]{1,0:T(8,128)S(1)} %get-tuple-element.48.starts, bf16[64,256]{1,0:T(8,128)(2,1)S(1)} %get-tuple-element.49.pieces), custom_call_target="tpu_custom_call" | custom-call | flops 100000000 | bytes 1000000 | tf_op jit(solution)/shard_map/pallas_call | solution.py:393
  24.2 0.1 collective-permute-start.5
  24.3 1.0 %shard_map.51.second = bf16[192,1792]{1,0:T(8,128)(2,1)S(1)} custom-call(bf16[192,256]{1,0:T(8,128)(2,1)S(1)} %get-tuple-element.45.turned, bf16[192,256]{1,0:T(8,128)(2,1)S(1)} %get-tuple-element.46.lower, bf16[16,256]{1,0:T(8,128)(2,1)S(1)} %shard_map.50.left), custom_call_target="tpu_custom_call" | custom-call | flops 100000000 | bytes 1000000 | tf_op jit(solution)/shard_map/pallas_call | solution.py:393
  25.3 0.2 collective-permute-done.5.right
  25.4 0.7 %shard_map.52 = (bf16[216,128]{1,0:T(8,128)(2,1)S(1)}, f32[8,128]{1,0:T(8,128)S(1)}) custom-call(bf16[192,1792]{1,0:T(8,128)(2,1)S(1)} %shard_map.51.second, bf16[16,256]{1,0:T(8,128)(2,1)S(1)} %collective-permute-done.5.right, f32[8,128]{1,0:T(8,128)S(1)} %get-tuple-element.50.log_in), custom_call_target="tpu_custom_call" | custom-call | flops 100000000 | bytes 1000000 | tf_op jit(solution)/shard_map/pallas_call | solution.py:393
  26.1 1.9 %collective-permute-start.6 = (bf16[216,128]{1,0:T(8,128)(2,1)S(1)}, bf16[216,128]{1,0:T(8,128)(2,1)S(1)}, u32[]{:S(2)}, u32[]{:S(2)}) collective-permute-start(bf16[216,128]{1,0:T(8,128)(2,1)S(1)} %get-tuple-element.51.own), channel_id=1, source_target_pairs={{0,20},{4,16},{8,28},{12,24},{16,4},{20,0},{24,12},{28,8},{1,21},{... | collective-permute-start | bytes 165896 | tf_op jit(solution)/shard_map/ppermute | solution.py:408
  28.0 0.4 %shard_map.53 = (bf16[192,256]{1,0:T(8,128)(2,1)S(1)}, bf16[192,256]{1,0:T(8,128)(2,1)S(1)}) custom-call(bf16[216,128]{1,0:T(8,128)(2,1)S(1)} %get-tuple-element.51.own), custom_call_target="tpu_custom_call" | custom-call | flops 100000000 | bytes 1000000 | tf_op jit(solution)/shard_map/pallas_call | solution.py:393
  28.4 1.5 %collective-permute-done.6.other = bf16[216,128]{1,0:T(8,128)(2,1)S(1)} collective-permute-done((bf16[216,128]{1,0:T(8,128)(2,1)S(1)}, bf16[216,128]{1,0:T(8,128)(2,1)S(1)}, u32[]{:S(2)}, u32[]{:S(2)}) %collective-permute-start.6) | collective-permute-done | bytes 55328 | tf_op jit(solution)/shard_map/ppermute | solution.py:408
  29.9 0.8 %shard_map.54 = (bf16[192,256]{1,0:T(8,128)(2,1)S(1)}, bf16[192,256]{1,0:T(8,128)(2,1)S(1)}, bf16[216,128]{1,0:T(8,128)(2,1)S(1)}) custom-call(bf16[192,256]{1,0:T(8,128)(2,1)S(1)} %get-tuple-element.52.wide, bf16[192,256]{1,0:T(8,128)(2,1)S(1)} %get-tuple-element.53.product, bf16[216,128]{1,0:T(8,128)(2,1)S(1)} %collective-permute-done.6.other), custom_call_target="tpu_custom_call" | custom-call | flops 100000000 | bytes 1000000 | tf_op jit(solution)/shard_map/pallas_call | solution.py:393
  30.7 3.6 %collective-permute-start.7 = (bf16[216,128]{1,0:T(8,128)(2,1)S(1)}, bf16[216,128]{1,0:T(8,128)(2,1)S(1)}, u32[]{:S(2)}, u32[]{:S(2)}) collective-permute-start(bf16[216,128]{1,0:T(8,128)(2,1)S(1)} %get-tuple-element.58.own), channel_id=1, source_target_pairs={{0,7},{1,4},{2,5},{3,6},{4,1},{5,2},{6,3},{7,0},{8,13},{9,14},{10,... | collective-permute-start | bytes 165896 | tf_op jit(solution)/shard_map/ppermute | solution.py:425
  34.3 0.3 shard_map.55
  34.6 1.7 %collective-permute-done.7.other = bf16[216,128]{1,0:T(8,128)(2,1)S(1)} collective-permute-done((bf16[216,128]{1,0:T(8,128)(2,1)S(1)}, bf16[216,128]{1,0:T(8,128)(2,1)S(1)}, u32[]{:S(2)}, u32[]{:S(2)}) %collective-permute-start.7) | collective-permute-done | bytes 55328 | tf_op jit(solution)/shard_map/ppermute | solution.py:425
  36.3 0.8 %shard_map.56.left = bf16[16,256]{1,0:T(8,128)(2,1)S(1)} custom-call(bf16[216,128]{1,0:T(8,128)(2,1)S(1)} %get-tuple-element.58.own, bf16[216,128]{1,0:T(8,128)(2,1)S(1)} %collective-permute-done.7.other, f32[32,256]{1,0:T(8,128)S(1)} %get-tuple-element.59.starts, bf16[64,256]{1,0:T(8,128)(2,1)S(1)} %get-tuple-element.60.pieces), custom_call_target="tpu_custom_call" | custom-call | flops 100000000 | bytes 1000000 | tf_op jit(solution)/shard_map/pallas_call | solution.py:393
  37.1 0.1 collective-permute-start.8
  37.2 1.0 %shard_map.57.second = bf16[192,1792]{1,0:T(8,128)(2,1)S(1)} custom-call(bf16[192,256]{1,0:T(8,128)(2,1)S(1)} %get-tuple-element.56.turned, bf16[192,256]{1,0:T(8,128)(2,1)S(1)} %get-tuple-element.57.lower, bf16[16,256]{1,0:T(8,128)(2,1)S(1)} %shard_map.56.left), custom_call_target="tpu_custom_call" | custom-call | flops 100000000 | bytes 1000000 | tf_op jit(solution)/shard_map/pallas_call | solution.py:393
  38.2 0.2 collective-permute-done.8.right
  38.4 1.7 %shard_map.58 = (f32[144,144]{1,0:T(8,128)}, f32[1,1]{1,0:T(1,128)}) custom-call(bf16[192,1792]{1,0:T(8,128)(2,1)S(1)} %shard_map.57.second, bf16[16,256]{1,0:T(8,128)(2,1)S(1)} %collective-permute-done.8.right, f32[8,128]{1,0:T(8,128)S(1)} %get-tuple-element.61.log_in), custom_call_target="tpu_custom_call" | custom-call | flops 100000000 | bytes 1000000 | tf_op jit(solution)/shard_map/pallas_call | solution.py:393
  (2 shorter events, 0.0 us)
Async XLA Ops:
  0.6 1.8 %collective-permute-start = (f32[144,144]{1,0:T(8,128)}, f32[144,144]{1,0:T(8,128)S(1)}, u32[]{:S(2)}, u32[]{:S(2)}) collective-permute-start(f32[144,144]{1,0:T(8,128)} %bitcast.2), channel_id=1, source_target_pairs={{0,4},{4,0},{8,12},{12,8},{16,20},{20,16},{24,28},{28,24},{1,5},{5... | collective-permute-start | bytes 248840 | tf_op jit(solution)/shard_map/ppermute | solution.py:408
  1.2 0.9 %copy-start = (f32[1,1,144,144]{3,2,1,0:T(8,128)S(1)}, f32[1,1,144,144]{3,2,1,0:T(8,128)}, u32[]{:S(2)}) copy-start(f32[1,1,144,144]{3,2,1,0:T(8,128)} %param.2) | copy-start | bytes 248836
  2.1 6.4 %copy-start.1 = (f32[3,12,144]{2,1,0:T(8,128)S(1)}, f32[3,12,144]{2,1,0:T(8,128)}, u32[]{:S(2)}) copy-start(f32[3,12,144]{2,1,0:T(8,128)} %start.5) | copy-start | bytes 62212
  3.7 6.7 %collective-permute-start.1 = (bf16[216,128]{1,0:T(8,128)(2,1)S(1)}, bf16[216,128]{1,0:T(8,128)(2,1)S(1)}, u32[]{:S(2)}, u32[]{:S(2)}) collective-permute-start(bf16[216,128]{1,0:T(8,128)(2,1)S(1)} %get-tuple-element.37.own), channel_id=1, source_target_pairs={{0,7},{1,4},{2,5},{3,6},{4,1},{5,2},{6,3},{7,0},{8,13},{9,14},{10,... | collective-permute-start | bytes 165896 | tf_op jit(solution)/shard_map/ppermute | solution.py:425
  11.3 1.2 %collective-permute-start.2 = (bf16[16,256]{1,0:T(8,128)(2,1)S(1)}, bf16[16,256]{1,0:T(8,128)(2,1)S(1)}, u32[]{:S(2)}, u32[]{:S(2)}) collective-permute-start(bf16[16,256]{1,0:T(8,128)(2,1)S(1)} %shard_map.44.left), channel_id=1, source_target_pairs={{0,4},{4,0},{8,12},{12,8},{16,20},{20,16},{24,28},{28,24},{1,5},{5... | collective-permute-start | bytes 24584 | tf_op jit(solution)/shard_map/ppermute | solution.py:408
  13.2 3.8 %collective-permute-start.3 = (bf16[216,128]{1,0:T(8,128)(2,1)S(1)}, bf16[216,128]{1,0:T(8,128)(2,1)S(1)}, u32[]{:S(2)}, u32[]{:S(2)}) collective-permute-start(bf16[216,128]{1,0:T(8,128)(2,1)S(1)} %get-tuple-element.40.own), channel_id=1, source_target_pairs={{0,12},{4,8},{8,4},{12,0},{16,28},{20,24},{24,20},{28,16},{1,13},{... | collective-permute-start | bytes 165896 | tf_op jit(solution)/shard_map/ppermute | solution.py:408
  17.8 5.5 %collective-permute-start.4 = (bf16[216,128]{1,0:T(8,128)(2,1)S(1)}, bf16[216,128]{1,0:T(8,128)(2,1)S(1)}, u32[]{:S(2)}, u32[]{:S(2)}) collective-permute-start(bf16[216,128]{1,0:T(8,128)(2,1)S(1)} %get-tuple-element.47.own), channel_id=1, source_target_pairs={{0,7},{1,4},{2,5},{3,6},{4,1},{5,2},{6,3},{7,0},{8,13},{9,14},{10,... | collective-permute-start | bytes 165896 | tf_op jit(solution)/shard_map/ppermute | solution.py:425
  24.2 1.2 %collective-permute-start.5 = (bf16[16,256]{1,0:T(8,128)(2,1)S(1)}, bf16[16,256]{1,0:T(8,128)(2,1)S(1)}, u32[]{:S(2)}, u32[]{:S(2)}) collective-permute-start(bf16[16,256]{1,0:T(8,128)(2,1)S(1)} %shard_map.50.left), channel_id=1, source_target_pairs={{0,4},{4,0},{8,12},{12,8},{16,20},{20,16},{24,28},{28,24},{1,5},{5... | collective-permute-start | bytes 24584 | tf_op jit(solution)/shard_map/ppermute | solution.py:408
  26.1 3.8 %collective-permute-start.6 = (bf16[216,128]{1,0:T(8,128)(2,1)S(1)}, bf16[216,128]{1,0:T(8,128)(2,1)S(1)}, u32[]{:S(2)}, u32[]{:S(2)}) collective-permute-start(bf16[216,128]{1,0:T(8,128)(2,1)S(1)} %get-tuple-element.51.own), channel_id=1, source_target_pairs={{0,20},{4,16},{8,28},{12,24},{16,4},{20,0},{24,12},{28,8},{1,21},{... | collective-permute-start | bytes 165896 | tf_op jit(solution)/shard_map/ppermute | solution.py:408
  30.7 5.6 %collective-permute-start.7 = (bf16[216,128]{1,0:T(8,128)(2,1)S(1)}, bf16[216,128]{1,0:T(8,128)(2,1)S(1)}, u32[]{:S(2)}, u32[]{:S(2)}) collective-permute-start(bf16[216,128]{1,0:T(8,128)(2,1)S(1)} %get-tuple-element.58.own), channel_id=1, source_target_pairs={{0,7},{1,4},{2,5},{3,6},{4,1},{5,2},{6,3},{7,0},{8,13},{9,14},{10,... | collective-permute-start | bytes 165896 | tf_op jit(solution)/shard_map/ppermute | solution.py:425
  37.1 1.2 %collective-permute-start.8 = (bf16[16,256]{1,0:T(8,128)(2,1)S(1)}, bf16[16,256]{1,0:T(8,128)(2,1)S(1)}, u32[]{:S(2)}, u32[]{:S(2)}) collective-permute-start(bf16[16,256]{1,0:T(8,128)(2,1)S(1)} %shard_map.56.left), channel_id=1, source_target_pairs={{0,4},{4,0},{8,12},{12,8},{16,20},{20,16},{24,28},{28,24},{1,5},{5... | collective-permute-start | bytes 24584 | tf_op jit(solution)/shard_map/ppermute | solution.py:408

commit v8 on v7

--- a/solution.py
+++ b/solution.py
@@ -60,35 +60,56 @@
     return one_hot((i == source) & (s < CHI) & (t < CHI))
 
 
-def row_spread(turn):
-    i, j = iota((ROWS, CHI * CHI), 0), iota((ROWS, CHI * CHI), 1)
-    s, t = group(i), minor(i)
-    source = jnp.where(turn, t * CHI + s, s * CHI + t)
-    return one_hot((j == source) & (t < CHI))
-
-
-def swapped_tiles(x, fold):
+def swapped_tiles(x, fold, other=None):
     lane_group = group(iota((PAD, 128), 1))
     zero = jnp.zeros((PAD, 128), x.dtype)
+
+    def tile(array, p, side):
+        return array[p * PAD : (p + 1) * PAD, side * 128 : side * 128 + 128] if p < CHI else zero
+
+    sources, span = {}, 8 if other is None else 4
+    high = lax.bitwise_and(lane_group, 4) != 0
+    for p in range(CHI if other is None else PAD):
+        for side in range(2):
+            if other is None:
+                sources[p, side] = tile(x, p, side)
+            elif p & 4:
+                sources[p, side] = jnp.where(high, tile(x, p, side), tile(other, p ^ 4, side))
+            else:
+                sources[p, side] = jnp.where(high, tile(other, p ^ 4, side), tile(x, p, side))
     tiles = []
     for s in range(CHI):
         pair = []
         for side in range(2):
             lift = FOLD // PAD if fold and side and s >= CHI // 2 else 0
-            tile = zero
-            for p in range(side * 8, min(side * 8 + 8, CHI)):
-                at = (s >> 3) * 128
-                piece = x[p * PAD : (p + 1) * PAD, at : at + 128]
-                shift = (p + lift - s) % 8 * PAD
+            out = zero
+            for p in range(span):
+                source = (side * 8 + (s & 7 & -span)) | p
+                if other is None and source >= CHI:
+                    continue
+                shift = (p + lift - s % span) % 8 * PAD
+                piece = sources[source, s >> 3]
                 piece = pltpu.roll(piece, shift, 1) if shift else piece
-                tile = jnp.where(lane_group == (p & 7) + lift, piece, tile)
-            pair.append(tile)
+                here = lax.bitwise_and(lane_group, span - 1) == p
+                if lift:
+                    here = lane_group == p + lift
+                out = jnp.where(here, piece, out)
+            pair.append(out)
         tiles.append(pair)
     return tiles
 
 
-def block_swap(x):
-    return jnp.concatenate([jnp.concatenate(pair, axis=1) for pair in swapped_tiles(x, False)], axis=0)
+def block_swap(x, other=None):
+    tiles = swapped_tiles(x, False, other)
+    return jnp.concatenate([jnp.concatenate(pair, axis=1) for pair in tiles], axis=0)
+
+
+def product_both(a, b):
+    zero = jnp.zeros((PAD, b.shape[1]), b.dtype)
+    blocks = [b[s * PAD : (s + 1) * PAD] if s < CHI else zero for s in range(PAD)]
+    plain = mm(a, jnp.concatenate(blocks, axis=0), NT)
+    moved = mm(a, jnp.concatenate([blocks[s ^ 4] for s in range(PAD)], axis=0), NT)
+    return plain.astype(BF16), moved.astype(BF16)
 
 
 def widen(x):
@@ -152,13 +173,12 @@
 
 
 def product_part(x):
-    product = mm(row_swap(x), x, NT).astype(BF16)
-    return block_swap(widen(product))
+    return block_swap(*product_both(row_swap(x), x))
 
 
 def outer_part(first, second):
-    outer = mm(first, row_swap(second), NT).astype(BF16)
-    tiles = swapped_tiles(widen(outer), True)
+    outer, moved = product_both(first, row_swap(second))
+    tiles = swapped_tiles(outer, True, moved)
     half = CHI // 2
     side = folded(*(jnp.concatenate([t[1] for t in part], axis=0) for part in (tiles[:half], tiles[half:])))
     return compact(jnp.concatenate([t[0] for t in tiles] + [side], axis=0))
@@ -282,8 +302,7 @@
 
 
 def third(second_ref, right, kron_ref):
-    tile = one_hot(minor(iota((PAD, LANES), 1)) == iota((PAD, LANES), 0))
-    values = mm(right, tile, TN)
+    values = jnp.concatenate([right] * PAD, axis=0).T.astype(F32)
     lane_group = group(iota((CHI * CHI, LANES), 1))
     lane_group = jnp.where(lane_group < CHI, lane_group, lane_group - FOLD // PAD)
     entry = iota((CHI * CHI, LANES), 0)
@@ -301,8 +320,11 @@
 
 
 def placed(site, mirror, lower):
-    spaced = mm(row_spread(lower), site).astype(BF16)
-    return block_swap(mm(spaced, spread_matrix(mirror)).astype(BF16))
+    legs = site.astype(F32).reshape(CHI, CHI, CHI * CHI)
+    legs = jnp.where(lower, jnp.transpose(legs, (1, 0, 2)), legs)
+    rest = jnp.zeros((CHI, PAD - CHI, CHI * CHI), F32)
+    rows = jnp.concatenate([legs, rest], axis=1).reshape(ROWS, CHI * CHI).astype(BF16)
+    return block_swap(mm(rows, spread_matrix(mirror)).astype(BF16))
 
 
 def pick(own_first, own, other):
@@ -382,8 +404,9 @@
     mean = mean_square(merged)
     log_o[...] = (log_in[...] + 0.5 * jnp.log(mean))[:1, :1]
     wide = block_swap(merged.astype(BF16))
-    narrow = mm(wide, spread_matrix(roles(LEVELS - 1)[3]), NT).astype(BF16)
-    coarse_o[...] = mm(row_spread(True), narrow, TN) * lax.rsqrt(mean)
+    narrow = mm(wide, spread_matrix(roles(LEVELS - 1)[3]), NT) * lax.rsqrt(mean)
+    legs = jnp.transpose(narrow.reshape(CHI, PAD, CHI * CHI)[:, :CHI], (1, 0, 2))
+    coarse_o[...] = legs.reshape(CHI * CHI, CHI * CHI)
 
 
 def call(kernel, outs, scratch=()):

time: 40.2 us -> 39.4 us (0.980)
  Pallas kernels: 13.3 us -> 12.4 us
    pallas_call x18, Pallas kernels: 13.3 us -> 12.4 us  [run(): pl.pallas_call(kernel, out_shape=[jax.ShapeDtypeStruct(s, d) for s, d in...]
where the time goes in v8:
time: 39.4 us; the launch traced here: 39.3 us
  starting transfers between devices  16.4 us (42%)
  Pallas kernels  12.4 us (31%)
  waiting for transfers between devices  8.7 us (22%)
  local copies, waits for them, and re-layouts  0.92 us (2%)
  between operations  0.79 us (2%)
    pallas_call x18, Pallas kernels, run(): pl.pallas_call(kernel, out_shape=[jax.ShapeDtypeStruct(s, d) for s, d in...  12.4 us
    ppermute x3, starting transfers between devices, from_bond(): return lax.ppermute(array, ('row', 'col'), pairs)  11.9 us
    ppermute x3, waiting for transfers between devices, from_bond(): return lax.ppermute(array, ('row', 'col'), pairs)  4.86 us
    ppermute x6, starting transfers between devices, from_partner(): return lax.ppermute(array, 'row', [(i, i ^ flip) for i in range(count)])  4.54 us
    ppermute x6, waiting for transfers between devices, from_partner(): return lax.ppermute(array, 'row', [(i, i ^ flip) for i in range(count)])  3.84 us
    unnamed x4, local copies, waits for them, and re-layouts  0.92 us
  transfers between devices with their start and end apart: 9, of which 9 were waited for; matrix products, arithmetic and copies ran while one was open for 0% of the time, Pallas kernels for 12%

profile of v8, /device:TPU:0, one launch (start us, length us, event | category | flops | bytes accessed | tf_op | source)
XLA Modules:
  0.0 39.3 jit_solution(14121128187178120325)
XLA Ops:
  0.6 0.6 %collective-permute-start = (f32[144,144]{1,0:T(8,128)}, f32[144,144]{1,0:T(8,128)S(1)}, u32[]{:S(2)}, u32[]{:S(2)}) collective-permute-start(f32[144,144]{1,0:T(8,128)} %bitcast.2), channel_id=1, source_target_pairs={{0,4},{4,0},{8,12},{12,8},{16,20},{20,16},{24,28},{28,24},{1,5},{5... | collective-permute-start | bytes 248840 | tf_op jit(solution)/shard_map/ppermute | solution.py:431
  1.2 0.0 copy-start
  1.2 0.9 %copy-done = f32[1,1,144,144]{3,2,1,0:T(8,128)S(1)} copy-done((f32[1,1,144,144]{3,2,1,0:T(8,128)S(1)}, f32[1,1,144,144]{3,2,1,0:T(8,128)}, u32[]{:S(2)}) %copy-start) | copy-done | bytes 82968
  2.1 0.0 copy-start.1
  2.1 0.3 collective-permute-done.other
  2.4 1.2 %shard_map.42 = (bf16[192,256]{1,0:T(8,128)(2,1)S(1)}, bf16[192,256]{1,0:T(8,128)(2,1)S(1)}, bf16[216,128]{1,0:T(8,128)(2,1)S(1)}) custom-call(bf16[144,144]{1,0:T(8,128)(2,1)S(1)} %shard_map.41.own, f32[144,144]{1,0:T(8,128)S(1)} %collective-permute-done.other), custom_call_target="tpu_custom_call" | custom-call | flops 100000000 | bytes 1000000 | tf_op jit(solution)/shard_map/pallas_call | solution.py:416
  3.6 4.8 %collective-permute-start.1 = (bf16[216,128]{1,0:T(8,128)(2,1)S(1)}, bf16[216,128]{1,0:T(8,128)(2,1)S(1)}, u32[]{:S(2)}, u32[]{:S(2)}) collective-permute-start(bf16[216,128]{1,0:T(8,128)(2,1)S(1)} %get-tuple-element.37.own), channel_id=1, source_target_pairs={{0,7},{1,4},{2,5},{3,6},{4,1},{5,2},{6,3},{7,0},{8,13},{9,14},{10,... | collective-permute-start | bytes 165896 | tf_op jit(solution)/shard_map/ppermute | solution.py:448
  8.4 0.0 copy-done.1
  8.4 0.4 shard_map.43
  8.8 1.6 %collective-permute-done.1.other = bf16[216,128]{1,0:T(8,128)(2,1)S(1)} collective-permute-done((bf16[216,128]{1,0:T(8,128)(2,1)S(1)}, bf16[216,128]{1,0:T(8,128)(2,1)S(1)}, u32[]{:S(2)}, u32[]{:S(2)}) %collective-permute-start.1) | collective-permute-done | bytes 55328 | tf_op jit(solution)/shard_map/ppermute | solution.py:448
  10.3 0.8 %shard_map.44.left = bf16[16,256]{1,0:T(8,128)(2,1)S(1)} custom-call(bf16[216,128]{1,0:T(8,128)(2,1)S(1)} %get-tuple-element.37.own, bf16[216,128]{1,0:T(8,128)(2,1)S(1)} %collective-permute-done.1.other, f32[32,256]{1,0:T(8,128)S(1)} %get-tuple-element.38.starts, bf16[64,256]{1,0:T(8,128)(2,1)S(1)} %get-tuple-element.39.pieces), custom_call_target="tpu_custom_call" | custom-call | flops 100000000 | bytes 1000000 | tf_op jit(solution)/shard_map/pallas_call | solution.py:416
  11.2 0.1 collective-permute-start.2
  11.2 1.0 %shard_map.45.second = bf16[192,1792]{1,0:T(8,128)(2,1)S(1)} custom-call(bf16[192,256]{1,0:T(8,128)(2,1)S(1)} %get-tuple-element.35.turned, bf16[192,256]{1,0:T(8,128)(2,1)S(1)} %get-tuple-element.36.lower, bf16[16,256]{1,0:T(8,128)(2,1)S(1)} %shard_map.44.left), custom_call_target="tpu_custom_call" | custom-call | flops 100000000 | bytes 1000000 | tf_op jit(solution)/shard_map/pallas_call | solution.py:416
  12.2 0.2 collective-permute-done.2.right
  12.4 0.5 %shard_map.46 = (bf16[216,128]{1,0:T(8,128)(2,1)S(1)}, f32[8,128]{1,0:T(8,128)S(1)}) custom-call(bf16[192,1792]{1,0:T(8,128)(2,1)S(1)} %shard_map.45.second, bf16[16,256]{1,0:T(8,128)(2,1)S(1)} %collective-permute-done.2.right, f32[8,128]{1,0:T(8,128)S(1)} %broadcast_in_dim.6.log_in), custom_call_target="tpu_custom_call" | custom-call | flops 100000000 | bytes 1000000 | tf_op jit(solution)/shard_map/pallas_call | solution.py:416
  12.9 1.9 %collective-permute-start.3 = (bf16[216,128]{1,0:T(8,128)(2,1)S(1)}, bf16[216,128]{1,0:T(8,128)(2,1)S(1)}, u32[]{:S(2)}, u32[]{:S(2)}) collective-permute-start(bf16[216,128]{1,0:T(8,128)(2,1)S(1)} %get-tuple-element.40.own), channel_id=1, source_target_pairs={{0,12},{4,8},{8,4},{12,0},{16,28},{20,24},{24,20},{28,16},{1,13},{... | collective-permute-start | bytes 165896 | tf_op jit(solution)/shard_map/ppermute | solution.py:431
  14.8 0.4 shard_map.47
  15.2 1.5 %collective-permute-done.3.other = bf16[216,128]{1,0:T(8,128)(2,1)S(1)} collective-permute-done((bf16[216,128]{1,0:T(8,128)(2,1)S(1)}, bf16[216,128]{1,0:T(8,128)(2,1)S(1)}, u32[]{:S(2)}, u32[]{:S(2)}) %collective-permute-start.3) | collective-permute-done | bytes 55328 | tf_op jit(solution)/shard_map/ppermute | solution.py:431
  16.8 0.8 %shard_map.48 = (bf16[192,256]{1,0:T(8,128)(2,1)S(1)}, bf16[192,256]{1,0:T(8,128)(2,1)S(1)}, bf16[216,128]{1,0:T(8,128)(2,1)S(1)}) custom-call(bf16[192,256]{1,0:T(8,128)(2,1)S(1)} %get-tuple-element.41.wide, bf16[192,256]{1,0:T(8,128)(2,1)S(1)} %get-tuple-element.42.product, bf16[216,128]{1,0:T(8,128)(2,1)S(1)} %collective-permute-done.3.other), custom_call_target="tpu_custom_call" | custom-call | flops 100000000 | bytes 1000000 | tf_op jit(solution)/shard_map/pallas_call | solution.py:416
  17.5 3.6 %collective-permute-start.4 = (bf16[216,128]{1,0:T(8,128)(2,1)S(1)}, bf16[216,128]{1,0:T(8,128)(2,1)S(1)}, u32[]{:S(2)}, u32[]{:S(2)}) collective-permute-start(bf16[216,128]{1,0:T(8,128)(2,1)S(1)} %get-tuple-element.47.own), channel_id=1, source_target_pairs={{0,7},{1,4},{2,5},{3,6},{4,1},{5,2},{6,3},{7,0},{8,13},{9,14},{10,... | collective-permute-start | bytes 165896 | tf_op jit(solution)/shard_map/ppermute | solution.py:448
  21.1 0.4 shard_map.49
  21.5 1.6 %collective-permute-done.4.other = bf16[216,128]{1,0:T(8,128)(2,1)S(1)} collective-permute-done((bf16[216,128]{1,0:T(8,128)(2,1)S(1)}, bf16[216,128]{1,0:T(8,128)(2,1)S(1)}, u32[]{:S(2)}, u32[]{:S(2)}) %collective-permute-start.4) | collective-permute-done | bytes 55328 | tf_op jit(solution)/shard_map/ppermute | solution.py:448
  23.1 0.8 %shard_map.50.left = bf16[16,256]{1,0:T(8,128)(2,1)S(1)} custom-call(bf16[216,128]{1,0:T(8,128)(2,1)S(1)} %get-tuple-element.47.own, bf16[216,128]{1,0:T(8,128)(2,1)S(1)} %collective-permute-done.4.other, f32[32,256]{1,0:T(8,128)S(1)} %get-tuple-element.48.starts, bf16[64,256]{1,0:T(8,128)(2,1)S(1)} %get-tuple-element.49.pieces), custom_call_target="tpu_custom_call" | custom-call | flops 100000000 | bytes 1000000 | tf_op jit(solution)/shard_map/pallas_call | solution.py:416
  23.9 0.1 collective-permute-start.5
  24.0 1.0 %shard_map.51.second = bf16[192,1792]{1,0:T(8,128)(2,1)S(1)} custom-call(bf16[192,256]{1,0:T(8,128)(2,1)S(1)} %get-tuple-element.45.turned, bf16[192,256]{1,0:T(8,128)(2,1)S(1)} %get-tuple-element.46.lower, bf16[16,256]{1,0:T(8,128)(2,1)S(1)} %shard_map.50.left), custom_call_target="tpu_custom_call" | custom-call | flops 100000000 | bytes 1000000 | tf_op jit(solution)/shard_map/pallas_call | solution.py:416
  25.0 0.2 collective-permute-done.5.right
  25.2 0.5 %shard_map.52 = (bf16[216,128]{1,0:T(8,128)(2,1)S(1)}, f32[8,128]{1,0:T(8,128)S(1)}) custom-call(bf16[192,1792]{1,0:T(8,128)(2,1)S(1)} %shard_map.51.second, bf16[16,256]{1,0:T(8,128)(2,1)S(1)} %collective-permute-done.5.right, f32[8,128]{1,0:T(8,128)S(1)} %get-tuple-element.50.log_in), custom_call_target="tpu_custom_call" | custom-call | flops 100000000 | bytes 1000000 | tf_op jit(solution)/shard_map/pallas_call | solution.py:416
  25.7 1.9 %collective-permute-start.6 = (bf16[216,128]{1,0:T(8,128)(2,1)S(1)}, bf16[216,128]{1,0:T(8,128)(2,1)S(1)}, u32[]{:S(2)}, u32[]{:S(2)}) collective-permute-start(bf16[216,128]{1,0:T(8,128)(2,1)S(1)} %get-tuple-element.51.own), channel_id=1, source_target_pairs={{0,20},{4,16},{8,28},{12,24},{16,4},{20,0},{24,12},{28,8},{1,21},{... | collective-permute-start | bytes 165896 | tf_op jit(solution)/shard_map/ppermute | solution.py:431
  27.6 0.4 shard_map.53
  28.0 1.5 %collective-permute-done.6.other = bf16[216,128]{1,0:T(8,128)(2,1)S(1)} collective-permute-done((bf16[216,128]{1,0:T(8,128)(2,1)S(1)}, bf16[216,128]{1,0:T(8,128)(2,1)S(1)}, u32[]{:S(2)}, u32[]{:S(2)}) %collective-permute-start.6) | collective-permute-done | bytes 55328 | tf_op jit(solution)/shard_map/ppermute | solution.py:431
  29.5 0.8 %shard_map.54 = (bf16[192,256]{1,0:T(8,128)(2,1)S(1)}, bf16[192,256]{1,0:T(8,128)(2,1)S(1)}, bf16[216,128]{1,0:T(8,128)(2,1)S(1)}) custom-call(bf16[192,256]{1,0:T(8,128)(2,1)S(1)} %get-tuple-element.52.wide, bf16[192,256]{1,0:T(8,128)(2,1)S(1)} %get-tuple-element.53.product, bf16[216,128]{1,0:T(8,128)(2,1)S(1)} %collective-permute-done.6.other), custom_call_target="tpu_custom_call" | custom-call | flops 100000000 | bytes 1000000 | tf_op jit(solution)/shard_map/pallas_call | solution.py:416
  30.3 3.6 %collective-permute-start.7 = (bf16[216,128]{1,0:T(8,128)(2,1)S(1)}, bf16[216,128]{1,0:T(8,128)(2,1)S(1)}, u32[]{:S(2)}, u32[]{:S(2)}) collective-permute-start(bf16[216,128]{1,0:T(8,128)(2,1)S(1)} %get-tuple-element.58.own), channel_id=1, source_target_pairs={{0,7},{1,4},{2,5},{3,6},{4,1},{5,2},{6,3},{7,0},{8,13},{9,14},{10,... | collective-permute-start | bytes 165896 | tf_op jit(solution)/shard_map/ppermute | solution.py:448
  33.8 0.3 shard_map.55
  34.1 1.7 %collective-permute-done.7.other = bf16[216,128]{1,0:T(8,128)(2,1)S(1)} collective-permute-done((bf16[216,128]{1,0:T(8,128)(2,1)S(1)}, bf16[216,128]{1,0:T(8,128)(2,1)S(1)}, u32[]{:S(2)}, u32[]{:S(2)}) %collective-permute-start.7) | collective-permute-done | bytes 55328 | tf_op jit(solution)/shard_map/ppermute | solution.py:448
  35.8 0.8 %shard_map.56.left = bf16[16,256]{1,0:T(8,128)(2,1)S(1)} custom-call(bf16[216,128]{1,0:T(8,128)(2,1)S(1)} %get-tuple-element.58.own, bf16[216,128]{1,0:T(8,128)(2,1)S(1)} %collective-permute-done.7.other, f32[32,256]{1,0:T(8,128)S(1)} %get-tuple-element.59.starts, bf16[64,256]{1,0:T(8,128)(2,1)S(1)} %get-tuple-element.60.pieces), custom_call_target="tpu_custom_call" | custom-call | flops 100000000 | bytes 1000000 | tf_op jit(solution)/shard_map/pallas_call | solution.py:416
  36.7 0.1 collective-permute-start.8
  36.7 1.0 %shard_map.57.second = bf16[192,1792]{1,0:T(8,128)(2,1)S(1)} custom-call(bf16[192,256]{1,0:T(8,128)(2,1)S(1)} %get-tuple-element.56.turned, bf16[192,256]{1,0:T(8,128)(2,1)S(1)} %get-tuple-element.57.lower, bf16[16,256]{1,0:T(8,128)(2,1)S(1)} %shard_map.56.left), custom_call_target="tpu_custom_call" | custom-call | flops 100000000 | bytes 1000000 | tf_op jit(solution)/shard_map/pallas_call | solution.py:416
  37.7 0.2 collective-permute-done.8.right
  37.9 1.4 %shard_map.58 = (f32[144,144]{1,0:T(8,128)}, f32[1,1]{1,0:T(1,128)}) custom-call(bf16[192,1792]{1,0:T(8,128)(2,1)S(1)} %shard_map.57.second, bf16[16,256]{1,0:T(8,128)(2,1)S(1)} %collective-permute-done.8.right, f32[8,128]{1,0:T(8,128)S(1)} %get-tuple-element.61.log_in), custom_call_target="tpu_custom_call" | custom-call | flops 100000000 | bytes 1000000 | tf_op jit(solution)/shard_map/pallas_call | solution.py:416
  (2 shorter events, 0.0 us)
Async XLA Ops:
  0.6 1.8 %collective-permute-start = (f32[144,144]{1,0:T(8,128)}, f32[144,144]{1,0:T(8,128)S(1)}, u32[]{:S(2)}, u32[]{:S(2)}) collective-permute-start(f32[144,144]{1,0:T(8,128)} %bitcast.2), channel_id=1, source_target_pairs={{0,4},{4,0},{8,12},{12,8},{16,20},{20,16},{24,28},{28,24},{1,5},{5... | collective-permute-start | bytes 248840 | tf_op jit(solution)/shard_map/ppermute | solution.py:431
  1.2 0.9 %copy-start = (f32[1,1,144,144]{3,2,1,0:T(8,128)S(1)}, f32[1,1,144,144]{3,2,1,0:T(8,128)}, u32[]{:S(2)}) copy-start(f32[1,1,144,144]{3,2,1,0:T(8,128)} %param.2) | copy-start | bytes 248836
  2.1 6.3 %copy-start.1 = (f32[3,12,144]{2,1,0:T(8,128)S(1)}, f32[3,12,144]{2,1,0:T(8,128)}, u32[]{:S(2)}) copy-start(f32[3,12,144]{2,1,0:T(8,128)} %start.5) | copy-start | bytes 62212
  3.6 6.7 %collective-permute-start.1 = (bf16[216,128]{1,0:T(8,128)(2,1)S(1)}, bf16[216,128]{1,0:T(8,128)(2,1)S(1)}, u32[]{:S(2)}, u32[]{:S(2)}) collective-permute-start(bf16[216,128]{1,0:T(8,128)(2,1)S(1)} %get-tuple-element.37.own), channel_id=1, source_target_pairs={{0,7},{1,4},{2,5},{3,6},{4,1},{5,2},{6,3},{7,0},{8,13},{9,14},{10,... | collective-permute-start | bytes 165896 | tf_op jit(solution)/shard_map/ppermute | solution.py:448
  11.2 1.2 %collective-permute-start.2 = (bf16[16,256]{1,0:T(8,128)(2,1)S(1)}, bf16[16,256]{1,0:T(8,128)(2,1)S(1)}, u32[]{:S(2)}, u32[]{:S(2)}) collective-permute-start(bf16[16,256]{1,0:T(8,128)(2,1)S(1)} %shard_map.44.left), channel_id=1, source_target_pairs={{0,4},{4,0},{8,12},{12,8},{16,20},{20,16},{24,28},{28,24},{1,5},{5... | collective-permute-start | bytes 24584 | tf_op jit(solution)/shard_map/ppermute | solution.py:431
  12.9 3.8 %collective-permute-start.3 = (bf16[216,128]{1,0:T(8,128)(2,1)S(1)}, bf16[216,128]{1,0:T(8,128)(2,1)S(1)}, u32[]{:S(2)}, u32[]{:S(2)}) collective-permute-start(bf16[216,128]{1,0:T(8,128)(2,1)S(1)} %get-tuple-element.40.own), channel_id=1, source_target_pairs={{0,12},{4,8},{8,4},{12,0},{16,28},{20,24},{24,20},{28,16},{1,13},{... | collective-permute-start | bytes 165896 | tf_op jit(solution)/shard_map/ppermute | solution.py:431
  17.5 5.5 %collective-permute-start.4 = (bf16[216,128]{1,0:T(8,128)(2,1)S(1)}, bf16[216,128]{1,0:T(8,128)(2,1)S(1)}, u32[]{:S(2)}, u32[]{:S(2)}) collective-permute-start(bf16[216,128]{1,0:T(8,128)(2,1)S(1)} %get-tuple-element.47.own), channel_id=1, source_target_pairs={{0,7},{1,4},{2,5},{3,6},{4,1},{5,2},{6,3},{7,0},{8,13},{9,14},{10,... | collective-permute-start | bytes 165896 | tf_op jit(solution)/shard_map/ppermute | solution.py:448
  23.9 1.2 %collective-permute-start.5 = (bf16[16,256]{1,0:T(8,128)(2,1)S(1)}, bf16[16,256]{1,0:T(8,128)(2,1)S(1)}, u32[]{:S(2)}, u32[]{:S(2)}) collective-permute-start(bf16[16,256]{1,0:T(8,128)(2,1)S(1)} %shard_map.50.left), channel_id=1, source_target_pairs={{0,4},{4,0},{8,12},{12,8},{16,20},{20,16},{24,28},{28,24},{1,5},{5... | collective-permute-start | bytes 24584 | tf_op jit(solution)/shard_map/ppermute | solution.py:431
  25.7 3.8 %collective-permute-start.6 = (bf16[216,128]{1,0:T(8,128)(2,1)S(1)}, bf16[216,128]{1,0:T(8,128)(2,1)S(1)}, u32[]{:S(2)}, u32[]{:S(2)}) collective-permute-start(bf16[216,128]{1,0:T(8,128)(2,1)S(1)} %get-tuple-element.51.own), channel_id=1, source_target_pairs={{0,20},{4,16},{8,28},{12,24},{16,4},{20,0},{24,12},{28,8},{1,21},{... | collective-permute-start | bytes 165896 | tf_op jit(solution)/shard_map/ppermute | solution.py:431
  30.3 5.6 %collective-permute-start.7 = (bf16[216,128]{1,0:T(8,128)(2,1)S(1)}, bf16[216,128]{1,0:T(8,128)(2,1)S(1)}, u32[]{:S(2)}, u32[]{:S(2)}) collective-permute-start(bf16[216,128]{1,0:T(8,128)(2,1)S(1)} %get-tuple-element.58.own), channel_id=1, source_target_pairs={{0,7},{1,4},{2,5},{3,6},{4,1},{5,2},{6,3},{7,0},{8,13},{9,14},{10,... | collective-permute-start | bytes 165896 | tf_op jit(solution)/shard_map/ppermute | solution.py:448
  36.7 1.2 %collective-permute-start.8 = (bf16[16,256]{1,0:T(8,128)(2,1)S(1)}, bf16[16,256]{1,0:T(8,128)(2,1)S(1)}, u32[]{:S(2)}, u32[]{:S(2)}) collective-permute-start(bf16[16,256]{1,0:T(8,128)(2,1)S(1)} %shard_map.56.left), channel_id=1, source_target_pairs={{0,4},{4,0},{8,12},{12,8},{16,20},{20,16},{24,28},{28,24},{1,5},{5... | collective-permute-start | bytes 24584 | tf_op jit(solution)/shard_map/ppermute | solution.py:431

commit v9 on v8

--- a/solution.py
+++ b/solution.py
@@ -104,11 +104,13 @@
     return jnp.concatenate([jnp.concatenate(pair, axis=1) for pair in tiles], axis=0)
 
 
-def product_both(a, b):
+def product_both(a, b, scale=None):
     zero = jnp.zeros((PAD, b.shape[1]), b.dtype)
     blocks = [b[s * PAD : (s + 1) * PAD] if s < CHI else zero for s in range(PAD)]
     plain = mm(a, jnp.concatenate(blocks, axis=0), NT)
     moved = mm(a, jnp.concatenate([blocks[s ^ 4] for s in range(PAD)], axis=0), NT)
+    if scale is not None:
+        plain, moved = plain * scale, moved * scale
     return plain.astype(BF16), moved.astype(BF16)
 
 
@@ -172,8 +174,8 @@
     return jnp.concatenate([turned, rest], axis=1).reshape(x.shape).astype(BF16)
 
 
-def product_part(x):
-    return block_swap(*product_both(row_swap(x), x))
+def product_part(x, scale=None):
+    return block_swap(*product_both(row_swap(x), x, scale))
 
 
 def outer_part(first, second):
@@ -197,37 +199,67 @@
     return fold3(plain), fold3(turned)
 
 
-def orthonormal(y):
+def row_products(y):
     pieces = parts2(y)
     high, low = pieces[:PAD], pieces[PAD:]
     gram = fold2(mm(pieces, high, NT)) + mm(high, low, NT)
-    width = y.shape[1]
+    return [jnp.broadcast_to(gram[:, k : k + 1], (PAD, 128)) for k in range(CHI)]
+
+
+def line(x, k):
+    return jnp.broadcast_to(x[k : k + 1, :], x.shape)
+
+
+def twice(x, width):
+    return jnp.concatenate([x] * (width // 128), axis=1)
+
+
+def exact_orthonormal(y):
+    cols = row_products(y)
     row = iota((PAD, 128), 0)
-    cols = [jnp.broadcast_to(gram[:, k : k + 1], (PAD, 128)) for k in range(CHI)]
-    floors = [jnp.broadcast_to(cols[k][k : k + 1, :], (PAD, 128)) * PIVOT for k in range(CHI)]
     scale = jnp.zeros((PAD, 128), F32)
-    good = jnp.ones((PAD, 128), F32)
     for k in range(CHI):
-        pivot = jnp.broadcast_to(cols[k][k : k + 1, :], (PAD, 128))
-        good = jnp.where(pivot >= floors[k], good, 0.0)
-        inverse = lax.rsqrt(pivot)
+        inverse = lax.rsqrt(line(cols[k], k))
         scale = jnp.where(row == k, inverse, scale)
         factor = jnp.where(row > k, cols[k] * (inverse * inverse), 0.0)
         for j in range(k + 1, CHI):
-            cols[j] = cols[j] - factor * jnp.broadcast_to(cols[j][k : k + 1, :], (PAD, 128))
-        wide = jnp.concatenate([factor] * (width // 128), axis=1)
-        y = y - wide * jnp.broadcast_to(y[k : k + 1, :], (PAD, width))
-    return y * jnp.concatenate([scale] * (width // 128), axis=1), good
+            cols[j] = cols[j] - factor * line(cols[j], k)
+        y = y - twice(factor, y.shape[1]) * line(y, k)
+    return y * twice(scale, y.shape[1])
+
+
+def orthonormal(y):
+    cols = row_products(y)
+    width = y.shape[1]
+    row = iota((PAD, 128), 0)
+    floors = [line(cols[k], k) * PIVOT for k in range(CHI)]
+    scale, inner = jnp.zeros((PAD, 128), F32), jnp.zeros((PAD, 128), F32)
+    good = jnp.ones((PAD, 128), F32)
+    for k in range(0, CHI, 2):
+        here, after = cols[k], cols[k + 1]
+        top, side, low = line(here, k), line(here, k + 1), line(after, k + 1)
+        det = top * low - side * side
+        good = jnp.where((top >= floors[k]) & (det >= floors[k + 1] * top), good, 0.0)
+        over, rest = 1.0 / det, row > k + 1
+        first = jnp.where(rest, (low * here - side * after) * over, 0.0)
+        second = jnp.where(rest, (top * after - side * here) * over, 0.0)
+        for j in range(k + 2, CHI):
+            cols[j] = cols[j] - first * line(cols[j], k) - second * line(cols[j], k + 1)
+        y = y - twice(first, width) * line(y, k) - twice(second, width) * line(y, k + 1)
+        scale = jnp.where(row == k, lax.rsqrt(top), scale)
+        scale = jnp.where(row == k + 1, lax.rsqrt(det / top), scale)
+        inner = jnp.where(row == k + 1, side / top, inner)
+    y = y - twice(inner, width) * pltpu.roll(y, 1, 0)
+    return y * twice(scale, width), good
 
 
 def exact_iso(own, other, start, start_turned, shift, swap):
     pieces = parts3(start)
     image = fold3(mm(pieces, own, NT) + mm(pieces, other, NT))
-    basis, _ = orthonormal(widen(image) + shift * start_turned)
+    basis = exact_orthonormal(widen(image) + shift * start_turned)
     pieces = parts3(basis)
     image = fold3(mm(pieces[:, :ROWS], own) + mm(pieces[:, :ROWS], other))
-    basis, _ = orthonormal(image + shift * fold3(mm(pieces, swap)))
-    return basis
+    return exact_orthonormal(image + shift * fold3(mm(pieces, swap)))
 
 
 def iso_kernel(own, other, starts, pieces, iso_o):
@@ -254,7 +286,7 @@
     basis, good = orthonormal(image + fold2(mm(parts, swap)))
     iso_o[...] = basis.astype(BF16)
 
-    @pl.when(jnp.logical_not(jnp.min(good[:1]) > 0.5))
+    @pl.when(jnp.logical_not(good[0, 0] > 0.5))
     def _():
         basis = exact_iso(own, other, starts[:PAD], starts[PAD:], shift, swap)
         iso_o[...] = basis.astype(BF16)
@@ -352,18 +384,29 @@
     gram_o[...] = outer_part(*products)
 
 
-def own_kernel(own, wide_o, product_o):
+def mean_square(lines):
+    mean = jnp.sum(lines, axis=1, keepdims=True) / (CHI**4) + 1e-06
+    return jnp.broadcast_to(mean, (8, 128))
+
+
+def scaled_product(x):
+    mean = mean_square(jnp.sum(jnp.square(x.astype(F32)), axis=0, keepdims=True))
+    return product_part(x, twice(1.0 / mean[:1], LANES)), mean
+
+
+def own_kernel(own, wide_o, product_o, mean_o):
     wide = unfold(spaced(own[...]))
     wide_o[...] = wide
-    product_o[...] = product_part(wide)
-
-
-def gram_kernel(level, wide, product, other, first_o, second_o, gram_o):
+    product_o[...], mean_o[...] = scaled_product(wide)
+
+
+def gram_kernel(level, wide, product, mean, other, first_o, second_o, gram_o, scale_o):
     own_first = roles(level)[0]
     theirs = unfold(spaced(other[...]))
-    products = pick(own_first, product[...], product_part(theirs))
-    gram_o[...] = outer_part(*products)
+    other_product, other_mean = scaled_product(theirs)
+    gram_o[...] = outer_part(*pick(own_first, product[...], other_product))
     first_o[...], second_o[...] = pick(own_first, wide[...], theirs)
+    scale_o[...] = lax.rsqrt(mean[...]) * lax.rsqrt(other_mean)
 
 
 def turn_kernel(level, first, second, start, turned_o, lower_o, starts_o, pieces_o):
@@ -384,27 +427,26 @@
     first_second(turned[...], lower[...], left[...], second_o, first)
 
 
-def mean_square(merged):
-    lines = jnp.sum(merged * merged, axis=0, keepdims=True)
-    total = jnp.sum(lines[:, :128] + 0.5 * lines[:, 128:], axis=1, keepdims=True)
-    return total / (CHI**4) + 1e-06
-
-
-def third_kernel(second, right, log_in, next_o, log_o, kron):
+def third_kernel(second, right, *refs):
+    *scales, next_o, kron = refs
     merged = third(second, right[...], kron)
-    mean = mean_square(merged)
     half = ROWS // 2
     side = folded(merged[:half, 128:], merged[half:, 128:])
-    next_o[...] = compact(jnp.concatenate([merged[:, :128], side], axis=0) * lax.rsqrt(mean))
-    log_o[...] = log_in[...] + 0.5 * jnp.log(mean)
-
-
-def last_kernel(second, right, log_in, coarse_o, log_o, kron):
-    merged = third(second, right[...], kron)
-    mean = mean_square(merged)
-    log_o[...] = (log_in[...] + 0.5 * jnp.log(mean))[:1, :1]
+    merged = jnp.concatenate([merged[:, :128], side], axis=0)
+    for scale in scales:
+        merged = merged * scale[:1]
+    next_o[...] = compact(merged)
+
+
+def last_kernel(second, right, scale, *refs):
+    *means, coarse_o, log_o, kron = refs
+    merged = third(second, right[...], kron) * twice(scale[:1], LANES)
+    lines = jnp.sum(merged * merged, axis=0, keepdims=True)
+    mean = mean_square(lines[:, :128] + 0.5 * lines[:, 128:])
+    log_o[...] = 0.5 * sum(jnp.log(m[:1, :1]) for m in [*means, mean])
     wide = block_swap(merged.astype(BF16))
-    narrow = mm(wide, spread_matrix(roles(LEVELS - 1)[3]), NT) * lax.rsqrt(mean)
+    narrow = mm(wide, spread_matrix(roles(LEVELS - 1)[3]), NT)
+    narrow = narrow * twice(lax.rsqrt(mean[:1]), LANES)[:, : CHI * CHI]
     legs = jnp.transpose(narrow.reshape(CHI, PAD, CHI * CHI)[:, :CHI], (1, 0, 2))
     coarse_o[...] = legs.reshape(CHI * CHI, CHI * CHI)
 
@@ -450,9 +492,9 @@
 
 def per_device(site_tensors, start_basis):
     square = CHI * CHI
-    mat, packed, logs = ((ROWS, LANES), BF16), ((CHI * CHI * 3 // 2, 128), BF16), ((8, 128), F32)
+    mat, packed, one = ((ROWS, LANES), BF16), ((CHI * CHI * 3 // 2, 128), BF16), ((8, 128), F32)
     kron, firsts = [pltpu.VMEM((SECOND, LANES), BF16)], [pltpu.VMEM((CHI * ROWS, LANES), BF16)]
-    log_total = jnp.zeros(*logs)
+    scales, means = [], []
     own = site_tensors[0, 0]
     for level in range(LEVELS):
         if level == 0:
@@ -461,10 +503,11 @@
             first, lower, gram = call(first_gram_kernel, [mat, mat, packed])(own, other)
         else:
             other = from_partner(own, 1 << level | 1)
-            wide, product = call(own_kernel, [mat, mat])(own)
-            first, lower, gram = call(
-                functools.partial(gram_kernel, level), [mat, mat, packed]
-            )(wide, product, other)
+            wide, product, mean = call(own_kernel, [mat, mat, one])(own)
+            first, lower, gram, scale = call(
+                functools.partial(gram_kernel, level), [mat, mat, packed, one]
+            )(wide, product, mean, other)
+            scales, means = [scale], [*means, mean]
         gram_other = from_bond(gram)
         turned, lower, starts, pieces = call(
             functools.partial(turn_kernel, level),
@@ -474,10 +517,10 @@
         right = from_partner(left, 1)
         (second,) = call(second_kernel, [((ROWS, SECOND), BF16)], firsts)(turned, lower, left)
         if level < LEVELS - 1:
-            own, log_total = call(third_kernel, [packed, logs], kron)(second, right, log_total)
+            (own,) = call(third_kernel, [packed], kron)(second, right, *scales)
         else:
             coarse, log_total = call(last_kernel, [((square, square), F32), ((1, 1), F32)], kron)(
-                second, right, log_total
+                second, right, *scales, *means
             )
     return (coarse[None, None], log_total)
 

time: 39.4 us -> 39.2 us (level)
  no operation moved by 1% of the time
where the time goes in v9:
time: 39.2 us; the launch traced here: 39 us
  starting transfers between devices  16.4 us (42%)
  Pallas kernels  12.2 us (31%)
  waiting for transfers between devices  8.7 us (22%)
  local copies, waits for them, and re-layouts  0.92 us (2%)
  between operations  0.79 us (2%)
    pallas_call x18, Pallas kernels, run(): pl.pallas_call(kernel, out_shape=[jax.ShapeDtypeStruct(s, d) for s, d in...  12.2 us
    ppermute x3, starting transfers between devices, from_bond(): return lax.ppermute(array, ('row', 'col'), pairs)  11.9 us
    ppermute x3, waiting for transfers between devices, from_bond(): return lax.ppermute(array, ('row', 'col'), pairs)  4.88 us
    ppermute x6, starting transfers between devices, from_partner(): return lax.ppermute(array, 'row', [(i, i ^ flip) for i in range(count)])  4.53 us
    ppermute x6, waiting for transfers between devices, from_partner(): return lax.ppermute(array, 'row', [(i, i ^ flip) for i in range(count)])  3.82 us
    unnamed x4, local copies, waits for them, and re-layouts  0.92 us
  transfers between devices with their start and end apart: 9, of which 9 were waited for; matrix products, arithmetic and copies ran while one was open for 0% of the time, Pallas kernels for 12%

profile of v9, /device:TPU:0, one launch (start us, length us, event | category | flops | bytes accessed | tf_op | source)
XLA Modules:
  0.0 39.0 jit_solution(11466648250365033628)
XLA Ops:
  0.6 0.6 %collective-permute-start = (f32[144,144]{1,0:T(8,128)}, f32[144,144]{1,0:T(8,128)S(1)}, u32[]{:S(2)}, u32[]{:S(2)}) collective-permute-start(f32[144,144]{1,0:T(8,128)} %bitcast.2), channel_id=1, source_target_pairs={{0,4},{4,0},{8,12},{12,8},{16,20},{20,16},{24,28},{28,24},{1,5},{5... | collective-permute-start | bytes 248840 | tf_op jit(solution)/shard_map/ppermute | solution.py:473
  1.2 0.0 copy-start
  1.2 0.9 %copy-done = f32[1,1,144,144]{3,2,1,0:T(8,128)S(1)} copy-done((f32[1,1,144,144]{3,2,1,0:T(8,128)S(1)}, f32[1,1,144,144]{3,2,1,0:T(8,128)}, u32[]{:S(2)}) %copy-start) | copy-done | bytes 82968
  2.1 0.0 copy-start.1
  2.1 0.3 collective-permute-done.other
  2.4 1.2 %shard_map.42 = (bf16[192,256]{1,0:T(8,128)(2,1)S(1)}, bf16[192,256]{1,0:T(8,128)(2,1)S(1)}, bf16[216,128]{1,0:T(8,128)(2,1)S(1)}) custom-call(bf16[144,144]{1,0:T(8,128)(2,1)S(1)} %shard_map.41.own, f32[144,144]{1,0:T(8,128)S(1)} %collective-permute-done.other), custom_call_target="tpu_custom_call" | custom-call | flops 100000000 | bytes 1000000 | tf_op jit(solution)/shard_map/pallas_call | solution.py:458
  3.6 4.8 %collective-permute-start.1 = (bf16[216,128]{1,0:T(8,128)(2,1)S(1)}, bf16[216,128]{1,0:T(8,128)(2,1)S(1)}, u32[]{:S(2)}, u32[]{:S(2)}) collective-permute-start(bf16[216,128]{1,0:T(8,128)(2,1)S(1)} %get-tuple-element.37.own), channel_id=1, source_target_pairs={{0,7},{1,4},{2,5},{3,6},{4,1},{5,2},{6,3},{7,0},{8,13},{9,14},{10,... | collective-permute-start | bytes 165896 | tf_op jit(solution)/shard_map/ppermute | solution.py:490
  8.4 0.0 copy-done.1
  8.4 0.4 shard_map.43
  8.8 1.6 %collective-permute-done.1.other = bf16[216,128]{1,0:T(8,128)(2,1)S(1)} collective-permute-done((bf16[216,128]{1,0:T(8,128)(2,1)S(1)}, bf16[216,128]{1,0:T(8,128)(2,1)S(1)}, u32[]{:S(2)}, u32[]{:S(2)}) %collective-permute-start.1) | collective-permute-done | bytes 55328 | tf_op jit(solution)/shard_map/ppermute | solution.py:490
  10.3 0.8 %shard_map.44.left = bf16[16,256]{1,0:T(8,128)(2,1)S(1)} custom-call(bf16[216,128]{1,0:T(8,128)(2,1)S(1)} %get-tuple-element.37.own, bf16[216,128]{1,0:T(8,128)(2,1)S(1)} %collective-permute-done.1.other, f32[32,256]{1,0:T(8,128)S(1)} %get-tuple-element.38.starts, bf16[64,256]{1,0:T(8,128)(2,1)S(1)} %get-tuple-element.39.pieces), custom_call_target="tpu_custom_call" | custom-call | flops 100000000 | bytes 1000000 | tf_op jit(solution)/shard_map/pallas_call | solution.py:458
  11.1 0.1 collective-permute-start.2
  11.2 1.0 %shard_map.45.second = bf16[192,1792]{1,0:T(8,128)(2,1)S(1)} custom-call(bf16[192,256]{1,0:T(8,128)(2,1)S(1)} %get-tuple-element.35.turned, bf16[192,256]{1,0:T(8,128)(2,1)S(1)} %get-tuple-element.36.lower, bf16[16,256]{1,0:T(8,128)(2,1)S(1)} %shard_map.44.left), custom_call_target="tpu_custom_call" | custom-call | flops 100000000 | bytes 1000000 | tf_op jit(solution)/shard_map/pallas_call | solution.py:458
  12.2 0.2 collective-permute-done.2.right
  12.4 0.4 %shard_map.46.own = bf16[216,128]{1,0:T(8,128)(2,1)S(1)} custom-call(bf16[192,1792]{1,0:T(8,128)(2,1)S(1)} %shard_map.45.second, bf16[16,256]{1,0:T(8,128)(2,1)S(1)} %collective-permute-done.2.right), custom_call_target="tpu_custom_call" | custom-call | flops 100000000 | bytes 1000000 | tf_op jit(solution)/shard_map/pallas_call | solution.py:458
  12.8 1.9 %collective-permute-start.3 = (bf16[216,128]{1,0:T(8,128)(2,1)S(1)}, bf16[216,128]{1,0:T(8,128)(2,1)S(1)}, u32[]{:S(2)}, u32[]{:S(2)}) collective-permute-start(bf16[216,128]{1,0:T(8,128)(2,1)S(1)} %shard_map.46.own), channel_id=1, source_target_pairs={{0,12},{4,8},{8,4},{12,0},{16,28},{20,24},{24,20},{28,16},{1,13},{... | collective-permute-start | bytes 165896 | tf_op jit(solution)/shard_map/ppermute | solution.py:473
  14.7 0.4 %shard_map.47 = (bf16[192,256]{1,0:T(8,128)(2,1)S(1)}, bf16[192,256]{1,0:T(8,128)(2,1)S(1)}, f32[8,128]{1,0:T(8,128)S(1)}) custom-call(bf16[216,128]{1,0:T(8,128)(2,1)S(1)} %shard_map.46.own), custom_call_target="tpu_custom_call" | custom-call | flops 100000000 | bytes 1000000 | tf_op jit(solution)/shard_map/pallas_call | solution.py:458
  15.1 1.5 %collective-permute-done.3.other = bf16[216,128]{1,0:T(8,128)(2,1)S(1)} collective-permute-done((bf16[216,128]{1,0:T(8,128)(2,1)S(1)}, bf16[216,128]{1,0:T(8,128)(2,1)S(1)}, u32[]{:S(2)}, u32[]{:S(2)}) %collective-permute-start.3) | collective-permute-done | bytes 55328 | tf_op jit(solution)/shard_map/ppermute | solution.py:473
  16.6 0.8 %shard_map.48 = (bf16[192,256]{1,0:T(8,128)(2,1)S(1)}, bf16[192,256]{1,0:T(8,128)(2,1)S(1)}, bf16[216,128]{1,0:T(8,128)(2,1)S(1)}, f32[8,128]{1,0:T(8,128)S(1)}) custom-call(bf16[192,256]{1,0:T(8,128)(2,1)S(1)} %get-tuple-element.40.wide, bf16[192,256]{1,0:T(8,128)(2,1)S(1)} %get-tuple-element.41.product, f32[8,128]{1,0:T(8,128)S(1)} %get-tuple-element.42.mean.refs_0_, ...), custom_call_target="tpu_custom_call" | custom-call | flops 100000000 | bytes 1000000 | tf_op jit(solution)/shard_map/pallas_call | solution.py:458
  17.4 3.6 %collective-permute-start.4 = (bf16[216,128]{1,0:T(8,128)(2,1)S(1)}, bf16[216,128]{1,0:T(8,128)(2,1)S(1)}, u32[]{:S(2)}, u32[]{:S(2)}) collective-permute-start(bf16[216,128]{1,0:T(8,128)(2,1)S(1)} %get-tuple-element.47.own), channel_id=1, source_target_pairs={{0,7},{1,4},{2,5},{3,6},{4,1},{5,2},{6,3},{7,0},{8,13},{9,14},{10,... | collective-permute-start | bytes 165896 | tf_op jit(solution)/shard_map/ppermute | solution.py:490
  21.0 0.4 shard_map.49
  21.4 1.6 %collective-permute-done.4.other = bf16[216,128]{1,0:T(8,128)(2,1)S(1)} collective-permute-done((bf16[216,128]{1,0:T(8,128)(2,1)S(1)}, bf16[216,128]{1,0:T(8,128)(2,1)S(1)}, u32[]{:S(2)}, u32[]{:S(2)}) %collective-permute-start.4) | collective-permute-done | bytes 55328 | tf_op jit(solution)/shard_map/ppermute | solution.py:490
  22.9 0.8 %shard_map.50.left = bf16[16,256]{1,0:T(8,128)(2,1)S(1)} custom-call(bf16[216,128]{1,0:T(8,128)(2,1)S(1)} %get-tuple-element.47.own, bf16[216,128]{1,0:T(8,128)(2,1)S(1)} %collective-permute-done.4.other, f32[32,256]{1,0:T(8,128)S(1)} %get-tuple-element.48.starts, bf16[64,256]{1,0:T(8,128)(2,1)S(1)} %get-tuple-element.49.pieces), custom_call_target="tpu_custom_call" | custom-call | flops 100000000 | bytes 1000000 | tf_op jit(solution)/shard_map/pallas_call | solution.py:458
  23.8 0.1 collective-permute-start.5
  23.9 1.0 %shard_map.51.second = bf16[192,1792]{1,0:T(8,128)(2,1)S(1)} custom-call(bf16[192,256]{1,0:T(8,128)(2,1)S(1)} %get-tuple-element.45.turned, bf16[192,256]{1,0:T(8,128)(2,1)S(1)} %get-tuple-element.46.lower, bf16[16,256]{1,0:T(8,128)(2,1)S(1)} %shard_map.50.left), custom_call_target="tpu_custom_call" | custom-call | flops 100000000 | bytes 1000000 | tf_op jit(solution)/shard_map/pallas_call | solution.py:458
  24.8 0.2 collective-permute-done.5.right
  25.0 0.4 %shard_map.52.own = bf16[216,128]{1,0:T(8,128)(2,1)S(1)} custom-call(bf16[192,1792]{1,0:T(8,128)(2,1)S(1)} %shard_map.51.second, bf16[16,256]{1,0:T(8,128)(2,1)S(1)} %collective-permute-done.5.right, f32[8,128]{1,0:T(8,128)S(1)} %get-tuple-element.50.refs_0_), custom_call_target="tpu_custom_call" | custom-call | flops 100000000 | bytes 1000000 | tf_op jit(solution)/shard_map/pallas_call | solution.py:458
  25.4 1.9 %collective-permute-start.6 = (bf16[216,128]{1,0:T(8,128)(2,1)S(1)}, bf16[216,128]{1,0:T(8,128)(2,1)S(1)}, u32[]{:S(2)}, u32[]{:S(2)}) collective-permute-start(bf16[216,128]{1,0:T(8,128)(2,1)S(1)} %shard_map.52.own), channel_id=1, source_target_pairs={{0,20},{4,16},{8,28},{12,24},{16,4},{20,0},{24,12},{28,8},{1,21},{... | collective-permute-start | bytes 165896 | tf_op jit(solution)/shard_map/ppermute | solution.py:473
  27.3 0.4 %shard_map.53 = (bf16[192,256]{1,0:T(8,128)(2,1)S(1)}, bf16[192,256]{1,0:T(8,128)(2,1)S(1)}, f32[8,128]{1,0:T(8,128)S(1)}) custom-call(bf16[216,128]{1,0:T(8,128)(2,1)S(1)} %shard_map.52.own), custom_call_target="tpu_custom_call" | custom-call | flops 100000000 | bytes 1000000 | tf_op jit(solution)/shard_map/pallas_call | solution.py:458
  27.7 1.5 %collective-permute-done.6.other = bf16[216,128]{1,0:T(8,128)(2,1)S(1)} collective-permute-done((bf16[216,128]{1,0:T(8,128)(2,1)S(1)}, bf16[216,128]{1,0:T(8,128)(2,1)S(1)}, u32[]{:S(2)}, u32[]{:S(2)}) %collective-permute-start.6) | collective-permute-done | bytes 55328 | tf_op jit(solution)/shard_map/ppermute | solution.py:473
  29.2 0.8 %shard_map.54 = (bf16[192,256]{1,0:T(8,128)(2,1)S(1)}, bf16[192,256]{1,0:T(8,128)(2,1)S(1)}, bf16[216,128]{1,0:T(8,128)(2,1)S(1)}, f32[8,128]{1,0:T(8,128)S(1)}) custom-call(bf16[192,256]{1,0:T(8,128)(2,1)S(1)} %get-tuple-element.51.wide, bf16[192,256]{1,0:T(8,128)(2,1)S(1)} %get-tuple-element.52.product, f32[8,128]{1,0:T(8,128)S(1)} %get-tuple-element.53.mean.refs_1_, ...), custom_call_target="tpu_custom_call" | custom-call | flops 100000000 | bytes 1000000 | tf_op jit(solution)/shard_map/pallas_call | solution.py:458
  30.0 3.6 %collective-permute-start.7 = (bf16[216,128]{1,0:T(8,128)(2,1)S(1)}, bf16[216,128]{1,0:T(8,128)(2,1)S(1)}, u32[]{:S(2)}, u32[]{:S(2)}) collective-permute-start(bf16[216,128]{1,0:T(8,128)(2,1)S(1)} %get-tuple-element.58.own), channel_id=1, source_target_pairs={{0,7},{1,4},{2,5},{3,6},{4,1},{5,2},{6,3},{7,0},{8,13},{9,14},{10,... | collective-permute-start | bytes 165896 | tf_op jit(solution)/shard_map/ppermute | solution.py:490
  33.6 0.3 shard_map.55
  33.8 1.7 %collective-permute-done.7.other = bf16[216,128]{1,0:T(8,128)(2,1)S(1)} collective-permute-done((bf16[216,128]{1,0:T(8,128)(2,1)S(1)}, bf16[216,128]{1,0:T(8,128)(2,1)S(1)}, u32[]{:S(2)}, u32[]{:S(2)}) %collective-permute-start.7) | collective-permute-done | bytes 55328 | tf_op jit(solution)/shard_map/ppermute | solution.py:490
  35.6 0.8 %shard_map.56.left = bf16[16,256]{1,0:T(8,128)(2,1)S(1)} custom-call(bf16[216,128]{1,0:T(8,128)(2,1)S(1)} %get-tuple-element.58.own, bf16[216,128]{1,0:T(8,128)(2,1)S(1)} %collective-permute-done.7.other, f32[32,256]{1,0:T(8,128)S(1)} %get-tuple-element.59.starts, bf16[64,256]{1,0:T(8,128)(2,1)S(1)} %get-tuple-element.60.pieces), custom_call_target="tpu_custom_call" | custom-call | flops 100000000 | bytes 1000000 | tf_op jit(solution)/shard_map/pallas_call | solution.py:458
  36.4 0.1 collective-permute-start.8
  36.5 1.0 %shard_map.57.second = bf16[192,1792]{1,0:T(8,128)(2,1)S(1)} custom-call(bf16[192,256]{1,0:T(8,128)(2,1)S(1)} %get-tuple-element.56.turned, bf16[192,256]{1,0:T(8,128)(2,1)S(1)} %get-tuple-element.57.lower, bf16[16,256]{1,0:T(8,128)(2,1)S(1)} %shard_map.56.left), custom_call_target="tpu_custom_call" | custom-call | flops 100000000 | bytes 1000000 | tf_op jit(solution)/shard_map/pallas_call | solution.py:458
  37.5 0.2 collective-permute-done.8.right
  37.6 1.4 %shard_map.58 = (f32[144,144]{1,0:T(8,128)}, f32[1,1]{1,0:T(1,128)}) custom-call(bf16[192,1792]{1,0:T(8,128)(2,1)S(1)} %shard_map.57.second, bf16[16,256]{1,0:T(8,128)(2,1)S(1)} %collective-permute-done.8.right, f32[8,128]{1,0:T(8,128)S(1)} %get-tuple-element.61.scale, f32[8,128]{1,0:T(8,128)S(1)} %get-tuple-element.42.mean.refs_0_, ...), custom_call_target="tpu_custom_call" | custom-call | flops 100000000 | bytes 1000000 | tf_op jit(solution)/shard_map/pallas_call | solution.py:458
  (1 shorter events, 0.0 us)
Async XLA Ops:
  0.6 1.8 %collective-permute-start = (f32[144,144]{1,0:T(8,128)}, f32[144,144]{1,0:T(8,128)S(1)}, u32[]{:S(2)}, u32[]{:S(2)}) collective-permute-start(f32[144,144]{1,0:T(8,128)} %bitcast.2), channel_id=1, source_target_pairs={{0,4},{4,0},{8,12},{12,8},{16,20},{20,16},{24,28},{28,24},{1,5},{5... | collective-permute-start | bytes 248840 | tf_op jit(solution)/shard_map/ppermute | solution.py:473
  1.2 0.9 %copy-start = (f32[1,1,144,144]{3,2,1,0:T(8,128)S(1)}, f32[1,1,144,144]{3,2,1,0:T(8,128)}, u32[]{:S(2)}) copy-start(f32[1,1,144,144]{3,2,1,0:T(8,128)} %param.2) | copy-start | bytes 248836
  2.1 6.3 %copy-start.1 = (f32[3,12,144]{2,1,0:T(8,128)S(1)}, f32[3,12,144]{2,1,0:T(8,128)}, u32[]{:S(2)}) copy-start(f32[3,12,144]{2,1,0:T(8,128)} %start.5) | copy-start | bytes 62212
  3.6 6.7 %collective-permute-start.1 = (bf16[216,128]{1,0:T(8,128)(2,1)S(1)}, bf16[216,128]{1,0:T(8,128)(2,1)S(1)}, u32[]{:S(2)}, u32[]{:S(2)}) collective-permute-start(bf16[216,128]{1,0:T(8,128)(2,1)S(1)} %get-tuple-element.37.own), channel_id=1, source_target_pairs={{0,7},{1,4},{2,5},{3,6},{4,1},{5,2},{6,3},{7,0},{8,13},{9,14},{10,... | collective-permute-start | bytes 165896 | tf_op jit(solution)/shard_map/ppermute | solution.py:490
  11.1 1.2 %collective-permute-start.2 = (bf16[16,256]{1,0:T(8,128)(2,1)S(1)}, bf16[16,256]{1,0:T(8,128)(2,1)S(1)}, u32[]{:S(2)}, u32[]{:S(2)}) collective-permute-start(bf16[16,256]{1,0:T(8,128)(2,1)S(1)} %shard_map.44.left), channel_id=1, source_target_pairs={{0,4},{4,0},{8,12},{12,8},{16,20},{20,16},{24,28},{28,24},{1,5},{5... | collective-permute-start | bytes 24584 | tf_op jit(solution)/shard_map/ppermute | solution.py:473
  12.8 3.8 %collective-permute-start.3 = (bf16[216,128]{1,0:T(8,128)(2,1)S(1)}, bf16[216,128]{1,0:T(8,128)(2,1)S(1)}, u32[]{:S(2)}, u32[]{:S(2)}) collective-permute-start(bf16[216,128]{1,0:T(8,128)(2,1)S(1)} %shard_map.46.own), channel_id=1, source_target_pairs={{0,12},{4,8},{8,4},{12,0},{16,28},{20,24},{24,20},{28,16},{1,13},{... | collective-permute-start | bytes 165896 | tf_op jit(solution)/shard_map/ppermute | solution.py:473
  17.4 5.6 %collective-permute-start.4 = (bf16[216,128]{1,0:T(8,128)(2,1)S(1)}, bf16[216,128]{1,0:T(8,128)(2,1)S(1)}, u32[]{:S(2)}, u32[]{:S(2)}) collective-permute-start(bf16[216,128]{1,0:T(8,128)(2,1)S(1)} %get-tuple-element.47.own), channel_id=1, source_target_pairs={{0,7},{1,4},{2,5},{3,6},{4,1},{5,2},{6,3},{7,0},{8,13},{9,14},{10,... | collective-permute-start | bytes 165896 | tf_op jit(solution)/shard_map/ppermute | solution.py:490
  23.8 1.2 %collective-permute-start.5 = (bf16[16,256]{1,0:T(8,128)(2,1)S(1)}, bf16[16,256]{1,0:T(8,128)(2,1)S(1)}, u32[]{:S(2)}, u32[]{:S(2)}) collective-permute-start(bf16[16,256]{1,0:T(8,128)(2,1)S(1)} %shard_map.50.left), channel_id=1, source_target_pairs={{0,4},{4,0},{8,12},{12,8},{16,20},{20,16},{24,28},{28,24},{1,5},{5... | collective-permute-start | bytes 24584 | tf_op jit(solution)/shard_map/ppermute | solution.py:473
  25.4 3.8 %collective-permute-start.6 = (bf16[216,128]{1,0:T(8,128)(2,1)S(1)}, bf16[216,128]{1,0:T(8,128)(2,1)S(1)}, u32[]{:S(2)}, u32[]{:S(2)}) collective-permute-start(bf16[216,128]{1,0:T(8,128)(2,1)S(1)} %shard_map.52.own), channel_id=1, source_target_pairs={{0,20},{4,16},{8,28},{12,24},{16,4},{20,0},{24,12},{28,8},{1,21},{... | collective-permute-start | bytes 165896 | tf_op jit(solution)/shard_map/ppermute | solution.py:473
  30.0 5.6 %collective-permute-start.7 = (bf16[216,128]{1,0:T(8,128)(2,1)S(1)}, bf16[216,128]{1,0:T(8,128)(2,1)S(1)}, u32[]{:S(2)}, u32[]{:S(2)}) collective-permute-start(bf16[216,128]{1,0:T(8,128)(2,1)S(1)} %get-tuple-element.58.own), channel_id=1, source_target_pairs={{0,7},{1,4},{2,5},{3,6},{4,1},{5,2},{6,3},{7,0},{8,13},{9,14},{10,... | collective-permute-start | bytes 165896 | tf_op jit(solution)/shard_map/ppermute | solution.py:490
  36.4 1.2 %collective-permute-start.8 = (bf16[16,256]{1,0:T(8,128)(2,1)S(1)}, bf16[16,256]{1,0:T(8,128)(2,1)S(1)}, u32[]{:S(2)}, u32[]{:S(2)}) collective-permute-start(bf16[16,256]{1,0:T(8,128)(2,1)S(1)} %shard_map.56.left), channel_id=1, source_target_pairs={{0,4},{4,0},{8,12},{12,8},{16,20},{20,16},{24,28},{28,24},{1,5},{5... | collective-permute-start | bytes 24584 | tf_op jit(solution)/shard_map/ppermute | solution.py:473

commit v10 on v9

--- a/solution.py
+++ b/solution.py
@@ -58,6 +58,13 @@
     s, t = group(j), minor(j)
     source = jnp.where(mirror, t * CHI + s, s * CHI + t)
     return one_hot((i == source) & (s < CHI) & (t < CHI))
+
+
+def gather_matrix(mirror):
+    i, j = iota((LANES, CHI * CHI), 0), iota((LANES, CHI * CHI), 1)
+    s, t = group(i), minor(i)
+    source = jnp.where(mirror, t * CHI + s, s * CHI + t)
+    return one_hot((j == source) & (s < CHI) & (t < CHI))
 
 
 def swapped_tiles(x, fold, other=None):
@@ -104,6 +111,27 @@
     return jnp.concatenate([jnp.concatenate(pair, axis=1) for pair in tiles], axis=0)
 
 
+def joined(x):
+    x = spaced(x)
+    lane = iota((PAD, 128), 1)
+    sides = []
+    for k in range(CHI):
+        at = ROWS + (k >> 3) * PAD
+        shift = -(k & 7) * PAD % 128
+        side = pltpu.roll(x[at : at + PAD], shift, 1) if shift else x[at : at + PAD]
+        sides.append(jnp.where(lane < PAD, side, jnp.zeros_like(side)))
+    return jnp.concatenate([x[:ROWS], jnp.concatenate(sides, axis=0)], axis=1)
+
+
+def split(x):
+    lane_group = group(iota((PAD, 128), 1))
+    tails = [jnp.zeros((PAD, 128), x.dtype)] * 2
+    for k in range(CHI):
+        block = x[k * PAD : (k + 1) * PAD, 128:]
+        tails[k >> 3] = jnp.where(lane_group == (k & 7), block, tails[k >> 3])
+    return jnp.concatenate([x[:, :128], *tails], axis=0)
+
+
 def product_both(a, b, scale=None):
     zero = jnp.zeros((PAD, b.shape[1]), b.dtype)
     blocks = [b[s * PAD : (s + 1) * PAD] if s < CHI else zero for s in range(PAD)]
@@ -186,8 +214,13 @@
     return compact(jnp.concatenate([t[0] for t in tiles] + [side], axis=0))
 
 
-def turn(first):
-    return widen(row_swap(first.T[:ROWS]))
+def turn(first, compact_lanes):
+    if not compact_lanes:
+        return widen(row_swap(first.T[:ROWS]))
+    legs = first.T[: CHI * CHI].astype(F32).reshape(CHI, CHI, ROWS)
+    rest = jnp.zeros((CHI, PAD - CHI, ROWS), F32)
+    legs = jnp.concatenate([jnp.transpose(legs, (1, 0, 2)), rest], axis=1)
+    return widen(legs.reshape(ROWS, ROWS).astype(BF16))
 
 
 def start_body(start, swap):
@@ -298,10 +331,10 @@
     return s, entry - s * CHI
 
 
-def packing():
-    s, t = packed_pair(iota((LANES, ROWS), 0))
-    j = iota((LANES, ROWS), 1)
-    return one_hot((group(j) == s) & (minor(j) == t))
+def packing(compact_lanes):
+    s, t = packed_pair(iota((LANES, LANES), 1))
+    j = iota((LANES, LANES), 0)
+    return one_hot(j == (s * CHI + t if compact_lanes else s * PAD + t))
 
 
 def first_second(turned, lower, left, second_ref, first_ref):
@@ -333,10 +366,18 @@
             second_ref[rows, at : at + 128] = tails[side]
 
 
-def third(second_ref, right, kron_ref):
-    values = jnp.concatenate([right] * PAD, axis=0).T.astype(F32)
-    lane_group = group(iota((CHI * CHI, LANES), 1))
-    lane_group = jnp.where(lane_group < CHI, lane_group, lane_group - FOLD // PAD)
+def third(second_ref, right, kron_ref, packed):
+    lane = iota((CHI * CHI, LANES), 1)
+    if packed:
+        right = right.astype(F32)
+        rest = jnp.concatenate([right[128 % CHI : CHI], right[:CHI]], axis=0)
+        rows = [right[:CHI]] * (128 // CHI) + [right[: 128 % CHI]] + [rest] * 8
+        values = jnp.concatenate(rows, axis=0).astype(BF16)
+        lane_group = packed_pair(lane)[0]
+    else:
+        values = jnp.concatenate([right] * PAD, axis=0)
+        lane_group = jnp.minimum(group(lane), CHI)
+    values = values.T.astype(F32)
     entry = iota((CHI * CHI, LANES), 0)
     kept = lax.shift_right_logical(entry * 171, 11) == lane_group
     for k in range(CHI):
@@ -375,11 +416,11 @@
     cast_o[...] = own[...].astype(BF16)
 
 
-def first_gram_kernel(own, other, first_o, second_o, gram_o):
+def first_gram_kernel(own, other, mine_o, theirs_o, gram_o):
     own_first, _, own_lower, mirror = roles(0)
     mine = placed(own[...], mirror, own_lower)
     theirs = placed(other[...].astype(BF16), mirror, jnp.logical_not(own_lower))
-    first_o[...], second_o[...] = pick(own_first, mine, theirs)
+    mine_o[...], theirs_o[...] = mine, theirs
     products = pick(own_first, product_part(mine), product_part(theirs))
     gram_o[...] = outer_part(*products)
 
@@ -395,25 +436,24 @@
 
 
 def own_kernel(own, wide_o, product_o, mean_o):
-    wide = unfold(spaced(own[...]))
+    wide = joined(own[...])
     wide_o[...] = wide
     product_o[...], mean_o[...] = scaled_product(wide)
 
 
-def gram_kernel(level, wide, product, mean, other, first_o, second_o, gram_o, scale_o):
-    own_first = roles(level)[0]
-    theirs = unfold(spaced(other[...]))
-    other_product, other_mean = scaled_product(theirs)
-    gram_o[...] = outer_part(*pick(own_first, product[...], other_product))
-    first_o[...], second_o[...] = pick(own_first, wide[...], theirs)
+def gram_kernel(level, product, mean, other, gram_o, scale_o):
+    other_product, other_mean = scaled_product(joined(other[...]))
+    gram_o[...] = outer_part(*pick(roles(level)[0], product[...], other_product))
     scale_o[...] = lax.rsqrt(mean[...]) * lax.rsqrt(other_mean)
 
 
-def turn_kernel(level, first, second, start, turned_o, lower_o, starts_o, pieces_o):
-    turned_o[...] = turn(first[...])
-    lower_o[...] = mm(second[:, :ROWS], packing(), NT).astype(BF16)
+def turn_kernel(level, own, other, start, turned_o, lower_o, starts_o, pieces_o):
+    later = level > 0
+    own_first, first_upper, _, _ = roles(level)
+    first, second = pick(own_first, own[...], joined(other[...]) if later else other[...])
+    turned_o[...] = turn(first, later)
+    lower_o[...] = mm(second, packing(later)).astype(BF16)
     plain, turned = start_body(start[level], swap_matrix())
-    first_upper = roles(level)[1]
     here = jnp.where(first_upper, plain, turned)
     starts_o[:PAD] = here
     starts_o[PAD:] = jnp.where(first_upper, turned, plain)
@@ -429,10 +469,7 @@
 
 def third_kernel(second, right, *refs):
     *scales, next_o, kron = refs
-    merged = third(second, right[...], kron)
-    half = ROWS // 2
-    side = folded(merged[:half, 128:], merged[half:, 128:])
-    merged = jnp.concatenate([merged[:, :128], side], axis=0)
+    merged = split(third(second, right[...], kron, True))
     for scale in scales:
         merged = merged * scale[:1]
     next_o[...] = compact(merged)
@@ -440,12 +477,11 @@
 
 def last_kernel(second, right, scale, *refs):
     *means, coarse_o, log_o, kron = refs
-    merged = third(second, right[...], kron) * twice(scale[:1], LANES)
-    lines = jnp.sum(merged * merged, axis=0, keepdims=True)
-    mean = mean_square(lines[:, :128] + 0.5 * lines[:, 128:])
+    merged = third(second, right[...], kron, False) * twice(scale[:1], LANES)
+    mean = mean_square(jnp.sum(merged * merged, axis=0, keepdims=True))
     log_o[...] = 0.5 * sum(jnp.log(m[:1, :1]) for m in [*means, mean])
     wide = block_swap(merged.astype(BF16))
-    narrow = mm(wide, spread_matrix(roles(LEVELS - 1)[3]), NT)
+    narrow = mm(wide, gather_matrix(roles(LEVELS - 1)[3]))
     narrow = narrow * twice(lax.rsqrt(mean[:1]), LANES)[:, : CHI * CHI]
     legs = jnp.transpose(narrow.reshape(CHI, PAD, CHI * CHI)[:, :CHI], (1, 0, 2))
     coarse_o[...] = legs.reshape(CHI * CHI, CHI * CHI)
@@ -492,7 +528,9 @@
 
 def per_device(site_tensors, start_basis):
     square = CHI * CHI
-    mat, packed, one = ((ROWS, LANES), BF16), ((CHI * CHI * 3 // 2, 128), BF16), ((8, 128), F32)
+    mat, one = ((ROWS, LANES), BF16), ((8, 128), F32)
+    gram_shape = ((CHI * CHI * 3 // 2, 128), BF16)
+    sent = ((CHI * (CHI + 2), 128), BF16)
     kron, firsts = [pltpu.VMEM((SECOND, LANES), BF16)], [pltpu.VMEM((CHI * ROWS, LANES), BF16)]
     scales, means = [], []
     own = site_tensors[0, 0]
@@ -500,24 +538,24 @@
         if level == 0:
             other = from_partner(own, 1)
             (own,) = call(cast_kernel, [((square, square), BF16)])(own)
-            first, lower, gram = call(first_gram_kernel, [mat, mat, packed])(own, other)
+            own, other, gram = call(first_gram_kernel, [mat, mat, gram_shape])(own, other)
         else:
             other = from_partner(own, 1 << level | 1)
-            wide, product, mean = call(own_kernel, [mat, mat, one])(own)
-            first, lower, gram, scale = call(
-                functools.partial(gram_kernel, level), [mat, mat, packed, one]
-            )(wide, product, mean, other)
+            own, product, mean = call(own_kernel, [mat, mat, one])(own)
+            gram, scale = call(functools.partial(gram_kernel, level), [gram_shape, one])(
+                product, mean, other
+            )
             scales, means = [scale], [*means, mean]
         gram_other = from_bond(gram)
         turned, lower, starts, pieces = call(
             functools.partial(turn_kernel, level),
             [mat, mat, ((2 * PAD, LANES), F32), ((4 * PAD, LANES), BF16)],
-        )(first, lower, start_basis)
+        )(own, other, start_basis)
         (left,) = call(iso_kernel, [((PAD, LANES), BF16)])(gram, gram_other, starts, pieces)
         right = from_partner(left, 1)
         (second,) = call(second_kernel, [((ROWS, SECOND), BF16)], firsts)(turned, lower, left)
         if level < LEVELS - 1:
-            (own,) = call(third_kernel, [packed], kron)(second, right, *scales)
+            (own,) = call(third_kernel, [sent], kron)(second, right, *scales)
         else:
             coarse, log_total = call(last_kernel, [((square, square), F32), ((1, 1), F32)], kron)(
                 second, right, *scales, *means

time: 39.2 us -> 38.8 us (0.990)
    ppermute x6, waiting for transfers between devices: 3.82 us -> 3.39 us  [from_partner(): return lax.ppermute(array, 'row', [(i, i ^ flip) for i in range(count)])]
where the time goes in v10:
time: 38.8 us; the launch traced here: 38.6 us
  starting transfers between devices  16.2 us (42%)
  Pallas kernels  12.2 us (31%)
  waiting for transfers between devices  8.45 us (22%)
  local copies, waits for them, and re-layouts  0.92 us (2%)
  between operations  0.78 us (2%)
    pallas_call x18, Pallas kernels, run(): pl.pallas_call(kernel, out_shape=[jax.ShapeDtypeStruct(s, d) for s, d in...  12.2 us
    ppermute x3, starting transfers between devices, from_bond(): return lax.ppermute(array, ('row', 'col'), pairs)  11.8 us
    ppermute x3, waiting for transfers between devices, from_bond(): return lax.ppermute(array, ('row', 'col'), pairs)  5.07 us
    ppermute x6, starting transfers between devices, from_partner(): return lax.ppermute(array, 'row', [(i, i ^ flip) for i in range(count)])  4.44 us
    ppermute x6, waiting for transfers between devices, from_partner(): return lax.ppermute(array, 'row', [(i, i ^ flip) for i in range(count)])  3.39 us
    unnamed x4, local copies, waits for them, and re-layouts  0.92 us
  transfers between devices with their start and end apart: 9, of which 9 were waited for; matrix products, arithmetic and copies ran while one was open for 0% of the time, Pallas kernels for 12%

profile of v10, /device:TPU:0, one launch (start us, length us, event | category | flops | bytes accessed | tf_op | source)
XLA Modules:
  0.0 38.6 jit_solution(7186845635406281683)
XLA Ops:
  0.6 0.6 %collective-permute-start = (f32[144,144]{1,0:T(8,128)}, f32[144,144]{1,0:T(8,128)S(1)}, u32[]{:S(2)}, u32[]{:S(2)}) collective-permute-start(f32[144,144]{1,0:T(8,128)} %bitcast.2), channel_id=1, source_target_pairs={{0,4},{4,0},{8,12},{12,8},{16,20},{20,16},{24,28},{28,24},{1,5},{5... | collective-permute-start | bytes 248840 | tf_op jit(solution)/shard_map/ppermute | solution.py:509
  1.2 0.0 copy-start
  1.2 0.9 %copy-done = f32[1,1,144,144]{3,2,1,0:T(8,128)S(1)} copy-done((f32[1,1,144,144]{3,2,1,0:T(8,128)S(1)}, f32[1,1,144,144]{3,2,1,0:T(8,128)}, u32[]{:S(2)}) %copy-start) | copy-done | bytes 82968
  2.1 0.0 copy-start.1
  2.1 0.3 collective-permute-done.other
  2.4 1.2 %shard_map.42 = (bf16[192,256]{1,0:T(8,128)(2,1)S(1)}, bf16[192,256]{1,0:T(8,128)(2,1)S(1)}, bf16[216,128]{1,0:T(8,128)(2,1)S(1)}) custom-call(bf16[144,144]{1,0:T(8,128)(2,1)S(1)} %shard_map.41.own, f32[144,144]{1,0:T(8,128)S(1)} %collective-permute-done.other), custom_call_target="tpu_custom_call" | custom-call | flops 100000000 | bytes 1000000 | tf_op jit(solution)/shard_map/pallas_call | solution.py:494
  3.6 4.8 %collective-permute-start.1 = (bf16[216,128]{1,0:T(8,128)(2,1)S(1)}, bf16[216,128]{1,0:T(8,128)(2,1)S(1)}, u32[]{:S(2)}, u32[]{:S(2)}) collective-permute-start(bf16[216,128]{1,0:T(8,128)(2,1)S(1)} %get-tuple-element.33.own), channel_id=1, source_target_pairs={{0,7},{1,4},{2,5},{3,6},{4,1},{5,2},{6,3},{7,0},{8,13},{9,14},{10,... | collective-permute-start | bytes 165896 | tf_op jit(solution)/shard_map/ppermute | solution.py:526
  8.4 0.0 copy-done.1
  8.4 0.4 shard_map.43
  8.8 1.6 %collective-permute-done.1.other = bf16[216,128]{1,0:T(8,128)(2,1)S(1)} collective-permute-done((bf16[216,128]{1,0:T(8,128)(2,1)S(1)}, bf16[216,128]{1,0:T(8,128)(2,1)S(1)}, u32[]{:S(2)}, u32[]{:S(2)}) %collective-permute-start.1) | collective-permute-done | bytes 55328 | tf_op jit(solution)/shard_map/ppermute | solution.py:526
  10.3 0.8 %shard_map.44.left = bf16[16,256]{1,0:T(8,128)(2,1)S(1)} custom-call(bf16[216,128]{1,0:T(8,128)(2,1)S(1)} %get-tuple-element.33.own, bf16[216,128]{1,0:T(8,128)(2,1)S(1)} %collective-permute-done.1.other, f32[32,256]{1,0:T(8,128)S(1)} %get-tuple-element.34.starts, bf16[64,256]{1,0:T(8,128)(2,1)S(1)} %get-tuple-element.35.pieces), custom_call_target="tpu_custom_call" | custom-call | flops 100000000 | bytes 1000000 | tf_op jit(solution)/shard_map/pallas_call | solution.py:494
  11.1 0.1 collective-permute-start.2
  11.2 1.0 %shard_map.45.second = bf16[192,1792]{1,0:T(8,128)(2,1)S(1)} custom-call(bf16[192,256]{1,0:T(8,128)(2,1)S(1)} %get-tuple-element.31.turned, bf16[192,256]{1,0:T(8,128)(2,1)S(1)} %get-tuple-element.32.lower, bf16[16,256]{1,0:T(8,128)(2,1)S(1)} %shard_map.44.left), custom_call_target="tpu_custom_call" | custom-call | flops 100000000 | bytes 1000000 | tf_op jit(solution)/shard_map/pallas_call | solution.py:494
  12.2 0.2 collective-permute-done.2.right
  12.4 0.4 %shard_map.46.own = bf16[168,128]{1,0:T(8,128)(2,1)S(1)} custom-call(bf16[192,1792]{1,0:T(8,128)(2,1)S(1)} %shard_map.45.second, bf16[16,256]{1,0:T(8,128)(2,1)S(1)} %collective-permute-done.2.right), custom_call_target="tpu_custom_call" | custom-call | flops 100000000 | bytes 1000000 | tf_op jit(solution)/shard_map/pallas_call | solution.py:494
  12.8 1.9 %collective-permute-start.3 = (bf16[168,128]{1,0:T(8,128)(2,1)S(1)}, bf16[168,128]{1,0:T(8,128)(2,1)S(1)}, u32[]{:S(2)}, u32[]{:S(2)}) collective-permute-start(bf16[168,128]{1,0:T(8,128)(2,1)S(1)} %shard_map.46.own), channel_id=1, source_target_pairs={{0,12},{4,8},{8,4},{12,0},{16,28},{20,24},{24,20},{28,16},{1,13},{... | collective-permute-start | bytes 129032 | tf_op jit(solution)/shard_map/ppermute | solution.py:509
  14.7 0.4 %shard_map.47 = (bf16[192,256]{1,0:T(8,128)(2,1)S(1)}, bf16[192,256]{1,0:T(8,128)(2,1)S(1)}, f32[8,128]{1,0:T(8,128)S(1)}) custom-call(bf16[168,128]{1,0:T(8,128)(2,1)S(1)} %shard_map.46.own), custom_call_target="tpu_custom_call" | custom-call | flops 100000000 | bytes 1000000 | tf_op jit(solution)/shard_map/pallas_call | solution.py:494
  15.1 1.3 %collective-permute-done.3.other = bf16[168,128]{1,0:T(8,128)(2,1)S(1)} collective-permute-done((bf16[168,128]{1,0:T(8,128)(2,1)S(1)}, bf16[168,128]{1,0:T(8,128)(2,1)S(1)}, u32[]{:S(2)}, u32[]{:S(2)}) %collective-permute-start.3) | collective-permute-done | bytes 43040 | tf_op jit(solution)/shard_map/ppermute | solution.py:509
  16.4 0.8 %shard_map.49 = (bf16[216,128]{1,0:T(8,128)(2,1)S(1)}, f32[8,128]{1,0:T(8,128)S(1)}) custom-call(bf16[192,256]{1,0:T(8,128)(2,1)S(1)} %get-tuple-element.39.product, f32[8,128]{1,0:T(8,128)S(1)} %get-tuple-element.40.mean.refs_0_, bf16[168,128]{1,0:T(8,128)(2,1)S(1)} %collective-permute-done.3.other), custom_call_target="tpu_custom_call" | custom-call | flops 100000000 | bytes 1000000 | tf_op jit(solution)/shard_map/pallas_call | solution.py:494
  17.2 3.5 %collective-permute-start.4 = (bf16[216,128]{1,0:T(8,128)(2,1)S(1)}, bf16[216,128]{1,0:T(8,128)(2,1)S(1)}, u32[]{:S(2)}, u32[]{:S(2)}) collective-permute-start(bf16[216,128]{1,0:T(8,128)(2,1)S(1)} %get-tuple-element.41.own), channel_id=1, source_target_pairs={{0,7},{1,4},{2,5},{3,6},{4,1},{5,2},{6,3},{7,0},{8,13},{9,14},{10,... | collective-permute-start | bytes 165896 | tf_op jit(solution)/shard_map/ppermute | solution.py:526
  20.7 0.4 shard_map.48
  21.1 1.7 %collective-permute-done.4.other = bf16[216,128]{1,0:T(8,128)(2,1)S(1)} collective-permute-done((bf16[216,128]{1,0:T(8,128)(2,1)S(1)}, bf16[216,128]{1,0:T(8,128)(2,1)S(1)}, u32[]{:S(2)}, u32[]{:S(2)}) %collective-permute-start.4) | collective-permute-done | bytes 55328 | tf_op jit(solution)/shard_map/ppermute | solution.py:526
  22.8 0.8 %shard_map.50.left = bf16[16,256]{1,0:T(8,128)(2,1)S(1)} custom-call(bf16[216,128]{1,0:T(8,128)(2,1)S(1)} %get-tuple-element.41.own, bf16[216,128]{1,0:T(8,128)(2,1)S(1)} %collective-permute-done.4.other, f32[32,256]{1,0:T(8,128)S(1)} %get-tuple-element.42.starts, bf16[64,256]{1,0:T(8,128)(2,1)S(1)} %get-tuple-element.43.pieces), custom_call_target="tpu_custom_call" | custom-call | flops 100000000 | bytes 1000000 | tf_op jit(solution)/shard_map/pallas_call | solution.py:494
  23.6 0.1 collective-permute-start.5
  23.7 1.0 %shard_map.51.second = bf16[192,1792]{1,0:T(8,128)(2,1)S(1)} custom-call(bf16[192,256]{1,0:T(8,128)(2,1)S(1)} %get-tuple-element.37.turned, bf16[192,256]{1,0:T(8,128)(2,1)S(1)} %get-tuple-element.38.lower, bf16[16,256]{1,0:T(8,128)(2,1)S(1)} %shard_map.50.left), custom_call_target="tpu_custom_call" | custom-call | flops 100000000 | bytes 1000000 | tf_op jit(solution)/shard_map/pallas_call | solution.py:494
  24.7 0.2 collective-permute-done.5.right
  24.8 0.4 %shard_map.52.own = bf16[168,128]{1,0:T(8,128)(2,1)S(1)} custom-call(bf16[192,1792]{1,0:T(8,128)(2,1)S(1)} %shard_map.51.second, bf16[16,256]{1,0:T(8,128)(2,1)S(1)} %collective-permute-done.5.right, f32[8,128]{1,0:T(8,128)S(1)} %get-tuple-element.44.refs_0_), custom_call_target="tpu_custom_call" | custom-call | flops 100000000 | bytes 1000000 | tf_op jit(solution)/shard_map/pallas_call | solution.py:494
  25.3 1.8 %collective-permute-start.6 = (bf16[168,128]{1,0:T(8,128)(2,1)S(1)}, bf16[168,128]{1,0:T(8,128)(2,1)S(1)}, u32[]{:S(2)}, u32[]{:S(2)}) collective-permute-start(bf16[168,128]{1,0:T(8,128)(2,1)S(1)} %shard_map.52.own), channel_id=1, source_target_pairs={{0,20},{4,16},{8,28},{12,24},{16,4},{20,0},{24,12},{28,8},{1,21},{... | collective-permute-start | bytes 129032 | tf_op jit(solution)/shard_map/ppermute | solution.py:509
  27.1 0.4 %shard_map.53 = (bf16[192,256]{1,0:T(8,128)(2,1)S(1)}, bf16[192,256]{1,0:T(8,128)(2,1)S(1)}, f32[8,128]{1,0:T(8,128)S(1)}) custom-call(bf16[168,128]{1,0:T(8,128)(2,1)S(1)} %shard_map.52.own), custom_call_target="tpu_custom_call" | custom-call | flops 100000000 | bytes 1000000 | tf_op jit(solution)/shard_map/pallas_call | solution.py:494
  27.5 1.3 %collective-permute-done.6.other = bf16[168,128]{1,0:T(8,128)(2,1)S(1)} collective-permute-done((bf16[168,128]{1,0:T(8,128)(2,1)S(1)}, bf16[168,128]{1,0:T(8,128)(2,1)S(1)}, u32[]{:S(2)}, u32[]{:S(2)}) %collective-permute-start.6) | collective-permute-done | bytes 43040 | tf_op jit(solution)/shard_map/ppermute | solution.py:509
  28.8 0.8 %shard_map.55 = (bf16[216,128]{1,0:T(8,128)(2,1)S(1)}, f32[8,128]{1,0:T(8,128)S(1)}) custom-call(bf16[192,256]{1,0:T(8,128)(2,1)S(1)} %get-tuple-element.48.product, f32[8,128]{1,0:T(8,128)S(1)} %get-tuple-element.49.mean.refs_1_, bf16[168,128]{1,0:T(8,128)(2,1)S(1)} %collective-permute-done.6.other), custom_call_target="tpu_custom_call" | custom-call | flops 100000000 | bytes 1000000 | tf_op jit(solution)/shard_map/pallas_call | solution.py:494
  29.6 3.5 %collective-permute-start.7 = (bf16[216,128]{1,0:T(8,128)(2,1)S(1)}, bf16[216,128]{1,0:T(8,128)(2,1)S(1)}, u32[]{:S(2)}, u32[]{:S(2)}) collective-permute-start(bf16[216,128]{1,0:T(8,128)(2,1)S(1)} %get-tuple-element.50.own), channel_id=1, source_target_pairs={{0,7},{1,4},{2,5},{3,6},{4,1},{5,2},{6,3},{7,0},{8,13},{9,14},{10,... | collective-permute-start | bytes 165896 | tf_op jit(solution)/shard_map/ppermute | solution.py:526
  33.1 0.3 shard_map.54
  33.4 1.8 %collective-permute-done.7.other = bf16[216,128]{1,0:T(8,128)(2,1)S(1)} collective-permute-done((bf16[216,128]{1,0:T(8,128)(2,1)S(1)}, bf16[216,128]{1,0:T(8,128)(2,1)S(1)}, u32[]{:S(2)}, u32[]{:S(2)}) %collective-permute-start.7) | collective-permute-done | bytes 55328 | tf_op jit(solution)/shard_map/ppermute | solution.py:526
  35.2 0.8 %shard_map.56.left = bf16[16,256]{1,0:T(8,128)(2,1)S(1)} custom-call(bf16[216,128]{1,0:T(8,128)(2,1)S(1)} %get-tuple-element.50.own, bf16[216,128]{1,0:T(8,128)(2,1)S(1)} %collective-permute-done.7.other, f32[32,256]{1,0:T(8,128)S(1)} %get-tuple-element.51.starts, bf16[64,256]{1,0:T(8,128)(2,1)S(1)} %get-tuple-element.52.pieces), custom_call_target="tpu_custom_call" | custom-call | flops 100000000 | bytes 1000000 | tf_op jit(solution)/shard_map/pallas_call | solution.py:494
  36.0 0.1 collective-permute-start.8
  36.1 1.0 %shard_map.57.second = bf16[192,1792]{1,0:T(8,128)(2,1)S(1)} custom-call(bf16[192,256]{1,0:T(8,128)(2,1)S(1)} %get-tuple-element.46.turned, bf16[192,256]{1,0:T(8,128)(2,1)S(1)} %get-tuple-element.47.lower, bf16[16,256]{1,0:T(8,128)(2,1)S(1)} %shard_map.56.left), custom_call_target="tpu_custom_call" | custom-call | flops 100000000 | bytes 1000000 | tf_op jit(solution)/shard_map/pallas_call | solution.py:494
  37.1 0.2 collective-permute-done.8.right
  37.3 1.4 %shard_map.58 = (f32[144,144]{1,0:T(8,128)}, f32[1,1]{1,0:T(1,128)}) custom-call(bf16[192,1792]{1,0:T(8,128)(2,1)S(1)} %shard_map.57.second, bf16[16,256]{1,0:T(8,128)(2,1)S(1)} %collective-permute-done.8.right, f32[8,128]{1,0:T(8,128)S(1)} %get-tuple-element.53.scale, f32[8,128]{1,0:T(8,128)S(1)} %get-tuple-element.40.mean.refs_0_, ...), custom_call_target="tpu_custom_call" | custom-call | flops 100000000 | bytes 1000000 | tf_op jit(solution)/shard_map/pallas_call | solution.py:494
  (1 shorter events, 0.0 us)
Async XLA Ops:
  0.6 1.8 %collective-permute-start = (f32[144,144]{1,0:T(8,128)}, f32[144,144]{1,0:T(8,128)S(1)}, u32[]{:S(2)}, u32[]{:S(2)}) collective-permute-start(f32[144,144]{1,0:T(8,128)} %bitcast.2), channel_id=1, source_target_pairs={{0,4},{4,0},{8,12},{12,8},{16,20},{20,16},{24,28},{28,24},{1,5},{5... | collective-permute-start | bytes 248840 | tf_op jit(solution)/shard_map/ppermute | solution.py:509
  1.2 0.9 %copy-start = (f32[1,1,144,144]{3,2,1,0:T(8,128)S(1)}, f32[1,1,144,144]{3,2,1,0:T(8,128)}, u32[]{:S(2)}) copy-start(f32[1,1,144,144]{3,2,1,0:T(8,128)} %param.2) | copy-start | bytes 248836
  2.1 6.3 %copy-start.1 = (f32[3,12,144]{2,1,0:T(8,128)S(1)}, f32[3,12,144]{2,1,0:T(8,128)}, u32[]{:S(2)}) copy-start(f32[3,12,144]{2,1,0:T(8,128)} %start.5) | copy-start | bytes 62212
  3.6 6.7 %collective-permute-start.1 = (bf16[216,128]{1,0:T(8,128)(2,1)S(1)}, bf16[216,128]{1,0:T(8,128)(2,1)S(1)}, u32[]{:S(2)}, u32[]{:S(2)}) collective-permute-start(bf16[216,128]{1,0:T(8,128)(2,1)S(1)} %get-tuple-element.33.own), channel_id=1, source_target_pairs={{0,7},{1,4},{2,5},{3,6},{4,1},{5,2},{6,3},{7,0},{8,13},{9,14},{10,... | collective-permute-start | bytes 165896 | tf_op jit(solution)/shard_map/ppermute | solution.py:526
  11.1 1.2 %collective-permute-start.2 = (bf16[16,256]{1,0:T(8,128)(2,1)S(1)}, bf16[16,256]{1,0:T(8,128)(2,1)S(1)}, u32[]{:S(2)}, u32[]{:S(2)}) collective-permute-start(bf16[16,256]{1,0:T(8,128)(2,1)S(1)} %shard_map.44.left), channel_id=1, source_target_pairs={{0,4},{4,0},{8,12},{12,8},{16,20},{20,16},{24,28},{28,24},{1,5},{5... | collective-permute-start | bytes 24584 | tf_op jit(solution)/shard_map/ppermute | solution.py:509
  12.8 3.6 %collective-permute-start.3 = (bf16[168,128]{1,0:T(8,128)(2,1)S(1)}, bf16[168,128]{1,0:T(8,128)(2,1)S(1)}, u32[]{:S(2)}, u32[]{:S(2)}) collective-permute-start(bf16[168,128]{1,0:T(8,128)(2,1)S(1)} %shard_map.46.own), channel_id=1, source_target_pairs={{0,12},{4,8},{8,4},{12,0},{16,28},{20,24},{24,20},{28,16},{1,13},{... | collective-permute-start | bytes 129032 | tf_op jit(solution)/shard_map/ppermute | solution.py:509
  17.2 5.6 %collective-permute-start.4 = (bf16[216,128]{1,0:T(8,128)(2,1)S(1)}, bf16[216,128]{1,0:T(8,128)(2,1)S(1)}, u32[]{:S(2)}, u32[]{:S(2)}) collective-permute-start(bf16[216,128]{1,0:T(8,128)(2,1)S(1)} %get-tuple-element.41.own), channel_id=1, source_target_pairs={{0,7},{1,4},{2,5},{3,6},{4,1},{5,2},{6,3},{7,0},{8,13},{9,14},{10,... | collective-permute-start | bytes 165896 | tf_op jit(solution)/shard_map/ppermute | solution.py:526
  23.6 1.2 %collective-permute-start.5 = (bf16[16,256]{1,0:T(8,128)(2,1)S(1)}, bf16[16,256]{1,0:T(8,128)(2,1)S(1)}, u32[]{:S(2)}, u32[]{:S(2)}) collective-permute-start(bf16[16,256]{1,0:T(8,128)(2,1)S(1)} %shard_map.50.left), channel_id=1, source_target_pairs={{0,4},{4,0},{8,12},{12,8},{16,20},{20,16},{24,28},{28,24},{1,5},{5... | collective-permute-start | bytes 24584 | tf_op jit(solution)/shard_map/ppermute | solution.py:509
  25.3 3.5 %collective-permute-start.6 = (bf16[168,128]{1,0:T(8,128)(2,1)S(1)}, bf16[168,128]{1,0:T(8,128)(2,1)S(1)}, u32[]{:S(2)}, u32[]{:S(2)}) collective-permute-start(bf16[168,128]{1,0:T(8,128)(2,1)S(1)} %shard_map.52.own), channel_id=1, source_target_pairs={{0,20},{4,16},{8,28},{12,24},{16,4},{20,0},{24,12},{28,8},{1,21},{... | collective-permute-start | bytes 129032 | tf_op jit(solution)/shard_map/ppermute | solution.py:509
  29.6 5.6 %collective-permute-start.7 = (bf16[216,128]{1,0:T(8,128)(2,1)S(1)}, bf16[216,128]{1,0:T(8,128)(2,1)S(1)}, u32[]{:S(2)}, u32[]{:S(2)}) collective-permute-start(bf16[216,128]{1,0:T(8,128)(2,1)S(1)} %get-tuple-element.50.own), channel_id=1, source_target_pairs={{0,7},{1,4},{2,5},{3,6},{4,1},{5,2},{6,3},{7,0},{8,13},{9,14},{10,... | collective-permute-start | bytes 165896 | tf_op jit(solution)/shard_map/ppermute | solution.py:526
  36.0 1.2 %collective-permute-start.8 = (bf16[16,256]{1,0:T(8,128)(2,1)S(1)}, bf16[16,256]{1,0:T(8,128)(2,1)S(1)}, u32[]{:S(2)}, u32[]{:S(2)}) collective-permute-start(bf16[16,256]{1,0:T(8,128)(2,1)S(1)} %shard_map.56.left), channel_id=1, source_target_pairs={{0,4},{4,0},{8,12},{12,8},{16,20},{20,16},{24,28},{28,24},{1,5},{5... | collective-permute-start | bytes 24584 | tf_op jit(solution)/shard_map/ppermute | solution.py:509

commit v11 on v10

--- a/solution.py
+++ b/solution.py
@@ -18,7 +18,6 @@
 LANES = PAD * PAD
 VMEM_BYTES = 8 << 20
 SECOND = (CHI + 2) * 128
-FOLD = 64
 PIVOT = 1.0 / 64
 F32 = jnp.float32
 BF16 = jnp.bfloat16
@@ -46,11 +45,6 @@
 
 def one_hot(mask):
     return jnp.where(mask, 1.0, 0.0).astype(BF16)
-
-
-def swap_matrix(rows=LANES):
-    i, j = iota((rows, LANES), 0), iota((rows, LANES), 1)
-    return one_hot((group(i) == minor(j)) & (minor(i) == group(j)))
 
 
 def spread_matrix(mirror):
@@ -67,7 +61,7 @@
     return one_hot((j == source) & (s < CHI) & (t < CHI))
 
 
-def swapped_tiles(x, fold, other=None):
+def swapped_tiles(x, other=None):
     lane_group = group(iota((PAD, 128), 1))
     zero = jnp.zeros((PAD, 128), x.dtype)
 
@@ -88,26 +82,22 @@
     for s in range(CHI):
         pair = []
         for side in range(2):
-            lift = FOLD // PAD if fold and side and s >= CHI // 2 else 0
             out = zero
             for p in range(span):
                 source = (side * 8 + (s & 7 & -span)) | p
                 if other is None and source >= CHI:
                     continue
-                shift = (p + lift - s % span) % 8 * PAD
+                shift = (p - s % span) % 8 * PAD
                 piece = sources[source, s >> 3]
                 piece = pltpu.roll(piece, shift, 1) if shift else piece
-                here = lax.bitwise_and(lane_group, span - 1) == p
-                if lift:
-                    here = lane_group == p + lift
-                out = jnp.where(here, piece, out)
+                out = jnp.where(lax.bitwise_and(lane_group, span - 1) == p, piece, out)
             pair.append(out)
         tiles.append(pair)
     return tiles
 
 
 def block_swap(x, other=None):
-    tiles = swapped_tiles(x, False, other)
+    tiles = swapped_tiles(x, other)
     return jnp.concatenate([jnp.concatenate(pair, axis=1) for pair in tiles], axis=0)
 
 
@@ -169,8 +159,75 @@
     return (y[2 * n :] + y[n : 2 * n]) + y[:n]
 
 
-def folded(first, last):
-    return jnp.where(iota(first.shape, 1) < FOLD, first, last)
+def compact(x):
+    blocks = x.shape[0] // PAD
+    legs = x.astype(F32).reshape(blocks, PAD, 128)[:, :CHI]
+    return legs.reshape(blocks * CHI, 128).astype(BF16)
+
+
+def spaced(x):
+    blocks = x.shape[0] // CHI
+    legs = x.astype(F32).reshape(blocks, CHI, 128)
+    rest = jnp.zeros((blocks, PAD - CHI, 128), F32)
+    return jnp.concatenate([legs, rest], axis=1).reshape(blocks * PAD, 128).astype(BF16)
+
+
+def joined(x):
+    x = spaced(x)
+    lane = iota((PAD, 128), 1)
+    sides = []
+    for k in range(CHI):
+        at = ROWS + (k >> 3) * PAD
+        shift = -(k & 7) * PAD % 128
+        side = pltpu.roll(x[at : at + PAD], shift, 1) if shift else x[at : at + PAD]
+        sides.append(jnp.where(lane < PAD, side, jnp.zeros_like(side)))
+    return jnp.concatenate([x[:ROWS], jnp.concatenate(sides, axis=0)], axis=1)
+
+
+def split(x):
+    lane_group = group(iota((PAD, 128), 1))
+    tails = [jnp.zeros((PAD, 128), x.dtype)] * 2
+    for k in range(CHI):
+        block = x[k * PAD : (k + 1) * PAD, 128:]
+        tails[k >> 3] = jnp.where(lane_group == (k & 7), block, tails[k >> 3])
+    return jnp.concatenate([x[:, :128], *tails], axis=0)
+
+
+def product_both(a, b, scale=None):
+    zero = jnp.zeros((PAD, b.shape[1]), b.dtype)
+    blocks = [b[s * PAD : (s + 1) * PAD] if s < CHI else zero for s in range(PAD)]
+    plain = mm(a, jnp.concatenate(blocks, axis=0), NT)
+    moved = mm(a, jnp.concatenate([blocks[s ^ 4] for s in range(PAD)], axis=0), NT)
+    if scale is not None:
+        plain, moved = plain * scale, moved * scale
+    return plain.astype(BF16), moved.astype(BF16)
+
+
+def widen(x):
+    return jnp.concatenate([x, jnp.zeros((x.shape[0], LANES - x.shape[1]), x.dtype)], axis=1)
+
+
+def parts3(x):
+    a = x.astype(BF16)
+    rest = x - a.astype(F32)
+    b = rest.astype(BF16)
+    c = (rest - b.astype(F32)).astype(BF16)
+    return jnp.concatenate([a, b, c], axis=0)
+
+
+def parts2(x):
+    a = x.astype(BF16)
+    return jnp.concatenate([a, (x - a.astype(F32)).astype(BF16)], axis=0)
+
+
+def fold2(y):
+    n = y.shape[0] // 2
+    return y[n:] + y[:n]
+
+
+def fold3(y):
+    n = y.shape[0] // 3
+    return (y[2 * n :] + y[n : 2 * n]) + y[:n]
 
 
 def compact(x):
@@ -207,11 +264,24 @@
 
 
 def outer_part(first, second):
-    outer, moved = product_both(first, row_swap(second))
-    tiles = swapped_tiles(outer, True, moved)
-    half = CHI // 2
-    side = folded(*(jnp.concatenate([t[1] for t in part], axis=0) for part in (tiles[:half], tiles[half:])))
-    return compact(jnp.concatenate([t[0] for t in tiles] + [side], axis=0))
+    outer = widen(mm(first, row_swap(second), NT).astype(BF16))
+    lane = iota((PAD, 128), 1)
+    tiles = []
+    for s in range(CHI):
+        tile = jnp.zeros((PAD, 128), BF16)
+        for p in range(128 // CHI + 1):
+            at = (s >> 3) * 128
+            piece = outer[p * PAD : (p + 1) * PAD, at : at + 128]
+            shift = (p * CHI - (s & 7) * PAD) % 128
+            piece = pltpu.roll(piece, shift, 1) if shift else piece
+            tile = jnp.where((lane >= p * CHI) & (lane < p * CHI + CHI), piece, tile)
+        tiles.append(tile)
+    cut = CHI * (CHI - 1) - 128
+    for side in range(2):
+        pieces = [outer[p * PAD : (p + 1) * PAD, side * 128 : side * 128 + 128] for p in (CHI - 2, CHI - 1)]
+        before = pltpu.roll(pieces[0], (cut - CHI) % 128, 1)
+        tiles.append(jnp.where(minor(lane) < cut, before, pltpu.roll(pieces[1], cut, 1)))
+    return compact(jnp.concatenate(tiles, axis=0))
 
 
 def turn(first, compact_lanes):
@@ -223,13 +293,23 @@
     return widen(legs.reshape(ROWS, ROWS).astype(BF16))
 
 
-def start_body(start, swap):
+def quotient(index):
+    return lax.shift_right_logical(index * 171, 11)
+
+
+def natural_matrix():
+    i, j = iota((LANES, LANES), 0), iota((LANES, LANES), 1)
+    return one_hot((j == minor(i) * CHI + group(i)) & (minor(i) < CHI) & (group(i) < CHI))
+
+
+def start_body(start, first_upper):
     start = jnp.concatenate([start, jnp.zeros((PAD - CHI, CHI * CHI), F32)], axis=0)
     pieces = parts3(start)
-    spread = spread_matrix(False)
-    plain = mm(pieces, spread)
-    turned = mm(plain.astype(BF16), swap)
-    return fold3(plain), fold3(turned)
+    i, j = iota((CHI * CHI, LANES), 0), iota((CHI * CHI, LANES), 1)
+    s = quotient(j)
+    swapped = fold3(mm(pieces, one_hot((i == (j - s * CHI) * CHI + s) & (s < CHI))))
+    turned = fold3(mm(pieces, spread_matrix(first_upper)))
+    return jnp.where(first_upper, widen(start), swapped), turned
 
 
 def row_products(y):
@@ -286,48 +366,53 @@
     return y * twice(scale, width), good
 
 
-def exact_iso(own, other, start, start_turned, shift, swap):
+def exact_iso(own, other, start, start_turned, shift, natural):
     pieces = parts3(start)
     image = fold3(mm(pieces, own, NT) + mm(pieces, other, NT))
     basis = exact_orthonormal(widen(image) + shift * start_turned)
     pieces = parts3(basis)
     image = fold3(mm(pieces[:, :ROWS], own) + mm(pieces[:, :ROWS], other))
-    return exact_orthonormal(image + shift * fold3(mm(pieces, swap)))
-
-
-def iso_kernel(own, other, starts, pieces, iso_o):
-    swap = swap_matrix()
-    grams = [spaced(own[...]), spaced(other[...])]
-    doubled = [
-        jnp.concatenate([g[:ROWS], jnp.concatenate([g[ROWS:]] * 2, axis=0)], axis=1) for g in grams
-    ]
-    total = doubled[0].astype(F32) + doubled[1].astype(F32)
+    return exact_orthonormal(image + shift * fold3(mm(pieces, natural)))
+
+
+def first_image(gram, pieces):
+    gram = spaced(gram)
+    shared = [gram[ROWS : ROWS + PAD]] * 8 + [gram[ROWS + PAD :]] * (CHI - 8)
+    shared = jnp.concatenate([gram[:ROWS], jnp.concatenate(shared, axis=0)], axis=1)
     i, j = iota((ROWS, LANES), 0), iota((ROWS, LANES), 1)
-    place = jnp.where(j < 128, j, 128 + lax.bitwise_and(j, FOLD - 1))
-    valid = (j < 128) | ((lax.bitwise_and(j, 127) < FOLD) == (i < ROWS // 2))
-    diagonal = valid & (group(i) == minor(place)) & (minor(i) == group(place))
-    trace = jnp.sum(jnp.where(diagonal, total, 0.0), axis=0, keepdims=True)
-    shift = jnp.sum(trace, axis=1, keepdims=True) / (CHI * CHI)
+    entry = minor(i) * CHI + group(i)
+    place = jnp.where(entry < 128, entry, entry + lax.bitwise_and(group(i), 7) * PAD)
+    diagonal = (j == place) & (minor(i) < CHI)
+    trace = jnp.sum(jnp.where(diagonal, shared.astype(F32), 0.0), axis=0, keepdims=True)
+    images = mm(pieces, shared, NT)
+    image = images[: 2 * PAD]
+    block = lax.bitwise_and(group(iota((2 * PAD, ROWS), 1)), 7)
+    for k in range(1, 8):
+        image = jnp.where(block == k, images[2 * PAD * k : 2 * PAD * (k + 1)], image)
+    return widen(fold2(image)), jnp.sum(trace, axis=1, keepdims=True)
+
+
+def iso_kernel(own, own_image, own_trace, other, starts, pieces, iso_o):
+    natural = natural_matrix()
+    image, trace = first_image(other[...], pieces[...])
+    shift = (own_trace[:1, :1] + trace) / (CHI * CHI)
     unit = 1.0 / shift
-    image = mm(pieces[...], doubled[0], NT) + mm(pieces[...], doubled[1], NT)
-    lane = iota((2 * PAD, ROWS), 1)
-    image = jnp.where(lane < ROWS // 2, image[: 2 * PAD], image[2 * PAD :])
-    image = widen(fold2(image)) * unit + starts[PAD:]
+    image = (own_image[...] + image) * unit + starts[PAD:]
     parts = parts2(image)
-    own, other = unfold(grams[0]), unfold(grams[1])
+    own, other = own[...], joined(other[...])
     image = fold2(mm(parts[:, :ROWS], own) + mm(parts[:, :ROWS], other)) * unit
-    basis, good = orthonormal(image + fold2(mm(parts, swap)))
+    basis, good = orthonormal(image + fold2(mm(parts, natural)))
     iso_o[...] = basis.astype(BF16)
 
     @pl.when(jnp.logical_not(good[0, 0] > 0.5))
     def _():
-        basis = exact_iso(own, other, starts[:PAD], starts[PAD:], shift, swap)
+        basis = exact_iso(own, other, starts[:PAD], starts[PAD:], shift, natural)
         iso_o[...] = basis.astype(BF16)
 
 
 def packed_pair(index):
     entry = jnp.where(index < 128, index, 128 + minor(index))
-    s = lax.shift_right_logical(entry * 171, 11)
+    s = quotient(entry)
     return s, entry - s * CHI
 
 
@@ -339,10 +424,10 @@
 
 def first_second(turned, lower, left, second_ref, first_ref):
     lane = iota((PAD, LANES), 1)
-    masked = [jnp.where(group(lane) == k, left.astype(F32), 0.0) for k in range(CHI)]
+    masked = [jnp.where(quotient(lane) == k, left.astype(F32), 0.0) for k in range(CHI)]
     masked = jnp.concatenate(masked, axis=0).astype(BF16)
     i, j = iota((LANES, LANES), 0), iota((LANES, LANES), 1)
-    values = mm(masked, one_hot(minor(i) == group(j)))
+    values = mm(masked, one_hot(i - quotient(i) * CHI == group(j)))
     eye = minor(lane) == iota((PAD, LANES), 0)
     for a in range(CHI):
         blocks = []
@@ -379,9 +464,9 @@
         lane_group = jnp.minimum(group(lane), CHI)
     values = values.T.astype(F32)
     entry = iota((CHI * CHI, LANES), 0)
-    kept = lax.shift_right_logical(entry * 171, 11) == lane_group
+    kept = quotient(entry) == lane_group
     for k in range(CHI):
-        block = values[k * PAD : k * PAD + CHI, :]
+        block = values[k * CHI : (k + 1) * CHI, :]
         tall = jnp.concatenate([block] * CHI, axis=0)
         tall = jnp.where(kept, tall, 0.0).astype(BF16)
         kron_ref[k * 128 : (k + 1) * 128, :] = tall[:128]
@@ -447,20 +532,28 @@
     scale_o[...] = lax.rsqrt(mean[...]) * lax.rsqrt(other_mean)
 
 
-def turn_kernel(level, own, other, start, turned_o, lower_o, starts_o, pieces_o):
+def turn_kernel(
+    level, own, other, gram, start, turned_o, lower_o, starts_o, pieces_o, wide_o, image_o, trace_o
+):
     later = level > 0
     own_first, first_upper, _, _ = roles(level)
     first, second = pick(own_first, own[...], joined(other[...]) if later else other[...])
     turned_o[...] = turn(first, later)
     lower_o[...] = mm(second, packing(later)).astype(BF16)
-    plain, turned = start_body(start[level], swap_matrix())
-    here = jnp.where(first_upper, plain, turned)
-    starts_o[:PAD] = here
-    starts_o[PAD:] = jnp.where(first_upper, turned, plain)
-    pieces = parts2(here)
-    pieces_o[: 2 * PAD] = pieces
-    lifted = pltpu.roll(pieces[:, 128:], FOLD, 1)
-    pieces_o[2 * PAD :] = jnp.concatenate([pieces[:, :128], lifted], axis=1)
+    here, turned = start_body(start[level], first_upper)
+    starts_o[:PAD], starts_o[PAD:] = here, turned
+    parts = parts2(here)
+    place = iota((2 * PAD, 128), 1)
+    pieces = []
+    for k in range(8):
+        side = pltpu.roll(parts[:, 128:], k * PAD, 1) if k else parts[:, 128:]
+        side = jnp.where(group(place) == k, side, jnp.zeros_like(side))
+        pieces.append(jnp.concatenate([parts[:, :128], side], axis=1))
+    pieces = jnp.concatenate(pieces, axis=0)
+    pieces_o[...] = pieces
+    wide_o[...] = joined(gram[...])
+    image_o[...], trace = first_image(gram[...], pieces)
+    trace_o[...] = jnp.broadcast_to(trace, trace_o.shape)
 
 
 def second_kernel(turned, lower, left, second_o, first):
@@ -529,7 +622,6 @@
 def per_device(site_tensors, start_basis):
     square = CHI * CHI
     mat, one = ((ROWS, LANES), BF16), ((8, 128), F32)
-    gram_shape = ((CHI * CHI * 3 // 2, 128), BF16)
     sent = ((CHI * (CHI + 2), 128), BF16)
     kron, firsts = [pltpu.VMEM((SECOND, LANES), BF16)], [pltpu.VMEM((CHI * ROWS, LANES), BF16)]
     scales, means = [], []
@@ -538,20 +630,30 @@
         if level == 0:
             other = from_partner(own, 1)
             (own,) = call(cast_kernel, [((square, square), BF16)])(own)
-            own, other, gram = call(first_gram_kernel, [mat, mat, gram_shape])(own, other)
+            own, other, gram = call(first_gram_kernel, [mat, mat, sent])(own, other)
         else:
             other = from_partner(own, 1 << level | 1)
             own, product, mean = call(own_kernel, [mat, mat, one])(own)
-            gram, scale = call(functools.partial(gram_kernel, level), [gram_shape, one])(
+            gram, scale = call(functools.partial(gram_kernel, level), [sent, one])(
                 product, mean, other
             )
             scales, means = [scale], [*means, mean]
         gram_other = from_bond(gram)
-        turned, lower, starts, pieces = call(
+        turned, lower, starts, pieces, wide, image, trace = call(
             functools.partial(turn_kernel, level),
-            [mat, mat, ((2 * PAD, LANES), F32), ((4 * PAD, LANES), BF16)],
-        )(own, other, start_basis)
-        (left,) = call(iso_kernel, [((PAD, LANES), BF16)])(gram, gram_other, starts, pieces)
+            [
+                mat,
+                mat,
+                ((2 * PAD, LANES), F32),
+                ((16 * PAD, LANES), BF16),
+                mat,
+                ((PAD, LANES), F32),
+                one,
+            ],
+        )(own, other, gram, start_basis)
+        (left,) = call(iso_kernel, [((PAD, LANES), BF16)])(
+            wide, image, trace, gram_other, starts, pieces
+        )
         right = from_partner(left, 1)
         (second,) = call(second_kernel, [((ROWS, SECOND), BF16)], firsts)(turned, lower, left)
         if level < LEVELS - 1:

time: 38.8 us -> 38.2 us (0.985)
  waiting for transfers between devices: 8.45 us -> 7.44 us
    ppermute x3, waiting for transfers between devices: 5.07 us -> 4.03 us  [from_bond(): return lax.ppermute(array, ('row', 'col'), pairs)]
  transfers between devices with their start and end apart: 9 -> 9, of which waited for: 9 -> 9; matrix products, arithmetic and copies ran while one was open for 0% -> 0% of each run, Pallas kernels for 12% -> 13%
where the time goes in v11:
time: 38.2 us; the launch traced here: 38.1 us
  starting transfers between devices  16.4 us (43%)
  Pallas kernels  12.5 us (33%)
  waiting for transfers between devices  7.44 us (19%)
  local copies, waits for them, and re-layouts  0.92 us (2%)
  between operations  0.78 us (2%)
    pallas_call x18, Pallas kernels, run(): pl.pallas_call(kernel, out_shape=[jax.ShapeDtypeStruct(s, d) for s, d in...  12.5 us
    ppermute x3, starting transfers between devices, from_bond(): return lax.ppermute(array, ('row', 'col'), pairs)  12 us
    ppermute x6, starting transfers between devices, from_partner(): return lax.ppermute(array, 'row', [(i, i ^ flip) for i in range(count)])  4.42 us
    ppermute x3, waiting for transfers between devices, from_bond(): return lax.ppermute(array, ('row', 'col'), pairs)  4.03 us
    ppermute x6, waiting for transfers between devices, from_partner(): return lax.ppermute(array, 'row', [(i, i ^ flip) for i in range(count)])  3.41 us
    unnamed x4, local copies, waits for them, and re-layouts  0.92 us
  transfers between devices with their start and end apart: 9, of which 9 were waited for; matrix products, arithmetic and copies ran while one was open for 0% of the time, Pallas kernels for 13%

profile of v11, /device:TPU:0, one launch (start us, length us, event | category | flops | bytes accessed | tf_op | source)
XLA Modules:
  0.0 38.1 jit_solution(16665836393369314237)
XLA Ops:
  0.6 0.6 %collective-permute-start = (f32[144,144]{1,0:T(8,128)}, f32[144,144]{1,0:T(8,128)S(1)}, u32[]{:S(2)}, u32[]{:S(2)}) collective-permute-start(f32[144,144]{1,0:T(8,128)} %bitcast.2), channel_id=1, source_target_pairs={{0,4},{4,0},{8,12},{12,8},{16,20},{20,16},{24,28},{28,24},{1,5},{5... | collective-permute-start | bytes 248840 | tf_op jit(solution)/shard_map/ppermute | solution.py:602
  1.2 0.0 copy-start
  1.2 0.9 %copy-done = f32[1,1,144,144]{3,2,1,0:T(8,128)S(1)} copy-done((f32[1,1,144,144]{3,2,1,0:T(8,128)S(1)}, f32[1,1,144,144]{3,2,1,0:T(8,128)}, u32[]{:S(2)}) %copy-start) | copy-done | bytes 82968
  2.1 0.0 copy-start.1
  2.1 0.3 collective-permute-done.other
  2.4 1.2 %shard_map.42 = (bf16[192,256]{1,0:T(8,128)(2,1)S(1)}, bf16[192,256]{1,0:T(8,128)(2,1)S(1)}, bf16[168,128]{1,0:T(8,128)(2,1)S(1)}) custom-call(bf16[144,144]{1,0:T(8,128)(2,1)S(1)} %shard_map.41.own, f32[144,144]{1,0:T(8,128)S(1)} %collective-permute-done.other), custom_call_target="tpu_custom_call" | custom-call | flops 100000000 | bytes 1000000 | tf_op jit(solution)/shard_map/pallas_call | solution.py:587
  3.6 4.8 %collective-permute-start.1 = (bf16[168,128]{1,0:T(8,128)(2,1)S(1)}, bf16[168,128]{1,0:T(8,128)(2,1)S(1)}, u32[]{:S(2)}, u32[]{:S(2)}) collective-permute-start(bf16[168,128]{1,0:T(8,128)(2,1)S(1)} %get-tuple-element.40.gram), channel_id=1, source_target_pairs={{0,7},{1,4},{2,5},{3,6},{4,1},{5,2},{6,3},{7,0},{8,13},{9,14},{10,... | collective-permute-start | bytes 129032 | tf_op jit(solution)/shard_map/ppermute | solution.py:619
  8.4 0.0 copy-done.1
  8.4 0.5 %shard_map.43 = (bf16[192,256]{1,0:T(8,128)(2,1)S(1)}, bf16[192,256]{1,0:T(8,128)(2,1)S(1)}, f32[32,256]{1,0:T(8,128)S(1)}, bf16[256,256]{1,0:T(8,128)(2,1)S(1)}...) custom-call(bf16[192,256]{1,0:T(8,128)(2,1)S(1)} %get-tuple-element.38.own, ...), custom_call_target="tpu_custom_call" | custom-call | flops 100000000 | bytes 1000000 | tf_op jit(solution)/shard_map/pallas_call | solution.py:587
  8.9 1.3 %collective-permute-done.1.other = bf16[168,128]{1,0:T(8,128)(2,1)S(1)} collective-permute-done((bf16[168,128]{1,0:T(8,128)(2,1)S(1)}, bf16[168,128]{1,0:T(8,128)(2,1)S(1)}, u32[]{:S(2)}, u32[]{:S(2)}) %collective-permute-start.1) | collective-permute-done | bytes 43040 | tf_op jit(solution)/shard_map/ppermute | solution.py:619
  10.2 0.8 %shard_map.44.left = bf16[16,256]{1,0:T(8,128)(2,1)S(1)} custom-call(bf16[192,256]{1,0:T(8,128)(2,1)S(1)} %get-tuple-element.43.own, f32[16,256]{1,0:T(8,128)S(1)} %get-tuple-element.44.own_image, f32[8,128]{1,0:T(8,128)S(1)} %get-tuple-element.45.own_trace, bf16[168,128]{1,0:T(8,128)(2,1)S(1)} %collective-permute-done.1.other, ...), custom_call_target="tpu_custom_call" | custom-call | flops 100000000 | bytes 1000000 | tf_op jit(solution)/shard_map/pallas_call | solution.py:587
  11.0 0.1 collective-permute-start.2
  11.1 1.0 %shard_map.45.second = bf16[192,1792]{1,0:T(8,128)(2,1)S(1)} custom-call(bf16[192,256]{1,0:T(8,128)(2,1)S(1)} %get-tuple-element.41.turned, bf16[192,256]{1,0:T(8,128)(2,1)S(1)} %get-tuple-element.42.lower, bf16[16,256]{1,0:T(8,128)(2,1)S(1)} %shard_map.44.left), custom_call_target="tpu_custom_call" | custom-call | flops 100000000 | bytes 1000000 | tf_op jit(solution)/shard_map/pallas_call | solution.py:587
  12.1 0.2 collective-permute-done.2.right
  12.3 0.4 %shard_map.46.own = bf16[168,128]{1,0:T(8,128)(2,1)S(1)} custom-call(bf16[192,1792]{1,0:T(8,128)(2,1)S(1)} %shard_map.45.second, bf16[16,256]{1,0:T(8,128)(2,1)S(1)} %collective-permute-done.2.right), custom_call_target="tpu_custom_call" | custom-call | flops 100000000 | bytes 1000000 | tf_op jit(solution)/shard_map/pallas_call | solution.py:587
  12.7 1.8 %collective-permute-start.3 = (bf16[168,128]{1,0:T(8,128)(2,1)S(1)}, bf16[168,128]{1,0:T(8,128)(2,1)S(1)}, u32[]{:S(2)}, u32[]{:S(2)}) collective-permute-start(bf16[168,128]{1,0:T(8,128)(2,1)S(1)} %shard_map.46.own), channel_id=1, source_target_pairs={{0,12},{4,8},{8,4},{12,0},{16,28},{20,24},{24,20},{28,16},{1,13},{... | collective-permute-start | bytes 129032 | tf_op jit(solution)/shard_map/ppermute | solution.py:602
  14.5 0.4 %shard_map.47 = (bf16[192,256]{1,0:T(8,128)(2,1)S(1)}, bf16[192,256]{1,0:T(8,128)(2,1)S(1)}, f32[8,128]{1,0:T(8,128)S(1)}) custom-call(bf16[168,128]{1,0:T(8,128)(2,1)S(1)} %shard_map.46.own), custom_call_target="tpu_custom_call" | custom-call | flops 100000000 | bytes 1000000 | tf_op jit(solution)/shard_map/pallas_call | solution.py:587
  14.9 1.3 %collective-permute-done.3.other = bf16[168,128]{1,0:T(8,128)(2,1)S(1)} collective-permute-done((bf16[168,128]{1,0:T(8,128)(2,1)S(1)}, bf16[168,128]{1,0:T(8,128)(2,1)S(1)}, u32[]{:S(2)}, u32[]{:S(2)}) %collective-permute-start.3) | collective-permute-done | bytes 43040 | tf_op jit(solution)/shard_map/ppermute | solution.py:602
  16.2 0.8 %shard_map.48 = (bf16[168,128]{1,0:T(8,128)(2,1)S(1)}, f32[8,128]{1,0:T(8,128)S(1)}) custom-call(bf16[192,256]{1,0:T(8,128)(2,1)S(1)} %get-tuple-element.49.product, f32[8,128]{1,0:T(8,128)S(1)} %get-tuple-element.50.mean.refs_0_, bf16[168,128]{1,0:T(8,128)(2,1)S(1)} %collective-permute-done.3.other), custom_call_target="tpu_custom_call" | custom-call | flops 100000000 | bytes 1000000 | tf_op jit(solution)/shard_map/pallas_call | solution.py:587
  17.1 3.6 %collective-permute-start.4 = (bf16[168,128]{1,0:T(8,128)(2,1)S(1)}, bf16[168,128]{1,0:T(8,128)(2,1)S(1)}, u32[]{:S(2)}, u32[]{:S(2)}) collective-permute-start(bf16[168,128]{1,0:T(8,128)(2,1)S(1)} %get-tuple-element.51.gram), channel_id=1, source_target_pairs={{0,7},{1,4},{2,5},{3,6},{4,1},{5,2},{6,3},{7,0},{8,13},{9,14},{10,... | collective-permute-start | bytes 129032 | tf_op jit(solution)/shard_map/ppermute | solution.py:619
  20.7 0.4 %shard_map.49 = (bf16[192,256]{1,0:T(8,128)(2,1)S(1)}, bf16[192,256]{1,0:T(8,128)(2,1)S(1)}, f32[32,256]{1,0:T(8,128)S(1)}, bf16[256,256]{1,0:T(8,128)(2,1)S(1)}...) custom-call(bf16[192,256]{1,0:T(8,128)(2,1)S(1)} %get-tuple-element.48.own, ...), custom_call_target="tpu_custom_call" | custom-call | flops 100000000 | bytes 1000000 | tf_op jit(solution)/shard_map/pallas_call | solution.py:587
  21.1 1.3 %collective-permute-done.4.other = bf16[168,128]{1,0:T(8,128)(2,1)S(1)} collective-permute-done((bf16[168,128]{1,0:T(8,128)(2,1)S(1)}, bf16[168,128]{1,0:T(8,128)(2,1)S(1)}, u32[]{:S(2)}, u32[]{:S(2)}) %collective-permute-start.4) | collective-permute-done | bytes 43040 | tf_op jit(solution)/shard_map/ppermute | solution.py:619
  22.4 0.8 %shard_map.50.left = bf16[16,256]{1,0:T(8,128)(2,1)S(1)} custom-call(bf16[192,256]{1,0:T(8,128)(2,1)S(1)} %get-tuple-element.54.own, f32[16,256]{1,0:T(8,128)S(1)} %get-tuple-element.55.own_image, f32[8,128]{1,0:T(8,128)S(1)} %get-tuple-element.56.own_trace, bf16[168,128]{1,0:T(8,128)(2,1)S(1)} %collective-permute-done.4.other, ...), custom_call_target="tpu_custom_call" | custom-call | flops 100000000 | bytes 1000000 | tf_op jit(solution)/shard_map/pallas_call | solution.py:587
  23.2 0.1 collective-permute-start.5
  23.3 1.0 %shard_map.51.second = bf16[192,1792]{1,0:T(8,128)(2,1)S(1)} custom-call(bf16[192,256]{1,0:T(8,128)(2,1)S(1)} %get-tuple-element.52.turned, bf16[192,256]{1,0:T(8,128)(2,1)S(1)} %get-tuple-element.53.lower, bf16[16,256]{1,0:T(8,128)(2,1)S(1)} %shard_map.50.left), custom_call_target="tpu_custom_call" | custom-call | flops 100000000 | bytes 1000000 | tf_op jit(solution)/shard_map/pallas_call | solution.py:587
  24.3 0.2 collective-permute-done.5.right
  24.4 0.4 %shard_map.52.own = bf16[168,128]{1,0:T(8,128)(2,1)S(1)} custom-call(bf16[192,1792]{1,0:T(8,128)(2,1)S(1)} %shard_map.51.second, bf16[16,256]{1,0:T(8,128)(2,1)S(1)} %collective-permute-done.5.right, f32[8,128]{1,0:T(8,128)S(1)} %get-tuple-element.59.refs_0_), custom_call_target="tpu_custom_call" | custom-call | flops 100000000 | bytes 1000000 | tf_op jit(solution)/shard_map/pallas_call | solution.py:587
  24.9 1.9 %collective-permute-start.6 = (bf16[168,128]{1,0:T(8,128)(2,1)S(1)}, bf16[168,128]{1,0:T(8,128)(2,1)S(1)}, u32[]{:S(2)}, u32[]{:S(2)}) collective-permute-start(bf16[168,128]{1,0:T(8,128)(2,1)S(1)} %shard_map.52.own), channel_id=1, source_target_pairs={{0,20},{4,16},{8,28},{12,24},{16,4},{20,0},{24,12},{28,8},{1,21},{... | collective-permute-start | bytes 129032 | tf_op jit(solution)/shard_map/ppermute | solution.py:602
  26.8 0.4 %shard_map.53 = (bf16[192,256]{1,0:T(8,128)(2,1)S(1)}, bf16[192,256]{1,0:T(8,128)(2,1)S(1)}, f32[8,128]{1,0:T(8,128)S(1)}) custom-call(bf16[168,128]{1,0:T(8,128)(2,1)S(1)} %shard_map.52.own), custom_call_target="tpu_custom_call" | custom-call | flops 100000000 | bytes 1000000 | tf_op jit(solution)/shard_map/pallas_call | solution.py:587
  27.2 1.3 %collective-permute-done.6.other = bf16[168,128]{1,0:T(8,128)(2,1)S(1)} collective-permute-done((bf16[168,128]{1,0:T(8,128)(2,1)S(1)}, bf16[168,128]{1,0:T(8,128)(2,1)S(1)}, u32[]{:S(2)}, u32[]{:S(2)}) %collective-permute-start.6) | collective-permute-done | bytes 43040 | tf_op jit(solution)/shard_map/ppermute | solution.py:602
  28.5 0.8 %shard_map.54 = (bf16[168,128]{1,0:T(8,128)(2,1)S(1)}, f32[8,128]{1,0:T(8,128)S(1)}) custom-call(bf16[192,256]{1,0:T(8,128)(2,1)S(1)} %get-tuple-element.61.product, f32[8,128]{1,0:T(8,128)S(1)} %get-tuple-element.62.mean.refs_1_, bf16[168,128]{1,0:T(8,128)(2,1)S(1)} %collective-permute-done.6.other), custom_call_target="tpu_custom_call" | custom-call | flops 100000000 | bytes 1000000 | tf_op jit(solution)/shard_map/pallas_call | solution.py:587
  29.3 3.6 %collective-permute-start.7 = (bf16[168,128]{1,0:T(8,128)(2,1)S(1)}, bf16[168,128]{1,0:T(8,128)(2,1)S(1)}, u32[]{:S(2)}, u32[]{:S(2)}) collective-permute-start(bf16[168,128]{1,0:T(8,128)(2,1)S(1)} %get-tuple-element.63.gram), channel_id=1, source_target_pairs={{0,7},{1,4},{2,5},{3,6},{4,1},{5,2},{6,3},{7,0},{8,13},{9,14},{10,... | collective-permute-start | bytes 129032 | tf_op jit(solution)/shard_map/ppermute | solution.py:619
  32.9 0.3 shard_map.55
  33.2 1.4 %collective-permute-done.7.other = bf16[168,128]{1,0:T(8,128)(2,1)S(1)} collective-permute-done((bf16[168,128]{1,0:T(8,128)(2,1)S(1)}, bf16[168,128]{1,0:T(8,128)(2,1)S(1)}, u32[]{:S(2)}, u32[]{:S(2)}) %collective-permute-start.7) | collective-permute-done | bytes 43040 | tf_op jit(solution)/shard_map/ppermute | solution.py:619
  34.6 0.8 %shard_map.56.left = bf16[16,256]{1,0:T(8,128)(2,1)S(1)} custom-call(bf16[192,256]{1,0:T(8,128)(2,1)S(1)} %get-tuple-element.66.own, f32[16,256]{1,0:T(8,128)S(1)} %get-tuple-element.67.own_image, f32[8,128]{1,0:T(8,128)S(1)} %get-tuple-element.68.own_trace, bf16[168,128]{1,0:T(8,128)(2,1)S(1)} %collective-permute-done.7.other, ...), custom_call_target="tpu_custom_call" | custom-call | flops 100000000 | bytes 1000000 | tf_op jit(solution)/shard_map/pallas_call | solution.py:587
  35.5 0.1 collective-permute-start.8
  35.5 1.0 %shard_map.57.second = bf16[192,1792]{1,0:T(8,128)(2,1)S(1)} custom-call(bf16[192,256]{1,0:T(8,128)(2,1)S(1)} %get-tuple-element.64.turned, bf16[192,256]{1,0:T(8,128)(2,1)S(1)} %get-tuple-element.65.lower, bf16[16,256]{1,0:T(8,128)(2,1)S(1)} %shard_map.56.left), custom_call_target="tpu_custom_call" | custom-call | flops 100000000 | bytes 1000000 | tf_op jit(solution)/shard_map/pallas_call | solution.py:587
  36.5 0.2 collective-permute-done.8.right
  36.7 1.4 %shard_map.58 = (f32[144,144]{1,0:T(8,128)}, f32[1,1]{1,0:T(1,128)}) custom-call(bf16[192,1792]{1,0:T(8,128)(2,1)S(1)} %shard_map.57.second, bf16[16,256]{1,0:T(8,128)(2,1)S(1)} %collective-permute-done.8.right, f32[8,128]{1,0:T(8,128)S(1)} %get-tuple-element.71.scale, f32[8,128]{1,0:T(8,128)S(1)} %get-tuple-element.50.mean.refs_0_, ...), custom_call_target="tpu_custom_call" | custom-call | flops 100000000 | bytes 1000000 | tf_op jit(solution)/shard_map/pallas_call | solution.py:587
  (1 shorter events, 0.0 us)
Async XLA Ops:
  0.6 1.8 %collective-permute-start = (f32[144,144]{1,0:T(8,128)}, f32[144,144]{1,0:T(8,128)S(1)}, u32[]{:S(2)}, u32[]{:S(2)}) collective-permute-start(f32[144,144]{1,0:T(8,128)} %bitcast.2), channel_id=1, source_target_pairs={{0,4},{4,0},{8,12},{12,8},{16,20},{20,16},{24,28},{28,24},{1,5},{5... | collective-permute-start | bytes 248840 | tf_op jit(solution)/shard_map/ppermute | solution.py:602
  1.2 0.9 %copy-start = (f32[1,1,144,144]{3,2,1,0:T(8,128)S(1)}, f32[1,1,144,144]{3,2,1,0:T(8,128)}, u32[]{:S(2)}) copy-start(f32[1,1,144,144]{3,2,1,0:T(8,128)} %param.2) | copy-start | bytes 248836
  2.1 6.3 %copy-start.1 = (f32[3,12,144]{2,1,0:T(8,128)S(1)}, f32[3,12,144]{2,1,0:T(8,128)}, u32[]{:S(2)}) copy-start(f32[3,12,144]{2,1,0:T(8,128)} %start.5) | copy-start | bytes 62212
  3.6 6.6 %collective-permute-start.1 = (bf16[168,128]{1,0:T(8,128)(2,1)S(1)}, bf16[168,128]{1,0:T(8,128)(2,1)S(1)}, u32[]{:S(2)}, u32[]{:S(2)}) collective-permute-start(bf16[168,128]{1,0:T(8,128)(2,1)S(1)} %get-tuple-element.40.gram), channel_id=1, source_target_pairs={{0,7},{1,4},{2,5},{3,6},{4,1},{5,2},{6,3},{7,0},{8,13},{9,14},{10,... | collective-permute-start | bytes 129032 | tf_op jit(solution)/shard_map/ppermute | solution.py:619
  11.0 1.2 %collective-permute-start.2 = (bf16[16,256]{1,0:T(8,128)(2,1)S(1)}, bf16[16,256]{1,0:T(8,128)(2,1)S(1)}, u32[]{:S(2)}, u32[]{:S(2)}) collective-permute-start(bf16[16,256]{1,0:T(8,128)(2,1)S(1)} %shard_map.44.left), channel_id=1, source_target_pairs={{0,4},{4,0},{8,12},{12,8},{16,20},{20,16},{24,28},{28,24},{1,5},{5... | collective-permute-start | bytes 24584 | tf_op jit(solution)/shard_map/ppermute | solution.py:602
  12.7 3.5 %collective-permute-start.3 = (bf16[168,128]{1,0:T(8,128)(2,1)S(1)}, bf16[168,128]{1,0:T(8,128)(2,1)S(1)}, u32[]{:S(2)}, u32[]{:S(2)}) collective-permute-start(bf16[168,128]{1,0:T(8,128)(2,1)S(1)} %shard_map.46.own), channel_id=1, source_target_pairs={{0,12},{4,8},{8,4},{12,0},{16,28},{20,24},{24,20},{28,16},{1,13},{... | collective-permute-start | bytes 129032 | tf_op jit(solution)/shard_map/ppermute | solution.py:602
  17.1 5.3 %collective-permute-start.4 = (bf16[168,128]{1,0:T(8,128)(2,1)S(1)}, bf16[168,128]{1,0:T(8,128)(2,1)S(1)}, u32[]{:S(2)}, u32[]{:S(2)}) collective-permute-start(bf16[168,128]{1,0:T(8,128)(2,1)S(1)} %get-tuple-element.51.gram), channel_id=1, source_target_pairs={{0,7},{1,4},{2,5},{3,6},{4,1},{5,2},{6,3},{7,0},{8,13},{9,14},{10,... | collective-permute-start | bytes 129032 | tf_op jit(solution)/shard_map/ppermute | solution.py:619
  23.2 1.2 %collective-permute-start.5 = (bf16[16,256]{1,0:T(8,128)(2,1)S(1)}, bf16[16,256]{1,0:T(8,128)(2,1)S(1)}, u32[]{:S(2)}, u32[]{:S(2)}) collective-permute-start(bf16[16,256]{1,0:T(8,128)(2,1)S(1)} %shard_map.50.left), channel_id=1, source_target_pairs={{0,4},{4,0},{8,12},{12,8},{16,20},{20,16},{24,28},{28,24},{1,5},{5... | collective-permute-start | bytes 24584 | tf_op jit(solution)/shard_map/ppermute | solution.py:602
  24.9 3.6 %collective-permute-start.6 = (bf16[168,128]{1,0:T(8,128)(2,1)S(1)}, bf16[168,128]{1,0:T(8,128)(2,1)S(1)}, u32[]{:S(2)}, u32[]{:S(2)}) collective-permute-start(bf16[168,128]{1,0:T(8,128)(2,1)S(1)} %shard_map.52.own), channel_id=1, source_target_pairs={{0,20},{4,16},{8,28},{12,24},{16,4},{20,0},{24,12},{28,8},{1,21},{... | collective-permute-start | bytes 129032 | tf_op jit(solution)/shard_map/ppermute | solution.py:602
  29.3 5.3 %collective-permute-start.7 = (bf16[168,128]{1,0:T(8,128)(2,1)S(1)}, bf16[168,128]{1,0:T(8,128)(2,1)S(1)}, u32[]{:S(2)}, u32[]{:S(2)}) collective-permute-start(bf16[168,128]{1,0:T(8,128)(2,1)S(1)} %get-tuple-element.63.gram), channel_id=1, source_target_pairs={{0,7},{1,4},{2,5},{3,6},{4,1},{5,2},{6,3},{7,0},{8,13},{9,14},{10,... | collective-permute-start | bytes 129032 | tf_op jit(solution)/shard_map/ppermute | solution.py:619
  35.5 1.2 %collective-permute-start.8 = (bf16[16,256]{1,0:T(8,128)(2,1)S(1)}, bf16[16,256]{1,0:T(8,128)(2,1)S(1)}, u32[]{:S(2)}, u32[]{:S(2)}) collective-permute-start(bf16[16,256]{1,0:T(8,128)(2,1)S(1)} %shard_map.56.left), channel_id=1, source_target_pairs={{0,4},{4,0},{8,12},{12,8},{16,20},{20,16},{24,28},{28,24},{1,5},{5... | collective-permute-start | bytes 24584 | tf_op jit(solution)/shard_map/ppermute | solution.py:602

commit v12 on v11

--- a/solution.py
+++ b/solution.py
@@ -47,9 +47,9 @@
     return jnp.where(mask, 1.0, 0.0).astype(BF16)
 
 
-def spread_matrix(mirror):
+def spread_matrix(mirror, flip=0):
     i, j = iota((CHI * CHI, LANES), 0), iota((CHI * CHI, LANES), 1)
-    s, t = group(j), minor(j)
+    s, t = lax.bitwise_xor(group(j), flip), minor(j)
     source = jnp.where(mirror, t * CHI + s, s * CHI + t)
     return one_hot((i == source) & (s < CHI) & (t < CHI))
 
@@ -477,12 +477,13 @@
     return mm(second_ref[...], kron_ref[...])
 
 
-def placed(site, mirror, lower):
+def spread(site, mirror, lower):
     legs = site.astype(F32).reshape(CHI, CHI, CHI * CHI)
     legs = jnp.where(lower, jnp.transpose(legs, (1, 0, 2)), legs)
     rest = jnp.zeros((CHI, PAD - CHI, CHI * CHI), F32)
     rows = jnp.concatenate([legs, rest], axis=1).reshape(ROWS, CHI * CHI).astype(BF16)
-    return block_swap(mm(rows, spread_matrix(mirror)).astype(BF16))
+    plain = mm(rows, spread_matrix(mirror)).astype(BF16)
+    return plain, mm(rows, spread_matrix(mirror, 4)).astype(BF16)
 
 
 def pick(own_first, own, other):
@@ -497,14 +498,15 @@
     return [flag != 0 for flag in flags]
 
 
-def cast_kernel(own, cast_o):
-    cast_o[...] = own[...].astype(BF16)
-
-
-def first_gram_kernel(own, other, mine_o, theirs_o, gram_o):
+def spread_kernel(own, plain_o, flipped_o):
+    _, _, own_lower, mirror = roles(0)
+    plain_o[...], flipped_o[...] = spread(own[...], mirror, own_lower)
+
+
+def first_gram_kernel(plain, flipped, other, mine_o, theirs_o, gram_o):
     own_first, _, own_lower, mirror = roles(0)
-    mine = placed(own[...], mirror, own_lower)
-    theirs = placed(other[...].astype(BF16), mirror, jnp.logical_not(own_lower))
+    mine = block_swap(plain[...], flipped[...])
+    theirs = block_swap(*spread(other[...], mirror, jnp.logical_not(own_lower)))
     mine_o[...], theirs_o[...] = mine, theirs
     products = pick(own_first, product_part(mine), product_part(theirs))
     gram_o[...] = outer_part(*products)
@@ -515,19 +517,19 @@
     return jnp.broadcast_to(mean, (8, 128))
 
 
-def scaled_product(x):
-    mean = mean_square(jnp.sum(jnp.square(x.astype(F32)), axis=0, keepdims=True))
+def scaled_product(sent, x):
+    mean = mean_square(jnp.sum(jnp.square(sent.astype(F32)), axis=0, keepdims=True))
     return product_part(x, twice(1.0 / mean[:1], LANES)), mean
 
 
 def own_kernel(own, wide_o, product_o, mean_o):
     wide = joined(own[...])
     wide_o[...] = wide
-    product_o[...], mean_o[...] = scaled_product(wide)
+    product_o[...], mean_o[...] = scaled_product(own[...], wide)
 
 
 def gram_kernel(level, product, mean, other, gram_o, scale_o):
-    other_product, other_mean = scaled_product(joined(other[...]))
+    other_product, other_mean = scaled_product(other[...], joined(other[...]))
     gram_o[...] = outer_part(*pick(roles(level)[0], product[...], other_product))
     scale_o[...] = lax.rsqrt(mean[...]) * lax.rsqrt(other_mean)
 
@@ -629,8 +631,8 @@
     for level in range(LEVELS):
         if level == 0:
             other = from_partner(own, 1)
-            (own,) = call(cast_kernel, [((square, square), BF16)])(own)
-            own, other, gram = call(first_gram_kernel, [mat, mat, sent])(own, other)
+            plain, flipped = call(spread_kernel, [mat, mat])(own)
+            own, other, gram = call(first_gram_kernel, [mat, mat, sent])(plain, flipped, other)
         else:
             other = from_partner(own, 1 << level | 1)
             own, product, mean = call(own_kernel, [mat, mat, one])(own)

time: 38.2 us -> 38.1 us (level)
  transfers between devices with their start and end apart: 9 -> 9, of which waited for: 9 -> 9; matrix products, arithmetic and copies ran while one was open for 0% -> 0% of each run, Pallas kernels for 13% -> 14%
where the time goes in v12:
time: 38.1 us; the launch traced here: 38 us
  starting transfers between devices  16.4 us (43%)
  Pallas kernels  12.6 us (33%)
  waiting for transfers between devices  7.23 us (19%)
  local copies, waits for them, and re-layouts  0.91 us (2%)
  between operations  0.78 us (2%)
    pallas_call x18, Pallas kernels, run(): pl.pallas_call(kernel, out_shape=[jax.ShapeDtypeStruct(s, d) for s, d in...  12.6 us
    ppermute x3, starting transfers between devices, from_bond(): return lax.ppermute(array, ('row', 'col'), pairs)  12 us
    ppermute x6, starting transfers between devices, from_partner(): return lax.ppermute(array, 'row', [(i, i ^ flip) for i in range(count)])  4.41 us
    ppermute x3, waiting for transfers between devices, from_bond(): return lax.ppermute(array, ('row', 'col'), pairs)  4.03 us
    ppermute x6, waiting for transfers between devices, from_partner(): return lax.ppermute(array, 'row', [(i, i ^ flip) for i in range(count)])  3.2 us
    unnamed x4, local copies, waits for them, and re-layouts  0.91 us
  transfers between devices with their start and end apart: 9, of which 9 were waited for; matrix products, arithmetic and copies ran while one was open for 0% of the time, Pallas kernels for 14%

profile of v12, /device:TPU:0, one launch (start us, length us, event | category | flops | bytes accessed | tf_op | source)
XLA Modules:
  0.0 38.0 jit_solution(12326163421233073124)
XLA Ops:
  0.6 0.6 %collective-permute-start = (f32[144,144]{1,0:T(8,128)}, f32[144,144]{1,0:T(8,128)S(1)}, u32[]{:S(2)}, u32[]{:S(2)}) collective-permute-start(f32[144,144]{1,0:T(8,128)} %bitcast.2), channel_id=1, source_target_pairs={{0,4},{4,0},{8,12},{12,8},{16,20},{20,16},{24,28},{28,24},{1,5},{5... | collective-permute-start | bytes 248840 | tf_op jit(solution)/shard_map/ppermute | solution.py:604
  1.2 0.0 copy-start
  1.2 0.9 %copy-done = f32[1,1,144,144]{3,2,1,0:T(8,128)S(1)} copy-done((f32[1,1,144,144]{3,2,1,0:T(8,128)S(1)}, f32[1,1,144,144]{3,2,1,0:T(8,128)}, u32[]{:S(2)}) %copy-start) | copy-done | bytes 82968
  2.1 0.2 shard_map.41
  2.3 0.1 collective-permute-done.other
  2.4 0.0 copy-start.1
  2.4 1.1 %shard_map.42 = (bf16[192,256]{1,0:T(8,128)(2,1)S(1)}, bf16[192,256]{1,0:T(8,128)(2,1)S(1)}, bf16[168,128]{1,0:T(8,128)(2,1)S(1)}) custom-call(bf16[192,256]{1,0:T(8,128)(2,1)S(1)} %get-tuple-element.40.plain, bf16[192,256]{1,0:T(8,128)(2,1)S(1)} %get-tuple-element.41.flipped, f32[144,144]{1,0:T(8,128)S(1)} %collective-permute-done.other), custom_call_target="tpu_custom_call" | custom-call | flops 100000000 | bytes 1000000 | tf_op jit(solution)/shard_map/pallas_call | solution.py:589
  3.5 4.8 %collective-permute-start.1 = (bf16[168,128]{1,0:T(8,128)(2,1)S(1)}, bf16[168,128]{1,0:T(8,128)(2,1)S(1)}, u32[]{:S(2)}, u32[]{:S(2)}) collective-permute-start(bf16[168,128]{1,0:T(8,128)(2,1)S(1)} %get-tuple-element.44.gram), channel_id=1, source_target_pairs={{0,7},{1,4},{2,5},{3,6},{4,1},{5,2},{6,3},{7,0},{8,13},{9,14},{10,... | collective-permute-start | bytes 129032 | tf_op jit(solution)/shard_map/ppermute | solution.py:621
  8.3 0.0 copy-done.1
  8.3 0.5 %shard_map.43 = (bf16[192,256]{1,0:T(8,128)(2,1)S(1)}, bf16[192,256]{1,0:T(8,128)(2,1)S(1)}, f32[32,256]{1,0:T(8,128)S(1)}, bf16[256,256]{1,0:T(8,128)(2,1)S(1)}...) custom-call(bf16[192,256]{1,0:T(8,128)(2,1)S(1)} %get-tuple-element.42.own, ...), custom_call_target="tpu_custom_call" | custom-call | flops 100000000 | bytes 1000000 | tf_op jit(solution)/shard_map/pallas_call | solution.py:589
  8.7 1.3 %collective-permute-done.1.other = bf16[168,128]{1,0:T(8,128)(2,1)S(1)} collective-permute-done((bf16[168,128]{1,0:T(8,128)(2,1)S(1)}, bf16[168,128]{1,0:T(8,128)(2,1)S(1)}, u32[]{:S(2)}, u32[]{:S(2)}) %collective-permute-start.1) | collective-permute-done | bytes 43040 | tf_op jit(solution)/shard_map/ppermute | solution.py:621
  10.1 0.8 %shard_map.44.left = bf16[16,256]{1,0:T(8,128)(2,1)S(1)} custom-call(bf16[192,256]{1,0:T(8,128)(2,1)S(1)} %get-tuple-element.47.own, f32[16,256]{1,0:T(8,128)S(1)} %get-tuple-element.48.own_image, f32[8,128]{1,0:T(8,128)S(1)} %get-tuple-element.49.own_trace, bf16[168,128]{1,0:T(8,128)(2,1)S(1)} %collective-permute-done.1.other, ...), custom_call_target="tpu_custom_call" | custom-call | flops 100000000 | bytes 1000000 | tf_op jit(solution)/shard_map/pallas_call | solution.py:589
  10.9 0.1 collective-permute-start.2
  11.0 1.0 %shard_map.45.second = bf16[192,1792]{1,0:T(8,128)(2,1)S(1)} custom-call(bf16[192,256]{1,0:T(8,128)(2,1)S(1)} %get-tuple-element.45.turned, bf16[192,256]{1,0:T(8,128)(2,1)S(1)} %get-tuple-element.46.lower, bf16[16,256]{1,0:T(8,128)(2,1)S(1)} %shard_map.44.left), custom_call_target="tpu_custom_call" | custom-call | flops 100000000 | bytes 1000000 | tf_op jit(solution)/shard_map/pallas_call | solution.py:589
  12.0 0.2 collective-permute-done.2.right
  12.2 0.4 %shard_map.46.own = bf16[168,128]{1,0:T(8,128)(2,1)S(1)} custom-call(bf16[192,1792]{1,0:T(8,128)(2,1)S(1)} %shard_map.45.second, bf16[16,256]{1,0:T(8,128)(2,1)S(1)} %collective-permute-done.2.right), custom_call_target="tpu_custom_call" | custom-call | flops 100000000 | bytes 1000000 | tf_op jit(solution)/shard_map/pallas_call | solution.py:589
  12.6 1.8 %collective-permute-start.3 = (bf16[168,128]{1,0:T(8,128)(2,1)S(1)}, bf16[168,128]{1,0:T(8,128)(2,1)S(1)}, u32[]{:S(2)}, u32[]{:S(2)}) collective-permute-start(bf16[168,128]{1,0:T(8,128)(2,1)S(1)} %shard_map.46.own), channel_id=1, source_target_pairs={{0,12},{4,8},{8,4},{12,0},{16,28},{20,24},{24,20},{28,16},{1,13},{... | collective-permute-start | bytes 129032 | tf_op jit(solution)/shard_map/ppermute | solution.py:604
  14.3 0.4 %shard_map.47 = (bf16[192,256]{1,0:T(8,128)(2,1)S(1)}, bf16[192,256]{1,0:T(8,128)(2,1)S(1)}, f32[8,128]{1,0:T(8,128)S(1)}) custom-call(bf16[168,128]{1,0:T(8,128)(2,1)S(1)} %shard_map.46.own), custom_call_target="tpu_custom_call" | custom-call | flops 100000000 | bytes 1000000 | tf_op jit(solution)/shard_map/pallas_call | solution.py:589
  14.8 1.3 %collective-permute-done.3.other = bf16[168,128]{1,0:T(8,128)(2,1)S(1)} collective-permute-done((bf16[168,128]{1,0:T(8,128)(2,1)S(1)}, bf16[168,128]{1,0:T(8,128)(2,1)S(1)}, u32[]{:S(2)}, u32[]{:S(2)}) %collective-permute-start.3) | collective-permute-done | bytes 43040 | tf_op jit(solution)/shard_map/ppermute | solution.py:604
  16.1 0.8 %shard_map.48 = (bf16[168,128]{1,0:T(8,128)(2,1)S(1)}, f32[8,128]{1,0:T(8,128)S(1)}) custom-call(bf16[192,256]{1,0:T(8,128)(2,1)S(1)} %get-tuple-element.53.product, f32[8,128]{1,0:T(8,128)S(1)} %get-tuple-element.54.mean.refs_0_, bf16[168,128]{1,0:T(8,128)(2,1)S(1)} %collective-permute-done.3.other), custom_call_target="tpu_custom_call" | custom-call | flops 100000000 | bytes 1000000 | tf_op jit(solution)/shard_map/pallas_call | solution.py:589
  16.9 3.6 %collective-permute-start.4 = (bf16[168,128]{1,0:T(8,128)(2,1)S(1)}, bf16[168,128]{1,0:T(8,128)(2,1)S(1)}, u32[]{:S(2)}, u32[]{:S(2)}) collective-permute-start(bf16[168,128]{1,0:T(8,128)(2,1)S(1)} %get-tuple-element.55.gram), channel_id=1, source_target_pairs={{0,7},{1,4},{2,5},{3,6},{4,1},{5,2},{6,3},{7,0},{8,13},{9,14},{10,... | collective-permute-start | bytes 129032 | tf_op jit(solution)/shard_map/ppermute | solution.py:621
  20.5 0.4 %shard_map.49 = (bf16[192,256]{1,0:T(8,128)(2,1)S(1)}, bf16[192,256]{1,0:T(8,128)(2,1)S(1)}, f32[32,256]{1,0:T(8,128)S(1)}, bf16[256,256]{1,0:T(8,128)(2,1)S(1)}...) custom-call(bf16[192,256]{1,0:T(8,128)(2,1)S(1)} %get-tuple-element.52.own, ...), custom_call_target="tpu_custom_call" | custom-call | flops 100000000 | bytes 1000000 | tf_op jit(solution)/shard_map/pallas_call | solution.py:589
  20.9 1.3 %collective-permute-done.4.other = bf16[168,128]{1,0:T(8,128)(2,1)S(1)} collective-permute-done((bf16[168,128]{1,0:T(8,128)(2,1)S(1)}, bf16[168,128]{1,0:T(8,128)(2,1)S(1)}, u32[]{:S(2)}, u32[]{:S(2)}) %collective-permute-start.4) | collective-permute-done | bytes 43040 | tf_op jit(solution)/shard_map/ppermute | solution.py:621
  22.2 0.8 %shard_map.50.left = bf16[16,256]{1,0:T(8,128)(2,1)S(1)} custom-call(bf16[192,256]{1,0:T(8,128)(2,1)S(1)} %get-tuple-element.58.own, f32[16,256]{1,0:T(8,128)S(1)} %get-tuple-element.59.own_image, f32[8,128]{1,0:T(8,128)S(1)} %get-tuple-element.60.own_trace, bf16[168,128]{1,0:T(8,128)(2,1)S(1)} %collective-permute-done.4.other, ...), custom_call_target="tpu_custom_call" | custom-call | flops 100000000 | bytes 1000000 | tf_op jit(solution)/shard_map/pallas_call | solution.py:589
  23.1 0.1 collective-permute-start.5
  23.1 1.0 %shard_map.51.second = bf16[192,1792]{1,0:T(8,128)(2,1)S(1)} custom-call(bf16[192,256]{1,0:T(8,128)(2,1)S(1)} %get-tuple-element.56.turned, bf16[192,256]{1,0:T(8,128)(2,1)S(1)} %get-tuple-element.57.lower, bf16[16,256]{1,0:T(8,128)(2,1)S(1)} %shard_map.50.left), custom_call_target="tpu_custom_call" | custom-call | flops 100000000 | bytes 1000000 | tf_op jit(solution)/shard_map/pallas_call | solution.py:589
  24.1 0.2 collective-permute-done.5.right
  24.3 0.4 %shard_map.52.own = bf16[168,128]{1,0:T(8,128)(2,1)S(1)} custom-call(bf16[192,1792]{1,0:T(8,128)(2,1)S(1)} %shard_map.51.second, bf16[16,256]{1,0:T(8,128)(2,1)S(1)} %collective-permute-done.5.right, f32[8,128]{1,0:T(8,128)S(1)} %get-tuple-element.63.refs_0_), custom_call_target="tpu_custom_call" | custom-call | flops 100000000 | bytes 1000000 | tf_op jit(solution)/shard_map/pallas_call | solution.py:589
  24.7 1.9 %collective-permute-start.6 = (bf16[168,128]{1,0:T(8,128)(2,1)S(1)}, bf16[168,128]{1,0:T(8,128)(2,1)S(1)}, u32[]{:S(2)}, u32[]{:S(2)}) collective-permute-start(bf16[168,128]{1,0:T(8,128)(2,1)S(1)} %shard_map.52.own), channel_id=1, source_target_pairs={{0,20},{4,16},{8,28},{12,24},{16,4},{20,0},{24,12},{28,8},{1,21},{... | collective-permute-start | bytes 129032 | tf_op jit(solution)/shard_map/ppermute | solution.py:604
  26.6 0.4 %shard_map.53 = (bf16[192,256]{1,0:T(8,128)(2,1)S(1)}, bf16[192,256]{1,0:T(8,128)(2,1)S(1)}, f32[8,128]{1,0:T(8,128)S(1)}) custom-call(bf16[168,128]{1,0:T(8,128)(2,1)S(1)} %shard_map.52.own), custom_call_target="tpu_custom_call" | custom-call | flops 100000000 | bytes 1000000 | tf_op jit(solution)/shard_map/pallas_call | solution.py:589
  27.1 1.3 %collective-permute-done.6.other = bf16[168,128]{1,0:T(8,128)(2,1)S(1)} collective-permute-done((bf16[168,128]{1,0:T(8,128)(2,1)S(1)}, bf16[168,128]{1,0:T(8,128)(2,1)S(1)}, u32[]{:S(2)}, u32[]{:S(2)}) %collective-permute-start.6) | collective-permute-done | bytes 43040 | tf_op jit(solution)/shard_map/ppermute | solution.py:604
  28.3 0.8 %shard_map.54 = (bf16[168,128]{1,0:T(8,128)(2,1)S(1)}, f32[8,128]{1,0:T(8,128)S(1)}) custom-call(bf16[192,256]{1,0:T(8,128)(2,1)S(1)} %get-tuple-element.65.product, f32[8,128]{1,0:T(8,128)S(1)} %get-tuple-element.66.mean.refs_1_, bf16[168,128]{1,0:T(8,128)(2,1)S(1)} %collective-permute-done.6.other), custom_call_target="tpu_custom_call" | custom-call | flops 100000000 | bytes 1000000 | tf_op jit(solution)/shard_map/pallas_call | solution.py:589
  29.2 3.6 %collective-permute-start.7 = (bf16[168,128]{1,0:T(8,128)(2,1)S(1)}, bf16[168,128]{1,0:T(8,128)(2,1)S(1)}, u32[]{:S(2)}, u32[]{:S(2)}) collective-permute-start(bf16[168,128]{1,0:T(8,128)(2,1)S(1)} %get-tuple-element.67.gram), channel_id=1, source_target_pairs={{0,7},{1,4},{2,5},{3,6},{4,1},{5,2},{6,3},{7,0},{8,13},{9,14},{10,... | collective-permute-start | bytes 129032 | tf_op jit(solution)/shard_map/ppermute | solution.py:621
  32.8 0.3 shard_map.55
  33.1 1.4 %collective-permute-done.7.other = bf16[168,128]{1,0:T(8,128)(2,1)S(1)} collective-permute-done((bf16[168,128]{1,0:T(8,128)(2,1)S(1)}, bf16[168,128]{1,0:T(8,128)(2,1)S(1)}, u32[]{:S(2)}, u32[]{:S(2)}) %collective-permute-start.7) | collective-permute-done | bytes 43040 | tf_op jit(solution)/shard_map/ppermute | solution.py:621
  34.5 0.8 %shard_map.56.left = bf16[16,256]{1,0:T(8,128)(2,1)S(1)} custom-call(bf16[192,256]{1,0:T(8,128)(2,1)S(1)} %get-tuple-element.70.own, f32[16,256]{1,0:T(8,128)S(1)} %get-tuple-element.71.own_image, f32[8,128]{1,0:T(8,128)S(1)} %get-tuple-element.72.own_trace, bf16[168,128]{1,0:T(8,128)(2,1)S(1)} %collective-permute-done.7.other, ...), custom_call_target="tpu_custom_call" | custom-call | flops 100000000 | bytes 1000000 | tf_op jit(solution)/shard_map/pallas_call | solution.py:589
  35.3 0.1 collective-permute-start.8
  35.4 1.0 %shard_map.57.second = bf16[192,1792]{1,0:T(8,128)(2,1)S(1)} custom-call(bf16[192,256]{1,0:T(8,128)(2,1)S(1)} %get-tuple-element.68.turned, bf16[192,256]{1,0:T(8,128)(2,1)S(1)} %get-tuple-element.69.lower, bf16[16,256]{1,0:T(8,128)(2,1)S(1)} %shard_map.56.left), custom_call_target="tpu_custom_call" | custom-call | flops 100000000 | bytes 1000000 | tf_op jit(solution)/shard_map/pallas_call | solution.py:589
  36.4 0.2 collective-permute-done.8.right
  36.6 1.4 %shard_map.58 = (f32[144,144]{1,0:T(8,128)}, f32[1,1]{1,0:T(1,128)}) custom-call(bf16[192,1792]{1,0:T(8,128)(2,1)S(1)} %shard_map.57.second, bf16[16,256]{1,0:T(8,128)(2,1)S(1)} %collective-permute-done.8.right, f32[8,128]{1,0:T(8,128)S(1)} %get-tuple-element.75.scale, f32[8,128]{1,0:T(8,128)S(1)} %get-tuple-element.54.mean.refs_0_, ...), custom_call_target="tpu_custom_call" | custom-call | flops 100000000 | bytes 1000000 | tf_op jit(solution)/shard_map/pallas_call | solution.py:589
Async XLA Ops:
  0.6 1.8 %collective-permute-start = (f32[144,144]{1,0:T(8,128)}, f32[144,144]{1,0:T(8,128)S(1)}, u32[]{:S(2)}, u32[]{:S(2)}) collective-permute-start(f32[144,144]{1,0:T(8,128)} %bitcast.2), channel_id=1, source_target_pairs={{0,4},{4,0},{8,12},{12,8},{16,20},{20,16},{24,28},{28,24},{1,5},{5... | collective-permute-start | bytes 248840 | tf_op jit(solution)/shard_map/ppermute | solution.py:604
  1.2 0.9 %copy-start = (f32[1,1,144,144]{3,2,1,0:T(8,128)S(1)}, f32[1,1,144,144]{3,2,1,0:T(8,128)}, u32[]{:S(2)}) copy-start(f32[1,1,144,144]{3,2,1,0:T(8,128)} %param.2) | copy-start | bytes 248836
  2.4 5.9 %copy-start.1 = (f32[3,12,144]{2,1,0:T(8,128)S(1)}, f32[3,12,144]{2,1,0:T(8,128)}, u32[]{:S(2)}) copy-start(f32[3,12,144]{2,1,0:T(8,128)} %start.5) | copy-start | bytes 62212
  3.5 6.6 %collective-permute-start.1 = (bf16[168,128]{1,0:T(8,128)(2,1)S(1)}, bf16[168,128]{1,0:T(8,128)(2,1)S(1)}, u32[]{:S(2)}, u32[]{:S(2)}) collective-permute-start(bf16[168,128]{1,0:T(8,128)(2,1)S(1)} %get-tuple-element.44.gram), channel_id=1, source_target_pairs={{0,7},{1,4},{2,5},{3,6},{4,1},{5,2},{6,3},{7,0},{8,13},{9,14},{10,... | collective-permute-start | bytes 129032 | tf_op jit(solution)/shard_map/ppermute | solution.py:621
  10.9 1.2 %collective-permute-start.2 = (bf16[16,256]{1,0:T(8,128)(2,1)S(1)}, bf16[16,256]{1,0:T(8,128)(2,1)S(1)}, u32[]{:S(2)}, u32[]{:S(2)}) collective-permute-start(bf16[16,256]{1,0:T(8,128)(2,1)S(1)} %shard_map.44.left), channel_id=1, source_target_pairs={{0,4},{4,0},{8,12},{12,8},{16,20},{20,16},{24,28},{28,24},{1,5},{5... | collective-permute-start | bytes 24584 | tf_op jit(solution)/shard_map/ppermute | solution.py:604
  12.6 3.5 %collective-permute-start.3 = (bf16[168,128]{1,0:T(8,128)(2,1)S(1)}, bf16[168,128]{1,0:T(8,128)(2,1)S(1)}, u32[]{:S(2)}, u32[]{:S(2)}) collective-permute-start(bf16[168,128]{1,0:T(8,128)(2,1)S(1)} %shard_map.46.own), channel_id=1, source_target_pairs={{0,12},{4,8},{8,4},{12,0},{16,28},{20,24},{24,20},{28,16},{1,13},{... | collective-permute-start | bytes 129032 | tf_op jit(solution)/shard_map/ppermute | solution.py:604
  16.9 5.3 %collective-permute-start.4 = (bf16[168,128]{1,0:T(8,128)(2,1)S(1)}, bf16[168,128]{1,0:T(8,128)(2,1)S(1)}, u32[]{:S(2)}, u32[]{:S(2)}) collective-permute-start(bf16[168,128]{1,0:T(8,128)(2,1)S(1)} %get-tuple-element.55.gram), channel_id=1, source_target_pairs={{0,7},{1,4},{2,5},{3,6},{4,1},{5,2},{6,3},{7,0},{8,13},{9,14},{10,... | collective-permute-start | bytes 129032 | tf_op jit(solution)/shard_map/ppermute | solution.py:621
  23.1 1.2 %collective-permute-start.5 = (bf16[16,256]{1,0:T(8,128)(2,1)S(1)}, bf16[16,256]{1,0:T(8,128)(2,1)S(1)}, u32[]{:S(2)}, u32[]{:S(2)}) collective-permute-start(bf16[16,256]{1,0:T(8,128)(2,1)S(1)} %shard_map.50.left), channel_id=1, source_target_pairs={{0,4},{4,0},{8,12},{12,8},{16,20},{20,16},{24,28},{28,24},{1,5},{5... | collective-permute-start | bytes 24584 | tf_op jit(solution)/shard_map/ppermute | solution.py:604
  24.7 3.6 %collective-permute-start.6 = (bf16[168,128]{1,0:T(8,128)(2,1)S(1)}, bf16[168,128]{1,0:T(8,128)(2,1)S(1)}, u32[]{:S(2)}, u32[]{:S(2)}) collective-permute-start(bf16[168,128]{1,0:T(8,128)(2,1)S(1)} %shard_map.52.own), channel_id=1, source_target_pairs={{0,20},{4,16},{8,28},{12,24},{16,4},{20,0},{24,12},{28,8},{1,21},{... | collective-permute-start | bytes 129032 | tf_op jit(solution)/shard_map/ppermute | solution.py:604
  29.2 5.3 %collective-permute-start.7 = (bf16[168,128]{1,0:T(8,128)(2,1)S(1)}, bf16[168,128]{1,0:T(8,128)(2,1)S(1)}, u32[]{:S(2)}, u32[]{:S(2)}) collective-permute-start(bf16[168,128]{1,0:T(8,128)(2,1)S(1)} %get-tuple-element.67.gram), channel_id=1, source_target_pairs={{0,7},{1,4},{2,5},{3,6},{4,1},{5,2},{6,3},{7,0},{8,13},{9,14},{10,... | collective-permute-start | bytes 129032 | tf_op jit(solution)/shard_map/ppermute | solution.py:621
  35.3 1.2 %collective-permute-start.8 = (bf16[16,256]{1,0:T(8,128)(2,1)S(1)}, bf16[16,256]{1,0:T(8,128)(2,1)S(1)}, u32[]{:S(2)}, u32[]{:S(2)}) collective-permute-start(bf16[16,256]{1,0:T(8,128)(2,1)S(1)} %shard_map.56.left), channel_id=1, source_target_pairs={{0,4},{4,0},{8,12},{12,8},{16,20},{20,16},{24,28},{28,24},{1,5},{5... | collective-permute-start | bytes 24584 | tf_op jit(solution)/shard_map/ppermute | solution.py:604

commit v13 on v12

--- a/solution.py
+++ b/solution.py
@@ -47,9 +47,9 @@
     return jnp.where(mask, 1.0, 0.0).astype(BF16)
 
 
-def spread_matrix(mirror, flip=0):
+def spread_matrix(mirror):
     i, j = iota((CHI * CHI, LANES), 0), iota((CHI * CHI, LANES), 1)
-    s, t = lax.bitwise_xor(group(j), flip), minor(j)
+    s, t = group(j), minor(j)
     source = jnp.where(mirror, t * CHI + s, s * CHI + t)
     return one_hot((i == source) & (s < CHI) & (t < CHI))
 
@@ -61,44 +61,70 @@
     return one_hot((j == source) & (s < CHI) & (t < CHI))
 
 
-def swapped_tiles(x, other=None):
-    lane_group = group(iota((PAD, 128), 1))
-    zero = jnp.zeros((PAD, 128), x.dtype)
-
-    def tile(array, p, side):
-        return array[p * PAD : (p + 1) * PAD, side * 128 : side * 128 + 128] if p < CHI else zero
-
-    sources, span = {}, 8 if other is None else 4
-    high = lax.bitwise_and(lane_group, 4) != 0
-    for p in range(CHI if other is None else PAD):
-        for side in range(2):
-            if other is None:
-                sources[p, side] = tile(x, p, side)
-            elif p & 4:
-                sources[p, side] = jnp.where(high, tile(x, p, side), tile(other, p ^ 4, side))
-            else:
-                sources[p, side] = jnp.where(high, tile(other, p ^ 4, side), tile(x, p, side))
-    tiles = []
-    for s in range(CHI):
-        pair = []
-        for side in range(2):
-            out = zero
-            for p in range(span):
-                source = (side * 8 + (s & 7 & -span)) | p
-                if other is None and source >= CHI:
-                    continue
-                shift = (p - s % span) % 8 * PAD
-                piece = sources[source, s >> 3]
-                piece = pltpu.roll(piece, shift, 1) if shift else piece
-                out = jnp.where(lax.bitwise_and(lane_group, span - 1) == p, piece, out)
-            pair.append(out)
-        tiles.append(pair)
+def placed_tiles(x, blocks, width):
+    lane = iota((PAD, 128), 1)
+    lane_group = group(lane)
+    tiles = [jnp.zeros((PAD, 128), x.dtype)] * CHI
+    for side in range(2):
+        moves = {}
+        for s in range(side * 8, min(side * 8 + 8, CHI)):
+            for k, p in enumerate(blocks):
+                moves.setdefault((k * width - (s & 7) * PAD) % 128, []).append((k, p, s))
+        for shift, members in moves.items():
+            source = None
+            for _, p, s in members:
+                piece = x[p * PAD : (p + 1) * PAD, side * 128 : side * 128 + 128]
+                source = piece if source is None else jnp.where(lane_group == (s & 7), piece, source)
+            source = pltpu.roll(source, shift, 1) if shift else source
+            for k, _, s in members:
+                here = (lane >= k * width) & (lane < (k + 1) * width)
+                tiles[s] = jnp.where(here, source, tiles[s])
     return tiles
 
 
-def block_swap(x, other=None):
-    tiles = swapped_tiles(x, other)
-    return jnp.concatenate([jnp.concatenate(pair, axis=1) for pair in tiles], axis=0)
+def block_swap(x):
+    halves = [placed_tiles(x, range(8), PAD), placed_tiles(x, range(8, CHI), PAD)]
+    return jnp.concatenate([jnp.concatenate(pair, axis=1) for pair in zip(*halves)], axis=0)
+
+
+def widen(x):
+    return jnp.concatenate([x, jnp.zeros((x.shape[0], LANES - x.shape[1]), x.dtype)], axis=1)
+
+
+def parts3(x):
+    a = x.astype(BF16)
+    rest = x - a.astype(F32)
+    b = rest.astype(BF16)
+    c = (rest - b.astype(F32)).astype(BF16)
+    return jnp.concatenate([a, b, c], axis=0)
+
+
+def parts2(x):
+    a = x.astype(BF16)
+    return jnp.concatenate([a, (x - a.astype(F32)).astype(BF16)], axis=0)
+
+
+def fold2(y):
+    n = y.shape[0] // 2
+    return y[n:] + y[:n]
+
+
+def fold3(y):
+    n = y.shape[0] // 3
+    return (y[2 * n :] + y[n : 2 * n]) + y[:n]
+
+
+def compact(x):
+    blocks = x.shape[0] // PAD
+    legs = x.astype(F32).reshape(blocks, PAD, 128)[:, :CHI]
+    return legs.reshape(blocks * CHI, 128).astype(BF16)
+
+
+def spaced(x):
+    blocks = x.shape[0] // CHI
+    legs = x.astype(F32).reshape(blocks, CHI, 128)
+    rest = jnp.zeros((blocks, PAD - CHI, 128), F32)
+    return jnp.concatenate([legs, rest], axis=1).reshape(blocks * PAD, 128).astype(BF16)
 
 
 def joined(x):
@@ -122,136 +148,6 @@
     return jnp.concatenate([x[:, :128], *tails], axis=0)
 
 
-def product_both(a, b, scale=None):
-    zero = jnp.zeros((PAD, b.shape[1]), b.dtype)
-    blocks = [b[s * PAD : (s + 1) * PAD] if s < CHI else zero for s in range(PAD)]
-    plain = mm(a, jnp.concatenate(blocks, axis=0), NT)
-    moved = mm(a, jnp.concatenate([blocks[s ^ 4] for s in range(PAD)], axis=0), NT)
-    if scale is not None:
-        plain, moved = plain * scale, moved * scale
-    return plain.astype(BF16), moved.astype(BF16)
-
-
-def widen(x):
-    return jnp.concatenate([x, jnp.zeros((x.shape[0], LANES - x.shape[1]), x.dtype)], axis=1)
-
-
-def parts3(x):
-    a = x.astype(BF16)
-    rest = x - a.astype(F32)
-    b = rest.astype(BF16)
-    c = (rest - b.astype(F32)).astype(BF16)
-    return jnp.concatenate([a, b, c], axis=0)
-
-
-def parts2(x):
-    a = x.astype(BF16)
-    return jnp.concatenate([a, (x - a.astype(F32)).astype(BF16)], axis=0)
-
-
-def fold2(y):
-    n = y.shape[0] // 2
-    return y[n:] + y[:n]
-
-
-def fold3(y):
-    n = y.shape[0] // 3
-    return (y[2 * n :] + y[n : 2 * n]) + y[:n]
-
-
-def compact(x):
-    blocks = x.shape[0] // PAD
-    legs = x.astype(F32).reshape(blocks, PAD, 128)[:, :CHI]
-    return legs.reshape(blocks * CHI, 128).astype(BF16)
-
-
-def spaced(x):
-    blocks = x.shape[0] // CHI
-    legs = x.astype(F32).reshape(blocks, CHI, 128)
-    rest = jnp.zeros((blocks, PAD - CHI, 128), F32)
-    return jnp.concatenate([legs, rest], axis=1).reshape(blocks * PAD, 128).astype(BF16)
-
-
-def joined(x):
-    x = spaced(x)
-    lane = iota((PAD, 128), 1)
-    sides = []
-    for k in range(CHI):
-        at = ROWS + (k >> 3) * PAD
-        shift = -(k & 7) * PAD % 128
-        side = pltpu.roll(x[at : at + PAD], shift, 1) if shift else x[at : at + PAD]
-        sides.append(jnp.where(lane < PAD, side, jnp.zeros_like(side)))
-    return jnp.concatenate([x[:ROWS], jnp.concatenate(sides, axis=0)], axis=1)
-
-
-def split(x):
-    lane_group = group(iota((PAD, 128), 1))
-    tails = [jnp.zeros((PAD, 128), x.dtype)] * 2
-    for k in range(CHI):
-        block = x[k * PAD : (k + 1) * PAD, 128:]
-        tails[k >> 3] = jnp.where(lane_group == (k & 7), block, tails[k >> 3])
-    return jnp.concatenate([x[:, :128], *tails], axis=0)
-
-
-def product_both(a, b, scale=None):
-    zero = jnp.zeros((PAD, b.shape[1]), b.dtype)
-    blocks = [b[s * PAD : (s + 1) * PAD] if s < CHI else zero for s in range(PAD)]
-    plain = mm(a, jnp.concatenate(blocks, axis=0), NT)
-    moved = mm(a, jnp.concatenate([blocks[s ^ 4] for s in range(PAD)], axis=0), NT)
-    if scale is not None:
-        plain, moved = plain * scale, moved * scale
-    return plain.astype(BF16), moved.astype(BF16)
-
-
-def widen(x):
-    return jnp.concatenate([x, jnp.zeros((x.shape[0], LANES - x.shape[1]), x.dtype)], axis=1)
-
-
-def parts3(x):
-    a = x.astype(BF16)
-    rest = x - a.astype(F32)
-    b = rest.astype(BF16)
-    c = (rest - b.astype(F32)).astype(BF16)
-    return jnp.concatenate([a, b, c], axis=0)
-
-
-def parts2(x):
-    a = x.astype(BF16)
-    return jnp.concatenate([a, (x - a.astype(F32)).astype(BF16)], axis=0)
-
-
-def fold2(y):
-    n = y.shape[0] // 2
-    return y[n:] + y[:n]
-
-
-def fold3(y):
-    n = y.shape[0] // 3
-    return (y[2 * n :] + y[n : 2 * n]) + y[:n]
-
-
-def compact(x):
-    blocks = x.shape[0] // PAD
-    legs = x.astype(F32).reshape(blocks, PAD, 128)[:, :CHI]
-    return legs.reshape(blocks * CHI, 128).astype(BF16)
-
-
-def spaced(x):
-    blocks = x.shape[0] // CHI
-    legs = x.astype(F32).reshape(blocks, CHI, 128)
-    rest = jnp.zeros((blocks, PAD - CHI, 128), F32)
-    return jnp.concatenate([legs, rest], axis=1).reshape(blocks * PAD, 128).astype(BF16)
-
-
-def unfold(x):
-    side = x[ROWS:]
-    low = iota(side.shape, 1) < FOLD
-    zero = jnp.zeros_like(side)
-    first = jnp.where(low, side, zero)
-    last = jnp.where(low, pltpu.roll(side, 128 - FOLD, 1), zero)
-    return jnp.concatenate([x[:ROWS], jnp.concatenate([first, last], axis=0)], axis=1)
-
-
 def row_swap(x):
     legs = x.astype(F32).reshape(CHI, PAD, x.shape[1])[:, :CHI]
     turned = jnp.transpose(legs, (1, 0, 2))
@@ -260,22 +156,15 @@
 
 
 def product_part(x, scale=None):
-    return block_swap(*product_both(row_swap(x), x, scale))
+    product = mm(row_swap(x), x, NT)
+    product = product if scale is None else product * scale[:, :ROWS]
+    return block_swap(widen(product.astype(BF16)))
 
 
 def outer_part(first, second):
     outer = widen(mm(first, row_swap(second), NT).astype(BF16))
     lane = iota((PAD, 128), 1)
-    tiles = []
-    for s in range(CHI):
-        tile = jnp.zeros((PAD, 128), BF16)
-        for p in range(128 // CHI + 1):
-            at = (s >> 3) * 128
-            piece = outer[p * PAD : (p + 1) * PAD, at : at + 128]
-            shift = (p * CHI - (s & 7) * PAD) % 128
-            piece = pltpu.roll(piece, shift, 1) if shift else piece
-            tile = jnp.where((lane >= p * CHI) & (lane < p * CHI + CHI), piece, tile)
-        tiles.append(tile)
+    tiles = placed_tiles(outer, range(128 // CHI + 1), CHI)
     cut = CHI * (CHI - 1) - 128
     for side in range(2):
         pieces = [outer[p * PAD : (p + 1) * PAD, side * 128 : side * 128 + 128] for p in (CHI - 2, CHI - 1)]
@@ -482,8 +371,7 @@
     legs = jnp.where(lower, jnp.transpose(legs, (1, 0, 2)), legs)
     rest = jnp.zeros((CHI, PAD - CHI, CHI * CHI), F32)
     rows = jnp.concatenate([legs, rest], axis=1).reshape(ROWS, CHI * CHI).astype(BF16)
-    plain = mm(rows, spread_matrix(mirror)).astype(BF16)
-    return plain, mm(rows, spread_matrix(mirror, 4)).astype(BF16)
+    return mm(rows, spread_matrix(mirror)).astype(BF16)
 
 
 def pick(own_first, own, other):
@@ -498,15 +386,15 @@
     return [flag != 0 for flag in flags]
 
 
-def spread_kernel(own, plain_o, flipped_o):
+def spread_kernel(own, spread_o):
     _, _, own_lower, mirror = roles(0)
-    plain_o[...], flipped_o[...] = spread(own[...], mirror, own_lower)
-
-
-def first_gram_kernel(plain, flipped, other, mine_o, theirs_o, gram_o):
+    spread_o[...] = spread(own[...], mirror, own_lower)
+
+
+def first_gram_kernel(own, other, mine_o, theirs_o, gram_o):
     own_first, _, own_lower, mirror = roles(0)
-    mine = block_swap(plain[...], flipped[...])
-    theirs = block_swap(*spread(other[...], mirror, jnp.logical_not(own_lower)))
+    mine = block_swap(own[...])
+    theirs = block_swap(spread(other[...], mirror, jnp.logical_not(own_lower)))
     mine_o[...], theirs_o[...] = mine, theirs
     products = pick(own_first, product_part(mine), product_part(theirs))
     gram_o[...] = outer_part(*products)
@@ -631,8 +519,8 @@
     for level in range(LEVELS):
         if level == 0:
             other = from_partner(own, 1)
-            plain, flipped = call(spread_kernel, [mat, mat])(own)
-            own, other, gram = call(first_gram_kernel, [mat, mat, sent])(plain, flipped, other)
+            (own,) = call(spread_kernel, [mat])(own)
+            own, other, gram = call(first_gram_kernel, [mat, mat, sent])(own, other)
         else:
             other = from_partner(own, 1 << level | 1)
             own, product, mean = call(own_kernel, [mat, mat, one])(own)

time: 38.1 us -> 37.8 us (level)
  Pallas kernels: 12.6 us -> 12.1 us
    pallas_call x18, Pallas kernels: 12.6 us -> 12.1 us  [run(): pl.pallas_call(kernel, out_shape=[jax.ShapeDtypeStruct(s, d) for s, d in...]
  transfers between devices with their start and end apart: 9 -> 9, of which waited for: 9 -> 9; matrix products, arithmetic and copies ran while one was open for 0% -> 0% of each run, Pallas kernels for 14% -> 13%
where the time goes in v13:
time: 37.8 us; the launch traced here: 37.6 us
  starting transfers between devices  16.4 us (43%)
  Pallas kernels  12.1 us (32%)
  waiting for transfers between devices  7.33 us (19%)
  local copies, waits for them, and re-layouts  0.92 us (2%)
  between operations  0.79 us (2%)
    pallas_call x18, Pallas kernels, run(): pl.pallas_call(kernel, out_shape=[jax.ShapeDtypeStruct(s, d) for s, d in...  12.1 us
    ppermute x3, starting transfers between devices, from_bond(): return lax.ppermute(array, ('row', 'col'), pairs)  12 us
    ppermute x6, starting transfers between devices, from_partner(): return lax.ppermute(array, 'row', [(i, i ^ flip) for i in range(count)])  4.41 us
    ppermute x3, waiting for transfers between devices, from_bond(): return lax.ppermute(array, ('row', 'col'), pairs)  4.03 us
    ppermute x6, waiting for transfers between devices, from_partner(): return lax.ppermute(array, 'row', [(i, i ^ flip) for i in range(count)])  3.3 us
    unnamed x4, local copies, waits for them, and re-layouts  0.92 us
  transfers between devices with their start and end apart: 9, of which 9 were waited for; matrix products, arithmetic and copies ran while one was open for 0% of the time, Pallas kernels for 13%

profile of v13, /device:TPU:0, one launch (start us, length us, event | category | flops | bytes accessed | tf_op | source)
XLA Modules:
  0.0 37.6 jit_solution(957266255920922467)
XLA Ops:
  0.6 0.6 %collective-permute-start = (f32[144,144]{1,0:T(8,128)}, f32[144,144]{1,0:T(8,128)S(1)}, u32[]{:S(2)}, u32[]{:S(2)}) collective-permute-start(f32[144,144]{1,0:T(8,128)} %bitcast.2), channel_id=1, source_target_pairs={{0,4},{4,0},{8,12},{12,8},{16,20},{20,16},{24,28},{28,24},{1,5},{5... | collective-permute-start | bytes 248840 | tf_op jit(solution)/shard_map/ppermute | solution.py:492
  1.2 0.0 copy-start
  1.2 0.9 %copy-done = f32[1,1,144,144]{3,2,1,0:T(8,128)S(1)} copy-done((f32[1,1,144,144]{3,2,1,0:T(8,128)S(1)}, f32[1,1,144,144]{3,2,1,0:T(8,128)}, u32[]{:S(2)}) %copy-start) | copy-done | bytes 82968
  2.1 0.2 shard_map.41.own
  2.3 0.0 copy-start.1
  2.3 0.1 collective-permute-done.other
  2.4 1.0 %shard_map.42 = (bf16[192,256]{1,0:T(8,128)(2,1)S(1)}, bf16[192,256]{1,0:T(8,128)(2,1)S(1)}, bf16[168,128]{1,0:T(8,128)(2,1)S(1)}) custom-call(bf16[192,256]{1,0:T(8,128)(2,1)S(1)} %shard_map.41.own, f32[144,144]{1,0:T(8,128)S(1)} %collective-permute-done.other), custom_call_target="tpu_custom_call" | custom-call | flops 100000000 | bytes 1000000 | tf_op jit(solution)/shard_map/pallas_call | solution.py:477
  3.4 4.8 %collective-permute-start.1 = (bf16[168,128]{1,0:T(8,128)(2,1)S(1)}, bf16[168,128]{1,0:T(8,128)(2,1)S(1)}, u32[]{:S(2)}, u32[]{:S(2)}) collective-permute-start(bf16[168,128]{1,0:T(8,128)(2,1)S(1)} %get-tuple-element.40.gram), channel_id=1, source_target_pairs={{0,7},{1,4},{2,5},{3,6},{4,1},{5,2},{6,3},{7,0},{8,13},{9,14},{10,... | collective-permute-start | bytes 129032 | tf_op jit(solution)/shard_map/ppermute | solution.py:509
  8.1 0.0 copy-done.1
  8.1 0.5 %shard_map.43 = (bf16[192,256]{1,0:T(8,128)(2,1)S(1)}, bf16[192,256]{1,0:T(8,128)(2,1)S(1)}, f32[32,256]{1,0:T(8,128)S(1)}, bf16[256,256]{1,0:T(8,128)(2,1)S(1)}...) custom-call(bf16[192,256]{1,0:T(8,128)(2,1)S(1)} %get-tuple-element.38.own, ...), custom_call_target="tpu_custom_call" | custom-call | flops 100000000 | bytes 1000000 | tf_op jit(solution)/shard_map/pallas_call | solution.py:477
  8.6 1.3 %collective-permute-done.1.other = bf16[168,128]{1,0:T(8,128)(2,1)S(1)} collective-permute-done((bf16[168,128]{1,0:T(8,128)(2,1)S(1)}, bf16[168,128]{1,0:T(8,128)(2,1)S(1)}, u32[]{:S(2)}, u32[]{:S(2)}) %collective-permute-start.1) | collective-permute-done | bytes 43040 | tf_op jit(solution)/shard_map/ppermute | solution.py:509
  9.9 0.8 %shard_map.44.left = bf16[16,256]{1,0:T(8,128)(2,1)S(1)} custom-call(bf16[192,256]{1,0:T(8,128)(2,1)S(1)} %get-tuple-element.43.own, f32[16,256]{1,0:T(8,128)S(1)} %get-tuple-element.44.own_image, f32[8,128]{1,0:T(8,128)S(1)} %get-tuple-element.45.own_trace, bf16[168,128]{1,0:T(8,128)(2,1)S(1)} %collective-permute-done.1.other, ...), custom_call_target="tpu_custom_call" | custom-call | flops 100000000 | bytes 1000000 | tf_op jit(solution)/shard_map/pallas_call | solution.py:477
  10.8 0.1 collective-permute-start.2
  10.9 1.0 %shard_map.45.second = bf16[192,1792]{1,0:T(8,128)(2,1)S(1)} custom-call(bf16[192,256]{1,0:T(8,128)(2,1)S(1)} %get-tuple-element.41.turned, bf16[192,256]{1,0:T(8,128)(2,1)S(1)} %get-tuple-element.42.lower, bf16[16,256]{1,0:T(8,128)(2,1)S(1)} %shard_map.44.left), custom_call_target="tpu_custom_call" | custom-call | flops 100000000 | bytes 1000000 | tf_op jit(solution)/shard_map/pallas_call | solution.py:477
  11.9 0.2 collective-permute-done.2.right
  12.0 0.4 %shard_map.46.own = bf16[168,128]{1,0:T(8,128)(2,1)S(1)} custom-call(bf16[192,1792]{1,0:T(8,128)(2,1)S(1)} %shard_map.45.second, bf16[16,256]{1,0:T(8,128)(2,1)S(1)} %collective-permute-done.2.right), custom_call_target="tpu_custom_call" | custom-call | flops 100000000 | bytes 1000000 | tf_op jit(solution)/shard_map/pallas_call | solution.py:477
  12.4 1.8 %collective-permute-start.3 = (bf16[168,128]{1,0:T(8,128)(2,1)S(1)}, bf16[168,128]{1,0:T(8,128)(2,1)S(1)}, u32[]{:S(2)}, u32[]{:S(2)}) collective-permute-start(bf16[168,128]{1,0:T(8,128)(2,1)S(1)} %shard_map.46.own), channel_id=1, source_target_pairs={{0,12},{4,8},{8,4},{12,0},{16,28},{20,24},{24,20},{28,16},{1,13},{... | collective-permute-start | bytes 129032 | tf_op jit(solution)/shard_map/ppermute | solution.py:492
  14.2 0.4 shard_map.47
  14.6 1.4 %collective-permute-done.3.other = bf16[168,128]{1,0:T(8,128)(2,1)S(1)} collective-permute-done((bf16[168,128]{1,0:T(8,128)(2,1)S(1)}, bf16[168,128]{1,0:T(8,128)(2,1)S(1)}, u32[]{:S(2)}, u32[]{:S(2)}) %collective-permute-start.3) | collective-permute-done | bytes 43040 | tf_op jit(solution)/shard_map/ppermute | solution.py:492
  16.0 0.7 %shard_map.48 = (bf16[168,128]{1,0:T(8,128)(2,1)S(1)}, f32[8,128]{1,0:T(8,128)S(1)}) custom-call(bf16[192,256]{1,0:T(8,128)(2,1)S(1)} %get-tuple-element.49.product, f32[8,128]{1,0:T(8,128)S(1)} %get-tuple-element.50.mean.refs_0_, bf16[168,128]{1,0:T(8,128)(2,1)S(1)} %collective-permute-done.3.other), custom_call_target="tpu_custom_call" | custom-call | flops 100000000 | bytes 1000000 | tf_op jit(solution)/shard_map/pallas_call | solution.py:477
  16.7 3.6 %collective-permute-start.4 = (bf16[168,128]{1,0:T(8,128)(2,1)S(1)}, bf16[168,128]{1,0:T(8,128)(2,1)S(1)}, u32[]{:S(2)}, u32[]{:S(2)}) collective-permute-start(bf16[168,128]{1,0:T(8,128)(2,1)S(1)} %get-tuple-element.51.gram), channel_id=1, source_target_pairs={{0,7},{1,4},{2,5},{3,6},{4,1},{5,2},{6,3},{7,0},{8,13},{9,14},{10,... | collective-permute-start | bytes 129032 | tf_op jit(solution)/shard_map/ppermute | solution.py:509
  20.3 0.4 %shard_map.49 = (bf16[192,256]{1,0:T(8,128)(2,1)S(1)}, bf16[192,256]{1,0:T(8,128)(2,1)S(1)}, f32[32,256]{1,0:T(8,128)S(1)}, bf16[256,256]{1,0:T(8,128)(2,1)S(1)}...) custom-call(bf16[192,256]{1,0:T(8,128)(2,1)S(1)} %get-tuple-element.48.own, ...), custom_call_target="tpu_custom_call" | custom-call | flops 100000000 | bytes 1000000 | tf_op jit(solution)/shard_map/pallas_call | solution.py:477
  20.7 1.3 %collective-permute-done.4.other = bf16[168,128]{1,0:T(8,128)(2,1)S(1)} collective-permute-done((bf16[168,128]{1,0:T(8,128)(2,1)S(1)}, bf16[168,128]{1,0:T(8,128)(2,1)S(1)}, u32[]{:S(2)}, u32[]{:S(2)}) %collective-permute-start.4) | collective-permute-done | bytes 43040 | tf_op jit(solution)/shard_map/ppermute | solution.py:509
  22.0 0.8 %shard_map.50.left = bf16[16,256]{1,0:T(8,128)(2,1)S(1)} custom-call(bf16[192,256]{1,0:T(8,128)(2,1)S(1)} %get-tuple-element.54.own, f32[16,256]{1,0:T(8,128)S(1)} %get-tuple-element.55.own_image, f32[8,128]{1,0:T(8,128)S(1)} %get-tuple-element.56.own_trace, bf16[168,128]{1,0:T(8,128)(2,1)S(1)} %collective-permute-done.4.other, ...), custom_call_target="tpu_custom_call" | custom-call | flops 100000000 | bytes 1000000 | tf_op jit(solution)/shard_map/pallas_call | solution.py:477
  22.8 0.1 collective-permute-start.5
  22.9 1.0 %shard_map.51.second = bf16[192,1792]{1,0:T(8,128)(2,1)S(1)} custom-call(bf16[192,256]{1,0:T(8,128)(2,1)S(1)} %get-tuple-element.52.turned, bf16[192,256]{1,0:T(8,128)(2,1)S(1)} %get-tuple-element.53.lower, bf16[16,256]{1,0:T(8,128)(2,1)S(1)} %shard_map.50.left), custom_call_target="tpu_custom_call" | custom-call | flops 100000000 | bytes 1000000 | tf_op jit(solution)/shard_map/pallas_call | solution.py:477
  23.9 0.2 collective-permute-done.5.right
  24.1 0.4 %shard_map.52.own = bf16[168,128]{1,0:T(8,128)(2,1)S(1)} custom-call(bf16[192,1792]{1,0:T(8,128)(2,1)S(1)} %shard_map.51.second, bf16[16,256]{1,0:T(8,128)(2,1)S(1)} %collective-permute-done.5.right, f32[8,128]{1,0:T(8,128)S(1)} %get-tuple-element.59.refs_0_), custom_call_target="tpu_custom_call" | custom-call | flops 100000000 | bytes 1000000 | tf_op jit(solution)/shard_map/pallas_call | solution.py:477
  24.5 1.9 %collective-permute-start.6 = (bf16[168,128]{1,0:T(8,128)(2,1)S(1)}, bf16[168,128]{1,0:T(8,128)(2,1)S(1)}, u32[]{:S(2)}, u32[]{:S(2)}) collective-permute-start(bf16[168,128]{1,0:T(8,128)(2,1)S(1)} %shard_map.52.own), channel_id=1, source_target_pairs={{0,20},{4,16},{8,28},{12,24},{16,4},{20,0},{24,12},{28,8},{1,21},{... | collective-permute-start | bytes 129032 | tf_op jit(solution)/shard_map/ppermute | solution.py:492
  26.4 0.4 shard_map.53
  26.8 1.3 %collective-permute-done.6.other = bf16[168,128]{1,0:T(8,128)(2,1)S(1)} collective-permute-done((bf16[168,128]{1,0:T(8,128)(2,1)S(1)}, bf16[168,128]{1,0:T(8,128)(2,1)S(1)}, u32[]{:S(2)}, u32[]{:S(2)}) %collective-permute-start.6) | collective-permute-done | bytes 43040 | tf_op jit(solution)/shard_map/ppermute | solution.py:492
  28.1 0.7 %shard_map.54 = (bf16[168,128]{1,0:T(8,128)(2,1)S(1)}, f32[8,128]{1,0:T(8,128)S(1)}) custom-call(bf16[192,256]{1,0:T(8,128)(2,1)S(1)} %get-tuple-element.61.product, f32[8,128]{1,0:T(8,128)S(1)} %get-tuple-element.62.mean.refs_1_, bf16[168,128]{1,0:T(8,128)(2,1)S(1)} %collective-permute-done.6.other), custom_call_target="tpu_custom_call" | custom-call | flops 100000000 | bytes 1000000 | tf_op jit(solution)/shard_map/pallas_call | solution.py:477
  28.8 3.6 %collective-permute-start.7 = (bf16[168,128]{1,0:T(8,128)(2,1)S(1)}, bf16[168,128]{1,0:T(8,128)(2,1)S(1)}, u32[]{:S(2)}, u32[]{:S(2)}) collective-permute-start(bf16[168,128]{1,0:T(8,128)(2,1)S(1)} %get-tuple-element.63.gram), channel_id=1, source_target_pairs={{0,7},{1,4},{2,5},{3,6},{4,1},{5,2},{6,3},{7,0},{8,13},{9,14},{10,... | collective-permute-start | bytes 129032 | tf_op jit(solution)/shard_map/ppermute | solution.py:509
  32.5 0.3 shard_map.55
  32.8 1.4 %collective-permute-done.7.other = bf16[168,128]{1,0:T(8,128)(2,1)S(1)} collective-permute-done((bf16[168,128]{1,0:T(8,128)(2,1)S(1)}, bf16[168,128]{1,0:T(8,128)(2,1)S(1)}, u32[]{:S(2)}, u32[]{:S(2)}) %collective-permute-start.7) | collective-permute-done | bytes 43040 | tf_op jit(solution)/shard_map/ppermute | solution.py:509
  34.2 0.8 %shard_map.56.left = bf16[16,256]{1,0:T(8,128)(2,1)S(1)} custom-call(bf16[192,256]{1,0:T(8,128)(2,1)S(1)} %get-tuple-element.66.own, f32[16,256]{1,0:T(8,128)S(1)} %get-tuple-element.67.own_image, f32[8,128]{1,0:T(8,128)S(1)} %get-tuple-element.68.own_trace, bf16[168,128]{1,0:T(8,128)(2,1)S(1)} %collective-permute-done.7.other, ...), custom_call_target="tpu_custom_call" | custom-call | flops 100000000 | bytes 1000000 | tf_op jit(solution)/shard_map/pallas_call | solution.py:477
  35.0 0.1 collective-permute-start.8
  35.1 1.0 %shard_map.57.second = bf16[192,1792]{1,0:T(8,128)(2,1)S(1)} custom-call(bf16[192,256]{1,0:T(8,128)(2,1)S(1)} %get-tuple-element.64.turned, bf16[192,256]{1,0:T(8,128)(2,1)S(1)} %get-tuple-element.65.lower, bf16[16,256]{1,0:T(8,128)(2,1)S(1)} %shard_map.56.left), custom_call_target="tpu_custom_call" | custom-call | flops 100000000 | bytes 1000000 | tf_op jit(solution)/shard_map/pallas_call | solution.py:477
  36.1 0.2 collective-permute-done.8.right
  36.3 1.4 %shard_map.58 = (f32[144,144]{1,0:T(8,128)}, f32[1,1]{1,0:T(1,128)}) custom-call(bf16[192,1792]{1,0:T(8,128)(2,1)S(1)} %shard_map.57.second, bf16[16,256]{1,0:T(8,128)(2,1)S(1)} %collective-permute-done.8.right, f32[8,128]{1,0:T(8,128)S(1)} %get-tuple-element.71.scale, f32[8,128]{1,0:T(8,128)S(1)} %get-tuple-element.50.mean.refs_0_, ...), custom_call_target="tpu_custom_call" | custom-call | flops 100000000 | bytes 1000000 | tf_op jit(solution)/shard_map/pallas_call | solution.py:477
Async XLA Ops:
  0.6 1.8 %collective-permute-start = (f32[144,144]{1,0:T(8,128)}, f32[144,144]{1,0:T(8,128)S(1)}, u32[]{:S(2)}, u32[]{:S(2)}) collective-permute-start(f32[144,144]{1,0:T(8,128)} %bitcast.2), channel_id=1, source_target_pairs={{0,4},{4,0},{8,12},{12,8},{16,20},{20,16},{24,28},{28,24},{1,5},{5... | collective-permute-start | bytes 248840 | tf_op jit(solution)/shard_map/ppermute | solution.py:492
  1.2 0.9 %copy-start = (f32[1,1,144,144]{3,2,1,0:T(8,128)S(1)}, f32[1,1,144,144]{3,2,1,0:T(8,128)}, u32[]{:S(2)}) copy-start(f32[1,1,144,144]{3,2,1,0:T(8,128)} %param.2) | copy-start | bytes 248836
  2.3 5.8 %copy-start.1 = (f32[3,12,144]{2,1,0:T(8,128)S(1)}, f32[3,12,144]{2,1,0:T(8,128)}, u32[]{:S(2)}) copy-start(f32[3,12,144]{2,1,0:T(8,128)} %start.5) | copy-start | bytes 62212
  3.4 6.6 %collective-permute-start.1 = (bf16[168,128]{1,0:T(8,128)(2,1)S(1)}, bf16[168,128]{1,0:T(8,128)(2,1)S(1)}, u32[]{:S(2)}, u32[]{:S(2)}) collective-permute-start(bf16[168,128]{1,0:T(8,128)(2,1)S(1)} %get-tuple-element.40.gram), channel_id=1, source_target_pairs={{0,7},{1,4},{2,5},{3,6},{4,1},{5,2},{6,3},{7,0},{8,13},{9,14},{10,... | collective-permute-start | bytes 129032 | tf_op jit(solution)/shard_map/ppermute | solution.py:509
  10.8 1.2 %collective-permute-start.2 = (bf16[16,256]{1,0:T(8,128)(2,1)S(1)}, bf16[16,256]{1,0:T(8,128)(2,1)S(1)}, u32[]{:S(2)}, u32[]{:S(2)}) collective-permute-start(bf16[16,256]{1,0:T(8,128)(2,1)S(1)} %shard_map.44.left), channel_id=1, source_target_pairs={{0,4},{4,0},{8,12},{12,8},{16,20},{20,16},{24,28},{28,24},{1,5},{5... | collective-permute-start | bytes 24584 | tf_op jit(solution)/shard_map/ppermute | solution.py:492
  12.4 3.5 %collective-permute-start.3 = (bf16[168,128]{1,0:T(8,128)(2,1)S(1)}, bf16[168,128]{1,0:T(8,128)(2,1)S(1)}, u32[]{:S(2)}, u32[]{:S(2)}) collective-permute-start(bf16[168,128]{1,0:T(8,128)(2,1)S(1)} %shard_map.46.own), channel_id=1, source_target_pairs={{0,12},{4,8},{8,4},{12,0},{16,28},{20,24},{24,20},{28,16},{1,13},{... | collective-permute-start | bytes 129032 | tf_op jit(solution)/shard_map/ppermute | solution.py:492
  16.7 5.3 %collective-permute-start.4 = (bf16[168,128]{1,0:T(8,128)(2,1)S(1)}, bf16[168,128]{1,0:T(8,128)(2,1)S(1)}, u32[]{:S(2)}, u32[]{:S(2)}) collective-permute-start(bf16[168,128]{1,0:T(8,128)(2,1)S(1)} %get-tuple-element.51.gram), channel_id=1, source_target_pairs={{0,7},{1,4},{2,5},{3,6},{4,1},{5,2},{6,3},{7,0},{8,13},{9,14},{10,... | collective-permute-start | bytes 129032 | tf_op jit(solution)/shard_map/ppermute | solution.py:509
  22.8 1.2 %collective-permute-start.5 = (bf16[16,256]{1,0:T(8,128)(2,1)S(1)}, bf16[16,256]{1,0:T(8,128)(2,1)S(1)}, u32[]{:S(2)}, u32[]{:S(2)}) collective-permute-start(bf16[16,256]{1,0:T(8,128)(2,1)S(1)} %shard_map.50.left), channel_id=1, source_target_pairs={{0,4},{4,0},{8,12},{12,8},{16,20},{20,16},{24,28},{28,24},{1,5},{5... | collective-permute-start | bytes 24584 | tf_op jit(solution)/shard_map/ppermute | solution.py:492
  24.5 3.6 %collective-permute-start.6 = (bf16[168,128]{1,0:T(8,128)(2,1)S(1)}, bf16[168,128]{1,0:T(8,128)(2,1)S(1)}, u32[]{:S(2)}, u32[]{:S(2)}) collective-permute-start(bf16[168,128]{1,0:T(8,128)(2,1)S(1)} %shard_map.52.own), channel_id=1, source_target_pairs={{0,20},{4,16},{8,28},{12,24},{16,4},{20,0},{24,12},{28,8},{1,21},{... | collective-permute-start | bytes 129032 | tf_op jit(solution)/shard_map/ppermute | solution.py:492
  28.8 5.3 %collective-permute-start.7 = (bf16[168,128]{1,0:T(8,128)(2,1)S(1)}, bf16[168,128]{1,0:T(8,128)(2,1)S(1)}, u32[]{:S(2)}, u32[]{:S(2)}) collective-permute-start(bf16[168,128]{1,0:T(8,128)(2,1)S(1)} %get-tuple-element.63.gram), channel_id=1, source_target_pairs={{0,7},{1,4},{2,5},{3,6},{4,1},{5,2},{6,3},{7,0},{8,13},{9,14},{10,... | collective-permute-start | bytes 129032 | tf_op jit(solution)/shard_map/ppermute | solution.py:509
  35.0 1.2 %collective-permute-start.8 = (bf16[16,256]{1,0:T(8,128)(2,1)S(1)}, bf16[16,256]{1,0:T(8,128)(2,1)S(1)}, u32[]{:S(2)}, u32[]{:S(2)}) collective-permute-start(bf16[16,256]{1,0:T(8,128)(2,1)S(1)} %shard_map.56.left), channel_id=1, source_target_pairs={{0,4},{4,0},{8,12},{12,8},{16,20},{20,16},{24,28},{28,24},{1,5},{5... | collective-permute-start | bytes 24584 | tf_op jit(solution)/shard_map/ppermute | solution.py:492

commit v14 on v13

--- a/solution.py
+++ b/solution.py
@@ -203,9 +203,13 @@
 
 def row_products(y):
     pieces = parts2(y)
-    high, low = pieces[:PAD], pieces[PAD:]
-    gram = fold2(mm(pieces, high, NT)) + mm(high, low, NT)
-    return [jnp.broadcast_to(gram[:, k : k + 1], (PAD, 128)) for k in range(CHI)]
+    gram = mm(pieces, pieces, NT)
+    near, cross = fold2(gram[:, :PAD]), gram[:PAD, PAD:]
+    return [
+        jnp.broadcast_to(near[:, k : k + 1], (PAD, 128))
+        + jnp.broadcast_to(cross[:, k : k + 1], (PAD, 128))
+        for k in range(CHI)
+    ]
 
 
 def line(x, k):

time: 37.8 us -> 37.6 us (level)
  no operation moved by 1% of the time
where the time goes in v14:
time: 37.6 us; the launch traced here: 37.5 us
  starting transfers between devices  16.4 us (44%)
  Pallas kernels  12 us (32%)
  waiting for transfers between devices  7.36 us (20%)
  local copies, waits for them, and re-layouts  0.92 us (2%)
  between operations  0.79 us (2%)
    ppermute x3, starting transfers between devices, from_bond(): return lax.ppermute(array, ('row', 'col'), pairs)  12 us
    pallas_call x18, Pallas kernels, run(): pl.pallas_call(kernel, out_shape=[jax.ShapeDtypeStruct(s, d) for s, d in...  12 us
    ppermute x6, starting transfers between devices, from_partner(): return lax.ppermute(array, 'row', [(i, i ^ flip) for i in range(count)])  4.4 us
    ppermute x3, waiting for transfers between devices, from_bond(): return lax.ppermute(array, ('row', 'col'), pairs)  4.03 us
    ppermute x6, waiting for transfers between devices, from_partner(): return lax.ppermute(array, 'row', [(i, i ^ flip) for i in range(count)])  3.32 us
    unnamed x4, local copies, waits for them, and re-layouts  0.92 us
  transfers between devices with their start and end apart: 9, of which 9 were waited for; matrix products, arithmetic and copies ran while one was open for 0% of the time, Pallas kernels for 13%

profile of v14, /device:TPU:0, one launch (start us, length us, event | category | flops | bytes accessed | tf_op | source)
XLA Modules:
  0.0 37.5 jit_solution(9431151310239879107)
XLA Ops:
  0.6 0.6 %collective-permute-start = (f32[144,144]{1,0:T(8,128)}, f32[144,144]{1,0:T(8,128)S(1)}, u32[]{:S(2)}, u32[]{:S(2)}) collective-permute-start(f32[144,144]{1,0:T(8,128)} %bitcast.2), channel_id=1, source_target_pairs={{0,4},{4,0},{8,12},{12,8},{16,20},{20,16},{24,28},{28,24},{1,5},{5... | collective-permute-start | bytes 248840 | tf_op jit(solution)/shard_map/ppermute | solution.py:496
  1.2 0.0 copy-start
  1.2 0.9 %copy-done = f32[1,1,144,144]{3,2,1,0:T(8,128)S(1)} copy-done((f32[1,1,144,144]{3,2,1,0:T(8,128)S(1)}, f32[1,1,144,144]{3,2,1,0:T(8,128)}, u32[]{:S(2)}) %copy-start) | copy-done | bytes 82968
  2.1 0.2 shard_map.41.own
  2.3 0.0 copy-start.1
  2.3 0.1 collective-permute-done.other
  2.4 1.0 %shard_map.42 = (bf16[192,256]{1,0:T(8,128)(2,1)S(1)}, bf16[192,256]{1,0:T(8,128)(2,1)S(1)}, bf16[168,128]{1,0:T(8,128)(2,1)S(1)}) custom-call(bf16[192,256]{1,0:T(8,128)(2,1)S(1)} %shard_map.41.own, f32[144,144]{1,0:T(8,128)S(1)} %collective-permute-done.other), custom_call_target="tpu_custom_call" | custom-call | flops 100000000 | bytes 1000000 | tf_op jit(solution)/shard_map/pallas_call | solution.py:481
  3.4 4.8 %collective-permute-start.1 = (bf16[168,128]{1,0:T(8,128)(2,1)S(1)}, bf16[168,128]{1,0:T(8,128)(2,1)S(1)}, u32[]{:S(2)}, u32[]{:S(2)}) collective-permute-start(bf16[168,128]{1,0:T(8,128)(2,1)S(1)} %get-tuple-element.40.gram), channel_id=1, source_target_pairs={{0,7},{1,4},{2,5},{3,6},{4,1},{5,2},{6,3},{7,0},{8,13},{9,14},{10,... | collective-permute-start | bytes 129032 | tf_op jit(solution)/shard_map/ppermute | solution.py:513
  8.1 0.0 copy-done.1
  8.1 0.5 %shard_map.43 = (bf16[192,256]{1,0:T(8,128)(2,1)S(1)}, bf16[192,256]{1,0:T(8,128)(2,1)S(1)}, f32[32,256]{1,0:T(8,128)S(1)}, bf16[256,256]{1,0:T(8,128)(2,1)S(1)}...) custom-call(bf16[192,256]{1,0:T(8,128)(2,1)S(1)} %get-tuple-element.38.own, ...), custom_call_target="tpu_custom_call" | custom-call | flops 100000000 | bytes 1000000 | tf_op jit(solution)/shard_map/pallas_call | solution.py:481
  8.6 1.3 %collective-permute-done.1.other = bf16[168,128]{1,0:T(8,128)(2,1)S(1)} collective-permute-done((bf16[168,128]{1,0:T(8,128)(2,1)S(1)}, bf16[168,128]{1,0:T(8,128)(2,1)S(1)}, u32[]{:S(2)}, u32[]{:S(2)}) %collective-permute-start.1) | collective-permute-done | bytes 43040 | tf_op jit(solution)/shard_map/ppermute | solution.py:513
  9.9 0.8 %shard_map.44.left = bf16[16,256]{1,0:T(8,128)(2,1)S(1)} custom-call(bf16[192,256]{1,0:T(8,128)(2,1)S(1)} %get-tuple-element.43.own, f32[16,256]{1,0:T(8,128)S(1)} %get-tuple-element.44.own_image, f32[8,128]{1,0:T(8,128)S(1)} %get-tuple-element.45.own_trace, bf16[168,128]{1,0:T(8,128)(2,1)S(1)} %collective-permute-done.1.other, ...), custom_call_target="tpu_custom_call" | custom-call | flops 100000000 | bytes 1000000 | tf_op jit(solution)/shard_map/pallas_call | solution.py:481
  10.7 0.1 collective-permute-start.2
  10.8 1.0 %shard_map.45.second = bf16[192,1792]{1,0:T(8,128)(2,1)S(1)} custom-call(bf16[192,256]{1,0:T(8,128)(2,1)S(1)} %get-tuple-element.41.turned, bf16[192,256]{1,0:T(8,128)(2,1)S(1)} %get-tuple-element.42.lower, bf16[16,256]{1,0:T(8,128)(2,1)S(1)} %shard_map.44.left), custom_call_target="tpu_custom_call" | custom-call | flops 100000000 | bytes 1000000 | tf_op jit(solution)/shard_map/pallas_call | solution.py:481
  11.8 0.2 collective-permute-done.2.right
  12.0 0.4 %shard_map.46.own = bf16[168,128]{1,0:T(8,128)(2,1)S(1)} custom-call(bf16[192,1792]{1,0:T(8,128)(2,1)S(1)} %shard_map.45.second, bf16[16,256]{1,0:T(8,128)(2,1)S(1)} %collective-permute-done.2.right), custom_call_target="tpu_custom_call" | custom-call | flops 100000000 | bytes 1000000 | tf_op jit(solution)/shard_map/pallas_call | solution.py:481
  12.4 1.8 %collective-permute-start.3 = (bf16[168,128]{1,0:T(8,128)(2,1)S(1)}, bf16[168,128]{1,0:T(8,128)(2,1)S(1)}, u32[]{:S(2)}, u32[]{:S(2)}) collective-permute-start(bf16[168,128]{1,0:T(8,128)(2,1)S(1)} %shard_map.46.own), channel_id=1, source_target_pairs={{0,12},{4,8},{8,4},{12,0},{16,28},{20,24},{24,20},{28,16},{1,13},{... | collective-permute-start | bytes 129032 | tf_op jit(solution)/shard_map/ppermute | solution.py:496
  14.1 0.4 shard_map.47
  14.5 1.4 %collective-permute-done.3.other = bf16[168,128]{1,0:T(8,128)(2,1)S(1)} collective-permute-done((bf16[168,128]{1,0:T(8,128)(2,1)S(1)}, bf16[168,128]{1,0:T(8,128)(2,1)S(1)}, u32[]{:S(2)}, u32[]{:S(2)}) %collective-permute-start.3) | collective-permute-done | bytes 43040 | tf_op jit(solution)/shard_map/ppermute | solution.py:496
  15.9 0.7 %shard_map.48 = (bf16[168,128]{1,0:T(8,128)(2,1)S(1)}, f32[8,128]{1,0:T(8,128)S(1)}) custom-call(bf16[192,256]{1,0:T(8,128)(2,1)S(1)} %get-tuple-element.49.product, f32[8,128]{1,0:T(8,128)S(1)} %get-tuple-element.50.mean.refs_0_, bf16[168,128]{1,0:T(8,128)(2,1)S(1)} %collective-permute-done.3.other), custom_call_target="tpu_custom_call" | custom-call | flops 100000000 | bytes 1000000 | tf_op jit(solution)/shard_map/pallas_call | solution.py:481
  16.6 3.6 %collective-permute-start.4 = (bf16[168,128]{1,0:T(8,128)(2,1)S(1)}, bf16[168,128]{1,0:T(8,128)(2,1)S(1)}, u32[]{:S(2)}, u32[]{:S(2)}) collective-permute-start(bf16[168,128]{1,0:T(8,128)(2,1)S(1)} %get-tuple-element.51.gram), channel_id=1, source_target_pairs={{0,7},{1,4},{2,5},{3,6},{4,1},{5,2},{6,3},{7,0},{8,13},{9,14},{10,... | collective-permute-start | bytes 129032 | tf_op jit(solution)/shard_map/ppermute | solution.py:513
  20.3 0.4 %shard_map.49 = (bf16[192,256]{1,0:T(8,128)(2,1)S(1)}, bf16[192,256]{1,0:T(8,128)(2,1)S(1)}, f32[32,256]{1,0:T(8,128)S(1)}, bf16[256,256]{1,0:T(8,128)(2,1)S(1)}...) custom-call(bf16[192,256]{1,0:T(8,128)(2,1)S(1)} %get-tuple-element.48.own, ...), custom_call_target="tpu_custom_call" | custom-call | flops 100000000 | bytes 1000000 | tf_op jit(solution)/shard_map/pallas_call | solution.py:481
  20.7 1.3 %collective-permute-done.4.other = bf16[168,128]{1,0:T(8,128)(2,1)S(1)} collective-permute-done((bf16[168,128]{1,0:T(8,128)(2,1)S(1)}, bf16[168,128]{1,0:T(8,128)(2,1)S(1)}, u32[]{:S(2)}, u32[]{:S(2)}) %collective-permute-start.4) | collective-permute-done | bytes 43040 | tf_op jit(solution)/shard_map/ppermute | solution.py:513
  22.0 0.8 %shard_map.50.left = bf16[16,256]{1,0:T(8,128)(2,1)S(1)} custom-call(bf16[192,256]{1,0:T(8,128)(2,1)S(1)} %get-tuple-element.54.own, f32[16,256]{1,0:T(8,128)S(1)} %get-tuple-element.55.own_image, f32[8,128]{1,0:T(8,128)S(1)} %get-tuple-element.56.own_trace, bf16[168,128]{1,0:T(8,128)(2,1)S(1)} %collective-permute-done.4.other, ...), custom_call_target="tpu_custom_call" | custom-call | flops 100000000 | bytes 1000000 | tf_op jit(solution)/shard_map/pallas_call | solution.py:481
  22.7 0.1 collective-permute-start.5
  22.8 1.0 %shard_map.51.second = bf16[192,1792]{1,0:T(8,128)(2,1)S(1)} custom-call(bf16[192,256]{1,0:T(8,128)(2,1)S(1)} %get-tuple-element.52.turned, bf16[192,256]{1,0:T(8,128)(2,1)S(1)} %get-tuple-element.53.lower, bf16[16,256]{1,0:T(8,128)(2,1)S(1)} %shard_map.50.left), custom_call_target="tpu_custom_call" | custom-call | flops 100000000 | bytes 1000000 | tf_op jit(solution)/shard_map/pallas_call | solution.py:481
  23.8 0.2 collective-permute-done.5.right
  24.0 0.4 %shard_map.52.own = bf16[168,128]{1,0:T(8,128)(2,1)S(1)} custom-call(bf16[192,1792]{1,0:T(8,128)(2,1)S(1)} %shard_map.51.second, bf16[16,256]{1,0:T(8,128)(2,1)S(1)} %collective-permute-done.5.right, f32[8,128]{1,0:T(8,128)S(1)} %get-tuple-element.59.refs_0_), custom_call_target="tpu_custom_call" | custom-call | flops 100000000 | bytes 1000000 | tf_op jit(solution)/shard_map/pallas_call | solution.py:481
  24.4 1.9 %collective-permute-start.6 = (bf16[168,128]{1,0:T(8,128)(2,1)S(1)}, bf16[168,128]{1,0:T(8,128)(2,1)S(1)}, u32[]{:S(2)}, u32[]{:S(2)}) collective-permute-start(bf16[168,128]{1,0:T(8,128)(2,1)S(1)} %shard_map.52.own), channel_id=1, source_target_pairs={{0,20},{4,16},{8,28},{12,24},{16,4},{20,0},{24,12},{28,8},{1,21},{... | collective-permute-start | bytes 129032 | tf_op jit(solution)/shard_map/ppermute | solution.py:496
  26.3 0.4 shard_map.53
  26.7 1.3 %collective-permute-done.6.other = bf16[168,128]{1,0:T(8,128)(2,1)S(1)} collective-permute-done((bf16[168,128]{1,0:T(8,128)(2,1)S(1)}, bf16[168,128]{1,0:T(8,128)(2,1)S(1)}, u32[]{:S(2)}, u32[]{:S(2)}) %collective-permute-start.6) | collective-permute-done | bytes 43040 | tf_op jit(solution)/shard_map/ppermute | solution.py:496
  28.0 0.7 %shard_map.54 = (bf16[168,128]{1,0:T(8,128)(2,1)S(1)}, f32[8,128]{1,0:T(8,128)S(1)}) custom-call(bf16[192,256]{1,0:T(8,128)(2,1)S(1)} %get-tuple-element.61.product, f32[8,128]{1,0:T(8,128)S(1)} %get-tuple-element.62.mean.refs_1_, bf16[168,128]{1,0:T(8,128)(2,1)S(1)} %collective-permute-done.6.other), custom_call_target="tpu_custom_call" | custom-call | flops 100000000 | bytes 1000000 | tf_op jit(solution)/shard_map/pallas_call | solution.py:481
  28.7 3.6 %collective-permute-start.7 = (bf16[168,128]{1,0:T(8,128)(2,1)S(1)}, bf16[168,128]{1,0:T(8,128)(2,1)S(1)}, u32[]{:S(2)}, u32[]{:S(2)}) collective-permute-start(bf16[168,128]{1,0:T(8,128)(2,1)S(1)} %get-tuple-element.63.gram), channel_id=1, source_target_pairs={{0,7},{1,4},{2,5},{3,6},{4,1},{5,2},{6,3},{7,0},{8,13},{9,14},{10,... | collective-permute-start | bytes 129032 | tf_op jit(solution)/shard_map/ppermute | solution.py:513
  32.4 0.3 shard_map.55
  32.7 1.4 %collective-permute-done.7.other = bf16[168,128]{1,0:T(8,128)(2,1)S(1)} collective-permute-done((bf16[168,128]{1,0:T(8,128)(2,1)S(1)}, bf16[168,128]{1,0:T(8,128)(2,1)S(1)}, u32[]{:S(2)}, u32[]{:S(2)}) %collective-permute-start.7) | collective-permute-done | bytes 43040 | tf_op jit(solution)/shard_map/ppermute | solution.py:513
  34.1 0.8 %shard_map.56.left = bf16[16,256]{1,0:T(8,128)(2,1)S(1)} custom-call(bf16[192,256]{1,0:T(8,128)(2,1)S(1)} %get-tuple-element.66.own, f32[16,256]{1,0:T(8,128)S(1)} %get-tuple-element.67.own_image, f32[8,128]{1,0:T(8,128)S(1)} %get-tuple-element.68.own_trace, bf16[168,128]{1,0:T(8,128)(2,1)S(1)} %collective-permute-done.7.other, ...), custom_call_target="tpu_custom_call" | custom-call | flops 100000000 | bytes 1000000 | tf_op jit(solution)/shard_map/pallas_call | solution.py:481
  34.9 0.1 collective-permute-start.8
  34.9 1.0 %shard_map.57.second = bf16[192,1792]{1,0:T(8,128)(2,1)S(1)} custom-call(bf16[192,256]{1,0:T(8,128)(2,1)S(1)} %get-tuple-element.64.turned, bf16[192,256]{1,0:T(8,128)(2,1)S(1)} %get-tuple-element.65.lower, bf16[16,256]{1,0:T(8,128)(2,1)S(1)} %shard_map.56.left), custom_call_target="tpu_custom_call" | custom-call | flops 100000000 | bytes 1000000 | tf_op jit(solution)/shard_map/pallas_call | solution.py:481
  35.9 0.2 collective-permute-done.8.right
  36.1 1.4 %shard_map.58 = (f32[144,144]{1,0:T(8,128)}, f32[1,1]{1,0:T(1,128)}) custom-call(bf16[192,1792]{1,0:T(8,128)(2,1)S(1)} %shard_map.57.second, bf16[16,256]{1,0:T(8,128)(2,1)S(1)} %collective-permute-done.8.right, f32[8,128]{1,0:T(8,128)S(1)} %get-tuple-element.71.scale, f32[8,128]{1,0:T(8,128)S(1)} %get-tuple-element.50.mean.refs_0_, ...), custom_call_target="tpu_custom_call" | custom-call | flops 100000000 | bytes 1000000 | tf_op jit(solution)/shard_map/pallas_call | solution.py:481
Async XLA Ops:
  0.6 1.8 %collective-permute-start = (f32[144,144]{1,0:T(8,128)}, f32[144,144]{1,0:T(8,128)S(1)}, u32[]{:S(2)}, u32[]{:S(2)}) collective-permute-start(f32[144,144]{1,0:T(8,128)} %bitcast.2), channel_id=1, source_target_pairs={{0,4},{4,0},{8,12},{12,8},{16,20},{20,16},{24,28},{28,24},{1,5},{5... | collective-permute-start | bytes 248840 | tf_op jit(solution)/shard_map/ppermute | solution.py:496
  1.2 0.9 %copy-start = (f32[1,1,144,144]{3,2,1,0:T(8,128)S(1)}, f32[1,1,144,144]{3,2,1,0:T(8,128)}, u32[]{:S(2)}) copy-start(f32[1,1,144,144]{3,2,1,0:T(8,128)} %param.2) | copy-start | bytes 248836
  2.3 5.8 %copy-start.1 = (f32[3,12,144]{2,1,0:T(8,128)S(1)}, f32[3,12,144]{2,1,0:T(8,128)}, u32[]{:S(2)}) copy-start(f32[3,12,144]{2,1,0:T(8,128)} %start.5) | copy-start | bytes 62212
  3.4 6.6 %collective-permute-start.1 = (bf16[168,128]{1,0:T(8,128)(2,1)S(1)}, bf16[168,128]{1,0:T(8,128)(2,1)S(1)}, u32[]{:S(2)}, u32[]{:S(2)}) collective-permute-start(bf16[168,128]{1,0:T(8,128)(2,1)S(1)} %get-tuple-element.40.gram), channel_id=1, source_target_pairs={{0,7},{1,4},{2,5},{3,6},{4,1},{5,2},{6,3},{7,0},{8,13},{9,14},{10,... | collective-permute-start | bytes 129032 | tf_op jit(solution)/shard_map/ppermute | solution.py:513
  10.7 1.2 %collective-permute-start.2 = (bf16[16,256]{1,0:T(8,128)(2,1)S(1)}, bf16[16,256]{1,0:T(8,128)(2,1)S(1)}, u32[]{:S(2)}, u32[]{:S(2)}) collective-permute-start(bf16[16,256]{1,0:T(8,128)(2,1)S(1)} %shard_map.44.left), channel_id=1, source_target_pairs={{0,4},{4,0},{8,12},{12,8},{16,20},{20,16},{24,28},{28,24},{1,5},{5... | collective-permute-start | bytes 24584 | tf_op jit(solution)/shard_map/ppermute | solution.py:496
  12.4 3.5 %collective-permute-start.3 = (bf16[168,128]{1,0:T(8,128)(2,1)S(1)}, bf16[168,128]{1,0:T(8,128)(2,1)S(1)}, u32[]{:S(2)}, u32[]{:S(2)}) collective-permute-start(bf16[168,128]{1,0:T(8,128)(2,1)S(1)} %shard_map.46.own), channel_id=1, source_target_pairs={{0,12},{4,8},{8,4},{12,0},{16,28},{20,24},{24,20},{28,16},{1,13},{... | collective-permute-start | bytes 129032 | tf_op jit(solution)/shard_map/ppermute | solution.py:496
  16.6 5.3 %collective-permute-start.4 = (bf16[168,128]{1,0:T(8,128)(2,1)S(1)}, bf16[168,128]{1,0:T(8,128)(2,1)S(1)}, u32[]{:S(2)}, u32[]{:S(2)}) collective-permute-start(bf16[168,128]{1,0:T(8,128)(2,1)S(1)} %get-tuple-element.51.gram), channel_id=1, source_target_pairs={{0,7},{1,4},{2,5},{3,6},{4,1},{5,2},{6,3},{7,0},{8,13},{9,14},{10,... | collective-permute-start | bytes 129032 | tf_op jit(solution)/shard_map/ppermute | solution.py:513
  22.7 1.2 %collective-permute-start.5 = (bf16[16,256]{1,0:T(8,128)(2,1)S(1)}, bf16[16,256]{1,0:T(8,128)(2,1)S(1)}, u32[]{:S(2)}, u32[]{:S(2)}) collective-permute-start(bf16[16,256]{1,0:T(8,128)(2,1)S(1)} %shard_map.50.left), channel_id=1, source_target_pairs={{0,4},{4,0},{8,12},{12,8},{16,20},{20,16},{24,28},{28,24},{1,5},{5... | collective-permute-start | bytes 24584 | tf_op jit(solution)/shard_map/ppermute | solution.py:496
  24.4 3.6 %collective-permute-start.6 = (bf16[168,128]{1,0:T(8,128)(2,1)S(1)}, bf16[168,128]{1,0:T(8,128)(2,1)S(1)}, u32[]{:S(2)}, u32[]{:S(2)}) collective-permute-start(bf16[168,128]{1,0:T(8,128)(2,1)S(1)} %shard_map.52.own), channel_id=1, source_target_pairs={{0,20},{4,16},{8,28},{12,24},{16,4},{20,0},{24,12},{28,8},{1,21},{... | collective-permute-start | bytes 129032 | tf_op jit(solution)/shard_map/ppermute | solution.py:496
  28.7 5.4 %collective-permute-start.7 = (bf16[168,128]{1,0:T(8,128)(2,1)S(1)}, bf16[168,128]{1,0:T(8,128)(2,1)S(1)}, u32[]{:S(2)}, u32[]{:S(2)}) collective-permute-start(bf16[168,128]{1,0:T(8,128)(2,1)S(1)} %get-tuple-element.63.gram), channel_id=1, source_target_pairs={{0,7},{1,4},{2,5},{3,6},{4,1},{5,2},{6,3},{7,0},{8,13},{9,14},{10,... | collective-permute-start | bytes 129032 | tf_op jit(solution)/shard_map/ppermute | solution.py:513
  34.9 1.2 %collective-permute-start.8 = (bf16[16,256]{1,0:T(8,128)(2,1)S(1)}, bf16[16,256]{1,0:T(8,128)(2,1)S(1)}, u32[]{:S(2)}, u32[]{:S(2)}) collective-permute-start(bf16[16,256]{1,0:T(8,128)(2,1)S(1)} %shard_map.56.left), channel_id=1, source_target_pairs={{0,4},{4,0},{8,12},{12,8},{16,20},{20,16},{24,28},{28,24},{1,5},{5... | collective-permute-start | bytes 24584 | tf_op jit(solution)/shard_map/ppermute | solution.py:496
